TPU v7x, 32 devices: a whole 2x2x4 slice. The times are simulated.
32 devices in a mesh: fsdp: 2 (over x), ctx: 4 (over z), tp: 4 (over y, core).
Axes of the slice: x: 2, y: 2, z: 4, core: 2. Of those that a mesh axis runs over, the one named last changes fastest.
Arguments:
- entering_activations: bfloat16 [4, 2048, 2048], P('fsdp', 'ctx'), may hold values from -6 to 6
- document_indices: int32 [4, 2048], P('fsdp'), may hold values from 0 to 10, never falling along the last dimension, each value on 1 to 800 neighbouring positions
- acceptor_matrix: bfloat16 [2048, 2048], P(('fsdp', 'ctx'), 'tp'), may hold values from -0.125 to 0.125
- lookup_matrix: bfloat16 [2048, 2048], P(('fsdp', 'ctx'), 'tp'), may hold values from -0.125 to 0.125
- payload_matrix: bfloat16 [2048, 2048], P(('fsdp', 'ctx'), 'tp'), may hold values from -0.125 to 0.125
- valve_matrix: bfloat16 [2048, 2048], P(('fsdp', 'ctx'), 'tp'), may hold values from -0.125 to 0.125
- result_matrix: bfloat16 [2048, 2048], P('tp', ('fsdp', 'ctx')), may hold values from -0.25 to 0.25
- ffn_lookup_matrix: bfloat16 [2048, 7168], P(('fsdp', 'ctx'), 'tp'), may hold values from -0.125 to 0.125
- ffn_payload_matrix: bfloat16 [7168, 2048], P('tp', ('fsdp', 'ctx')), may hold values from -0.0625 to 0.0625
- ffn_acceptor_matrix: bfloat16 [2048, 2048], P(('fsdp', 'ctx'), 'tp'), may hold values from -0.125 to 0.125
- first_standardize_scaling: float32 [2048], replicated, may hold values from 0.5 to 1.5
- first_standardize_offset: float32 [2048], replicated, may hold values from -0.8 to 0.8
- acceptor_lerp_factor: float32 [2048], replicated, may hold values from 0.05 to 0.95
- lookup_lerp_factor: float32 [2048], replicated, may hold values from 0.05 to 0.95
- payload_lerp_factor: float32 [2048], replicated, may hold values from 0.05 to 0.95
- valve_lerp_factor: float32 [2048], replicated, may hold values from 0.05 to 0.95
- token_fading: float32 [2048], replicated, may hold values from 0.9 to 0.9998
- diagonal_reward: float32 [2048], replicated, may hold values from -2 to 2
- subspace_standardize_scaling: float32 [2048], replicated, may hold values from 0.5 to 1.5
- subspace_standardize_offset: float32 [2048], replicated, may hold values from -0.8 to 0.8
- second_standardize_scaling: float32 [2048], replicated, may hold values from 0.5 to 1.5
- second_standardize_offset: float32 [2048], replicated, may hold values from -0.8 to 0.8
- ffn_lookup_lerp: float32 [2048], replicated, may hold values from 0.05 to 0.95
- ffn_acceptor_lerp: float32 [2048], replicated, may hold values from 0.05 to 0.95
- upstream_derivative: bfloat16 [4, 2048, 2048], P('fsdp', 'ctx', 'tp'), may hold values from -6 to 6
Outputs:
- result: bfloat16 [4, 2048, 2048], P('fsdp', 'ctx', 'tp')
- grad_inputs: float32 [4, 2048, 2048], P('fsdp', 'ctx')
- grad_time_recept: float32 [2048, 2048], P(('fsdp', 'ctx'), 'tp')
- grad_time_key: float32 [2048, 2048], P(('fsdp', 'ctx'), 'tp')
- grad_time_value: float32 [2048, 2048], P(('fsdp', 'ctx'), 'tp')
- grad_time_gate: float32 [2048, 2048], P(('fsdp', 'ctx'), 'tp')
- grad_time_output: float32 [2048, 2048], P('tp', ('fsdp', 'ctx'))
- grad_chan_key: float32 [2048, 7168], P(('fsdp', 'ctx'), 'tp')
- grad_chan_value: float32 [7168, 2048], P('tp', ('fsdp', 'ctx'))
- grad_chan_recept: float32 [2048, 2048], P(('fsdp', 'ctx'), 'tp')
- grad_first_gain: float32 [2048], P(('fsdp', 'ctx'))
- grad_first_bias: float32 [2048], P(('fsdp', 'ctx'))
- grad_mix_recept: float32 [2048], P(('fsdp', 'ctx'))
- grad_mix_key: float32 [2048], P(('fsdp', 'ctx'))
- grad_mix_value: float32 [2048], P(('fsdp', 'ctx'))
- grad_mix_gate: float32 [2048], P(('fsdp', 'ctx'))
- grad_time_decay: float32 [2048], P(('fsdp', 'ctx'))
- grad_time_bonus: float32 [2048], P(('fsdp', 'ctx'))
- grad_group_gain: float32 [2048], P(('fsdp', 'ctx'))
- grad_group_bias: float32 [2048], P(('fsdp', 'ctx'))
- grad_second_gain: float32 [2048], P(('fsdp', 'ctx'))
- grad_second_bias: float32 [2048], P(('fsdp', 'ctx'))
- grad_shift_key: float32 [2048], P(('fsdp', 'ctx'))
- grad_shift_recept: float32 [2048], P(('fsdp', 'ctx'))
Inputs may be any that keep to these rules, and one draw needn't show every extreme that they name: `document_indices`: segment numbers never fall along a sequence; each document has 1 to min(800, 2048) positions.
All inputs are finite; a program needn't handle non-finite values.
Results may differ from a plain program's by a relative error of at most 0.029.
Values may be sent and summed in bfloat16 or wider, within the bound.
A program may use at most 320 MiB of HBM per device.

v0:
```python
from functools import partial

import jax
import jax.numpy as jnp
from jax import lax
from jax.sharding import PartitionSpec as P

SUBSPACE_SIZE = 64
BLOCK = 64


HIGH = lax.Precision.HIGHEST
EPS = 1e-05
GROUP_EPS = 4.0


def shifted(x, axis, by):
    count = lax.axis_size(axis)
    pairs = [(i, i + by) for i in range(count) if 0 <= i + by < count]
    return lax.ppermute(x, axis, pairs)


def carried_in(x, axis, combine, identity):
    count, place = (lax.axis_size(axis), lax.axis_index(axis))
    everything = jax.tree.map(
        lambda part, kind: lax.all_gather(part.astype(kind), axis), x, (jnp.bfloat16, jnp.bfloat16)
    )
    start = jax.tree.map(
        lambda part, zero: jnp.broadcast_to(jnp.asarray(zero, part.dtype), part.shape), x, identity
    )

    def lap(k, before):
        reached = k < place
        new = combine(
            before, jax.tree.map(lambda part, own: part[k].astype(own.dtype), everything, x)
        )
        return jax.tree.map(lambda a, b: jnp.where(reached, a, b), new, before)

    return lax.fori_loop(0, count, lap, start)


def carried_in_2(x, axis, combine, identity):
    count, place = (lax.axis_size(axis), lax.axis_index(axis))
    everything = jax.tree.map(
        lambda part, kind: lax.all_gather(part.astype(kind), axis),
        x,
        jax.tree.map(lambda a: jnp.bfloat16 if a.dtype == jnp.float32 else a.dtype, x),
    )
    start = jax.tree.map(
        lambda part, zero: jnp.broadcast_to(jnp.asarray(zero, part.dtype), part.shape), x, identity
    )

    def lap(k, before):
        at = count - 1 - k
        reached = at > place
        new = combine(
            before, jax.tree.map(lambda part, own: part[at].astype(own.dtype), everything, x)
        )
        return jax.tree.map(lambda a, b: jnp.where(reached, a, b), new, before)

    return lax.fori_loop(0, count, lap, start)


def matmul(left, right):
    return jnp.dot(left, right, preferred_element_type=jnp.float32)


def matmul_tn(left, right):
    return lax.dot_general(
        left, right, (((0,), (0,)), ((), ())), preferred_element_type=jnp.float32
    )


def matmul_nt(left, right):
    return lax.dot_general(
        left, right, (((1,), (1,)), ((), ())), preferred_element_type=jnp.float32
    )


def fading_payload_tile(fading_exponent, reward_addend, memory_matrix_kept, fragment_collection):
    acceptor_entries, lookup_share, payload_share, seg_block, seg_start = fragment_collection
    length = acceptor_entries.shape[0]
    offsets = jnp.arange(length, dtype=jnp.float32)[:, None, None]
    rising = jnp.exp(offsets * fading_exponent)
    falling = jnp.exp(-(offsets + 1.0) * fading_exponent)
    closing = jnp.exp((float(length) - 1.0 - offsets) * fading_exponent)
    query_dec = acceptor_entries * rising
    key_dec = lookup_share * falling
    scores = jnp.einsum("thi,shi->hts", query_dec, key_dec, precision=HIGH)
    later_mask = (
        jnp.arange(length, dtype=jnp.int32)[:, None] > jnp.arange(length, dtype=jnp.int32)[None, :]
    )
    same_doc = seg_block[:, None] == seg_block[None, :]
    coefficient_collection = jnp.where(later_mask & same_doc, scores, jnp.zeros_like(scores))
    immediate_addend = jnp.sum(
        acceptor_entries * reward_addend * lookup_share, axis=-1, keepdims=True
    )
    live_mask = (seg_block == seg_start).astype(jnp.float32)[:, None, None]
    result = (
        jnp.einsum("hts,shj->thj", coefficient_collection, payload_share, precision=HIGH)
        + immediate_addend * payload_share
    )
    result = result + live_mask * jnp.einsum(
        "thi,hij->thj", query_dec, memory_matrix_kept, precision=HIGH
    )
    ending = (seg_block == seg_block[-1]).astype(jnp.float32)[:, None, None]
    key_end = lookup_share * closing * ending
    carried = jnp.exp(float(length) * fading_exponent) * live_mask[-1]
    new_state = carried[:, :, None] * memory_matrix_kept + jnp.einsum(
        "shi,shj->hij", key_end, payload_share, precision=HIGH
    )
    return (new_state, result)


def fading_payload_sweeper(
    acceptor_entries,
    lookup_share,
    payload_share,
    fading_coefficients,
    reward_coefficients,
    memory_matrix_kept,
    document_sweeper,
    document_begins,
):
    length = acceptor_entries.shape[0]
    blocks = length // BLOCK
    fading_exponent = jnp.log(fading_coefficients)

    def to_blocks(array):
        return array.reshape((blocks, BLOCK) + array.shape[1:])

    seg_blocks = document_sweeper.reshape(blocks, BLOCK)
    seg_starts = jnp.concatenate([document_begins, seg_blocks[:-1, -1]])
    scan_update = jax.checkpoint(partial(fading_payload_tile, fading_exponent, reward_coefficients))
    final_memory_matrix, block_outs = lax.scan(
        scan_update,
        memory_matrix_kept,
        (
            to_blocks(acceptor_entries),
            to_blocks(lookup_share),
            to_blocks(payload_share),
            seg_blocks,
            seg_starts,
        ),
    )
    return (block_outs.reshape(acceptor_entries.shape), final_memory_matrix)


def weighted_value_piece(
    segment_present,
    document_begins,
    acceptor_entries,
    lookup_share,
    payload_share,
    decay_quantity,
    reward_amount,
    incoming_state,
):
    mapped_function = jax.vmap(fading_payload_sweeper, in_axes=(0, 0, 0, None, None, 0, 0, 0))
    return mapped_function(
        acceptor_entries,
        lookup_share,
        payload_share,
        decay_quantity,
        reward_amount,
        incoming_state,
        segment_present,
        document_begins,
    )


def chain_step(earlier, later):
    return (earlier[0] * later[0], later[0][..., None] * earlier[1] + later[1])


def layer_norm(values, gain, bias_term):
    centered = values - jnp.mean(values, -1, keepdims=True)
    inverse = lax.rsqrt(jnp.mean(centered * centered, -1, keepdims=True) + EPS)
    unit_vals = centered * inverse
    return (unit_vals * gain + bias_term, unit_vals, inverse)


def norm_back(d_out, gain, unit_vals, inverse):
    scaled = d_out * gain
    d_in = inverse * (
        scaled
        - jnp.mean(scaled, -1, keepdims=True)
        - unit_vals * jnp.mean(scaled * unit_vals, -1, keepdims=True)
    )
    return (d_in, jnp.sum(d_out * unit_vals, axis=(0, 1)), jnp.sum(d_out, axis=(0, 1)))


def sharding_spec(vector, embedding_extent, start):
    return lax.dynamic_update_slice_in_dim(
        jnp.zeros((embedding_extent,), jnp.float32), vector.reshape(-1), start, 0
    )


def per_device(
    entering_activations,
    document_indices,
    acceptor_matrix,
    lookup_matrix,
    payload_matrix,
    valve_matrix,
    result_matrix,
    ffn_lookup_matrix,
    ffn_payload_matrix,
    ffn_acceptor_matrix,
    first_standardize_scaling,
    first_standardize_offset,
    acceptor_lerp_factor,
    lookup_lerp_factor,
    payload_lerp_factor,
    valve_lerp_factor,
    token_fading,
    diagonal_reward,
    subspace_standardize_scaling,
    subspace_standardize_offset,
    second_standardize_scaling,
    second_standardize_offset,
    ffn_lookup_lerp,
    ffn_acceptor_lerp,
    upstream_derivative,
):
    seqs_here, piece_len, embedding_extent = entering_activations.shape
    token_count = seqs_here * piece_len
    tp_count = lax.axis_size("tp")
    fourth_extent = embedding_extent // tp_count
    heads_here = fourth_extent // SUBSPACE_SIZE
    sharded_layout = lax.axis_index("tp") * fourth_extent
    ctx_place = lax.axis_index("ctx") * piece_len
    padded_seg = jnp.concatenate(
        [jnp.full((seqs_here, 1), -1, jnp.int32), document_indices], axis=1
    )
    segment_present = lax.dynamic_slice_in_dim(document_indices, ctx_place, piece_len, 1)
    seg_before = lax.dynamic_slice_in_dim(padded_seg, ctx_place, piece_len, 1)
    document_begins = seg_before[:, :1]
    keep_mask = (segment_present == seg_before).astype(jnp.float32)[:, :, None]
    w_recept, w_key, w_value, w_gate, w_chankey, w_chanrecept, w_output, w_chanvalue = (
        lax.all_gather(acceptor_matrix, ("fsdp", "ctx"), axis=0, tiled=True),
        lax.all_gather(lookup_matrix, ("fsdp", "ctx"), axis=0, tiled=True),
        lax.all_gather(payload_matrix, ("fsdp", "ctx"), axis=0, tiled=True),
        lax.all_gather(valve_matrix, ("fsdp", "ctx"), axis=0, tiled=True),
        lax.all_gather(ffn_lookup_matrix, ("fsdp", "ctx"), axis=0, tiled=True),
        lax.all_gather(ffn_acceptor_matrix, ("fsdp", "ctx"), axis=0, tiled=True),
        lax.all_gather(result_matrix, ("fsdp", "ctx"), axis=1, tiled=True),
        lax.all_gather(ffn_payload_matrix, ("fsdp", "ctx"), axis=1, tiled=True),
    )
    residual = entering_activations.astype(jnp.float32)
    normed, unit_one, inv_one = layer_norm(
        residual, first_standardize_scaling, first_standardize_offset
    )
    edge_one = shifted(normed[:, -1], "ctx", 1)
    prev_one = jnp.concatenate([edge_one[:, None], normed[:, :-1]], axis=1) * keep_mask
    delta_one = normed - prev_one
    mix_list = (acceptor_lerp_factor, lookup_lerp_factor, payload_lerp_factor, valve_lerp_factor)
    mixed_in = [
        (prev_one + mixer * delta_one).astype(jnp.bfloat16).reshape(token_count, embedding_extent)
        for mixer in mix_list
    ]
    recept_low = matmul(mixed_in[0], w_recept).astype(jnp.bfloat16)
    key_low = matmul(mixed_in[1], w_key).astype(jnp.bfloat16)
    value_low = matmul(mixed_in[2], w_value).astype(jnp.bfloat16)
    gate_pre = matmul(mixed_in[3], w_gate)
    gate_act = jax.nn.silu(gate_pre)
    split_shape = (seqs_here, piece_len, heads_here, SUBSPACE_SIZE)
    recept_f = recept_low.astype(jnp.float32).reshape(split_shape)
    key_f = key_low.astype(jnp.float32).reshape(split_shape)
    value_f = value_low.astype(jnp.float32).reshape(split_shape)
    decay_quantity = lax.dynamic_slice_in_dim(
        token_fading, sharded_layout, fourth_extent, 0
    ).reshape(heads_here, SUBSPACE_SIZE)
    reward_amount = lax.dynamic_slice_in_dim(
        diagonal_reward, sharded_layout, fourth_extent, 0
    ).reshape(heads_here, SUBSPACE_SIZE)
    ggain_q = lax.dynamic_slice_in_dim(
        subspace_standardize_scaling, sharded_layout, fourth_extent, 0
    ).reshape(heads_here, SUBSPACE_SIZE)
    gbias_q = lax.dynamic_slice_in_dim(
        subspace_standardize_offset, sharded_layout, fourth_extent, 0
    ).reshape(heads_here, SUBSPACE_SIZE)
    fading_exponent = jnp.log(decay_quantity)
    offsets = jnp.arange(piece_len, dtype=jnp.float32)[:, None, None]
    closing = jnp.exp((float(piece_len) - 1.0 - offsets) * fading_exponent)
    rising = jnp.exp(offsets * fading_exponent)
    ending = (segment_present == segment_present[:, -1:]).astype(jnp.float32)[:, :, None, None]
    carry_sums = jnp.einsum("bshi,bshj->bhij", key_f * closing * ending, value_f, precision=HIGH)
    alive_mask = (segment_present[:, -1] == document_begins[:, 0]).astype(jnp.float32)[
        :, None, None
    ]
    carry_mult = jnp.exp(float(piece_len) * fading_exponent) * alive_mask
    identity = (jnp.ones_like(carry_mult), jnp.zeros_like(carry_sums))
    incoming = carried_in((carry_mult, carry_sums), "ctx", chain_step, identity)[1]
    wkv_out, weighted_value_backward = jax.vjp(
        partial(weighted_value_piece, segment_present, document_begins),
        recept_f,
        key_f,
        value_f,
        decay_quantity,
        reward_amount,
        incoming,
    )
    timemix_result = wkv_out[0]
    centered = timemix_result - jnp.mean(timemix_result, -1, keepdims=True)
    inv_group = lax.rsqrt(jnp.mean(centered * centered, -1, keepdims=True) + GROUP_EPS)
    unit_group = centered * inv_group
    grouped = (unit_group * ggain_q + gbias_q).reshape(token_count, fourth_extent)
    joined_low = (grouped * gate_act).astype(jnp.bfloat16)
    mixed_out = lax.psum(matmul(joined_low, w_output).astype(jnp.bfloat16), "tp").astype(
        jnp.float32
    )
    middle = residual + mixed_out.reshape(seqs_here, piece_len, embedding_extent)
    normed_two, unit_two, inv_two = layer_norm(
        middle, second_standardize_scaling, second_standardize_offset
    )
    edge_two = shifted(normed_two[:, -1], "ctx", 1)
    prev_two = jnp.concatenate([edge_two[:, None], normed_two[:, :-1]], axis=1) * keep_mask
    delta_two = normed_two - prev_two
    key_in = (
        (prev_two + ffn_lookup_lerp * delta_two)
        .astype(jnp.bfloat16)
        .reshape(token_count, embedding_extent)
    )
    rec_in = (
        (prev_two + ffn_acceptor_lerp * delta_two)
        .astype(jnp.bfloat16)
        .reshape(token_count, embedding_extent)
    )
    key_pre = matmul(key_in, w_chankey)
    hidden = jnp.square(jax.nn.relu(key_pre)).astype(jnp.bfloat16)
    chan_sum = lax.psum_scatter(
        matmul(hidden, w_chanvalue).astype(jnp.bfloat16), "tp", scatter_dimension=1, tiled=True
    ).astype(jnp.float32)
    rec_gate = jax.nn.sigmoid(matmul(rec_in, w_chanrecept))
    middle_q = lax.dynamic_slice_in_dim(
        middle.reshape(token_count, embedding_extent), sharded_layout, fourth_extent, 1
    )
    result = (
        (middle_q + rec_gate * chan_sum)
        .astype(jnp.bfloat16)
        .reshape(seqs_here, piece_len, fourth_extent)
    )
    d_result = upstream_derivative.astype(jnp.float32).reshape(token_count, fourth_extent)
    d_chan = (d_result * rec_gate).astype(jnp.bfloat16)
    d_rec_pre = (d_result * chan_sum * rec_gate * (1.0 - rec_gate)).astype(jnp.bfloat16)
    d_chan_full = lax.all_gather(d_chan, "tp", axis=1, tiled=True)
    d_hidden = matmul_nt(d_chan_full, w_chanvalue)
    d_key_pre = (d_hidden * 2.0 * jax.nn.relu(key_pre)).astype(jnp.bfloat16)
    grad_chanvalue = matmul_tn(hidden, d_chan_full)
    grad_chankey = matmul_tn(key_in, d_key_pre)
    grad_chanrecept = matmul_tn(rec_in, d_rec_pre)
    full_shape = (seqs_here, piece_len, embedding_extent)
    d_key_in = matmul_nt(d_key_pre, w_chankey).reshape(full_shape)
    d_rec_in = matmul_nt(d_rec_pre, w_chanrecept).reshape(full_shape)
    d_norm_two = d_key_in * ffn_lookup_lerp + d_rec_in * ffn_acceptor_lerp
    d_prev_two = (
        d_key_in * (1.0 - ffn_lookup_lerp) + d_rec_in * (1.0 - ffn_acceptor_lerp)
    ) * keep_mask
    back_two = shifted(d_prev_two[:, 0], "ctx", -1)
    d_norm_two = d_norm_two + jnp.concatenate([d_prev_two[:, 1:], back_two[:, None]], axis=1)
    d_middle_part, g_second_gain, g_second_bias = norm_back(
        d_norm_two, second_standardize_scaling, unit_two, inv_two
    )
    chan_small_part = jnp.stack(
        [
            g_second_gain,
            g_second_bias,
            jnp.sum(d_key_in * delta_two, axis=(0, 1)),
            jnp.sum(d_rec_in * delta_two, axis=(0, 1)),
        ]
    )
    flat_part = d_middle_part.reshape(token_count, embedding_extent)
    own_cols = lax.dynamic_slice_in_dim(flat_part, sharded_layout, fourth_extent, 1) + d_result
    flat_part = lax.dynamic_update_slice_in_dim(flat_part, own_cols, sharded_layout, 1)
    d_middle, chan_small = (
        lax.psum(flat_part.astype(jnp.bfloat16), "tp").astype(jnp.float32),
        lax.psum(chan_small_part.astype(jnp.bfloat16), "tp").astype(jnp.float32),
    )
    d_mixed = d_middle.astype(jnp.bfloat16)
    grad_output = matmul_tn(joined_low, d_mixed)
    d_joined = matmul_nt(d_mixed, w_output)
    d_gate_act = d_joined * grouped
    d_grouped = (d_joined * gate_act).reshape(split_shape)
    attention_gradient, g_ggain, g_gbias = norm_back(d_grouped, ggain_q, unit_group, inv_group)
    gate_sig = jax.nn.sigmoid(gate_pre)
    d_gate_pre = (d_gate_act * gate_sig * (1.0 + gate_pre * (1.0 - gate_sig))).astype(jnp.bfloat16)
    live_mask = (segment_present == document_begins).astype(jnp.float32)[:, :, None, None]
    local_grad = jnp.einsum(
        "bthi,bthj->bhij", recept_f * rising * live_mask, attention_gradient, precision=HIGH
    )
    outgoing_state = carried_in_2((carry_mult, local_grad), "ctx", chain_step, identity)[1]
    (
        receptance_gradient,
        key_gradient,
        value_gradient,
        decay_gradient,
        reward_derivative,
        discarded_state,
    ) = weighted_value_backward((attention_gradient, outgoing_state))
    d_lows = [
        item.astype(jnp.bfloat16).reshape(token_count, fourth_extent)
        for item in (receptance_gradient, key_gradient, value_gradient)
    ] + [d_gate_pre]
    weights_time = (w_recept, w_key, w_value, w_gate)
    grads_time = [matmul_tn(mixed, grad_low) for mixed, grad_low in zip(mixed_in, d_lows)]
    d_mix_ins = [
        matmul_nt(grad_low, weight).reshape(full_shape)
        for grad_low, weight in zip(d_lows, weights_time)
    ]
    d_norm_one = sum((grad_in * mixer for grad_in, mixer in zip(d_mix_ins, mix_list)))
    d_prev_one = (
        sum((grad_in * (1.0 - mixer) for grad_in, mixer in zip(d_mix_ins, mix_list))) * keep_mask
    )
    back_one = shifted(d_prev_one[:, 0], "ctx", -1)
    d_norm_one = d_norm_one + jnp.concatenate([d_prev_one[:, 1:], back_one[:, None]], axis=1)
    d_input_part, g_first_gain, g_first_bias = norm_back(
        d_norm_one, first_standardize_scaling, unit_one, inv_one
    )
    time_small_part = jnp.stack(
        [g_first_gain, g_first_bias]
        + [jnp.sum(grad_in * delta_one, axis=(0, 1)) for grad_in in d_mix_ins]
        + [
            sharding_spec(decay_gradient, embedding_extent, sharded_layout),
            sharding_spec(reward_derivative, embedding_extent, sharded_layout),
            sharding_spec(g_ggain, embedding_extent, sharded_layout),
            sharding_spec(g_gbias, embedding_extent, sharded_layout),
        ]
    )
    d_input_sum, time_small = (
        lax.psum(
            d_input_part.reshape(token_count, embedding_extent).astype(jnp.bfloat16), "tp"
        ).astype(jnp.float32),
        lax.psum(time_small_part.astype(jnp.bfloat16), "tp").astype(jnp.float32),
    )
    grad_inputs = (d_middle + d_input_sum).reshape(full_shape)
    small_all = jnp.concatenate([time_small, chan_small], axis=0)
    all_done = (
        lax.psum_scatter(
            grads_time[0].astype(jnp.bfloat16), ("fsdp", "ctx"), scatter_dimension=0, tiled=True
        ).astype(jnp.float32),
        lax.psum_scatter(
            grads_time[1].astype(jnp.bfloat16), ("fsdp", "ctx"), scatter_dimension=0, tiled=True
        ).astype(jnp.float32),
        lax.psum_scatter(
            grads_time[2].astype(jnp.bfloat16), ("fsdp", "ctx"), scatter_dimension=0, tiled=True
        ).astype(jnp.float32),
        lax.psum_scatter(
            grads_time[3].astype(jnp.bfloat16), ("fsdp", "ctx"), scatter_dimension=0, tiled=True
        ).astype(jnp.float32),
        lax.psum_scatter(
            grad_output.astype(jnp.bfloat16), ("fsdp", "ctx"), scatter_dimension=1, tiled=True
        ).astype(jnp.float32),
        lax.psum_scatter(
            grad_chankey.astype(jnp.bfloat16), ("fsdp", "ctx"), scatter_dimension=0, tiled=True
        ).astype(jnp.float32),
        lax.psum_scatter(
            grad_chanvalue.astype(jnp.bfloat16), ("fsdp", "ctx"), scatter_dimension=1, tiled=True
        ).astype(jnp.float32),
        lax.psum_scatter(
            grad_chanrecept.astype(jnp.bfloat16), ("fsdp", "ctx"), scatter_dimension=0, tiled=True
        ).astype(jnp.float32),
        lax.psum_scatter(
            small_all.astype(jnp.bfloat16), ("fsdp", "ctx"), scatter_dimension=1, tiled=True
        ).astype(jnp.float32),
    )
    (
        g_recept,
        g_key,
        g_value,
        g_gate,
        g_output,
        g_chankey,
        g_chanvalue,
        g_chanrecept,
        small_owned,
    ) = all_done
    return (
        result,
        grad_inputs,
        g_recept,
        g_key,
        g_value,
        g_gate,
        g_output,
        g_chankey,
        g_chanvalue,
        g_chanrecept,
        small_owned[0],
        small_owned[1],
        small_owned[2],
        small_owned[3],
        small_owned[4],
        small_owned[5],
        small_owned[6],
        small_owned[7],
        small_owned[8],
        small_owned[9],
        small_owned[10],
        small_owned[11],
        small_owned[12],
        small_owned[13],
    )


def solution(mesh):
    return jax.shard_map(
        per_device,
        mesh=mesh,
        in_specs=(
            P("fsdp", "ctx", None),
            P("fsdp", None),
            P(("fsdp", "ctx"), "tp"),
            P(("fsdp", "ctx"), "tp"),
            P(("fsdp", "ctx"), "tp"),
            P(("fsdp", "ctx"), "tp"),
            P("tp", ("fsdp", "ctx")),
            P(("fsdp", "ctx"), "tp"),
            P("tp", ("fsdp", "ctx")),
            P(("fsdp", "ctx"), "tp"),
            P(),
            P(),
            P(),
            P(),
            P(),
            P(),
            P(),
            P(),
            P(),
            P(),
            P(),
            P(),
            P(),
            P(),
            P("fsdp", "ctx", "tp"),
        ),
        out_specs=(
            P("fsdp", "ctx", "tp"),
            P("fsdp", "ctx", None),
            P(("fsdp", "ctx"), "tp"),
            P(("fsdp", "ctx"), "tp"),
            P(("fsdp", "ctx"), "tp"),
            P(("fsdp", "ctx"), "tp"),
            P("tp", ("fsdp", "ctx")),
            P(("fsdp", "ctx"), "tp"),
            P("tp", ("fsdp", "ctx")),
            P(("fsdp", "ctx"), "tp"),
            P(("fsdp", "ctx")),
            P(("fsdp", "ctx")),
            P(("fsdp", "ctx")),
            P(("fsdp", "ctx")),
            P(("fsdp", "ctx")),
            P(("fsdp", "ctx")),
            P(("fsdp", "ctx")),
            P(("fsdp", "ctx")),
            P(("fsdp", "ctx")),
            P(("fsdp", "ctx")),
            P(("fsdp", "ctx")),
            P(("fsdp", "ctx")),
            P(("fsdp", "ctx")),
            P(("fsdp", "ctx")),
        ),
        check_vma=False,
    )
```

profile of v0, /device:TPU:0, one launch (start us, length us, event | category | flops | bytes accessed | tf_op | source)
XLA Modules:
  0.0 2092.5 jit_solution(2081542702184679693)
XLA Ops:
  19.9 5.0 collective-permute-start
  31.5 14.0 all_gather.45
  45.6 13.3 add_convert_fusion.3
  62.0 5.2 fusion.116
  71.5 40.3 %all-gather.14.cloned.1.call-done = bf16[2048,512]{1,0:T(8,128)(2,1)} async-done(((bf16[256,512]{1,0:T(8,128)(2,1)}), bf16[2048,512]{1,0:T(8,128)(2,1)}) %all-gather.14.cloned.1.call-update) | async-done | bytes 2097168 | tf_op jit(solution)/shard_map/all_gather | solution.py:243
  111.8 5.2 convolution_convert_fusion.11
  121.5 40.1 %all-gather.16.cloned.1.call-done = bf16[2048,512]{1,0:T(8,128)(2,1)} async-done(((bf16[256,512]{1,0:T(8,128)(2,1)}), bf16[2048,512]{1,0:T(8,128)(2,1)}) %all-gather.16.cloned.1.call-update) | async-done | bytes 2097168 | tf_op jit(solution)/shard_map/all_gather | solution.py:241
  161.6 5.2 fusion.115
  178.2 29.0 %all-gather = bf16[8,8,64,64]{3,2,1,0:T(8,128)(2,1)S(1)} all-gather(bf16[2,8,64,64]{3,2,1,0:T(8,128)(2,1)S(1)} %fusion.122), channel_id=2, replica_groups=mesh['fsdp'=2,'ctx'=4,'tp'=4] {'ctx'}, dimensions={0}, use_global_device_ids=true | all-gather | bytes 655360 | tf_op jit(solution)/shard_map/all_gather | solution.py:26
  208.9 5.2 copy.374
  215.2 4.9 copy_bitcast_fusion
  220.1 98.2 %while.75 = (s32[]{:T(128)}, f32[2,8,64,64]{3,2,1,0:T(8,128)S(1)}, f32[8,2,64,8,64]{4,2,3,1,0:T(8,128)}, f32[8,2,8,64,64]{4,3,2,1,0:T(8,128)}, f32[1,8,64]{2,1,0...) while((s32[]{:T(128)}, f32[2,8,64,64]{3,2,1,0:T(8,128)S(1)}, ...), condition=%wide.region_6.7_spmd.clone.clone, body=%wide.region_4.6_spmd.clone.clone.sunk | while | flops 202365632 | bytes 9354611 | solution.py:135
  331.2 7.5 copy.240
  342.2 9.1 multiply_convert_fusion.3
  351.3 6.3 convolution_convert_fusion.3
  359.1 84.5 %all-reduce.6.cloned.1.call-done = bf16[2,512,2048]{2,1,0:T(8,128)(2,1)} async-done(((bf16[2,512,2048]{2,1,0:T(8,128)(2,1)}), bf16[2,512,2048]{2,1,0:T(8,128)(2,1)}) %all-reduce.6.cloned.1.call-update) | async-done | bytes 4194320 | tf_op jit(solution)/shard_map/psum | solution.py:310
  443.6 4.8 fusion.132
  462.1 11.4 add_convert_fusion
  473.4 84.3 %all-gather.24.cloned.1.call-done = bf16[2048,1792]{1,0:T(8,128)(2,1)} async-done(((bf16[256,1792]{1,0:T(8,128)(2,1)}), bf16[2048,1792]{1,0:T(8,128)(2,1)}) %all-gather.24.cloned.1.call-update) | async-done | bytes 7340048 | tf_op jit(solution)/shard_map/all_gather | solution.py:245
  557.7 13.4 fusion.140
  571.1 99.0 %all-gather.26.cloned.1.call-done = bf16[1792,2048]{1,0:T(8,128)(2,1)} async-done(((bf16[1792,256]{1,0:T(8,128)(2,1)}), bf16[1792,2048]{1,0:T(8,128)(2,1)}) %all-gather.26.cloned.1.call-update) | async-done | bytes 7340048 | tf_op jit(solution)/shard_map/all_gather | solution.py:248
  670.1 13.5 convolution_convert_fusion.2
  683.6 35.9 %all-gather.22.cloned.1.call-done = bf16[2048,512]{1,0:T(8,128)(2,1)} async-done(((bf16[256,512]{1,0:T(8,128)(2,1)}), bf16[2048,512]{1,0:T(8,128)(2,1)}) %all-gather.22.cloned.1.call-update) | async-done | bytes 2097168 | tf_op jit(solution)/shard_map/all_gather | solution.py:246
  719.5 45.4 %reduce-scatter.11.cloned.1.call-done = bf16[1024,512]{1,0:T(8,128)(2,1)} async-done(((bf16[1024,2048]{1,0:T(8,128)(2,1)}), bf16[1024,512]{1,0:T(8,128)(2,1)}) %reduce-scatter.11.cloned.1.call-update) | async-done | bytes 1048592 | tf_op jit(solution)/shard_map/reduce_scatter | solution.py:332
  764.9 7.8 fusion.97
  772.8 7.8 fusion.142
  780.6 26.8 %all-gather.28.cloned.1.call-done = bf16[1024,2048]{1,0:T(8,128)(2,1)} async-done(((bf16[1024,512]{1,0:T(8,128)(2,1)}), bf16[1024,2048]{1,0:T(8,128)(2,1)}) %all-gather.28.cloned.1.call-update) | async-done | bytes 4194320 | tf_op jit(solution)/shard_map/all_gather | solution.py:347
  807.3 14.5 multiply_convert_fusion
  821.8 13.3 fusion.141
  835.1 15.7 multiply_reduce_fusion.11
  853.3 8.4 slice.145
  861.8 16.9 multiply_reduce_fusion.12
  878.7 9.6 fusion.133
  888.4 9.5 subtract_multiply_fusion
  904.7 5.9 copy.297
  925.8 62.0 %all-reduce.8.cloned.1.call-done = bf16[1024,2048]{1,0:T(8,128)(2,1)} async-done(((bf16[1024,2048]{1,0:T(8,128)(2,1)}), bf16[1024,2048]{1,0:T(8,128)(2,1)}) %all-reduce.8.cloned.1.call-update) | async-done | bytes 4194320 | tf_op jit(solution)/shard_map/psum | solution.py:377
  987.8 9.0 fusion.134
  1012.8 4.5 reshape.619
  1021.5 22.5 %all-gather.1 = bf16[8,8,64,64]{3,2,1,0:T(8,128)(2,1)S(1)} all-gather(bf16[2,8,64,64]{3,2,1,0:T(8,128)(2,1)S(1)} %fusion.117), channel_id=3, replica_groups=mesh['fsdp'=2,'ctx'=4,'tp'=4] {'ctx'}, dimensions={0}, use_global_device_ids=true | all-gather | bytes 655360 | tf_op jit(solution)/shard_map/all_gather | solution.py:45
  1048.3 9.6 fusion.94
  1063.6 154.8 %while.74 = (s32[]{:T(128)}, f32[8,64]{1,0:T(8,128)S(1)}, f32[8,64]{1,0:T(8,128)S(1)}, f32[2,8,64,64]{3,2,1,0:T(8,128)S(1)}, bf16[8,2,64,8,64]{2,4,3,1,0:T(8,128...) while((s32[]{:T(128)}, f32[8,64]{1,0:T(8,128)S(1)}, ...), condition=%wide.region_32.33_spmd.clone, body=%wide.region_20.32_spmd.clone.sunk | while | flops 456254720 | bytes 20558400 | solution.py:135
  1233.8 7.7 fusion.106
  1241.5 5.6 fusion.102
  1247.2 5.6 fusion.143
  1252.8 24.1 %multiply_reduce_fusion.13 = (bf16[2048]{0:T(1024)(128)(2,1)S(1)}, bf16[2048]{0:T(1024)(128)(2,1)S(1)}, bf16[2048]{0:T(1024)(128)(2,1)S(1)}, bf16[2048]{0:T(1024...) fusion(f32[1024,2048]{1,0:T(8,128)} %fusion.143, f32[2,512]{1,0:T(2,128)S(1)} %copy-done.49, ...), kind=kOutput, calls=%fused_computation.165 | convolution fusion | flops 2197807104 | bytes 66138112 | tf_op jit(solution)/shard_map/dot_general | solution.py:75
  1286.5 15.5 fusion.88
  1302.2 11.4 all-reduce.1
  1314.4 7.3 fusion.87
  1322.9 5.9 convolution_convert_fusion.6
  1328.9 6.1 convolution_convert_fusion.5
  1336.3 6.0 convolution_convert_fusion.8
  1343.9 6.0 convolution_convert_fusion.7
  1351.3 5.9 convolution_convert_fusion.9
  1357.3 13.2 convolution_convert_fusion
  1370.6 12.9 convolution_convert_fusion.1
  1390.3 65.3 %all-reduce.10.cloned.1.call-done = bf16[1024,2048]{1,0:T(8,128)(2,1)} async-done(((bf16[1024,2048]{1,0:T(8,128)(2,1)}), bf16[1024,2048]{1,0:T(8,128)(2,1)}) %all-reduce.10.cloned.1.call-update) | async-done | bytes 4194320 | tf_op jit(solution)/shard_map/psum | solution.py:431
  1455.6 8.8 convert_add_fusion.3
  1464.4 63.0 %reduce-scatter.19.cloned.1.call-done = bf16[256,512]{1,0:T(8,128)(2,1)} async-done(((bf16[2048,512]{1,0:T(8,128)(2,1)}), bf16[256,512]{1,0:T(8,128)(2,1)}) %reduce-scatter.19.cloned.1.call-update) | async-done | bytes 262160 | tf_op jit(solution)/shard_map/reduce_scatter | solution.py:448
  1529.2 69.5 %reduce-scatter.21.cloned.1.call-done = bf16[512,256]{1,0:T(8,128)(2,1)} async-done(((bf16[512,2048]{1,0:T(8,128)(2,1)}), bf16[512,256]{1,0:T(8,128)(2,1)}) %reduce-scatter.21.cloned.1.call-update) | async-done | bytes 262160 | tf_op jit(solution)/shard_map/reduce_scatter | solution.py:451
  1600.5 69.1 %reduce-scatter.15.cloned.1.call-done = bf16[256,512]{1,0:T(8,128)(2,1)} async-done(((bf16[2048,512]{1,0:T(8,128)(2,1)}), bf16[256,512]{1,0:T(8,128)(2,1)}) %reduce-scatter.15.cloned.1.call-update) | async-done | bytes 262160 | tf_op jit(solution)/shard_map/reduce_scatter | solution.py:442
  1671.4 69.1 %reduce-scatter.17.cloned.1.call-done = bf16[256,512]{1,0:T(8,128)(2,1)} async-done(((bf16[2048,512]{1,0:T(8,128)(2,1)}), bf16[256,512]{1,0:T(8,128)(2,1)}) %reduce-scatter.17.cloned.1.call-update) | async-done | bytes 262160 | tf_op jit(solution)/shard_map/reduce_scatter | solution.py:445
  1742.3 69.1 %reduce-scatter.13.cloned.1.call-done = bf16[256,512]{1,0:T(8,128)(2,1)} async-done(((bf16[2048,512]{1,0:T(8,128)(2,1)}), bf16[256,512]{1,0:T(8,128)(2,1)}) %reduce-scatter.13.cloned.1.call-update) | async-done | bytes 262160 | tf_op jit(solution)/shard_map/reduce_scatter | solution.py:439
  1813.2 134.2 %reduce-scatter.25.cloned.1.call-done = bf16[1792,256]{1,0:T(8,128)(2,1)} async-done(((bf16[1792,2048]{1,0:T(8,128)(2,1)}), bf16[1792,256]{1,0:T(8,128)(2,1)}) %reduce-scatter.25.cloned.1.call-update) | async-done | bytes 917520 | tf_op jit(solution)/shard_map/reduce_scatter | solution.py:457
  1949.9 133.0 %reduce-scatter.23.cloned.1.call-done = bf16[256,1792]{1,0:T(8,128)(2,1)} async-done(((bf16[2048,1792]{1,0:T(8,128)(2,1)}), bf16[256,1792]{1,0:T(8,128)(2,1)}) %reduce-scatter.23.cloned.1.call-update) | async-done | bytes 917520 | tf_op jit(solution)/shard_map/reduce_scatter | solution.py:454
  (798 shorter events, 439.7 us)
Async XLA Ops:
  7.2 54.8 %all-gather.12.cloned.1.call-start = ((), (), s32[]{:S(2)}) async-start(), calls=%async_computation.10 | async-start | bytes 2359296 | tf_op jit(solution)/shard_map/all_gather | solution.py:242
  7.9 103.9 %all-gather.14.cloned.1.call-start = ((), (), s32[]{:S(2)}) async-start(), calls=%async_computation.11 | async-start | bytes 2359296 | tf_op jit(solution)/shard_map/all_gather | solution.py:243
  8.7 152.9 %all-gather.16.cloned.1.call-start = ((), (), s32[]{:S(2)}) async-start(), calls=%async_computation.12 | async-start | bytes 2359296 | tf_op jit(solution)/shard_map/all_gather | solution.py:241
  9.4 332.7 %all-gather.18.cloned.1.call-start = ((), (), s32[]{:S(2)}) async-start(), calls=%async_computation.13 | async-start | bytes 2359296 | tf_op jit(solution)/shard_map/all_gather | solution.py:244
  10.0 341.3 %all-gather.20.cloned.1.call-start = ((), (), s32[]{:S(2)}) async-start(), calls=%async_computation.14 | async-start | bytes 2359296 | tf_op jit(solution)/shard_map/all_gather | solution.py:247
  13.5 32.1 %copy-start.41 = (f32[2,512]{1,0:T(2,128)}, f32[2,512]{1,0:T(2,128)S(1)}, u32[]{:S(2)}) copy-start(f32[2,512]{1,0:T(2,128)S(1)} %broadcast_multiply_fusion.10) | copy-start | bytes 12292
  14.8 30.8 %copy-start.43 = (f32[2,512]{1,0:T(2,128)}, f32[2,512]{1,0:T(2,128)S(1)}, u32[]{:S(2)}) copy-start(f32[2,512]{1,0:T(2,128)S(1)} %add_rsqrt_fusion.2) | copy-start | bytes 12292
  14.8 10.2 copy-start.55
  14.8 30.8 %copy-start.56 = (f32[2048]{0:T(1024)S(1)}, f32[2048]{0:T(1024)}, u32[]{:S(2)}) copy-start(f32[2048]{0:T(1024)} %param.45) | copy-start | bytes 24580
  14.8 30.8 %copy-start.58 = (f32[2048]{0:T(1024)S(1)}, f32[2048]{0:T(1024)}, u32[]{:S(2)}) copy-start(f32[2048]{0:T(1024)} %param.46) | copy-start | bytes 24580
  14.8 30.8 %copy-start.60 = (f32[2048]{0:T(1024)S(1)}, f32[2048]{0:T(1024)}, u32[]{:S(2)}) copy-start(f32[2048]{0:T(1024)} %param.47) | copy-start | bytes 24580
  14.8 30.8 %copy-start.62 = (f32[2048]{0:T(1024)S(1)}, f32[2048]{0:T(1024)}, u32[]{:S(2)}) copy-start(f32[2048]{0:T(1024)} %param.48) | copy-start | bytes 24580
  19.9 25.6 %collective-permute-start = (f32[2,2048]{1,0:T(2,128)S(1)}, f32[2,2048]{1,0:T(2,128)S(1)}, u32[]{:S(2)}, u32[]{:S(2)}) collective-permute-start(f32[2,2048]{1,0:T(2,128)S(1)} %bitcast.473), channel_id=1, source_target_pairs={{0,4},{4,8},{8,12},{1,5},{5,9},{9,13},{2,6},{6,10},{10,14},{3,7},{... | collective-permute-start | bytes 49160 | tf_op jit(solution)/shard_map/ppermute | solution.py:20
  24.9 418.7 %all-reduce.6.cloned.1.call-start = ((), (), s32[]{:S(2)}) async-start(), calls=%async_computation.15 | async-start | bytes 8388608 | tf_op jit(solution)/shard_map/psum | solution.py:310
  26.0 809.1 %copy-start.48 = (f32[2,512]{1,0:T(2,128)}, f32[2,512]{1,0:T(2,128)S(1)}, u32[]{:S(2)}) copy-start(f32[2,512]{1,0:T(2,128)S(1)} %get-tuple-element.1174) | copy-start | bytes 12292
  26.9 18.6 copy-start.65
  30.5 15.0 copy-start.67
  31.3 310.9 %copy-start.72 = (f32[512]{0:T(512)}, f32[512]{0:T(512)S(1)}, u32[]{:S(2)}) copy-start(f32[512]{0:T(512)S(1)} %dynamic_slice.155) | copy-start | bytes 6148
  45.5 13.4 copy-start.46
  166.8 6.7 copy-start.19
  208.9 6.3 copy-start.12
  318.3 6.0 copy-start.26
  318.3 6.0 copy-start.64
  318.3 6.0 copy-start.71
  357.5 200.1 %all-gather.24.cloned.1.call-start = ((), (), s32[]{:S(2)}) async-start(), calls=%async_computation.17 | async-start | bytes 8257536 | tf_op jit(solution)/shard_map/all_gather | solution.py:245
  358.3 311.8 %all-gather.26.cloned.1.call-start = ((), (), s32[]{:S(2)}) async-start(), calls=%async_computation.18 | async-start | bytes 8257536 | tf_op jit(solution)/shard_map/all_gather | solution.py:248
  359.0 360.5 %all-gather.22.cloned.1.call-start = ((), (), s32[]{:S(2)}) async-start(), calls=%async_computation.16 | async-start | bytes 2359296 | tf_op jit(solution)/shard_map/all_gather | solution.py:246
  443.6 5.9 copy-start.7
  451.4 10.7 copy-start.53
  451.4 10.7 copy-start.54
  456.8 5.2 collective-permute-start.1
  460.3 304.5 %reduce-scatter.11.cloned.1.call-start = ((), (), s32[]{:S(2)}) async-start(), calls=%async_computation.19 | async-start | bytes 5242880 | tf_op jit(solution)/shard_map/reduce_scatter | solution.py:332
  683.5 81.3 %copy-start.31 = (bf16[2,512,512]{2,1,0:T(8,128)(2,1)S(1)}, bf16[2,512,512]{2,1,0:T(8,128)(2,1)}, u32[]{:S(2)}) copy-start(bf16[2,512,512]{2,1,0:T(8,128)(2,1)} %param.57) | copy-start | bytes 3145732
  683.6 123.8 %all-gather.28.cloned.1.call-start = ((), (), s32[]{:S(2)}) async-start(), calls=%async_computation.20 | async-start | bytes 5242880 | tf_op jit(solution)/shard_map/all_gather | solution.py:347
  772.7 7.9 copy-start.78
  772.7 215.1 %all-reduce.8.cloned.1.call-start = ((), (), s32[]{:S(2)}) async-start(), calls=%async_computation.21 | async-start | bytes 8388608 | tf_op jit(solution)/shard_map/psum | solution.py:377
  821.8 13.3 copy-start.10
  851.7 10.0 copy-start.2
  851.8 10.0 collective-permute-start.2
  888.4 9.5 copy-start.32
  901.0 482.5 %reduce-scatter.27.cloned.1.call-start = ((), (), s32[]{:S(2)}) async-start(), calls=%async_computation.30 | async-start | bytes 2359296 | tf_op jit(solution)/shard_map/reduce_scatter | solution.py:460
  921.8 66.0 %copy-start.73 = (f32[512]{0:T(512)S(1)}, f32[512]{0:T(512)}, u32[]{:S(2)}) copy-start(f32[512]{0:T(512)} %copy-done.72) | copy-start | bytes 6148
  925.6 463.0 %reduce-scatter.29.cloned.1.call-start = ((), (), s32[]{:S(2)}) async-start(), calls=%async_computation.31 | async-start | bytes 73728 | tf_op jit(solution)/shard_map/reduce_scatter | solution.py:463
  996.8 7.5 copy-start.36
  996.8 7.5 copy-start.38
  1021.5 26.8 %copy-start.29 = (f32[2,8,64,8]{2,3,0,1:T(8,128)S(1)}, f32[2,8,64,8]{2,3,0,1:T(8,128)}, u32[]{:S(2)}) copy-start(f32[2,8,64,8]{2,3,0,1:T(8,128)} %copy-done.28) | copy-start | bytes 98308
  1021.5 26.8 %copy-start.34 = (f32[2,8,64,8]{2,3,0,1:T(8,128)S(1)}, f32[2,8,64,8]{2,3,0,1:T(8,128)}, u32[]{:S(2)}) copy-start(f32[2,8,64,8]{2,3,0,1:T(8,128)} %copy-done.33) | copy-start | bytes 98308
  1231.8 9.7 copy-start.13
  1233.8 7.7 copy-start.74
  1252.8 24.1 %copy-start.66 = (f32[8,64]{1,0:T(8,128)S(1)}, f32[8,64]{1,0:T(8,128)}, u32[]{:S(2)}) copy-start(f32[8,64]{1,0:T(8,128)} %copy-done.65) | copy-start | bytes 6148
  1278.1 6.1 collective-permute-start.3
  1279.5 7.0 copy-start.9
  1314.3 141.3 %all-reduce.10.cloned.1.call-start = ((), (), s32[]{:S(2)}) async-start(), calls=%async_computation.22 | async-start | bytes 8388608 | tf_op jit(solution)/shard_map/psum | solution.py:431
  1321.7 7.2 copy-start.80
  1321.7 205.7 %reduce-scatter.19.cloned.1.call-start = ((), (), s32[]{:S(2)}) async-start(), calls=%async_computation.26 | async-start | bytes 2359296 | tf_op jit(solution)/shard_map/reduce_scatter | solution.py:448
  1328.8 6.2 copy-start.18
  1328.8 269.9 %reduce-scatter.21.cloned.1.call-start = ((), (), s32[]{:S(2)}) async-start(), calls=%async_computation.27 | async-start | bytes 2359296 | tf_op jit(solution)/shard_map/reduce_scatter | solution.py:451
  1335.0 334.6 %reduce-scatter.15.cloned.1.call-start = ((), (), s32[]{:S(2)}) async-start(), calls=%async_computation.24 | async-start | bytes 2359296 | tf_op jit(solution)/shard_map/reduce_scatter | solution.py:442
  1336.3 6.1 copy-start.16
  1342.4 398.1 %reduce-scatter.17.cloned.1.call-start = ((), (), s32[]{:S(2)}) async-start(), calls=%async_computation.25 | async-start | bytes 2359296 | tf_op jit(solution)/shard_map/reduce_scatter | solution.py:445
  1343.9 6.1 copy-start.14
  1350.0 461.4 %reduce-scatter.13.cloned.1.call-start = ((), (), s32[]{:S(2)}) async-start(), calls=%async_computation.23 | async-start | bytes 2359296 | tf_op jit(solution)/shard_map/reduce_scatter | solution.py:439
  1357.2 590.1 %reduce-scatter.25.cloned.1.call-start = ((), (), s32[]{:S(2)}) async-start(), calls=%async_computation.29 | async-start | bytes 8257536 | tf_op jit(solution)/shard_map/reduce_scatter | solution.py:457
  1370.6 712.3 %reduce-scatter.23.cloned.1.call-start = ((), (), s32[]{:S(2)}) async-start(), calls=%async_computation.28 | async-start | bytes 8257536 | tf_op jit(solution)/shard_map/reduce_scatter | solution.py:454
  (43 other events, 150.9 us)
Sparse Core Ops, SparseCore 0:
  10.1 51.8 all-gather.11
  64.1 47.6 all-gather.13
  113.9 47.6 all-gather.15
  163.6 54.0 all-gather.17
  219.5 49.5 all-gather.19
  357.7 85.8 all-reduce.5
  445.7 111.9 all-gather.23
  559.7 110.3 all-gather.25
  672.2 47.2 all-gather.21
  721.9 42.9 reduce-scatter.10
  772.9 34.4 all-gather.27
  901.2 86.6 all-reduce.7
  991.4 68.7 reduce-scatter.26
  1314.4 54.3 reduce-scatter.28
  1371.1 84.5 all-reduce.9
  1459.0 68.3 reduce-scatter.18
  1530.8 67.8 reduce-scatter.20
  1602.1 67.3 reduce-scatter.14
  1673.1 67.3 reduce-scatter.16
  1743.9 67.4 reduce-scatter.12
  1815.0 132.3 reduce-scatter.24
  1950.9 131.8 reduce-scatter.22
where the time goes:
time: 2100 us; the launch traced here: 2090 us
  waiting for transfers between devices  1200 us (57%)
  matrix products  351 us (17%)
  other arithmetic  232 us (11%)
  local copies, waits for them, and re-layouts  202 us (10%)
  blocking collectives  76.9 us (4%)
    reduce_scatter x1, waiting for transfers between devices, per_device(): lax.psum_scatter(grad_chanvalue.astype(jnp.bfloat16), ('fsdp', 'ctx'), sc...  134 us
    reduce_scatter x1, waiting for transfers between devices, per_device(): lax.psum_scatter(grad_chankey.astype(jnp.bfloat16), ('fsdp', 'ctx'), scat...  133 us
    all_gather x1, waiting for transfers between devices, per_device(): lax.all_gather(ffn_payload_matrix, ('fsdp', 'ctx'), axis=1, tiled=True)  99 us
    dot_general x8, matrix products, matmul_nt(): lax.dot_general(left, right, (((1,), (1,)), ((), ())), preferred_element_...  87.4 us
    psum x1, waiting for transfers between devices, per_device(): lax.psum(matmul(joined_low, w_output).astype(jnp.bfloat16), 'tp')  84.5 us
    all_gather x1, waiting for transfers between devices, per_device(): lax.all_gather(ffn_lookup_matrix, ('fsdp', 'ctx'), axis=0, tiled=True)  84.3 us
    reduce_scatter x1, waiting for transfers between devices, per_device(): lax.psum_scatter(grad_output.astype(jnp.bfloat16), ('fsdp', 'ctx'), scatt...  69.5 us
    reduce_scatter x1, waiting for transfers between devices, per_device(): lax.psum_scatter(grads_time[2].astype(jnp.bfloat16), ('fsdp', 'ctx'), sca...  69.1 us
  transfers between devices with their start and end apart: 26, of which 19 were waited for; matrix products, arithmetic and copies ran while one was open for 32% of the time, Pallas kernels for 0%

commit v1 on v0

--- a/solution.py
+++ b/solution.py
@@ -20,45 +20,104 @@
     return lax.ppermute(x, axis, pairs)
 
 
-def carried_in(x, axis, combine, identity):
-    count, place = (lax.axis_size(axis), lax.axis_index(axis))
-    everything = jax.tree.map(
-        lambda part, kind: lax.all_gather(part.astype(kind), axis), x, (jnp.bfloat16, jnp.bfloat16)
-    )
-    start = jax.tree.map(
-        lambda part, zero: jnp.broadcast_to(jnp.asarray(zero, part.dtype), part.shape), x, identity
-    )
-
-    def lap(k, before):
-        reached = k < place
-        new = combine(
-            before, jax.tree.map(lambda part, own: part[k].astype(own.dtype), everything, x)
-        )
-        return jax.tree.map(lambda a, b: jnp.where(reached, a, b), new, before)
-
-    return lax.fori_loop(0, count, lap, start)
-
-
-def carried_in_2(x, axis, combine, identity):
-    count, place = (lax.axis_size(axis), lax.axis_index(axis))
-    everything = jax.tree.map(
-        lambda part, kind: lax.all_gather(part.astype(kind), axis),
-        x,
-        jax.tree.map(lambda a: jnp.bfloat16 if a.dtype == jnp.float32 else a.dtype, x),
-    )
-    start = jax.tree.map(
-        lambda part, zero: jnp.broadcast_to(jnp.asarray(zero, part.dtype), part.shape), x, identity
-    )
-
-    def lap(k, before):
-        at = count - 1 - k
-        reached = at > place
-        new = combine(
-            before, jax.tree.map(lambda part, own: part[at].astype(own.dtype), everything, x)
-        )
-        return jax.tree.map(lambda a, b: jnp.where(reached, a, b), new, before)
-
-    return lax.fori_loop(0, count, lap, start)
+def earlier_shift(x, axis, by):
+    count = lax.axis_size(axis)
+    return lax.ppermute(x, axis, [(i, i + by) for i in range(count) if 0 <= i + by < count])
+
+
+def carried(mult, sums, axis, toward):
+    count = lax.axis_size(axis)
+    low = (mult.astype(jnp.bfloat16), sums.astype(jnp.bfloat16))
+    arrived = [
+        jax.tree.map(lambda part: earlier_shift(part, axis, toward * by), low)
+        for by in range(1, count)
+    ]
+    state = jnp.zeros_like(sums)
+    for far_mult, far_sums in reversed(arrived):
+        state = far_mult.astype(jnp.float32)[..., None] * state + far_sums.astype(jnp.float32)
+    return state
+
+
+def partner(x, bit):
+    count = lax.axis_size("tp")
+    return lax.ppermute(x, "tp", [(i, i ^ bit) for i in range(count)])
+
+
+def halves(x, axis, bit):
+    size = x.shape[axis] // 2
+    mine = (lax.axis_index("tp") // bit) % 2
+    return (
+        lax.dynamic_slice_in_dim(x, mine * size, size, axis),
+        lax.dynamic_slice_in_dim(x, (1 - mine) * size, size, axis),
+    )
+
+
+def add_low(left, right):
+    return (left.astype(jnp.float32) + right.astype(jnp.float32)).astype(jnp.bfloat16)
+
+
+def ordered(mine, other, axis, bit):
+    first = (lax.axis_index("tp") // bit) % 2 == 0
+    return jnp.where(
+        first,
+        jnp.concatenate([mine, other], axis),
+        jnp.concatenate([other, mine], axis),
+    )
+
+
+def tp_sum(x):
+    mine, other = halves(x, 0, 1)
+    part = add_low(mine, partner(other, 1))
+    bit = 2
+    while bit < lax.axis_size("tp"):
+        part = add_low(part, partner(part, bit))
+        bit *= 2
+    return ordered(part, partner(part, 1), 0, 1)
+
+
+def whole_sum(x, axes):
+    for axis in axes:
+        count = lax.axis_size(axis)
+        bit = 1
+        while bit < count:
+            x = x + lax.ppermute(x, axis, [(i, i ^ bit) for i in range(count)])
+            bit *= 2
+    return x
+
+
+def tp_scatter(x):
+    count, place = lax.axis_size("tp"), lax.axis_index("tp")
+    width = x.shape[1] // count
+    parts = [
+        lax.dynamic_slice_in_dim(x, (place ^ relative) * width, width, 1)
+        for relative in range(count)
+    ]
+    bit = 1
+    while bit < count:
+        for relative in reversed(range(count)):
+            if relative & bit and relative & (bit - 1) == 0:
+                arrived = partner(parts[relative], bit)
+                parts[relative ^ bit] = add_low(parts[relative ^ bit], arrived)
+        bit *= 2
+    return parts[0]
+
+
+def tp_gather(x):
+    count, place = lax.axis_size("tp"), lax.axis_index("tp")
+    width = x.shape[1]
+    parts = {0: x}
+    bit = count // 2
+    while bit:
+        parts.update({relative ^ bit: partner(part, bit) for relative, part in parts.items()})
+        bit //= 2
+    whole = jnp.zeros((x.shape[0], width * count), x.dtype)
+    for relative, part in parts.items():
+        whole = lax.dynamic_update_slice_in_dim(whole, part, (place ^ relative) * width, 1)
+    return whole
+
+
+def after(value, *earlier):
+    return lax.optimization_barrier((value,) + earlier)
 
 
 def matmul(left, right):
@@ -167,10 +226,6 @@
         segment_present,
         document_begins,
     )
-
-
-def chain_step(earlier, later):
-    return (earlier[0] * later[0], later[0][..., None] * earlier[1] + later[1])
 
 
 def layer_norm(values, gain, bias_term):
@@ -237,16 +292,28 @@
     seg_before = lax.dynamic_slice_in_dim(padded_seg, ctx_place, piece_len, 1)
     document_begins = seg_before[:, :1]
     keep_mask = (segment_present == seg_before).astype(jnp.float32)[:, :, None]
-    w_recept, w_key, w_value, w_gate, w_chankey, w_chanrecept, w_output, w_chanvalue = (
-        lax.all_gather(acceptor_matrix, ("fsdp", "ctx"), axis=0, tiled=True),
-        lax.all_gather(lookup_matrix, ("fsdp", "ctx"), axis=0, tiled=True),
-        lax.all_gather(payload_matrix, ("fsdp", "ctx"), axis=0, tiled=True),
-        lax.all_gather(valve_matrix, ("fsdp", "ctx"), axis=0, tiled=True),
-        lax.all_gather(ffn_lookup_matrix, ("fsdp", "ctx"), axis=0, tiled=True),
-        lax.all_gather(ffn_acceptor_matrix, ("fsdp", "ctx"), axis=0, tiled=True),
-        lax.all_gather(result_matrix, ("fsdp", "ctx"), axis=1, tiled=True),
-        lax.all_gather(ffn_payload_matrix, ("fsdp", "ctx"), axis=1, tiled=True),
-    )
+    owners = ("fsdp", "ctx")
+    w_time = lax.all_gather(
+        jnp.concatenate(
+            [acceptor_matrix, lookup_matrix, payload_matrix, valve_matrix, result_matrix.T], axis=1
+        ),
+        owners,
+        axis=0,
+        tiled=True,
+    )
+    w_chan = lax.all_gather(
+        jnp.concatenate([ffn_acceptor_matrix, ffn_lookup_matrix, ffn_payload_matrix.T], axis=1),
+        owners,
+        axis=0,
+        tiled=True,
+    )
+    units = ffn_lookup_matrix.shape[1]
+    w_recept, w_key, w_value, w_gate, w_output_t = (
+        w_time[:, at * fourth_extent : (at + 1) * fourth_extent] for at in range(5)
+    )
+    w_chanrecept = w_chan[:, :fourth_extent]
+    w_chankey = w_chan[:, fourth_extent : fourth_extent + units]
+    w_chanvalue_t = w_chan[:, fourth_extent + units :]
     residual = entering_activations.astype(jnp.float32)
     normed, unit_one, inv_one = layer_norm(
         residual, first_standardize_scaling, first_standardize_offset
@@ -290,8 +357,7 @@
         :, None, None
     ]
     carry_mult = jnp.exp(float(piece_len) * fading_exponent) * alive_mask
-    identity = (jnp.ones_like(carry_mult), jnp.zeros_like(carry_sums))
-    incoming = carried_in((carry_mult, carry_sums), "ctx", chain_step, identity)[1]
+    incoming = carried(carry_mult, carry_sums, "ctx", 1)
     wkv_out, weighted_value_backward = jax.vjp(
         partial(weighted_value_piece, segment_present, document_begins),
         recept_f,
@@ -307,9 +373,7 @@
     unit_group = centered * inv_group
     grouped = (unit_group * ggain_q + gbias_q).reshape(token_count, fourth_extent)
     joined_low = (grouped * gate_act).astype(jnp.bfloat16)
-    mixed_out = lax.psum(matmul(joined_low, w_output).astype(jnp.bfloat16), "tp").astype(
-        jnp.float32
-    )
+    mixed_out = tp_sum(matmul_nt(joined_low, w_output_t).astype(jnp.bfloat16)).astype(jnp.float32)
     middle = residual + mixed_out.reshape(seqs_here, piece_len, embedding_extent)
     normed_two, unit_two, inv_two = layer_norm(
         middle, second_standardize_scaling, second_standardize_offset
@@ -327,12 +391,16 @@
         .astype(jnp.bfloat16)
         .reshape(token_count, embedding_extent)
     )
+    rec_gate = jax.nn.sigmoid(matmul(rec_in, w_chanrecept))
+    d_result = upstream_derivative.astype(jnp.float32).reshape(token_count, fourth_extent)
+    d_chan = (d_result * rec_gate).astype(jnp.bfloat16)
+    d_chan_full = tp_gather(d_chan)
     key_pre = matmul(key_in, w_chankey)
     hidden = jnp.square(jax.nn.relu(key_pre)).astype(jnp.bfloat16)
-    chan_sum = lax.psum_scatter(
-        matmul(hidden, w_chanvalue).astype(jnp.bfloat16), "tp", scatter_dimension=1, tiled=True
-    ).astype(jnp.float32)
-    rec_gate = jax.nn.sigmoid(matmul(rec_in, w_chanrecept))
+    grad_chanvalue = matmul_tn(hidden, d_chan_full).astype(jnp.bfloat16)
+    g_chanvalue = lax.psum_scatter(grad_chanvalue, owners, scatter_dimension=1, tiled=True)
+    hidden, grad_chanvalue = after(hidden, grad_chanvalue)
+    chan_sum = tp_scatter(matmul_nt(hidden, w_chanvalue_t).astype(jnp.bfloat16)).astype(jnp.float32)
     middle_q = lax.dynamic_slice_in_dim(
         middle.reshape(token_count, embedding_extent), sharded_layout, fourth_extent, 1
     )
@@ -341,13 +409,9 @@
         .astype(jnp.bfloat16)
         .reshape(seqs_here, piece_len, fourth_extent)
     )
-    d_result = upstream_derivative.astype(jnp.float32).reshape(token_count, fourth_extent)
-    d_chan = (d_result * rec_gate).astype(jnp.bfloat16)
     d_rec_pre = (d_result * chan_sum * rec_gate * (1.0 - rec_gate)).astype(jnp.bfloat16)
-    d_chan_full = lax.all_gather(d_chan, "tp", axis=1, tiled=True)
-    d_hidden = matmul_nt(d_chan_full, w_chanvalue)
+    d_hidden = matmul(d_chan_full, w_chanvalue_t)
     d_key_pre = (d_hidden * 2.0 * jax.nn.relu(key_pre)).astype(jnp.bfloat16)
-    grad_chanvalue = matmul_tn(hidden, d_chan_full)
     grad_chankey = matmul_tn(key_in, d_key_pre)
     grad_chanrecept = matmul_tn(rec_in, d_rec_pre)
     full_shape = (seqs_here, piece_len, embedding_extent)
@@ -373,13 +437,16 @@
     flat_part = d_middle_part.reshape(token_count, embedding_extent)
     own_cols = lax.dynamic_slice_in_dim(flat_part, sharded_layout, fourth_extent, 1) + d_result
     flat_part = lax.dynamic_update_slice_in_dim(flat_part, own_cols, sharded_layout, 1)
-    d_middle, chan_small = (
-        lax.psum(flat_part.astype(jnp.bfloat16), "tp").astype(jnp.float32),
-        lax.psum(chan_small_part.astype(jnp.bfloat16), "tp").astype(jnp.float32),
-    )
-    d_mixed = d_middle.astype(jnp.bfloat16)
-    grad_output = matmul_tn(joined_low, d_mixed)
-    d_joined = matmul_nt(d_mixed, w_output)
+    d_mixed = tp_sum(flat_part.astype(jnp.bfloat16))
+    grad_output_t = matmul_tn(d_mixed, joined_low)
+    grads_chan = jnp.concatenate(
+        [item.astype(jnp.bfloat16) for item in (grad_output_t, grad_chanrecept, grad_chankey)],
+        axis=1,
+    )
+    d_mixed, grads_chan, g_chanvalue = after(d_mixed, grads_chan, g_chanvalue)
+    d_middle = d_mixed.astype(jnp.float32)
+    g_chan = lax.psum_scatter(grads_chan, owners, scatter_dimension=0, tiled=True)
+    d_joined = matmul(d_mixed, w_output_t)
     d_gate_act = d_joined * grouped
     d_grouped = (d_joined * gate_act).reshape(split_shape)
     attention_gradient, g_ggain, g_gbias = norm_back(d_grouped, ggain_q, unit_group, inv_group)
@@ -389,7 +456,7 @@
     local_grad = jnp.einsum(
         "bthi,bthj->bhij", recept_f * rising * live_mask, attention_gradient, precision=HIGH
     )
-    outgoing_state = carried_in_2((carry_mult, local_grad), "ctx", chain_step, identity)[1]
+    outgoing_state = carried(carry_mult, local_grad, "ctx", -1)
     (
         receptance_gradient,
         key_gradient,
@@ -403,7 +470,15 @@
         for item in (receptance_gradient, key_gradient, value_gradient)
     ] + [d_gate_pre]
     weights_time = (w_recept, w_key, w_value, w_gate)
-    grads_time = [matmul_tn(mixed, grad_low) for mixed, grad_low in zip(mixed_in, d_lows)]
+    grads_time = jnp.concatenate(
+        [
+            matmul_tn(mixed, grad_low).astype(jnp.bfloat16)
+            for mixed, grad_low in zip(mixed_in, d_lows)
+        ],
+        axis=1,
+    )
+    *d_lows, grads_time, g_chan = after(d_lows[0], *d_lows[1:], grads_time, g_chan)
+    g_time = lax.psum_scatter(grads_time, owners, scatter_dimension=0, tiled=True)
     d_mix_ins = [
         matmul_nt(grad_low, weight).reshape(full_shape)
         for grad_low, weight in zip(d_lows, weights_time)
@@ -427,54 +502,26 @@
             sharding_spec(g_gbias, embedding_extent, sharded_layout),
         ]
     )
-    d_input_sum, time_small = (
-        lax.psum(
-            d_input_part.reshape(token_count, embedding_extent).astype(jnp.bfloat16), "tp"
-        ).astype(jnp.float32),
-        lax.psum(time_small_part.astype(jnp.bfloat16), "tp").astype(jnp.float32),
-    )
+    small_sum = whole_sum(
+        jnp.concatenate([time_small_part, chan_small_part], axis=0), ("tp", "fsdp", "ctx")
+    )
+    owned = embedding_extent // (lax.axis_size("fsdp") * lax.axis_size("ctx"))
+    small_owned = lax.dynamic_slice_in_dim(
+        small_sum, (lax.axis_index("fsdp") * lax.axis_size("ctx") + lax.axis_index("ctx")) * owned, owned, 1
+    )
+    d_input_sum = tp_sum(
+        d_input_part.reshape(token_count, embedding_extent).astype(jnp.bfloat16)
+    ).astype(jnp.float32)
     grad_inputs = (d_middle + d_input_sum).reshape(full_shape)
-    small_all = jnp.concatenate([time_small, chan_small], axis=0)
-    all_done = (
-        lax.psum_scatter(
-            grads_time[0].astype(jnp.bfloat16), ("fsdp", "ctx"), scatter_dimension=0, tiled=True
-        ).astype(jnp.float32),
-        lax.psum_scatter(
-            grads_time[1].astype(jnp.bfloat16), ("fsdp", "ctx"), scatter_dimension=0, tiled=True
-        ).astype(jnp.float32),
-        lax.psum_scatter(
-            grads_time[2].astype(jnp.bfloat16), ("fsdp", "ctx"), scatter_dimension=0, tiled=True
-        ).astype(jnp.float32),
-        lax.psum_scatter(
-            grads_time[3].astype(jnp.bfloat16), ("fsdp", "ctx"), scatter_dimension=0, tiled=True
-        ).astype(jnp.float32),
-        lax.psum_scatter(
-            grad_output.astype(jnp.bfloat16), ("fsdp", "ctx"), scatter_dimension=1, tiled=True
-        ).astype(jnp.float32),
-        lax.psum_scatter(
-            grad_chankey.astype(jnp.bfloat16), ("fsdp", "ctx"), scatter_dimension=0, tiled=True
-        ).astype(jnp.float32),
-        lax.psum_scatter(
-            grad_chanvalue.astype(jnp.bfloat16), ("fsdp", "ctx"), scatter_dimension=1, tiled=True
-        ).astype(jnp.float32),
-        lax.psum_scatter(
-            grad_chanrecept.astype(jnp.bfloat16), ("fsdp", "ctx"), scatter_dimension=0, tiled=True
-        ).astype(jnp.float32),
-        lax.psum_scatter(
-            small_all.astype(jnp.bfloat16), ("fsdp", "ctx"), scatter_dimension=1, tiled=True
-        ).astype(jnp.float32),
-    )
-    (
-        g_recept,
-        g_key,
-        g_value,
-        g_gate,
-        g_output,
-        g_chankey,
-        g_chanvalue,
-        g_chanrecept,
-        small_owned,
-    ) = all_done
+    g_chanvalue = g_chanvalue.astype(jnp.float32)
+    g_chan = g_chan.astype(jnp.float32)
+    g_time = g_time.astype(jnp.float32)
+    g_recept, g_key, g_value, g_gate = (
+        g_time[:, at * fourth_extent : (at + 1) * fourth_extent] for at in range(4)
+    )
+    g_output = g_chan[:, :fourth_extent].T
+    g_chanrecept = g_chan[:, fourth_extent : 2 * fourth_extent]
+    g_chankey = g_chan[:, 2 * fourth_extent :]
     return (
         result,
         grad_inputs,

time: 2100 us -> 1330 us (0.63)
  waiting for transfers between devices: 1200 us -> 320 us
  other arithmetic: 232 us -> 323 us
  blocking collectives: 76.9 us -> 0 us
  local copies, waits for them, and re-layouts: 202 us -> 259 us
  starting transfers between devices: 12.2 us -> 66.6 us
  matrix products: 351 us -> 328 us
    reduce_scatter x10 -> x3, waiting for transfers between devices: 652 us -> 0.02 us  [the longest x1 0.02 us: per_device(): lax.psum_scatter(grads_chan, owners, scatter_dimension=0, tiled=True)]
    all_gather x9 -> x2, waiting for transfers between devices: 329 us -> 108 us  [the longest x1 108 us: per_device(): lax.all_gather(jnp.concatenate([acceptor_matrix, lookup_matrix, payload_m...]
    psum x3 -> x0, waiting for transfers between devices: 212 us -> none  [the longest x1 84.5 us: per_device(): lax.psum(matmul(joined_low, w_output).astype(jnp.bfloat16), 'tp')]
    ppermute x0 -> x32, waiting for transfers between devices: none -> 211 us  [the longest x15 171 us: partner(): return lax.ppermute(x, 'tp', [(i, i ^ bit) for i in range(count)])]
    all_gather x3 -> x0, blocking collectives: 65.5 us -> none  [the longest x2 43 us: carried_in(): lax.all_gather(part.astype(kind), axis)]
    ppermute x0 -> x32, starting transfers between devices: none -> 39.1 us  [the longest x12 26.9 us: earlier_shift(): lax.ppermute(x, axis, [(i, i + by) for i in range(count) if 0 <= i + by <...]
    reduce_sum x2, other arithmetic: 32.4 us -> 64 us  [norm_back(): jnp.sum(d_out * unit_vals, axis=(0, 1))]
    concatenate x1 -> x3, other arithmetic: 0.65 us -> 27 us  [the longest x1 21.2 us: per_device(): jnp.concatenate([item.astype(jnp.bfloat16) for item in (grad_output_t, gr...]
  transfers between devices with their start and end apart: 26 -> 41, of which waited for: 19 -> 18; matrix products, arithmetic and copies ran while one was open for 32% -> 61% of each run, Pallas kernels for 0% -> 0%
where the time goes in v1:
time: 1330 us; the launch traced here: 1320 us
  matrix products  328 us (25%)
  other arithmetic  323 us (24%)
  waiting for transfers between devices  320 us (24%)
  local copies, waits for them, and re-layouts  259 us (19%)
  starting transfers between devices  66.6 us (5%)
  between operations  15.9 us (1%)
    ppermute x15, waiting for transfers between devices, partner(): return lax.ppermute(x, 'tp', [(i, i ^ bit) for i in range(count)])  171 us
    all_gather x1, waiting for transfers between devices, per_device(): lax.all_gather(jnp.concatenate([acceptor_matrix, lookup_matrix, payload_m...  108 us
    dot_general x8, matrix products, matmul(): return jnp.dot(left, right, preferred_element_type=jnp.float32)  68.9 us
    reduce_sum x2, other arithmetic, norm_back(): jnp.sum(d_out * unit_vals, axis=(0, 1))  64 us
    dot_general x8, matrix products, matmul_nt(): lax.dot_general(left, right, (((1,), (1,)), ((), ())), preferred_element_...  63.8 us
    dynamic_slice x64, local copies, waits for them, and re-layouts, fading_payload_sweeper(): lax.scan(scan_update, memory_matrix_kept, (to_blocks(acceptor_entries), t...  56.5 us
    dot_general x32, matrix products, fading_payload_tile(): scores = jnp.einsum('thi,shi->hts', query_dec, key_dec, precision=HIGH)  47 us
    dot_general x8, matrix products, matmul_tn(): lax.dot_general(left, right, (((0,), (0,)), ((), ())), preferred_element_...  43.6 us
  transfers between devices with their start and end apart: 41, of which 18 were waited for; matrix products, arithmetic and copies ran while one was open for 61% of the time, Pallas kernels for 0%

profile of v1, /device:TPU:0, one launch (start us, length us, event | category | flops | bytes accessed | tf_op | source)
XLA Modules:
  0.0 1315.7 jit_solution(866808443616291927)
XLA Ops:
  14.1 7.2 collective-permute-start.2
  44.7 13.4 %add_convert_fusion.3 = (bf16[2,512,2048]{2,1,0:T(8,128)(2,1)}, bf16[2,512,2048]{2,1,0:T(8,128)(2,1)}, bf16[2,512,2048]{2,1,0:T(8,128)(2,1)}, bf16[2,512,2048]{2,1,0:T(8,128)(2,1)}) fusion(f32[2048]{0:T(1024)S(1)} %copy-done.63, f32[2,512]{1,0:T(2,128)S(1)} %get-tuple-element.1014, f32[2,511,2048]{2,1,0:T(8,128)} %bitcast.422, ...), kind=kLoop, calls=%fused_computation.180 | loop fusion | flops 41943040 | bytes 29421568 | tf_op jit(solution)/shard_map/convert_element_type | solution.py:326
  58.1 108.2 %all-gather.3.cloned.1.call-done = bf16[2048,2560]{0,1:T(8,128)(2,1)} async-done(((bf16[256,2560]{0,1:T(8,128)(2,1)}), bf16[2048,2560]{0,1:T(8,128)(2,1)}) %all-gather.3.cloned.1.call-update) | async-done | bytes 10485776 | tf_op jit(solution)/shard_map/all_gather | solution.py:296
  166.3 5.2 fusion.149
  173.6 6.2 fusion.155
  185.9 5.2 fusion.146
  197.1 5.7 multiply_multiply_fusion.2
  206.3 4.1 collective-permute-start.5
  212.5 4.4 reshape_reshape.12
  219.3 8.5 copy_bitcast_fusion
  230.3 5.0 copy.413
  235.2 4.7 collective-permute-done.4
  241.5 98.4 %while.43 = (s32[]{:T(128)}, f32[2,8,64,64]{3,2,1,0:T(8,128)S(1)}, f32[8,2,64,8,64]{4,2,3,1,0:T(8,128)}, f32[8,2,8,64,64]{4,3,2,1,0:T(8,128)}, f32[1,8,64]{2,1,0...) while((s32[]{:T(128)}, f32[2,8,64,64]{3,2,1,0:T(8,128)S(1)}, ...), condition=%wide.region_4.5_spmd.clone.clone, body=%wide.region_2.4_spmd.clone.clone.sunk | while | flops 202365632 | bytes 9354611 | solution.py:194
  349.8 7.6 copy.274
  357.4 4.8 reshape.587
  365.2 9.4 multiply_convert_fusion.3
  374.6 4.3 convolution_convert_fusion.2
  382.6 4.4 collective-permute-done.7
  390.9 46.1 %collective-permute-done.8 = bf16[512,2048]{1,0:T(8,128)(2,1)S(1)} collective-permute-done((bf16[512,2048]{1,0:T(8,128)(2,1)S(1)}, bf16[512,2048]{1,0:T(8,128)(2,1)S(1)}, u32[]{:S(2)}, u32[]{:S(2)}) %collective-permute-start.8) | collective-permute-done | bytes 2097184 | tf_op jit(solution)/shard_map/ppermute | solution.py:43
  438.1 4.3 collective-permute-done.9
  442.3 7.5 convert_add_fusion
  455.1 22.2 %collective-permute-start.10 = (f32[2,2048]{1,0:T(2,128)S(1)}, f32[2,2048]{1,0:T(2,128)S(1)}, u32[]{:S(2)}, u32[]{:S(2)}) collective-permute-start(f32[2,2048]{1,0:T(2,128)S(1)} %bitcast.478), channel_id=1, source_target_pairs={{0,4},{4,8},{8,12},{1,5},{5,9},{9,13},{2,6},{6,10},{10,14},{3,7},{... | collective-permute-start | bytes 49160 | tf_op jit(solution)/shard_map/ppermute | solution.py:20
  478.8 15.0 %add_convert_fusion = (bf16[2,512,2048]{2,1,0:T(8,128)(2,1)}, bf16[2,512,2048]{2,1,0:T(8,128)(2,1)}) fusion(f32[2,511,2048]{2,1,0:T(8,128)S(1)} %bitcast.424, f32[2,1,2048]{2,1,0:T(1,128)S(1)} %broadcast_in_dim.132, f32[2048]{0:T(1024)S(1)} %copy-done.61, f32[2,512]{1,0:T(2,128)S(1)} %get-tuple-element.1014, f32[2048]{0:T(1024)S(1)} %copy-done.62, ...), kind=kLoop, calls=%fused_computation.175 | loop fusion | flops 33554432 | bytes 25210880 | tf_op jit(solution)/shard_map/convert_element_type | solution.py:386
  497.4 5.7 constant_dynamic-update-slice_fusion.12
  504.5 23.2 %collective-permute-done.11 = bf16[1024,512]{1,0:T(8,128)(2,1)} collective-permute-done((bf16[1024,512]{1,0:T(8,128)(2,1)}, bf16[1024,512]{1,0:T(8,128)(2,1)}, u32[]{:S(2)}, u32[]{:S(2)}) %collective-permute-start.11) | collective-permute-done | bytes 1048608 | tf_op jit(solution)/shard_map/ppermute | solution.py:43
  527.7 13.6 %multiply_convert_fusion.1 = (bf16[1024,1792]{1,0:T(8,128)(2,1)S(1)}, f32[1024,1792]{1,0:T(8,128)}) fusion(bf16[1024,2048]{1,0:T(8,128)(2,1)} %bitcast.454, bf16[2048,4096]{0,1:T(8,128)(2,1)} %all-gather.5.cloned.1.call-done), kind=kOutput, calls=%fused_computation.187 | convolution fusion | flops 7521697792 | bytes 22544384 | tf_op jit(solution)/shard_map/dot_general | solution.py:124
  546.6 12.3 convolution_convert_fusion.1
  559.0 11.1 fusion.103
  571.0 14.1 %multiply_convert_fusion = bf16[1024,1792]{1,0:T(8,128)(2,1)} fusion(f32[1024,1792]{1,0:T(8,128)} %get-tuple-element.1017, bf16[1024,2048]{1,0:T(8,128)(2,1)} %constant_dynamic-update-slice_fusion.9, bf16[2048,4096]{0,1:T(8,128)(2,1)} %all-gather.5.cloned.1.call-done), kind=kOutput, calls=%fused_computation.186 | convolution fusion | flops 7523532800 | bytes 22544384 | tf_op jit(solution)/shard_map/dot_general | solution.py:124
  587.0 13.3 %fusion.92 = f32[1024,2048]{1,0:T(8,128)} fusion(bf16[1024,1792]{1,0:T(8,128)(2,1)} %multiply_convert_fusion, bf16[2048,4096]{0,1:T(8,128)(2,1)} %all-gather.5.cloned.1.call-done), kind=kOutput, calls=%fused_computation.192 | convolution fusion | flops 7516192768 | bytes 19398656 | tf_op jit(solution)/shard_map/dot_general | solution.py:134
  600.3 10.7 collective-permute-done.16
  614.7 7.6 fusion.120
  622.3 14.0 %multiply_reduce_fusion.10 = (f32[2048]{0:T(1024)}, f32[2048]{0:T(1024)}, f32[2,512,2048]{2,1,0:T(8,128)}) fusion(f32[1024,2048]{1,0:T(8,128)} %fusion.120, f32[2,512]{1,0:T(2,128)S(1)} %get-tuple-element.1014, f32[2,511,2048]{2,1,0:T(8,128)} %bitcast.425, f32[2,1,2048]{2,1,0:T(1,128)S(1)} %broadcast_in_dim.132, f32[1024,2048]{1,0:T(8,128)} %fusion.92, ...), kind=kLoop, calls=%fused_computation.159 | loop fusion | flops 37744640 | bytes 42004480 | tf_op jit(solution)/shard_map/reduce_sum | solution.py:434
  638.6 8.5 slice.213
  647.1 23.4 %multiply_reduce_fusion.12 = (f32[2048]{0:T(1024)}, f32[2,512]{1,0:T(2,128)S(1)}, f32[2,512,2048]{2,1,0:T(8,128)}, f32[2,512,2048]{2,1,0:T(8,128)}) fusion(f32[2,512]{1,0:T(2,128)S(1)} %add_rsqrt_fusion.1, f32[2,512]{1,0:T(2,128)S(1)} %broadcast_multiply_fusion.9, bf16[2,512,2048]{2,1,0:T(8,128)(2,1)} %param.29, bf16[1024,2048]{1,0:T(8,128)(2,1)} %copy-done.3, ...), kind=kLoop, calls=%fused_computation.161 | loop fusion | flops 39842816 | bytes 54571008 | tf_op jit(solution)/shard_map/reduce_sum | solution.py:245
  670.5 10.7 fusion.174
  681.2 7.7 subtract_multiply_fusion
  690.6 4.1 collective-permute-done.18
  702.1 5.2 collective-permute-done.22
  707.3 5.8 copy.336
  717.1 27.7 %collective-permute-done.19 = bf16[512,2048]{1,0:T(8,128)(2,1)} collective-permute-done((bf16[512,2048]{1,0:T(8,128)(2,1)}, bf16[512,2048]{1,0:T(8,128)(2,1)}, u32[]{:S(2)}, u32[]{:S(2)}) %collective-permute-start.19) | collective-permute-done | bytes 2097184 | tf_op jit(solution)/shard_map/ppermute | solution.py:43
  747.9 10.3 convolution_convert_fusion
  765.6 21.2 %pad_maximum_fusion = bf16[2048,2816]{0,1:T(8,128)(2,1)} fusion(bf16[2048,1792]{0,1:T(8,128)(2,1)S(1)} %convolution_convert_fusion, bf16[2048,512]{0,1:T(8,128)(2,1)S(1)} %convolution_convert_fusion.7, bf16[2048,512]{0,1:T(8,128)(2,1)S(1)} %convolution_convert_fusion.8), kind=kLoop, calls=%fused_computation.138 | loop fusion | flops 34603008 | bytes 23068672 | tf_op jit(solution)/shard_map/concatenate | solution.py:442
  786.9 9.6 fusion.176
  819.1 6.2 convolution_convert_fusion.3
  826.2 9.5 fusion.102
  835.8 18.9 %collective-permute-done.25 = bf16[2,8,64,64]{3,2,1,0:T(8,128)(2,1)S(1)} collective-permute-done((bf16[2,8,64,64]{3,2,1,0:T(8,128)(2,1)S(1)}, bf16[2,8,64,64]{3,2,1,0:T(8,128)(2,1)S(1)}, u32[]{:S(2)}, u32[]{:S(2)}) %collective-permute-start.25) | collective-permute-done | bytes 131104 | tf_op jit(solution)/shard_map/ppermute | solution.py:25
  860.8 190.9 %while.42 = (s32[]{:T(128)}, f32[8,64]{1,0:T(8,128)S(1)}, f32[8,64]{1,0:T(8,128)S(1)}, f32[2,8,64,64]{3,2,1,0:T(8,128)S(1)}, bf16[8,2,64,8,64]{2,4,3,1,0:T(8,128...) while((s32[]{:T(128)}, f32[8,64]{1,0:T(8,128)S(1)}, ...), condition=%wide.region_26.27_spmd.clone, body=%wide.region_14.26_spmd.clone.sunk | while | flops 456254720 | bytes 27374368 | solution.py:194
  1051.7 4.3 copy.305
  1062.2 4.2 convert_element_type.416
  1072.5 4.7 convolution_convert_fusion.4
  1082.3 4.3 pad_maximum_fusion.2
  1090.7 8.9 fusion.135
  1099.6 7.2 fusion.139
  1106.9 7.4 fusion.127
  1114.3 14.0 %add_multiply_fusion = f32[2,512,2048]{2,1,0:T(8,128)} fusion(f32[2048]{0:T(1024)S(1)} %copy-done.85, f32[2048]{0:T(1024)S(1)} %copy-done.86, f32[2048]{0:T(1024)S(1)} %copy-done.87, f32[2048]{0:T(1024)S(1)} %copy-done.88, f32[2,512]{1,0:T(2,128)S(1)} %copy-done.60, f32[1024,2048]{1,0:T(8,128)} %fusion.127, f32[1024,2048]{1,0:T(8,128)} %fusion.135, ...), kind=kLoop, calls=%fused_computation.168 | loop fusion | flops 16777216 | bytes 41979904 | tf_op jit(solution)/shard_map/mul | solution.py:488
  1130.8 8.6 slice.215
  1139.5 40.7 %fusion.86 = (f32[2048]{0:T(1024)}, f32[2,512]{1,0:T(2,128)S(1)}, f32[2048]{0:T(1024)}, f32[2048]{0:T(1024)}, f32[2048]{0:T(1024)}, /*index=5*/f32[2048]{0:T(1024)}, f32[2,512,2048]{2,1,0:T(8,128)}, f32[2,512,2048]{2,1,0:T(8,128)}) fusion(bf16[2,512,2048]{2,1,0:T(8,128)(2,1)} %param.29, f32[2,512]{1,0:T(2,128)S(1)} %copy-done.76, ...), kind=kLoop, calls=%fused_computation.150 | loop fusion | flops 62903296 | bytes 104964096 | tf_op jit(solution)/shard_map/reduce_sum | solution.py:245
  1180.2 15.6 %fusion.175 = (f32[2048]{0:T(1024)}, f32[1024]{0:T(1024)S(1)}) fusion(f32[2048]{0:T(1024)S(1)} %copy-done.54, f32[2,512,2048]{2,1,0:T(8,128)} %get-tuple-element.951, f32[1024,2048]{1,0:T(8,128)} %fusion.127, f32[2048]{0:T(1024)S(1)} %copy-done.74, f32[1024,2048]{1,0:T(8,128)} %fusion.135, f32[2048]{0:T(1024)S(1)} %copy-done.71, f32[1024,2048]{1,0:T(8,128)} %fusion.139, ...), kind=kLoop, calls=%fused_computation.361 | loop fusion | flops 23065600 | bytes 41996288 | tf_op jit(solution)/shard_map/reduce_sum | solution.py:245
  1195.8 6.0 fusion.85
  1208.5 46.3 %collective-permute-done.29 = bf16[512,2048]{1,0:T(8,128)(2,1)S(1)} collective-permute-done((bf16[512,2048]{1,0:T(8,128)(2,1)S(1)}, bf16[512,2048]{1,0:T(8,128)(2,1)S(1)}, u32[]{:S(2)}, u32[]{:S(2)}) %collective-permute-start.29) | collective-permute-done | bytes 2097184 | tf_op jit(solution)/shard_map/ppermute | solution.py:43
  1269.1 4.3 collective-permute-done.32
  1273.5 5.0 collective-permute-done.33
  1296.1 7.5 convert_add_fusion.1
  (980 shorter events, 510.1 us)
Async XLA Ops:
  7.2 159.1 %all-gather.3.cloned.1.call-start = ((), (), s32[]{:S(2)}) async-start(), calls=%async_computation.3 | async-start | bytes 11796480 | tf_op jit(solution)/shard_map/all_gather | solution.py:296
  12.9 480.8 %all-gather.5.cloned.1.call-start = ((), (), s32[]{:S(2)}) async-start(), calls=%async_computation.4 | async-start | bytes 18874368 | tf_op jit(solution)/shard_map/all_gather | solution.py:304
  13.8 14.4 %copy-start = (bf16[2,512,2048]{2,1,0:T(8,128)(2,1)S(1)}, bf16[2,512,2048]{2,1,0:T(8,128)(2,1)}, u32[]{:S(2)}) copy-start(bf16[2,512,2048]{2,1,0:T(8,128)(2,1)} %param.29) | copy-start | bytes 12582916
  14.1 15.3 %copy-start.94 = (bf16[2,8,64]{2,1,0:T(8,128)(2,1)}, bf16[2,8,64]{2,1,0:T(8,128)(2,1)S(1)}, u32[]{:S(2)}) copy-start(bf16[2,8,64]{2,1,0:T(8,128)(2,1)S(1)} %multiply_convert_fusion.4) | copy-start | bytes 6148
  14.1 15.3 %copy-start.53 = (f32[2048]{0:T(1024)S(1)}, f32[2048]{0:T(1024)}, u32[]{:S(2)}) copy-start(f32[2048]{0:T(1024)} %param.39) | copy-start | bytes 24580
  14.1 15.3 %copy-start.79 = (f32[2048]{0:T(1024)S(1)}, f32[2048]{0:T(1024)}, u32[]{:S(2)}) copy-start(f32[2048]{0:T(1024)} %param.40) | copy-start | bytes 24580
  14.1 29.9 %collective-permute-start.2 = (bf16[2,8,64]{2,1,0:T(8,128)(2,1)S(1)}, bf16[2,8,64]{2,1,0:T(8,128)(2,1)S(1)}, u32[]{:S(2)}, u32[]{:S(2)}) collective-permute-start(bf16[2,8,64]{2,1,0:T(8,128)(2,1)S(1)} %multiply_convert_fusion.4), channel_id=1, source_target_pairs={{0,12},{1,13},{2,14},{3,15},{16,28},{17,29},{18,30},{19,31}} | collective-permute-start | bytes 6152 | tf_op jit(solution)/shard_map/ppermute | solution.py:25
  21.4 22.7 %collective-permute-start.1 = (bf16[2,8,64]{2,1,0:T(8,128)(2,1)S(1)}, bf16[2,8,64]{2,1,0:T(8,128)(2,1)S(1)}, u32[]{:S(2)}, u32[]{:S(2)}) collective-permute-start(bf16[2,8,64]{2,1,0:T(8,128)(2,1)S(1)} %multiply_convert_fusion.4), channel_id=1, source_target_pairs={{0,8},{4,12},{1,9},{5,13},{2,10},{6,14},{3,11},{7,15},{16,24},{20,... | collective-permute-start | bytes 6152 | tf_op jit(solution)/shard_map/ppermute | solution.py:25
  22.7 21.4 %collective-permute-start = (bf16[2,8,64]{2,1,0:T(8,128)(2,1)S(1)}, bf16[2,8,64]{2,1,0:T(8,128)(2,1)S(1)}, u32[]{:S(2)}, u32[]{:S(2)}) collective-permute-start(bf16[2,8,64]{2,1,0:T(8,128)(2,1)S(1)} %multiply_convert_fusion.4), channel_id=1, source_target_pairs={{0,4},{4,8},{8,12},{1,5},{5,9},{9,13},{2,6},{6,10},{10,14},{3,7},{... | collective-permute-start | bytes 6152 | tf_op jit(solution)/shard_map/ppermute | solution.py:25
  28.2 16.4 %copy-start.57 = (f32[2,512]{1,0:T(2,128)}, f32[2,512]{1,0:T(2,128)S(1)}, u32[]{:S(2)}) copy-start(f32[2,512]{1,0:T(2,128)S(1)} %broadcast_multiply_fusion.10) | copy-start | bytes 12292
  29.5 15.2 %copy-start.75 = (f32[2,512]{1,0:T(2,128)}, f32[2,512]{1,0:T(2,128)S(1)}, u32[]{:S(2)}) copy-start(f32[2,512]{1,0:T(2,128)S(1)} %add_rsqrt_fusion.2) | copy-start | bytes 12292
  34.6 10.0 collective-permute-start.3
  39.1 747.7 %reduce-scatter.4.cloned.1.call-start = ((), (), s32[]{:S(2)}) async-start(), calls=%async_computation.5 | async-start | bytes 8257536 | tf_op jit(solution)/shard_map/reduce_scatter | solution.py:401
  39.5 582.8 %copy-start.59 = (f32[2,512]{1,0:T(2,128)}, f32[2,512]{1,0:T(2,128)S(1)}, u32[]{:S(2)}) copy-start(f32[2,512]{1,0:T(2,128)S(1)} %get-tuple-element.1014) | copy-start | bytes 12292
  42.3 322.9 %copy-start.96 = (f32[512]{0:T(512)}, f32[512]{0:T(512)S(1)}, u32[]{:S(2)}) copy-start(f32[512]{0:T(512)S(1)} %dynamic_slice.154) | copy-start | bytes 6148
  43.1 322.1 %copy-start.91 = (f32[512]{0:T(512)}, f32[512]{0:T(512)S(1)}, u32[]{:S(2)}) copy-start(f32[512]{0:T(512)S(1)} %dynamic_slice.153) | copy-start | bytes 6148
  204.3 30.9 %collective-permute-start.6 = (bf16[2,8,64,64]{3,2,1,0:T(8,128)(2,1)S(1)}, bf16[2,8,64,64]{3,2,1,0:T(8,128)(2,1)}, u32[]{:S(2)}, u32[]{:S(2)}) collective-permute-start(bf16[2,8,64,64]{3,2,1,0:T(8,128)(2,1)S(1)} %fusion.165), channel_id=1, source_target_pairs={{0,4},{4,8},{8,12},{1,5},{5,9},{9,13},{2,6},{6,10},{10,14},{3,7},{... | collective-permute-start | bytes 393224 | tf_op jit(solution)/shard_map/ppermute | solution.py:25
  206.3 28.9 %collective-permute-start.5 = (bf16[2,8,64,64]{3,2,1,0:T(8,128)(2,1)S(1)}, bf16[2,8,64,64]{3,2,1,0:T(8,128)(2,1)}, u32[]{:S(2)}, u32[]{:S(2)}) collective-permute-start(bf16[2,8,64,64]{3,2,1,0:T(8,128)(2,1)S(1)} %fusion.165), channel_id=1, source_target_pairs={{0,8},{4,12},{1,9},{5,13},{2,10},{6,14},{3,11},{7,15},{16,24},{20,... | collective-permute-start | bytes 393224 | tf_op jit(solution)/shard_map/ppermute | solution.py:25
  210.4 29.5 %collective-permute-start.4 = (bf16[2,8,64,64]{3,2,1,0:T(8,128)(2,1)S(1)}, bf16[2,8,64,64]{3,2,1,0:T(8,128)(2,1)}, u32[]{:S(2)}, u32[]{:S(2)}) collective-permute-start(bf16[2,8,64,64]{3,2,1,0:T(8,128)(2,1)S(1)} %fusion.165), channel_id=1, source_target_pairs={{0,12},{1,13},{2,14},{3,15},{16,28},{17,29},{18,30},{19,31}} | collective-permute-start | bytes 393224 | tf_op jit(solution)/shard_map/ppermute | solution.py:25
  382.6 4.4 collective-permute-start.7
  389.3 47.7 %collective-permute-start.8 = (bf16[512,2048]{1,0:T(8,128)(2,1)S(1)}, bf16[512,2048]{1,0:T(8,128)(2,1)S(1)}, u32[]{:S(2)}, u32[]{:S(2)}) collective-permute-start(bf16[512,2048]{1,0:T(8,128)(2,1)S(1)} %add_convert_fusion.11), channel_id=1, source_target_pairs={{0,2},{1,3},{2,0},{3,1},{4,6},{5,7},{6,4},{7,5},{8,10},{9,11},{10,... | collective-permute-start | bytes 6291464 | tf_op jit(solution)/shard_map/ppermute | solution.py:43
  438.0 4.4 collective-permute-start.9
  449.9 28.8 %copy-start.3 = (bf16[1024,2048]{1,0:T(8,128)(2,1)}, bf16[1024,2048]{1,0:T(8,128)(2,1)S(1)}, u32[]{:S(2)}) copy-start(bf16[1024,2048]{1,0:T(8,128)(2,1)S(1)} %get-tuple-element.957) | copy-start | bytes 12582916
  452.9 25.8 %copy-start.61 = (f32[2048]{0:T(1024)S(1)}, f32[2048]{0:T(1024)}, u32[]{:S(2)}) copy-start(f32[2048]{0:T(1024)} %param.51) | copy-start | bytes 24580
  452.9 25.8 %copy-start.62 = (f32[2048]{0:T(1024)S(1)}, f32[2048]{0:T(1024)}, u32[]{:S(2)}) copy-start(f32[2048]{0:T(1024)} %param.52) | copy-start | bytes 24580
  455.0 23.7 %copy-start.14 = (f32[2,512,2048]{2,1,0:T(8,128)}, f32[2,512,2048]{2,1,0:T(8,128)S(1)}, u32[]{:S(2)}) copy-start(f32[2,512,2048]{2,1,0:T(8,128)S(1)} %multiply_add_fusion) | copy-start | bytes 25165828
  455.1 23.6 %collective-permute-start.10 = (f32[2,2048]{1,0:T(2,128)S(1)}, f32[2,2048]{1,0:T(2,128)S(1)}, u32[]{:S(2)}, u32[]{:S(2)}) collective-permute-start(f32[2,2048]{1,0:T(2,128)S(1)} %bitcast.478), channel_id=1, source_target_pairs={{0,4},{4,8},{8,12},{1,5},{5,9},{9,13},{2,6},{6,10},{10,14},{3,7},{... | collective-permute-start | bytes 49160 | tf_op jit(solution)/shard_map/ppermute | solution.py:20
  478.7 17.6 %copy-start.32 = (bf16[2,512,512]{2,1,0:T(8,128)(2,1)S(1)}, bf16[2,512,512]{2,1,0:T(8,128)(2,1)}, u32[]{:S(2)}) copy-start(bf16[2,512,512]{2,1,0:T(8,128)(2,1)} %param.53) | copy-start | bytes 3145732
  503.1 24.6 %collective-permute-start.11 = (bf16[1024,512]{1,0:T(8,128)(2,1)}, bf16[1024,512]{1,0:T(8,128)(2,1)}, u32[]{:S(2)}, u32[]{:S(2)}) collective-permute-start(bf16[1024,512]{1,0:T(8,128)(2,1)} %get-tuple-element.1021), channel_id=1, source_target_pairs={{0,2},{1,3},{2,0},{3,1},{4,6},{5,7},{6,4},{7,5},{8,10},{9,11},{10,... | collective-permute-start | bytes 3145736 | tf_op jit(solution)/shard_map/ppermute | solution.py:43
  504.5 39.9 %collective-permute-start.12 = (bf16[1024,512]{1,0:T(8,128)(2,1)}, bf16[1024,512]{1,0:T(8,128)(2,1)S(1)}, u32[]{:S(2)}, u32[]{:S(2)}) collective-permute-start(bf16[1024,512]{1,0:T(8,128)(2,1)} %get-tuple-element.1021), channel_id=1, source_target_pairs={{0,1},{1,0},{2,3},{3,2},{4,5},{5,4},{6,7},{7,6},{8,9},{9,8},{10,11... | collective-permute-start | bytes 3145736 | tf_op jit(solution)/shard_map/ppermute | solution.py:43
  527.7 17.8 %collective-permute-start.13 = (bf16[1024,512]{1,0:T(8,128)(2,1)}, bf16[1024,512]{1,0:T(8,128)(2,1)S(1)}, u32[]{:S(2)}, u32[]{:S(2)}) collective-permute-start(bf16[1024,512]{1,0:T(8,128)(2,1)} %collective-permute-done.11), channel_id=1, source_target_pairs={{0,1},{1,0},{2,3},{3,2},{4,5},{5,4},{6,7},{7,6},{8,9},{9,8},{10,11... | collective-permute-start | bytes 3145736 | tf_op jit(solution)/shard_map/ppermute | solution.py:43
  570.3 14.8 %collective-permute-start.15 = (bf16[1024,512]{1,0:T(8,128)(2,1)S(1)}, bf16[1024,512]{1,0:T(8,128)(2,1)S(1)}, u32[]{:S(2)}, u32[]{:S(2)}) collective-permute-start(bf16[1024,512]{1,0:T(8,128)(2,1)S(1)} %get-tuple-element.988), channel_id=1, source_target_pairs={{0,1},{1,0},{2,3},{3,2},{4,5},{5,4},{6,7},{7,6},{8,9},{9,8},{10,11... | collective-permute-start | bytes 3145736 | tf_op jit(solution)/shard_map/ppermute | solution.py:43
  570.9 29.4 %collective-permute-start.14 = (bf16[1024,512]{1,0:T(8,128)(2,1)S(1)}, bf16[1024,512]{1,0:T(8,128)(2,1)S(1)}, u32[]{:S(2)}, u32[]{:S(2)}) collective-permute-start(bf16[1024,512]{1,0:T(8,128)(2,1)S(1)} %get-tuple-element.987), channel_id=1, source_target_pairs={{0,1},{1,0},{2,3},{3,2},{4,5},{5,4},{6,7},{7,6},{8,9},{9,8},{10,11... | collective-permute-start | bytes 3145736 | tf_op jit(solution)/shard_map/ppermute | solution.py:43
  585.5 25.6 %collective-permute-start.16 = (bf16[1024,512]{1,0:T(8,128)(2,1)S(1)}, bf16[1024,512]{1,0:T(8,128)(2,1)S(1)}, u32[]{:S(2)}, u32[]{:S(2)}) collective-permute-start(bf16[1024,512]{1,0:T(8,128)(2,1)S(1)} %add_convert_fusion.13), channel_id=1, source_target_pairs={{0,2},{1,3},{2,0},{3,1},{4,6},{5,7},{6,4},{7,5},{8,10},{9,11},{10,... | collective-permute-start | bytes 3145736 | tf_op jit(solution)/shard_map/ppermute | solution.py:43
  637.2 9.9 collective-permute-start.17
  638.5 448.2 %reduce-scatter.6.cloned.1.call-start = ((), (), s32[]{:S(2)}) async-start(), calls=%async_computation.6 | async-start | bytes 12976128 | tf_op jit(solution)/shard_map/reduce_scatter | solution.py:448
  690.5 4.2 collective-permute-start.18
  696.8 48.0 %collective-permute-start.19 = (bf16[512,2048]{1,0:T(8,128)(2,1)}, bf16[512,2048]{1,0:T(8,128)(2,1)}, u32[]{:S(2)}, u32[]{:S(2)}) collective-permute-start(bf16[512,2048]{1,0:T(8,128)(2,1)} %add_convert_fusion.9), channel_id=1, source_target_pairs={{0,2},{1,3},{2,0},{3,1},{4,6},{5,7},{6,4},{7,5},{8,10},{9,11},{10,... | collective-permute-start | bytes 6291464 | tf_op jit(solution)/shard_map/ppermute | solution.py:43
  696.8 10.5 collective-permute-start.23
  698.1 9.2 collective-permute-start.22
  699.4 7.9 collective-permute-start.21
  717.1 30.8 %copy-start.31 = (bf16[2,512,2048]{2,1,0:T(8,128)(2,1)S(1)}, bf16[2,512,2048]{2,1,0:T(8,128)(2,1)}, u32[]{:S(2)}) copy-start(bf16[2,512,2048]{2,1,0:T(8,128)(2,1)} %get-tuple-element.978) | copy-start | bytes 12582916
  747.8 13.0 collective-permute-start.20
  765.6 21.2 %copy-start.97 = (f32[512]{0:T(512)S(1)}, f32[512]{0:T(512)}, u32[]{:S(2)}) copy-start(f32[512]{0:T(512)} %copy-done.96) | copy-start | bytes 6148
  812.5 23.3 %collective-permute-start.26 = (bf16[2,8,64,64]{3,2,1,0:T(8,128)(2,1)S(1)}, bf16[2,8,64,64]{3,2,1,0:T(8,128)(2,1)S(1)}, u32[]{:S(2)}, u32[]{:S(2)}) collective-permute-start(bf16[2,8,64,64]{3,2,1,0:T(8,128)(2,1)S(1)} %fusion.160), channel_id=1, source_target_pairs={{4,0},{8,4},{12,8},{5,1},{9,5},{13,9},{6,2},{10,6},{14,10},{7,3},{... | collective-permute-start | bytes 393224 | tf_op jit(solution)/shard_map/ppermute | solution.py:25
  813.8 40.9 %collective-permute-start.25 = (bf16[2,8,64,64]{3,2,1,0:T(8,128)(2,1)S(1)}, bf16[2,8,64,64]{3,2,1,0:T(8,128)(2,1)S(1)}, u32[]{:S(2)}, u32[]{:S(2)}) collective-permute-start(bf16[2,8,64,64]{3,2,1,0:T(8,128)(2,1)S(1)} %fusion.160), channel_id=1, source_target_pairs={{8,0},{12,4},{9,1},{13,5},{10,2},{14,6},{11,3},{15,7},{24,16},{28,... | collective-permute-start | bytes 393224 | tf_op jit(solution)/shard_map/ppermute | solution.py:25
  815.1 39.6 %collective-permute-start.24 = (bf16[2,8,64,64]{3,2,1,0:T(8,128)(2,1)S(1)}, bf16[2,8,64,64]{3,2,1,0:T(8,128)(2,1)S(1)}, u32[]{:S(2)}, u32[]{:S(2)}) collective-permute-start(bf16[2,8,64,64]{3,2,1,0:T(8,128)(2,1)S(1)} %fusion.160), channel_id=1, source_target_pairs={{12,0},{13,1},{14,2},{15,3},{28,16},{29,17},{30,18},{31,19}} | collective-permute-start | bytes 393224 | tf_op jit(solution)/shard_map/ppermute | solution.py:25
  825.4 478.2 %reduce-scatter.8.cloned.1.call-start = ((), (), s32[]{:S(2)}) async-start(), calls=%async_computation.7 | async-start | bytes 9437184 | tf_op jit(solution)/shard_map/reduce_scatter | solution.py:481
  835.8 25.1 %copy-start.35 = (f32[8,64]{1,0:T(8,128)S(1)}, f32[8,64]{1,0:T(8,128)}, u32[]{:S(2)}) copy-start(f32[8,64]{1,0:T(8,128)} %copy-done.34) | copy-start | bytes 6148
  1090.7 23.6 %copy-start.5 = (f32[1024,2048]{1,0:T(8,128)}, f32[1024,2048]{1,0:T(8,128)S(1)}, u32[]{:S(2)}) copy-start(f32[1024,2048]{1,0:T(8,128)S(1)} %fusion.131) | copy-start | bytes 25165828
  1129.3 10.1 collective-permute-start.27
  1202.0 4.2 collective-permute-start.28
  1207.0 49.4 %copy-start.99 = (f32[512]{0:T(512)S(1)}, f32[512]{0:T(512)}, u32[]{:S(2)}) copy-start(f32[512]{0:T(512)} %get-tuple-element.886) | copy-start | bytes 6148
  1207.0 50.6 %copy-start.98 = (f32[512]{0:T(512)S(1)}, f32[512]{0:T(512)}, u32[]{:S(2)}) copy-start(f32[512]{0:T(512)} %get-tuple-element.885) | copy-start | bytes 6148
  1207.0 51.2 %copy-start.83 = (f32[8,64]{1,0:T(8,128)S(1)}, f32[8,64]{1,0:T(8,128)}, u32[]{:S(2)}) copy-start(f32[8,64]{1,0:T(8,128)} %copy-done.82) | copy-start | bytes 6148
  1207.0 55.1 %copy-start.84 = (f32[2048]{0:T(1024)S(1)}, f32[2048]{0:T(1024)}, u32[]{:S(2)}) copy-start(f32[2048]{0:T(1024)} %get-tuple-element.865) | copy-start | bytes 24580
  1207.0 77.5 %copy-start.19 = (bf16[256,2816]{0,1:T(8,128)(2,1)S(1)}, bf16[256,2816]{0,1:T(8,128)(2,1)}, u32[]{:S(2)}) copy-start(bf16[256,2816]{0,1:T(8,128)(2,1)} %reduce-scatter.6.cloned.1.call-done) | copy-start | bytes 4325380
  1207.0 47.8 %collective-permute-start.29 = (bf16[512,2048]{1,0:T(8,128)(2,1)S(1)}, bf16[512,2048]{1,0:T(8,128)(2,1)S(1)}, u32[]{:S(2)}, u32[]{:S(2)}) collective-permute-start(bf16[512,2048]{1,0:T(8,128)(2,1)S(1)} %add_convert_fusion.7), channel_id=1, source_target_pairs={{0,2},{1,3},{2,0},{3,1},{4,6},{5,7},{6,4},{7,5},{8,10},{9,11},{10,... | collective-permute-start | bytes 6291464 | tf_op jit(solution)/shard_map/ppermute | solution.py:43
  1255.7 40.3 %collective-permute-start.30 = (bf16[512,2048]{1,0:T(8,128)(2,1)S(1)}, bf16[512,2048]{1,0:T(8,128)(2,1)}, u32[]{:S(2)}, u32[]{:S(2)}) collective-permute-start(bf16[512,2048]{1,0:T(8,128)(2,1)S(1)} %add_convert_fusion.6), channel_id=1, source_target_pairs={{0,1},{1,0},{2,3},{3,2},{4,5},{5,4},{6,7},{7,6},{8,9},{9,8},{10,11... | collective-permute-start | bytes 6291464 | tf_op jit(solution)/shard_map/ppermute | solution.py:43
  1265.0 1.6 collective-permute-start.31
  1267.6 5.8 collective-permute-start.32
  1273.5 5.0 collective-permute-start.33
  1279.2 6.1 collective-permute-start.34
  1286.9 7.8 collective-permute-start.35
  (137 other events, 696.3 us)
Sparse Core Ops, SparseCore 0:
  13.0 153.2 all-gather.2
  168.3 249.2 all-gather.4
  638.7 135.5 reduce-scatter.3
  825.5 201.8 reduce-scatter.5
  1086.9 145.0 reduce-scatter.7

commit v2 on v1

v2 whole, which is shorter than its diff:
```python
from functools import partial

import jax
import jax.numpy as jnp
from jax import lax
from jax.experimental import pallas as pl
from jax.experimental.pallas import tpu as pltpu
from jax.sharding import PartitionSpec as P

SUBSPACE_SIZE = 64
PAIR = 128
GROUP = 16
TILE = 256


EPS = 1e-05
GROUP_EPS = 4.0


def shifted(x, axis, by):
    count = lax.axis_size(axis)
    pairs = [(i, i + by) for i in range(count) if 0 <= i + by < count]
    return lax.ppermute(x, axis, pairs)


def earlier_shift(x, axis, by):
    count = lax.axis_size(axis)
    return lax.ppermute(x, axis, [(i, i + by) for i in range(count) if 0 <= i + by < count])


def carried(mult, sums, axis, toward):
    count = lax.axis_size(axis)
    low = (mult.astype(jnp.bfloat16), sums.astype(jnp.bfloat16))
    arrived = [
        jax.tree.map(lambda part: earlier_shift(part, axis, toward * by), low)
        for by in range(1, count)
    ]
    state = jnp.zeros_like(sums)
    for far_mult, far_sums in reversed(arrived):
        state = far_mult.astype(jnp.float32) * state + far_sums.astype(jnp.float32)
    return state


def partner(x, bit):
    count = lax.axis_size("tp")
    return lax.ppermute(x, "tp", [(i, i ^ bit) for i in range(count)])


def halves(x, axis, bit):
    size = x.shape[axis] // 2
    mine = (lax.axis_index("tp") // bit) % 2
    return (
        lax.dynamic_slice_in_dim(x, mine * size, size, axis),
        lax.dynamic_slice_in_dim(x, (1 - mine) * size, size, axis),
    )


def add_low(left, right):
    return (left.astype(jnp.float32) + right.astype(jnp.float32)).astype(jnp.bfloat16)


def ordered(mine, other, axis, bit):
    first = (lax.axis_index("tp") // bit) % 2 == 0
    return jnp.where(
        first,
        jnp.concatenate([mine, other], axis),
        jnp.concatenate([other, mine], axis),
    )


def tp_sum(x):
    mine, other = halves(x, 0, 1)
    part = add_low(mine, partner(other, 1))
    bit = 2
    while bit < lax.axis_size("tp"):
        part = add_low(part, partner(part, bit))
        bit *= 2
    return ordered(part, partner(part, 1), 0, 1)


def whole_sum(x, axes):
    for axis in axes:
        count = lax.axis_size(axis)
        bit = 1
        while bit < count:
            x = x + lax.ppermute(x, axis, [(i, i ^ bit) for i in range(count)])
            bit *= 2
    return x


def tp_scatter(x):
    count, place = lax.axis_size("tp"), lax.axis_index("tp")
    width = x.shape[1] // count
    parts = [
        lax.dynamic_slice_in_dim(x, (place ^ relative) * width, width, 1)
        for relative in range(count)
    ]
    bit = 1
    while bit < count:
        for relative in reversed(range(count)):
            if relative & bit and relative & (bit - 1) == 0:
                arrived = partner(parts[relative], bit)
                parts[relative ^ bit] = add_low(parts[relative ^ bit], arrived)
        bit *= 2
    return parts[0]


def tp_gather(x):
    count, place = lax.axis_size("tp"), lax.axis_index("tp")
    width = x.shape[1]
    parts = {0: x}
    bit = count // 2
    while bit:
        parts.update({relative ^ bit: partner(part, bit) for relative, part in parts.items()})
        bit //= 2
    whole = jnp.zeros((x.shape[0], width * count), x.dtype)
    for relative, part in parts.items():
        whole = lax.dynamic_update_slice_in_dim(whole, part, (place ^ relative) * width, 1)
    return whole


def after(value, *earlier):
    return lax.optimization_barrier((value,) + earlier)


def matmul(left, right):
    return jnp.dot(left, right, preferred_element_type=jnp.float32)


def matmul_tn(left, right):
    return lax.dot_general(
        left, right, (((0,), (0,)), ((), ())), preferred_element_type=jnp.float32
    )


def matmul_nt(left, right):
    return lax.dot_general(
        left, right, (((1,), (1,)), ((), ())), preferred_element_type=jnp.float32
    )


def dot_nn(left, right):
    return lax.dot_general(
        left, right, (((1,), (0,)), ((), ())), preferred_element_type=jnp.float32
    )


def lanes_of(shape):
    return lax.broadcasted_iota(jnp.int32, shape, len(shape) - 1)


def low_head(shape):
    return lanes_of(shape) < SUBSPACE_SIZE


def head_sum(x):
    first = low_head(x.shape)
    low = jnp.sum(jnp.where(first, x, 0.0), -1, keepdims=True)
    high = jnp.sum(jnp.where(first, 0.0, x), -1, keepdims=True)
    return jnp.where(first, low, high)


def fold_pair(both):
    return jnp.where(
        low_head((SUBSPACE_SIZE, PAIR)), both[:SUBSPACE_SIZE], both[SUBSPACE_SIZE:]
    )


def spread_pair(folded):
    first = low_head((SUBSPACE_SIZE, PAIR))
    return jnp.concatenate(
        [jnp.where(first, folded, 0.0), jnp.where(first, 0.0, folded)], axis=0
    ).astype(jnp.bfloat16)


def head_parts(x):
    first = low_head(x.shape)
    zero = jnp.zeros_like(x)
    return jnp.where(first, x, zero), jnp.where(first, zero, x)


def places(length):
    return lax.broadcasted_iota(jnp.int32, (length, PAIR), 0).astype(jnp.float32)


def carry_kernel(k_ref, v_ref, log_ref, cols_ref, out_ref):
    length = k_ref.shape[0]
    closing = jnp.exp((length - 1.0 - places(length)) * log_ref[...])
    ending = cols_ref[:, 2:3]
    k_end = (k_ref[...].astype(jnp.float32) * closing * ending).astype(jnp.bfloat16)
    out_ref[0, 0] = fold_pair(matmul_tn(v_ref[...], k_end))


def group_norm(attend):
    centered = attend - head_sum(attend) * (1.0 / SUBSPACE_SIZE)
    inverse = lax.rsqrt(head_sum(centered * centered) * (1.0 / SUBSPACE_SIZE) + GROUP_EPS)
    return centered * inverse, inverse


def mix_kernel(
    r_ref, k_ref, v_ref, gate_ref, log_ref, rows_ref, cols_ref, seg_ref, state_ref,
    joined_ref, attend_ref,
):
    length = r_ref.shape[0]
    at = places(length)
    log = log_ref[...]
    r = r_ref[...].astype(jnp.float32)
    k = k_ref[...].astype(jnp.float32)
    v = v_ref[...]
    q_low = (r * jnp.exp(at * log)).astype(jnp.bfloat16)
    k_low = (k * jnp.exp(-(at + 1.0) * log)).astype(jnp.bfloat16)
    state = spread_pair(state_ref[0, 0])
    bonus = head_sum(r * rows_ref[0:1, :] * k)
    base = bonus * v.astype(jnp.float32) + cols_ref[:, 1:2] * matmul_nt(q_low, state)
    step = min(length, TILE)
    for top in range(0, length, step):
        reach = top + step
        rows = slice(top, reach)
        keep = pair_mask(cols_ref[rows, 0:1], seg_ref[0, :, :reach], top, step, reach)
        parts = []
        for q_part in head_parts(q_low[rows]):
            scores = matmul_nt(q_part, k_low[:reach])
            scores = jnp.where(keep, scores, 0.0).astype(jnp.bfloat16)
            parts.append(dot_nn(scores, v[:reach]))
        attend = base[rows] + jnp.where(low_head(parts[0].shape), parts[0], parts[1])
        unit, _ = group_norm(attend)
        grouped = unit * rows_ref[1:2, :] + rows_ref[2:3, :]
        gate = gate_ref[rows, :]
        attend_ref[rows, :] = attend
        joined_ref[rows, :] = (grouped * (gate * jax.nn.sigmoid(gate))).astype(jnp.bfloat16)


def pair_mask(seg_col, seg_row, top, count, reach):
    later = lax.broadcasted_iota(jnp.int32, (count, reach), 0) + top
    return (seg_col == seg_row) & (later > lanes_of((count, reach)))


def pair_mask_t(seg_col, seg_row, top, count, start):
    width = seg_row.shape[1]
    earlier = lax.broadcasted_iota(jnp.int32, (count, width), 0) + top
    return (seg_col == seg_row) & (lanes_of((count, width)) + start > earlier)


def gate_back_kernel(
    dj_ref, attend_ref, gate_ref, r_ref, log_ref, rows_ref, cols_ref,
    dgate_ref, dattend_ref, state_ref, small_ref,
):
    length = r_ref.shape[0]
    d_joined = dj_ref[...]
    gate = gate_ref[...]
    unit, inverse = group_norm(attend_ref[...])
    gain = rows_ref[1:2, :]
    grouped = unit * gain + rows_ref[2:3, :]
    sig = jax.nn.sigmoid(gate)
    dgate_ref[...] = (d_joined * grouped * sig * (1.0 + gate * (1.0 - sig))).astype(jnp.bfloat16)
    d_grouped = d_joined * gate * sig
    sums = [
        jnp.sum(d_grouped * unit, axis=0, keepdims=True),
        jnp.sum(d_grouped, axis=0, keepdims=True),
    ]
    scaled = d_grouped * gain
    share = 1.0 / SUBSPACE_SIZE
    d_attend = (
        inverse * (scaled - head_sum(scaled) * share - unit * (head_sum(scaled * unit) * share))
    ).astype(jnp.bfloat16)
    dattend_ref[...] = d_attend
    rising = jnp.exp(places(length) * log_ref[...])
    q_live = (r_ref[...].astype(jnp.float32) * rising * cols_ref[:, 1:2]).astype(jnp.bfloat16)
    state_ref[0, 0] = fold_pair(matmul_tn(d_attend, q_live))
    collect(small_ref, sums)


def collect(small_ref, sums):
    pad = jnp.zeros((small_ref.shape[0] - len(sums), sums[0].shape[1]), jnp.float32)
    total = jnp.concatenate(sums + [pad], axis=0)

    @pl.when(pl.program_id(1) == 0)
    def _():
        small_ref[...] = total

    @pl.when(pl.program_id(1) > 0)
    def _():
        small_ref[...] += total


def mix_back_kernel(
    r_ref, k_ref, v_ref, da_ref, log_ref, rows_ref, cols_ref, seg_ref, state_ref, gstate_ref,
    mult_ref, dr_ref, dk_ref, dv_ref, small_ref,
):
    length = r_ref.shape[0]
    at = places(length)
    log = log_ref[...]
    reward = rows_ref[0:1, :]
    r = r_ref[...].astype(jnp.float32)
    k = k_ref[...].astype(jnp.float32)
    v = v_ref[...]
    da = da_ref[...]
    rising = jnp.exp(at * log)
    falling = jnp.exp(-(at + 1.0) * log)
    closing = jnp.exp((length - 1.0 - at) * log) * cols_ref[:, 2:3]
    q_low = (r * rising).astype(jnp.bfloat16)
    k_low = (k * falling).astype(jnp.bfloat16)
    k_end = (k * closing).astype(jnp.bfloat16)
    state, gstate = state_ref[0, 0], gstate_ref[0, 0]
    state_low, gstate_low = spread_pair(state), spread_pair(gstate)
    v_f, da_f = v.astype(jnp.float32), da.astype(jnp.float32)
    dot_va = head_sum(v_f * da_f)
    dk_end = dot_nn(v, gstate_low)
    dq_base = cols_ref[:, 1:2] * dot_nn(da, state_low)
    dv_base = head_sum(r * reward * k) * da_f + matmul_nt(k_end, gstate_low)
    q_f, k_f = q_low.astype(jnp.float32), k_low.astype(jnp.float32)
    d_log = jnp.sum((length - 1.0 - at) * k_end.astype(jnp.float32) * dk_end, 0, keepdims=True)
    d_log += length * mult_ref[0, 0] * jnp.sum(
        state.astype(jnp.bfloat16).astype(jnp.float32)
        * gstate.astype(jnp.bfloat16).astype(jnp.float32),
        0,
        keepdims=True,
    )
    step = min(length, TILE)
    for top in range(0, length, step):
        rows = slice(top, top + step)
        reach = top + step
        keep = pair_mask(cols_ref[rows, 0:1], seg_ref[0, :, :reach], top, step, reach)
        dq = []
        for da_part in head_parts(da[rows]):
            pull = jnp.where(keep, matmul_nt(da_part, v[:reach]), 0.0).astype(jnp.bfloat16)
            dq.append(dot_nn(pull, k_low[:reach]))
        first = low_head(dq[0].shape)
        dq = jnp.where(first, dq[0], dq[1]) + dq_base[rows]
        d_log += jnp.sum(at[rows] * q_f[rows] * dq, 0, keepdims=True)
        dr_ref[rows, :] = (dq * rising[rows] + reward * k[rows] * dot_va[rows]).astype(jnp.bfloat16)
        keep = pair_mask_t(cols_ref[rows, 0:1], seg_ref[0, :, top:], top, step, top)
        dk, dv = [], []
        for v_part, k_part in zip(head_parts(v[rows]), head_parts(k_low[rows])):
            pull = jnp.where(keep, matmul_nt(v_part, da[top:]), 0.0).astype(jnp.bfloat16)
            dk.append(dot_nn(pull, q_low[top:]))
            scores = jnp.where(keep, matmul_nt(k_part, q_low[top:]), 0.0).astype(jnp.bfloat16)
            dv.append(dot_nn(scores, da[top:]))
        dk = jnp.where(first, dk[0], dk[1])
        d_log -= jnp.sum((at[rows] + 1.0) * k_f[rows] * dk, 0, keepdims=True)
        dk_ref[rows, :] = (
            dk * falling[rows]
            + dk_end[rows] * closing[rows]
            + reward * r[rows] * dot_va[rows]
        ).astype(jnp.bfloat16)
        dv_ref[rows, :] = (jnp.where(first, dv[0], dv[1]) + dv_base[rows]).astype(jnp.bfloat16)
    collect(small_ref, [d_log * jnp.exp(-log), jnp.sum(r * k * dot_va, 0, keepdims=True)])


def pair_call(kernel, seqs, length, width, operands, outs, name, flops):
    pairs = width // PAIR
    specs = {
        "wide": pl.BlockSpec((length, PAIR), lambda p, s: (s, p)),
        "vector": pl.BlockSpec((1, PAIR), lambda p, s: (0, p)),
        "vectors": pl.BlockSpec((8, PAIR), lambda p, s: (0, p)),
        "cols": pl.BlockSpec((length, 4), lambda p, s: (s, 0)),
        "row": pl.BlockSpec((1, 1, length), lambda p, s: (s, 0, 0)),
        "state": pl.BlockSpec((1, 1, SUBSPACE_SIZE, PAIR), lambda p, s: (s, p, 0, 0)),
        "mult": pl.BlockSpec((1, 1, 1, PAIR), lambda p, s: (s, p, 0, 0)),
    }
    shapes = {
        "wide": (seqs * length, width),
        "vectors": (8, width),
        "state": (seqs, pairs, SUBSPACE_SIZE, PAIR),
    }
    kinds, arrays = zip(*operands)
    size = sum(array.size * array.dtype.itemsize for array in arrays)
    return pl.pallas_call(
        kernel,
        grid=(pairs, seqs),
        in_specs=[specs[kind] for kind in kinds],
        out_specs=[specs[kind] for kind, _ in outs],
        out_shape=[jax.ShapeDtypeStruct(shapes[kind], dtype) for kind, dtype in outs],
        cost_estimate=pl.CostEstimate(flops=flops, bytes_accessed=2 * size, transcendentals=0),
        name=name,
    )(*arrays)


def norm_rows(x, gain, bias_term):
    centered = x - jnp.mean(x, -1, keepdims=True)
    inverse = lax.rsqrt(jnp.mean(centered * centered, -1, keepdims=True) + EPS)
    unit = centered * inverse
    return unit * gain + bias_term, unit, inverse


def total_rows(refs, rows):
    total = refs[0][rows, :].astype(jnp.float32)
    for ref in refs[1:]:
        total = total + ref[rows, :].astype(jnp.float32)
    return total


def blend_kernel(parts, mixes, per_seq, *refs):
    x_refs, refs = refs[:parts], refs[parts:]
    keep_ref, edge_ref, norm_ref, mix_ref = refs[:4]
    outs, before = refs[4 : 4 + mixes], refs[4 + mixes]
    rows = x_refs[0].shape[0]

    @pl.when(pl.program_id(0) % per_seq == 0)
    def _():
        before[...] = jnp.broadcast_to(edge_ref[0], before.shape)

    def group(g, _):
        place = pl.ds(pl.multiple_of(g * GROUP, GROUP), GROUP)
        normed, _, _ = norm_rows(total_rows(x_refs, place), norm_ref[0:1, :], norm_ref[1:2, :])
        top = lax.broadcasted_iota(jnp.int32, normed.shape, 0) == 0
        previous = jnp.where(top, before[0:1, :], pltpu.roll(normed, 1, 0)) * keep_ref[place, 0:1]
        before[0:1, :] = normed[GROUP - 1 :, :]
        delta = normed - previous
        for at, out in enumerate(outs):
            out[place, :] = (previous + mix_ref[at : at + 1, :] * delta).astype(jnp.bfloat16)
        return 0

    lax.fori_loop(0, rows // GROUP, group, 0)


def blend(xs, keep, edge, norm, mixers, piece, name):
    tokens, width = xs[0].shape
    rows = min(piece, 256)
    mixes = mixers.shape[0]
    per_seq = piece // rows
    wide = pl.BlockSpec((rows, width), lambda i: (i, 0))
    return pl.pallas_call(
        partial(blend_kernel, len(xs), mixes, per_seq),
        grid=(tokens // rows,),
        in_specs=[wide] * len(xs)
        + [
            pl.BlockSpec((rows, 1), lambda i: (i, 0)),
            pl.BlockSpec((1, 1, width), lambda i: (i // per_seq, 0, 0)),
            pl.BlockSpec((2, width), lambda i: (0, 0)),
            pl.BlockSpec((mixes, width), lambda i: (0, 0)),
        ],
        out_specs=[wide] * mixes,
        out_shape=[jax.ShapeDtypeStruct((tokens, width), jnp.bfloat16)] * mixes,
        scratch_shapes=[pltpu.VMEM((8, width), jnp.float32)],
        cost_estimate=pl.CostEstimate(
            flops=20 * tokens * width,
            bytes_accessed=2 * tokens * width * (len(xs) + mixes),
            transcendentals=0,
        ),
        name=name,
    )(*xs, keep, edge, norm, mixers)


def blend_back_kernel(parts, mixes, per_seq, own, *refs):
    x_refs, refs = refs[:parts], refs[parts:]
    halo_refs, refs = refs[:parts], refs[parts:]
    grad_refs, refs = refs[:mixes], refs[mixes:]
    weight_refs, refs = refs[:mixes], refs[mixes:]
    keep_ref, edge_ref, back_ref, norm_ref, mix_ref = refs[:5]
    refs = refs[5:]
    own_refs, refs = refs[: 2 * own], refs[2 * own :]
    out_ref, small_ref, d_scr, unit_scr, inv_scr, sums, after_row = refs
    rows, width = x_refs[0].shape
    tiles = pl.num_programs(0)
    tile = tiles - 1 - pl.program_id(0)
    gain, bias_term = norm_ref[0:1, :], norm_ref[1:2, :]

    @pl.when(pl.program_id(0) == 0)
    def _():
        sums[...] = jnp.zeros_like(sums)

    @pl.when(tile % per_seq == per_seq - 1)
    def _():
        after_row[...] = jnp.broadcast_to(back_ref[0], after_row.shape)

    for at in range(mixes):
        d_scr[at] = matmul_nt(grad_refs[at][...], weight_refs[at][...])

    halo, _, _ = norm_rows(total_rows(halo_refs, slice(None)), gain, bias_term)
    first = jnp.where(tile % per_seq == 0, edge_ref[0], halo[GROUP - 1 :, :])

    def unit_group(g, _):
        place = pl.ds(pl.multiple_of(g * GROUP, GROUP), GROUP)
        _, unit, inverse = norm_rows(total_rows(x_refs, place), gain, bias_term)
        unit_scr[place, :] = unit
        inv_scr[place, :] = jnp.broadcast_to(inverse, (GROUP, inv_scr.shape[1]))
        return 0

    groups = rows // GROUP
    lax.fori_loop(0, groups, unit_group, 0)

    def group(step, _):
        g = groups - 1 - step
        start = pl.multiple_of(g * GROUP, GROUP)
        place = pl.ds(start, GROUP)
        unit = unit_scr[place, :]
        inverse = inv_scr[place, 0:1]
        keep = keep_ref[place, 0:1]
        normed = unit * gain + bias_term
        before_at = pl.multiple_of(jnp.maximum(start - 8, 0), 8)
        inside = unit_scr[pl.ds(before_at, 8), :][7:8, :] * gain + bias_term
        before = jnp.where(g == 0, first, inside)
        place_in = lax.broadcasted_iota(jnp.int32, normed.shape, 0)
        delta = normed - jnp.where(place_in == 0, before, pltpu.roll(normed, 1, 0)) * keep
        d_norm = jnp.zeros_like(normed)
        d_all = jnp.zeros_like(normed)
        for at in range(mixes):
            d_in = d_scr[at, place, :]
            d_norm = d_norm + d_in * mix_ref[at : at + 1, :]
            d_all = d_all + d_in
            product = d_in * delta
            sums[2 + at] += product[:8] + product[8:]
        d_prev = (d_all - d_norm) * keep
        d_next = jnp.where(
            place_in == GROUP - 1, after_row[0:1, :], pltpu.roll(d_prev, GROUP - 1, 0)
        )
        after_row[0:1, :] = d_prev[0:1, :]
        d_norm = d_norm + d_next
        product = d_norm * unit
        sums[0] += product[:8] + product[8:]
        sums[1] += d_norm[:8] + d_norm[8:]
        scaled = d_norm * gain
        d_in = inverse * (
            scaled
            - jnp.mean(scaled, -1, keepdims=True)
            - unit * jnp.mean(scaled * unit, -1, keepdims=True)
        )
        if own:
            extra = own_refs[0][place, :].astype(jnp.float32)
            extra = jnp.concatenate([extra] * (width // extra.shape[1]), axis=1)
            d_in = d_in + extra * own_refs[1][...]
        out_ref[place, :] = d_in.astype(jnp.bfloat16)
        return 0

    lax.fori_loop(0, groups, group, 0)

    @pl.when(pl.program_id(0) == tiles - 1)
    def _():
        for at in range(2 + mixes):
            small_ref[at : at + 1, :] = jnp.sum(sums[at], 0, keepdims=True)


def blend_back(xs, grads, weights, keep, edge, back, norm, mixers, piece, own, name):
    tokens, width = xs[0].shape
    rows = min(piece, 128)
    mixes = mixers.shape[0]
    per_seq = piece // rows
    tiles = tokens // rows

    def reverse(i):
        return tiles - 1 - i

    def halo_at(i):
        return (jnp.maximum(reverse(i) * (rows // GROUP) - 1, 0), 0)

    wide = pl.BlockSpec((rows, width), lambda i: (reverse(i), 0))
    per = pl.BlockSpec((1, 1, width), lambda i: (reverse(i) // per_seq, 0, 0))
    weight_specs, weight_arrays = [], []
    for (array, at), grad in zip(weights, grads):
        weight_specs.append(
            pl.BlockSpec(
                (width, grad.shape[1]), partial(lambda at, i: (0, at), at),
                pipeline_mode=pl.Buffered(1),
            )
        )
        weight_arrays.append(array)
    return pl.pallas_call(
        partial(blend_back_kernel, len(xs), mixes, per_seq, int(own is not None)),
        grid=(tiles,),
        in_specs=[wide] * len(xs)
        + [pl.BlockSpec((GROUP, width), halo_at)] * len(xs)
        + [pl.BlockSpec((rows, grad.shape[1]), lambda i: (reverse(i), 0)) for grad in grads]
        + weight_specs
        + [
            pl.BlockSpec((rows, 1), lambda i: (reverse(i), 0)),
            per,
            per,
            pl.BlockSpec((2, width), lambda i: (0, 0)),
            pl.BlockSpec((mixes, width), lambda i: (0, 0)),
        ]
        + (
            [
                pl.BlockSpec((rows, own[0].shape[1]), lambda i: (reverse(i), 0)),
                pl.BlockSpec((1, width), lambda i: (0, 0)),
            ]
            if own is not None
            else []
        ),
        out_specs=[wide, pl.BlockSpec((8, width), lambda i: (0, 0))],
        out_shape=[
            jax.ShapeDtypeStruct((tokens, width), jnp.bfloat16),
            jax.ShapeDtypeStruct((8, width), jnp.float32),
        ],
        scratch_shapes=[
            pltpu.VMEM((mixes, rows, width), jnp.float32),
            pltpu.VMEM((rows, width), jnp.float32),
            pltpu.VMEM((rows, PAIR), jnp.float32),
            pltpu.VMEM((2 + mixes, 8, width), jnp.float32),
            pltpu.VMEM((8, width), jnp.float32),
        ],
        cost_estimate=pl.CostEstimate(
            flops=2 * tokens * width * sum(grad.shape[1] for grad in grads),
            bytes_accessed=2 * tokens * width * 4,
            transcendentals=0,
        ),
        name=name,
    )(*xs, *xs, *grads, *weight_arrays, keep, edge, back, norm, mixers, *(own or ()))


def per_device(
    entering_activations,
    document_indices,
    acceptor_matrix,
    lookup_matrix,
    payload_matrix,
    valve_matrix,
    result_matrix,
    ffn_lookup_matrix,
    ffn_payload_matrix,
    ffn_acceptor_matrix,
    first_standardize_scaling,
    first_standardize_offset,
    acceptor_lerp_factor,
    lookup_lerp_factor,
    payload_lerp_factor,
    valve_lerp_factor,
    token_fading,
    diagonal_reward,
    subspace_standardize_scaling,
    subspace_standardize_offset,
    second_standardize_scaling,
    second_standardize_offset,
    ffn_lookup_lerp,
    ffn_acceptor_lerp,
    upstream_derivative,
):
    seqs_here, piece_len, embedding_extent = entering_activations.shape
    token_count = seqs_here * piece_len
    tp_count = lax.axis_size("tp")
    fourth_extent = embedding_extent // tp_count
    sharded_layout = lax.axis_index("tp") * fourth_extent
    ctx_place = lax.axis_index("ctx") * piece_len
    padded_seg = jnp.concatenate(
        [jnp.full((seqs_here, 1), -1, jnp.int32), document_indices], axis=1
    )
    segment_present = lax.dynamic_slice_in_dim(document_indices, ctx_place, piece_len, 1)
    seg_before = lax.dynamic_slice_in_dim(padded_seg, ctx_place, piece_len, 1)
    document_begins = seg_before[:, :1]
    pairs_here = fourth_extent // PAIR
    same_mask = segment_present == seg_before
    live_mask = segment_present == document_begins
    ending_mask = segment_present == segment_present[:, -1:]
    cols = jnp.stack([segment_present, live_mask, ending_mask, same_mask], axis=-1)
    cols = cols.astype(jnp.float32).reshape(token_count, 4)
    keep = same_mask.astype(jnp.float32).reshape(token_count, 1)
    keep_first = same_mask[:, :1].astype(jnp.float32)
    seg_row = segment_present.astype(jnp.float32)[:, None, :]
    owners = ("fsdp", "ctx")
    w_time = lax.all_gather(
        jnp.concatenate(
            [acceptor_matrix, lookup_matrix, payload_matrix, valve_matrix, result_matrix.T], axis=1
        ),
        owners,
        axis=0,
        tiled=True,
    )
    w_chan = lax.all_gather(
        jnp.concatenate([ffn_lookup_matrix, ffn_payload_matrix.T, ffn_acceptor_matrix], axis=1),
        owners,
        axis=0,
        tiled=True,
    )
    units = ffn_lookup_matrix.shape[1]
    w_recept, w_key, w_value, w_gate, w_output_t = (
        w_time[:, at * fourth_extent : (at + 1) * fourth_extent] for at in range(5)
    )
    w_chankey = w_chan[:, :units]
    w_chanvalue_t = w_chan[:, units : 2 * units]
    w_chanrecept = w_chan[:, 2 * units :]
    x_low = entering_activations.reshape(token_count, embedding_extent)
    norm_one = jnp.stack([first_standardize_scaling, first_standardize_offset])
    norm_two = jnp.stack([second_standardize_scaling, second_standardize_offset])
    mix_one = jnp.stack(
        [acceptor_lerp_factor, lookup_lerp_factor, payload_lerp_factor, valve_lerp_factor]
    )
    mix_two = jnp.stack([ffn_lookup_lerp, ffn_acceptor_lerp])

    def edge_from(last_rows, norm):
        last, _, _ = norm_rows(last_rows, norm[0], norm[1])
        return shifted(last, "ctx", 1)[:, None]

    def back_from(grads, weights, mixers):
        first = jnp.zeros((seqs_here, embedding_extent), jnp.float32)
        for at, (grad_low, weight) in enumerate(zip(grads, weights)):
            rows = grad_low.reshape(seqs_here, piece_len, -1)[:, 0]
            first = first + matmul_nt(rows, weight) * (1.0 - mixers[at])
        return shifted(first * keep_first, "ctx", -1)[:, None]

    edge_one = edge_from(entering_activations[:, -1].astype(jnp.float32), norm_one)
    mixed_in = blend((x_low,), keep, edge_one, norm_one, mix_one, piece_len, "blend_one")
    key_low = matmul(mixed_in[1], w_key).astype(jnp.bfloat16)
    value_low = matmul(mixed_in[2], w_value).astype(jnp.bfloat16)

    def own_share(vector):
        return lax.dynamic_slice_in_dim(vector, sharded_layout, fourth_extent, 0)[None]

    log_row = jnp.log(own_share(token_fading))
    vectors = jnp.concatenate(
        [own_share(diagonal_reward), own_share(subspace_standardize_scaling)]
        + [own_share(subspace_standardize_offset)] * 6
    )
    call = partial(pair_call, seqs=seqs_here, length=piece_len, width=fourth_extent)
    square = 2 * token_count * piece_len * fourth_extent
    (carry_sums,) = call(
        carry_kernel,
        operands=[("wide", key_low), ("wide", value_low), ("vector", log_row), ("cols", cols)],
        outs=[("state", jnp.float32)],
        name="carry",
        flops=square // 8,
    )
    alive_mask = (live_mask[:, -1]).astype(jnp.float32)[:, None, None, None]
    carry_mult = alive_mask * jnp.exp(float(piece_len) * log_row).reshape(1, pairs_here, 1, PAIR)
    incoming = carried(carry_mult, carry_sums, "ctx", 1)
    recept_low = matmul(mixed_in[0], w_recept).astype(jnp.bfloat16)
    gate_pre = matmul(mixed_in[3], w_gate)
    joined_low, attend = call(
        mix_kernel,
        operands=[
            ("wide", recept_low),
            ("wide", key_low),
            ("wide", value_low),
            ("wide", gate_pre),
            ("vector", log_row),
            ("vectors", vectors),
            ("cols", cols),
            ("row", seg_row),
            ("state", incoming),
        ],
        outs=[("wide", jnp.bfloat16), ("wide", jnp.float32)],
        name="mix",
        flops=2 * square,
    )
    mixed_out = tp_sum(matmul_nt(joined_low, w_output_t).astype(jnp.bfloat16))
    last_rows = entering_activations[:, -1].astype(jnp.float32) + mixed_out.reshape(
        seqs_here, piece_len, embedding_extent
    )[:, -1].astype(jnp.float32)
    edge_two = edge_from(last_rows, norm_two)
    key_in, rec_in = blend(
        (x_low, mixed_out), keep, edge_two, norm_two, mix_two, piece_len, "blend_two"
    )
    rec_gate = jax.nn.sigmoid(matmul(rec_in, w_chanrecept))
    d_result_low = upstream_derivative.reshape(token_count, fourth_extent)
    d_result = d_result_low.astype(jnp.float32)
    d_chan = (d_result * rec_gate).astype(jnp.bfloat16)
    d_chan_full = tp_gather(d_chan)
    key_pre = matmul(key_in, w_chankey)
    hidden = jnp.square(jax.nn.relu(key_pre)).astype(jnp.bfloat16)
    grad_chanvalue = matmul_tn(hidden, d_chan_full).astype(jnp.bfloat16)
    g_chanvalue = lax.psum_scatter(grad_chanvalue, owners, scatter_dimension=1, tiled=True)
    hidden, grad_chanvalue = after(hidden, grad_chanvalue)
    chan_sum = tp_scatter(matmul_nt(hidden, w_chanvalue_t).astype(jnp.bfloat16)).astype(jnp.float32)
    middle_q = lax.dynamic_slice_in_dim(x_low, sharded_layout, fourth_extent, 1).astype(
        jnp.float32
    ) + lax.dynamic_slice_in_dim(mixed_out, sharded_layout, fourth_extent, 1).astype(jnp.float32)
    result = (
        (middle_q + rec_gate * chan_sum)
        .astype(jnp.bfloat16)
        .reshape(seqs_here, piece_len, fourth_extent)
    )
    d_rec_pre = (d_result * chan_sum * rec_gate * (1.0 - rec_gate)).astype(jnp.bfloat16)
    d_hidden = matmul(d_chan_full, w_chanvalue_t)
    d_key_pre = (d_hidden * 2.0 * jax.nn.relu(key_pre)).astype(jnp.bfloat16)
    grad_chankey = matmul_tn(key_in, d_key_pre)
    grad_chanrecept = matmul_tn(rec_in, d_rec_pre)
    full_shape = (seqs_here, piece_len, embedding_extent)
    own_mask = (jnp.arange(embedding_extent) // fourth_extent == lax.axis_index("tp")).astype(
        jnp.float32
    )[None]
    d_middle_part, chan_small = blend_back(
        (x_low, mixed_out),
        (d_key_pre, d_rec_pre),
        ((w_chan, 0), (w_chan, 2 * units // fourth_extent)),
        keep,
        edge_two,
        back_from((d_key_pre, d_rec_pre), (w_chankey, w_chanrecept), mix_two),
        norm_two,
        mix_two,
        piece_len,
        (d_result_low, own_mask),
        "blend_two_back",
    )
    d_mixed = tp_sum(d_middle_part)
    grad_output_t = matmul_tn(d_mixed, joined_low)
    grads_chan = jnp.concatenate(
        [item.astype(jnp.bfloat16) for item in (grad_output_t, grad_chanrecept, grad_chankey)],
        axis=1,
    )
    d_mixed, grads_chan, g_chanvalue = after(d_mixed, grads_chan, g_chanvalue)
    g_chan = lax.psum_scatter(grads_chan, owners, scatter_dimension=0, tiled=True)
    d_joined = matmul(d_mixed, w_output_t)
    d_gate_pre, d_attend, local_grad, group_small = call(
        gate_back_kernel,
        operands=[
            ("wide", d_joined),
            ("wide", attend),
            ("wide", gate_pre),
            ("wide", recept_low),
            ("vector", log_row),
            ("vectors", vectors),
            ("cols", cols),
        ],
        outs=[
            ("wide", jnp.bfloat16),
            ("wide", jnp.bfloat16),
            ("state", jnp.float32),
            ("vectors", jnp.float32),
        ],
        name="gate_back",
        flops=square // 8,
    )
    outgoing_state = carried(carry_mult, local_grad, "ctx", -1)
    d_recept, d_key, d_value, state_small = call(
        mix_back_kernel,
        operands=[
            ("wide", recept_low),
            ("wide", key_low),
            ("wide", value_low),
            ("wide", d_attend),
            ("vector", log_row),
            ("vectors", vectors),
            ("cols", cols),
            ("row", seg_row),
            ("state", incoming),
            ("state", outgoing_state),
            ("mult", carry_mult),
        ],
        outs=[("wide", jnp.bfloat16)] * 3 + [("vectors", jnp.float32)],
        name="mix_back",
        flops=6 * square,
    )
    d_lows = [d_recept, d_key, d_value, d_gate_pre]
    weights_time = (w_recept, w_key, w_value, w_gate)
    grads_time = jnp.concatenate(
        [
            matmul_tn(mixed, grad_low).astype(jnp.bfloat16)
            for mixed, grad_low in zip(mixed_in, d_lows)
        ],
        axis=1,
    )
    *d_lows, grads_time, g_chan = after(d_lows[0], *d_lows[1:], grads_time, g_chan)
    g_time = lax.psum_scatter(grads_time, owners, scatter_dimension=0, tiled=True)
    d_input_part, time_small = blend_back(
        (x_low,),
        d_lows,
        [(w_time, at) for at in range(4)],
        keep,
        edge_one,
        back_from(d_lows, weights_time, mix_one),
        norm_one,
        mix_one,
        piece_len,
        None,
        "blend_one_back",
    )
    head_small = jnp.concatenate([state_small[:2], group_small[:2]])
    head_small = lax.dynamic_update_slice_in_dim(
        jnp.zeros((4, embedding_extent), jnp.float32), head_small, sharded_layout, 1
    )
    small_sum = whole_sum(
        jnp.concatenate([time_small[:6], head_small, chan_small[:4]], axis=0),
        ("tp", "fsdp", "ctx"),
    )
    owned = embedding_extent // (lax.axis_size("fsdp") * lax.axis_size("ctx"))
    small_owned = lax.dynamic_slice_in_dim(
        small_sum,
        (lax.axis_index("fsdp") * lax.axis_size("ctx") + lax.axis_index("ctx")) * owned,
        owned,
        1,
    )
    d_input_sum = tp_sum(d_input_part)
    grad_inputs = (d_mixed.astype(jnp.float32) + d_input_sum.astype(jnp.float32)).reshape(
        full_shape
    )
    g_chanvalue = g_chanvalue.astype(jnp.float32)
    g_chan = g_chan.astype(jnp.float32)
    g_time = g_time.astype(jnp.float32)
    g_recept, g_key, g_value, g_gate = (
        g_time[:, at * fourth_extent : (at + 1) * fourth_extent] for at in range(4)
    )
    g_output = g_chan[:, :fourth_extent].T
    g_chanrecept = g_chan[:, fourth_extent : 2 * fourth_extent]
    g_chankey = g_chan[:, 2 * fourth_extent :]
    return (
        result,
        grad_inputs,
        g_recept,
        g_key,
        g_value,
        g_gate,
        g_output,
        g_chankey,
        g_chanvalue,
        g_chanrecept,
    ) + tuple(small_owned[at] for at in range(14))


def solution(mesh):
    return jax.shard_map(
        per_device,
        mesh=mesh,
        in_specs=(
            P("fsdp", "ctx", None),
            P("fsdp", None),
            P(("fsdp", "ctx"), "tp"),
            P(("fsdp", "ctx"), "tp"),
            P(("fsdp", "ctx"), "tp"),
            P(("fsdp", "ctx"), "tp"),
            P("tp", ("fsdp", "ctx")),
            P(("fsdp", "ctx"), "tp"),
            P("tp", ("fsdp", "ctx")),
            P(("fsdp", "ctx"), "tp"),
            P(),
            P(),
            P(),
            P(),
            P(),
            P(),
            P(),
            P(),
            P(),
            P(),
            P(),
            P(),
            P(),
            P(),
            P("fsdp", "ctx", "tp"),
        ),
        out_specs=(
            P("fsdp", "ctx", "tp"),
            P("fsdp", "ctx", None),
            P(("fsdp", "ctx"), "tp"),
            P(("fsdp", "ctx"), "tp"),
            P(("fsdp", "ctx"), "tp"),
            P(("fsdp", "ctx"), "tp"),
            P("tp", ("fsdp", "ctx")),
            P(("fsdp", "ctx"), "tp"),
            P("tp", ("fsdp", "ctx")),
            P(("fsdp", "ctx"), "tp"),
            P(("fsdp", "ctx")),
            P(("fsdp", "ctx")),
            P(("fsdp", "ctx")),
            P(("fsdp", "ctx")),
            P(("fsdp", "ctx")),
            P(("fsdp", "ctx")),
            P(("fsdp", "ctx")),
            P(("fsdp", "ctx")),
            P(("fsdp", "ctx")),
            P(("fsdp", "ctx")),
            P(("fsdp", "ctx")),
            P(("fsdp", "ctx")),
            P(("fsdp", "ctx")),
            P(("fsdp", "ctx")),
        ),
        check_vma=False,
    )
```

time: 1330 us -> 1080 us (0.81)
  other arithmetic: 323 us -> 71.2 us
  Pallas kernels: 0 us -> 217 us
  waiting for transfers between devices: 320 us -> 528 us
  local copies, waits for them, and re-layouts: 259 us -> 51.9 us
  matrix products: 328 us -> 133 us
    pallas_call x0 -> x8, Pallas kernels: none -> 217 us  [the longest x2 123 us: blend_back(): pl.pallas_call(partial(blend_back_kernel, len(xs), mixes, per_seq, int(ow...]
    dot_general x106 -> x0, matrix products: 152 us -> none  [the longest x32 47 us: fading_payload_tile(): scores = jnp.einsum('thi,shi->hts', query_dec, key_dec, precision=HIGH)]
    reduce_sum x44 -> x4, other arithmetic: 133 us -> 0.66 us  [the longest x2 0.4 us: norm_rows(): inverse = lax.rsqrt(jnp.mean(centered * centered, -1, keepdims=True) + EPS)]
    reduce_scatter x1, waiting for transfers between devices: 0.02 us -> 108 us  [per_device(): lax.psum_scatter(grads_chan, owners, scatter_dimension=0, tiled=True)]
    all_gather x1, waiting for transfers between devices: 0.01 us -> 78 us  [per_device(): lax.all_gather(jnp.concatenate([ffn_lookup_matrix, ffn_payload_matrix.T,...]
    dynamic_slice x67 -> x3, local copies, waits for them, and re-layouts: 58.8 us -> 2.28 us  [own_share(): lax.dynamic_slice_in_dim(vector, sharded_layout, fourth_extent, 0)[None]]
    mul x54 -> x8, other arithmetic: 54.6 us -> 1.52 us  [the longest x1 1.37 us: per_device(): alive_mask * jnp.exp(float(piece_len) * log_row).reshape(1, pairs_here, 1...]
    dot_general x8, matrix products: 63.8 us -> 27.9 us  [matmul_nt(): lax.dot_general(left, right, (((1,), (1,)), ((), ())), preferred_element_...]
  transfers between devices with their start and end apart: 41 -> 41, of which waited for: 18 -> 25; matrix products, arithmetic and copies ran while one was open for 61% -> 19% of each run, Pallas kernels for 0% -> 20%
where the time goes in v2:
time: 1080 us; the launch traced here: 1070 us
  waiting for transfers between devices  528 us (49%)
  Pallas kernels  217 us (20%)
  matrix products  133 us (12%)
  other arithmetic  71.2 us (7%)
  starting transfers between devices  55.3 us (5%)
  local copies, waits for them, and re-layouts  51.9 us (5%)
  between operations  15.2 us (1%)
    ppermute x15, waiting for transfers between devices, partner(): return lax.ppermute(x, 'tp', [(i, i ^ bit) for i in range(count)])  187 us
    pallas_call x2, Pallas kernels, blend_back(): pl.pallas_call(partial(blend_back_kernel, len(xs), mixes, per_seq, int(ow...  123 us
    reduce_scatter x1, waiting for transfers between devices, per_device(): lax.psum_scatter(grads_chan, owners, scatter_dimension=0, tiled=True)  108 us
    all_gather x1, waiting for transfers between devices, per_device(): lax.all_gather(jnp.concatenate([acceptor_matrix, lookup_matrix, payload_m...  103 us
    all_gather x1, waiting for transfers between devices, per_device(): lax.all_gather(jnp.concatenate([ffn_lookup_matrix, ffn_payload_matrix.T,...  78 us
    dot_general x8, matrix products, matmul(): return jnp.dot(left, right, preferred_element_type=jnp.float32)  64.8 us
    pallas_call x4, Pallas kernels, pair_call(): pl.pallas_call(kernel, grid=(pairs, seqs), in_specs=[specs[kind] for kind...  49.5 us
    pallas_call x2, Pallas kernels, blend(): pl.pallas_call(partial(blend_kernel, len(xs), mixes, per_seq), grid=(toke...  44.1 us
  transfers between devices with their start and end apart: 41, of which 25 were waited for; matrix products, arithmetic and copies ran while one was open for 19% of the time, Pallas kernels for 20%

profile of v2, /device:TPU:0, one launch (start us, length us, event | category | flops | bytes accessed | tf_op | source)
XLA Modules:
  0.0 1071.5 jit_solution(6563585901603208670)
XLA Ops:
  14.2 2.9 pad_maximum_fusion.2
  19.7 7.0 collective-permute-start.3
  28.0 2.5 collective-permute-start.1
  41.4 22.9 %blend_one.1 = (bf16[1024,2048]{1,0:T(8,128)(2,1)}, bf16[1024,2048]{1,0:T(8,128)(2,1)}, bf16[1024,2048]{1,0:T(8,128)(2,1)}, bf16[1024,2048]{1,0:T(8,128)(2,1)}) custom-call(bf16[1024,2048]{1,0:T(8,128)(2,1)} %bitcast.159, f32[1024,1]{1,0:T(8,128)} %bitcast.169, f32[2,1,2048]{2,1,0:T(1,128)} %broadcast_in_dim.20.refs_2_.refs_11_, ...), custom_call_target="tpu_custom_call" | custom-call | flops 41943040 | bytes 20971520 | tf_op jit(solution)/shard_map/blend_one/pallas_call | solution.py:423
  64.3 103.0 %all-gather.3.cloned.1.call-done.refs_6_.refs_7_.refs_8_.refs_9_ = bf16[2048,2560]{1,0:T(8,128)(2,1)} async-done(((bf16[256,2560]{1,0:T(8,128)(2,1)}), bf16[2048,2560]{1,0:T(8,128)(2,1)}) %all-gather.3.cloned.1.call-update) | async-done | bytes 10485776 | tf_op jit(solution)/shard_map/all_gather | solution.py:650
  167.3 6.3 fusion.49.k_ref
  173.6 5.3 fusion.52.v_ref
  178.9 7.0 carry.1
  188.2 4.2 collective-permute-start.5
  194.3 6.3 fusion.46.r_ref
  200.6 5.3 fusion.35.gate_ref
  206.7 11.4 %mix.1 = (bf16[1024,512]{1,0:T(8,128)(2,1)}, f32[1024,512]{1,0:T(8,128)}) custom-call(bf16[1024,512]{1,0:T(8,128)(2,1)} %fusion.46.r_ref, bf16[1024,512]{1,0:T(8,128)(2,1)} %fusion.49.k_ref, bf16[1024,512]{1,0:T(8,128)(2,1)} %fusion.52.v_ref, f32[1024,512]{1,0:T(8,128)} %fusion.35.gate_ref, f32[1,512]{1,0:T(1,128)} %bitcast.192, ...), custom_call_target="tpu_custom_call" | custom-call | flops 1073741824 | bytes 11087872 | tf_op jit(solution)/shard_map/mix/pallas_call | solution.py:368
  218.0 4.3 convolution_convert_fusion.2
  225.9 4.4 collective-permute-done.7
  230.2 2.4 add_convert_fusion.5
  234.2 46.2 %collective-permute-done.8 = bf16[512,2048]{1,0:T(8,128)(2,1)S(1)} collective-permute-done((bf16[512,2048]{1,0:T(8,128)(2,1)S(1)}, bf16[512,2048]{1,0:T(8,128)(2,1)S(1)}, u32[]{:S(2)}, u32[]{:S(2)}) %collective-permute-start.8) | collective-permute-done | bytes 2097184 | tf_op jit(solution)/shard_map/ppermute | solution.py:46
  281.4 4.2 collective-permute-done.9
  285.6 3.7 maximum_select_fusion.refs_1_.refs_3_
  291.9 12.6 %collective-permute-start.10 = (f32[2,2048]{1,0:T(2,128)S(1)}, f32[2,2048]{1,0:T(2,128)S(1)}, u32[]{:S(2)}, u32[]{:S(2)}) collective-permute-start(f32[2,2048]{1,0:T(2,128)S(1)} %multiply_add_fusion), channel_id=1, source_target_pairs={{0,4},{4,8},{8,12},{1,5},{5,9},{9,13},{2,6},{6,10},{10,14},{3,7},{... | collective-permute-start | bytes 49160 | tf_op jit(solution)/shard_map/ppermute | solution.py:23
  306.7 21.2 %blend_two.1 = (bf16[1024,2048]{1,0:T(8,128)(2,1)}, bf16[1024,2048]{1,0:T(8,128)(2,1)}) custom-call(bf16[1024,2048]{1,0:T(8,128)(2,1)} %bitcast.160, bf16[1024,2048]{1,0:T(8,128)(2,1)} %copy-done, f32[1024,1]{1,0:T(8,128)} %bitcast.170, f32[2,1,2048]{2,1,0:T(1,128)} %copy.97.refs_3_.refs_9_, f32[2,2048]{1,0:T(2,128)} %get-tuple-element.202.refs_4_.refs_11_, ...), custom_call_target="tpu_custom_call" | custom-call | flops 41943040 | bytes 16777216 | tf_op jit(solution)/shard_map/blend_two/pallas_call | solution.py:423
  327.9 78.0 %all-gather.5.cloned.1.call-done.refs_6_.refs_7_ = bf16[2048,4096]{1,0:T(8,128)(2,1)} async-done(((bf16[256,4096]{1,0:T(8,128)(2,1)}), bf16[2048,4096]{1,0:T(8,128)(2,1)}) %all-gather.5.cloned.1.call-update) | async-done | bytes 16777232 | tf_op jit(solution)/shard_map/all_gather | solution.py:658
  405.9 2.6 broadcast_in_dim.49
  408.5 7.2 constant_dynamic-update-slice_fusion.7
  417.2 22.6 %collective-permute-done.11 = bf16[1024,512]{1,0:T(8,128)(2,1)S(1)} collective-permute-done((bf16[1024,512]{1,0:T(8,128)(2,1)S(1)}, bf16[1024,512]{1,0:T(8,128)(2,1)S(1)}, u32[]{:S(2)}, u32[]{:S(2)}) %collective-permute-start.11) | collective-permute-done | bytes 1048608 | tf_op jit(solution)/shard_map/ppermute | solution.py:46
  439.8 13.5 %multiply_convert_fusion.1 = (bf16[1024,1792]{1,0:T(8,128)(2,1)S(1)}, f32[1024,1792]{1,0:T(8,128)}) fusion(bf16[1024,2048]{1,0:T(8,128)(2,1)} %get-tuple-element.60, bf16[2048,4096]{1,0:T(8,128)(2,1)} %all-gather.5.cloned.1.call-done.refs_6_.refs_7_), kind=kOutput, calls=%fused_computation.6 | convolution fusion | flops 7521697792 | bytes 22544384 | tf_op jit(solution)/shard_map/dot_general | solution.py:127
  456.8 12.0 %convolution_convert_fusion.1 = bf16[1792,2048]{1,0:T(8,128)(2,1)} fusion(bf16[1024,1792]{1,0:T(8,128)(2,1)S(1)} %get-tuple-element.61, bf16[1024,2048]{1,0:T(8,128)(2,1)} %constant_dynamic-update-slice_fusion.4), kind=kOutput, calls=%fused_computation.4 | convolution fusion | flops 7519862784 | bytes 15204352 | tf_op jit(solution)/shard_map/dot_general | solution.py:131
  468.9 11.4 %fusion.10 = bf16[1024,2048]{1,0:T(8,128)(2,1)S(1)} fusion(bf16[1024,1792]{1,0:T(8,128)(2,1)} %copy-done.43, bf16[2048,4096]{1,0:T(8,128)(2,1)} %all-gather.5.cloned.1.call-done.refs_6_.refs_7_), kind=kOutput, calls=%fused_computation.24 | convolution fusion | flops 7518289920 | bytes 15204352 | tf_op jit(solution)/shard_map/dot_general | solution.py:137
  489.0 14.4 %multiply_convert_fusion.refs_4_ = bf16[1024,1792]{1,0:T(8,128)(2,1)} fusion(f32[1024,1792]{1,0:T(8,128)} %get-tuple-element.196, bf16[1024,2048]{1,0:T(8,128)(2,1)} %constant_dynamic-update-slice_fusion.4, bf16[2048,4096]{1,0:T(8,128)(2,1)} %all-gather.5.cloned.1.call-done.refs_6_.refs_7_), kind=kOutput, calls=%fused_computation.5 | convolution fusion | flops 7523532800 | bytes 22544384 | tf_op jit(solution)/shard_map/dot_general | solution.py:127
  506.4 6.8 collective-permute-done.16
  513.1 4.7 fusion.27
  520.4 5.3 collective-permute-done.17
  526.4 62.4 %blend_two_back.1 = (bf16[1024,2048]{1,0:T(8,128)(2,1)}, f32[8,2048]{1,0:T(8,128)}) custom-call(bf16[1024,2048]{1,0:T(8,128)(2,1)} %bitcast.162, bf16[1024,2048]{1,0:T(8,128)(2,1)} %copy-done, bf16[1024,2048]{1,0:T(8,128)(2,1)} %bitcast.163, bf16[1024,2048]{1,0:T(8,128)(2,1)} %copy-done, bf16[1024,1792]{1,0:T(8,128)(2,1)} %multiply_convert_fusion.refs_4_, ...), custom_call_target="tpu_custom_call" | custom-call | flops 9663676416 | bytes 16777216 | tf_op jit(solution)/shard_map/blend_two_back/pallas_call | solution.py:558
  590.8 4.1 collective-permute-done.18
  597.3 46.3 %collective-permute-done.19 = bf16[512,2048]{1,0:T(8,128)(2,1)S(1)} collective-permute-done((bf16[512,2048]{1,0:T(8,128)(2,1)S(1)}, bf16[512,2048]{1,0:T(8,128)(2,1)S(1)}, u32[]{:S(2)}, u32[]{:S(2)}) %collective-permute-start.19) | collective-permute-done | bytes 2097184 | tf_op jit(solution)/shard_map/ppermute | solution.py:46
  644.5 8.4 convolution_convert_fusion
  652.9 2.5 convolution_convert_fusion.7
  655.4 2.5 maximum_select_fusion.1
  657.9 2.5 convolution_convert_fusion.8
  660.4 21.0 %pad_maximum_fusion = bf16[2048,2816]{0,1:T(8,128)(2,1)} fusion(bf16[2048,1792]{0,1:T(8,128)(2,1)S(1)} %convolution_convert_fusion, bf16[2048,512]{0,1:T(8,128)(2,1)S(1)} %convolution_convert_fusion.7, bf16[2048,512]{0,1:T(8,128)(2,1)S(1)} %convolution_convert_fusion.8), kind=kLoop, calls=%fused_computation | loop fusion | flops 34603008 | bytes 23068672 | tf_op jit(solution)/shard_map/concatenate | solution.py:785
  686.0 2.6 collective-permute-done.22
  688.9 4.5 collective-permute-done.23
  693.4 6.6 fusion.31.dj_ref
  700.0 11.3 %gate_back.1 = (bf16[1024,512]{1,0:T(8,128)(2,1)}, bf16[1024,512]{1,0:T(8,128)(2,1)}, f32[2,4,64,128]{3,2,1,0:T(8,128)}, f32[8,512]{1,0:T(8,128)}) custom-call(f32[1024,512]{1,0:T(8,128)} %fusion.31.dj_ref, f32[1024,512]{1,0:T(8,128)} %get-tuple-element.64.attend_ref, f32[1024,512]{1,0:T(8,128)} %fusion.35.gate_ref, bf16[1024,512]{1,0:T(8,128)(2,1)} %fusion.46.r_ref, ...), custom_call_target="tpu_custom_call" | custom-call | flops 67108864 | bytes 14749696 | tf_op jit(solution)/shard_map/gate_back/pallas_call | solution.py:368
  716.2 4.9 convolution_convert_fusion.3
  721.0 3.6 collective-permute-done.26
  724.6 16.0 %collective-permute-done.25 = bf16[2,4,64,128]{3,2,1,0:T(8,128)(2,1)S(1)} collective-permute-done((bf16[2,4,64,128]{3,2,1,0:T(8,128)(2,1)S(1)}, bf16[2,4,64,128]{3,2,1,0:T(8,128)(2,1)S(1)}, u32[]{:S(2)}, u32[]{:S(2)}) %collective-permute-start.25) | collective-permute-done | bytes 131104 | tf_op jit(solution)/shard_map/ppermute | solution.py:28
  741.4 19.8 %mix_back.1 = (bf16[1024,512]{1,0:T(8,128)(2,1)}, bf16[1024,512]{1,0:T(8,128)(2,1)}, bf16[1024,512]{1,0:T(8,128)(2,1)}, f32[8,512]{1,0:T(8,128)}) custom-call(bf16[1024,512]{1,0:T(8,128)(2,1)} %fusion.46.r_ref, bf16[1024,512]{1,0:T(8,128)(2,1)} %fusion.49.k_ref, bf16[1024,512]{1,0:T(8,128)(2,1)} %fusion.52.v_ref, ...), custom_call_target="tpu_custom_call" | custom-call | flops 3221225472 | bytes 9523200 | tf_op jit(solution)/shard_map/mix_back/pallas_call | solution.py:368
  761.3 5.0 convolution_convert_fusion.4
  766.3 2.4 convolution_convert_fusion.5
  768.8 2.4 convolution_convert_fusion.6
  771.2 4.3 pad_maximum_fusion.1
  775.5 108.4 %reduce-scatter.6.cloned.1.call-done = bf16[256,2816]{0,1:T(8,128)(2,1)} async-done(((bf16[2048,2816]{0,1:T(8,128)(2,1)}), bf16[256,2816]{0,1:T(8,128)(2,1)}) %reduce-scatter.6.cloned.1.call-update) | async-done | bytes 1441808 | tf_op jit(solution)/shard_map/reduce_scatter | solution.py:790
  888.4 2.2 fusion.16
  892.9 2.9 fusion.14
  897.1 5.1 collective-permute-done.27
  902.8 61.0 %blend_one_back.1 = (bf16[1024,2048]{1,0:T(8,128)(2,1)}, f32[8,2048]{1,0:T(8,128)}) custom-call(bf16[1024,2048]{1,0:T(8,128)(2,1)} %bitcast.164, bf16[1024,2048]{1,0:T(8,128)(2,1)} %bitcast.165, bf16[1024,512]{1,0:T(8,128)(2,1)} %get-tuple-element.72.refs_2_, bf16[1024,512]{1,0:T(8,128)(2,1)} %get-tuple-element.73.refs_3_, ...), custom_call_target="tpu_custom_call" | custom-call | flops 8589934592 | bytes 16777216 | tf_op jit(solution)/shard_map/blend_one_back/pallas_call | solution.py:558
  965.7 4.1 collective-permute-done.28
  972.0 46.6 %collective-permute-done.29 = bf16[512,2048]{1,0:T(8,128)(2,1)S(1)} collective-permute-done((bf16[512,2048]{1,0:T(8,128)(2,1)S(1)}, bf16[512,2048]{1,0:T(8,128)(2,1)S(1)}, u32[]{:S(2)}, u32[]{:S(2)}) %collective-permute-start.29) | collective-permute-done | bytes 2097184 | tf_op jit(solution)/shard_map/ppermute | solution.py:46
  1021.6 2.3 collective-permute-done.31
  1025.1 4.4 collective-permute-done.32
  1030.7 3.9 collective-permute-done.33
  1035.6 2.5 convert_element_type.326
  1047.9 2.7 copy.113
  1052.0 7.3 convert_add_fusion
  (269 shorter events, 108.4 us)
Async XLA Ops:
  7.2 160.1 %all-gather.3.cloned.1.call-start = ((), (), s32[]{:S(2)}) async-start(), calls=%async_computation.3 | async-start | bytes 11796480 | tf_op jit(solution)/shard_map/all_gather | solution.py:650
  13.5 18.2 %copy-start.19 = (f32[2048]{0:T(1024)S(1)}, f32[2048]{0:T(1024)}, u32[]{:S(2)}) copy-start(f32[2048]{0:T(1024)} %param.36) | copy-start | bytes 24580
  13.5 18.2 %copy-start.20 = (f32[2048]{0:T(1024)S(1)}, f32[2048]{0:T(1024)}, u32[]{:S(2)}) copy-start(f32[2048]{0:T(1024)} %param.35) | copy-start | bytes 24580
  13.5 20.9 %copy-start.25 = (f32[2048]{0:T(1024)S(1)}, f32[2048]{0:T(1024)}, u32[]{:S(2)}) copy-start(f32[2048]{0:T(1024)} %param.37) | copy-start | bytes 24580
  13.5 20.9 %copy-start.27 = (f32[2048]{0:T(1024)S(1)}, f32[2048]{0:T(1024)}, u32[]{:S(2)}) copy-start(f32[2048]{0:T(1024)} %param.38) | copy-start | bytes 24580
  13.5 20.9 %copy-start.29 = (f32[2048]{0:T(1024)S(1)}, f32[2048]{0:T(1024)}, u32[]{:S(2)}) copy-start(f32[2048]{0:T(1024)} %param.39) | copy-start | bytes 24580
  13.5 20.9 %copy-start.31 = (f32[2048]{0:T(1024)S(1)}, f32[2048]{0:T(1024)}, u32[]{:S(2)}) copy-start(f32[2048]{0:T(1024)} %param.40) | copy-start | bytes 24580
  13.5 392.4 %all-gather.5.cloned.1.call-start = ((), (), s32[]{:S(2)}) async-start(), calls=%async_computation.4 | async-start | bytes 18874368 | tf_op jit(solution)/shard_map/all_gather | solution.py:658
  17.1 664.3 %reduce-scatter.4.cloned.1.call-start = ((), (), s32[]{:S(2)}) async-start(), calls=%async_computation.5 | async-start | bytes 8257536 | tf_op jit(solution)/shard_map/reduce_scatter | solution.py:750
  19.7 153.9 %copy-start.34 = (bf16[2,4,1,128]{3,2,1,0:T(2,128)(2,1)}, bf16[2,4,1,128]{3,2,1,0:T(2,128)(2,1)S(1)}, u32[]{:S(2)}) copy-start(bf16[2,4,1,128]{3,2,1,0:T(2,128)(2,1)S(1)} %get-tuple-element.158) | copy-start | bytes 6148
  19.7 21.0 %collective-permute-start.3 = (bf16[2,4,1,128]{3,2,1,0:T(2,128)(2,1)S(1)}, bf16[2,4,1,128]{3,2,1,0:T(2,128)(2,1)S(1)}, u32[]{:S(2)}, u32[]{:S(2)}) collective-permute-start(bf16[2,4,1,128]{3,2,1,0:T(2,128)(2,1)S(1)} %get-tuple-element.158), channel_id=1, source_target_pairs={{0,12},{1,13},{2,14},{3,15},{16,28},{17,29},{18,30},{19,31}} | collective-permute-start | bytes 6152 | tf_op jit(solution)/shard_map/ppermute | solution.py:28
  26.7 14.1 %collective-permute-start.2 = (bf16[2,4,1,128]{3,2,1,0:T(2,128)(2,1)S(1)}, bf16[2,4,1,128]{3,2,1,0:T(2,128)(2,1)S(1)}, u32[]{:S(2)}, u32[]{:S(2)}) collective-permute-start(bf16[2,4,1,128]{3,2,1,0:T(2,128)(2,1)S(1)} %get-tuple-element.158), channel_id=1, source_target_pairs={{0,8},{4,12},{1,9},{5,13},{2,10},{6,14},{3,11},{7,15},{16,24},{20,... | collective-permute-start | bytes 6152 | tf_op jit(solution)/shard_map/ppermute | solution.py:28
  28.0 12.8 %collective-permute-start.1 = (bf16[2,4,1,128]{3,2,1,0:T(2,128)(2,1)S(1)}, bf16[2,4,1,128]{3,2,1,0:T(2,128)(2,1)S(1)}, u32[]{:S(2)}, u32[]{:S(2)}) collective-permute-start(bf16[2,4,1,128]{3,2,1,0:T(2,128)(2,1)S(1)} %get-tuple-element.158), channel_id=1, source_target_pairs={{0,4},{4,8},{8,12},{1,5},{5,9},{9,13},{2,6},{6,10},{10,14},{3,7},{... | collective-permute-start | bytes 6152 | tf_op jit(solution)/shard_map/ppermute | solution.py:28
  31.8 9.0 collective-permute-start
  186.9 19.0 %collective-permute-start.6 = (bf16[2,4,64,128]{3,2,1,0:T(8,128)(2,1)S(1)}, bf16[2,4,64,128]{3,2,1,0:T(8,128)(2,1)S(1)}, u32[]{:S(2)}, u32[]{:S(2)}) collective-permute-start(bf16[2,4,64,128]{3,2,1,0:T(8,128)(2,1)S(1)} %convert_element_type.265), channel_id=1, source_target_pairs={{0,4},{4,8},{8,12},{1,5},{5,9},{9,13},{2,6},{6,10},{10,14},{3,7},{... | collective-permute-start | bytes 393224 | tf_op jit(solution)/shard_map/ppermute | solution.py:28
  188.2 17.7 %collective-permute-start.5 = (bf16[2,4,64,128]{3,2,1,0:T(8,128)(2,1)S(1)}, bf16[2,4,64,128]{3,2,1,0:T(8,128)(2,1)S(1)}, u32[]{:S(2)}, u32[]{:S(2)}) collective-permute-start(bf16[2,4,64,128]{3,2,1,0:T(8,128)(2,1)S(1)} %convert_element_type.265), channel_id=1, source_target_pairs={{0,8},{4,12},{1,9},{5,13},{2,10},{6,14},{3,11},{7,15},{16,24},{20,... | collective-permute-start | bytes 393224 | tf_op jit(solution)/shard_map/ppermute | solution.py:28
  192.4 13.5 %collective-permute-start.4 = (bf16[2,4,64,128]{3,2,1,0:T(8,128)(2,1)S(1)}, bf16[2,4,64,128]{3,2,1,0:T(8,128)(2,1)S(1)}, u32[]{:S(2)}, u32[]{:S(2)}) collective-permute-start(bf16[2,4,64,128]{3,2,1,0:T(8,128)(2,1)S(1)} %convert_element_type.265), channel_id=1, source_target_pairs={{0,12},{1,13},{2,14},{3,15},{16,28},{17,29},{18,30},{19,31}} | collective-permute-start | bytes 393224 | tf_op jit(solution)/shard_map/ppermute | solution.py:28
  225.9 4.4 collective-permute-start.7
  232.6 47.7 %collective-permute-start.8 = (bf16[512,2048]{1,0:T(8,128)(2,1)S(1)}, bf16[512,2048]{1,0:T(8,128)(2,1)S(1)}, u32[]{:S(2)}, u32[]{:S(2)}) collective-permute-start(bf16[512,2048]{1,0:T(8,128)(2,1)S(1)} %add_convert_fusion.5), channel_id=1, source_target_pairs={{0,2},{1,3},{2,0},{3,1},{4,6},{5,7},{6,4},{7,5},{8,10},{9,11},{10,... | collective-permute-start | bytes 6291464 | tf_op jit(solution)/shard_map/ppermute | solution.py:46
  281.2 4.4 collective-permute-start.9
  281.4 23.2 %copy-start.23 = (f32[2048]{0:T(1024)S(1)}, f32[2048]{0:T(1024)}, u32[]{:S(2)}) copy-start(f32[2048]{0:T(1024)} %param.47) | copy-start | bytes 24580
  281.4 23.2 %copy-start.24 = (f32[2048]{0:T(1024)S(1)}, f32[2048]{0:T(1024)}, u32[]{:S(2)}) copy-start(f32[2048]{0:T(1024)} %param.48) | copy-start | bytes 24580
  291.9 14.1 %collective-permute-start.10 = (f32[2,2048]{1,0:T(2,128)S(1)}, f32[2,2048]{1,0:T(2,128)S(1)}, u32[]{:S(2)}, u32[]{:S(2)}) collective-permute-start(f32[2,2048]{1,0:T(2,128)S(1)} %multiply_add_fusion), channel_id=1, source_target_pairs={{0,4},{4,8},{8,12},{1,5},{5,9},{9,13},{2,6},{6,10},{10,14},{3,7},{... | collective-permute-start | bytes 49160 | tf_op jit(solution)/shard_map/ppermute | solution.py:23
  327.9 80.6 %copy-start.9 = (bf16[2,512,512]{2,1,0:T(8,128)(2,1)S(1)}, bf16[2,512,512]{2,1,0:T(8,128)(2,1)}, u32[]{:S(2)}) copy-start(bf16[2,512,512]{2,1,0:T(8,128)(2,1)} %param.49) | copy-start | bytes 3145732
  415.6 24.2 %collective-permute-start.11 = (bf16[1024,512]{1,0:T(8,128)(2,1)S(1)}, bf16[1024,512]{1,0:T(8,128)(2,1)S(1)}, u32[]{:S(2)}, u32[]{:S(2)}) collective-permute-start(bf16[1024,512]{1,0:T(8,128)(2,1)S(1)} %get-tuple-element.200), channel_id=1, source_target_pairs={{0,2},{1,3},{2,0},{3,1},{4,6},{5,7},{6,4},{7,5},{8,10},{9,11},{10,... | collective-permute-start | bytes 3145736 | tf_op jit(solution)/shard_map/ppermute | solution.py:46
  417.2 37.3 %collective-permute-start.12 = (bf16[1024,512]{1,0:T(8,128)(2,1)S(1)}, bf16[1024,512]{1,0:T(8,128)(2,1)S(1)}, u32[]{:S(2)}, u32[]{:S(2)}) collective-permute-start(bf16[1024,512]{1,0:T(8,128)(2,1)S(1)} %get-tuple-element.200), channel_id=1, source_target_pairs={{0,1},{1,0},{2,3},{3,2},{4,5},{5,4},{6,7},{7,6},{8,9},{9,8},{10,11... | collective-permute-start | bytes 3145736 | tf_op jit(solution)/shard_map/ppermute | solution.py:46
  439.8 15.9 %collective-permute-start.13 = (bf16[1024,512]{1,0:T(8,128)(2,1)S(1)}, bf16[1024,512]{1,0:T(8,128)(2,1)S(1)}, u32[]{:S(2)}, u32[]{:S(2)}) collective-permute-start(bf16[1024,512]{1,0:T(8,128)(2,1)S(1)} %collective-permute-done.11), channel_id=1, source_target_pairs={{0,1},{1,0},{2,3},{3,2},{4,5},{5,4},{6,7},{7,6},{8,9},{9,8},{10,11... | collective-permute-start | bytes 3145736 | tf_op jit(solution)/shard_map/ppermute | solution.py:46
  482.5 3.1 collective-permute-start.15
  483.3 400.7 %reduce-scatter.6.cloned.1.call-start = ((), (), s32[]{:S(2)}) async-start(), calls=%async_computation.6 | async-start | bytes 12976128 | tf_op jit(solution)/shard_map/reduce_scatter | solution.py:790
  483.3 23.1 %collective-permute-start.14 = (bf16[1024,512]{1,0:T(8,128)(2,1)S(1)}, bf16[1024,512]{1,0:T(8,128)(2,1)}, u32[]{:S(2)}, u32[]{:S(2)}) collective-permute-start(bf16[1024,512]{1,0:T(8,128)(2,1)S(1)} %get-tuple-element.170), channel_id=1, source_target_pairs={{0,1},{1,0},{2,3},{3,2},{4,5},{5,4},{6,7},{7,6},{8,9},{9,8},{10,11... | collective-permute-start | bytes 3145736 | tf_op jit(solution)/shard_map/ppermute | solution.py:46
  485.5 18.8 %slice-start = ((s8[16777216]{0:T(1024)(128)(4,1)}), s8[4194304]{0:T(1024)(128)(4,1)S(1)}, s32[]{:S(2)}) async-start(s8[16777216]{0:T(1024)(128)(4,1)} %bitcast.166), calls=%async_computation.8 | async-start | bytes 8388608
  487.5 25.6 %collective-permute-start.16 = (bf16[1024,512]{1,0:T(8,128)(2,1)S(1)}, bf16[1024,512]{1,0:T(8,128)(2,1)}, u32[]{:S(2)}, u32[]{:S(2)}) collective-permute-start(bf16[1024,512]{1,0:T(8,128)(2,1)S(1)} %add_convert_fusion.7), channel_id=1, source_target_pairs={{0,2},{1,3},{2,0},{3,1},{4,6},{5,7},{6,4},{7,5},{8,10},{9,11},{10,... | collective-permute-start | bytes 3145736 | tf_op jit(solution)/shard_map/ppermute | solution.py:46
  489.0 15.4 %slice-start.1 = ((s8[16777216]{0:T(1024)(128)(4,1)}), s8[4194304]{0:T(1024)(128)(4,1)S(1)}, s32[]{:S(2)}) async-start(s8[16777216]{0:T(1024)(128)(4,1)} %bitcast.166), calls=%async_computation.9 | async-start | bytes 8388608
  489.0 15.4 %slice-start.2 = ((s8[16777216]{0:T(1024)(128)(4,1)}), s8[4194304]{0:T(1024)(128)(4,1)S(1)}, s32[]{:S(2)}) async-start(s8[16777216]{0:T(1024)(128)(4,1)} %bitcast.166), calls=%async_computation.10 | async-start | bytes 8388608
  489.0 15.4 %slice-start.3 = ((s8[16777216]{0:T(1024)(128)(4,1)}), s8[4194304]{0:T(1024)(128)(4,1)S(1)}, s32[]{:S(2)}) async-start(s8[16777216]{0:T(1024)(128)(4,1)} %bitcast.166), calls=%async_computation.11 | async-start | bytes 8388608
  518.5 7.2 collective-permute-start.17
  590.7 4.2 collective-permute-start.18
  594.9 49.6 %copy-start.41 = (bf16[1024,2048]{1,0:T(8,128)(2,1)S(1)}, bf16[1024,2048]{1,0:T(8,128)(2,1)}, u32[]{:S(2)}) copy-start(bf16[1024,2048]{1,0:T(8,128)(2,1)} %get-tuple-element.60) | copy-start | bytes 12582916
  595.8 48.6 %copy-start.10 = (bf16[1024,1792]{1,0:T(8,128)(2,1)S(1)}, bf16[1024,1792]{1,0:T(8,128)(2,1)}, u32[]{:S(2)}) copy-start(bf16[1024,1792]{1,0:T(8,128)(2,1)} %multiply_convert_fusion.refs_4_) | copy-start | bytes 11010052
  595.9 47.7 %collective-permute-start.19 = (bf16[512,2048]{1,0:T(8,128)(2,1)S(1)}, bf16[512,2048]{1,0:T(8,128)(2,1)S(1)}, u32[]{:S(2)}, u32[]{:S(2)}) collective-permute-start(bf16[512,2048]{1,0:T(8,128)(2,1)S(1)} %add_convert_fusion.3), channel_id=1, source_target_pairs={{0,2},{1,3},{2,0},{3,1},{4,6},{5,7},{6,4},{7,5},{8,10},{9,11},{10,... | collective-permute-start | bytes 6291464 | tf_op jit(solution)/shard_map/ppermute | solution.py:46
  644.4 11.0 %collective-permute-start.20 = (bf16[512,2048]{1,0:T(8,128)(2,1)S(1)}, bf16[512,2048]{1,0:T(8,128)(2,1)S(1)}, u32[]{:S(2)}, u32[]{:S(2)}) collective-permute-start(bf16[512,2048]{1,0:T(8,128)(2,1)S(1)} %add_convert_fusion.2), channel_id=1, source_target_pairs={{0,1},{1,0},{2,3},{3,2},{4,5},{5,4},{6,7},{7,6},{8,9},{9,8},{10,11... | collective-permute-start | bytes 6291464 | tf_op jit(solution)/shard_map/ppermute | solution.py:46
  681.5 377.8 %reduce-scatter.8.cloned.1.call-start = ((), (), s32[]{:S(2)}) async-start(), calls=%async_computation.7 | async-start | bytes 9437184 | tf_op jit(solution)/shard_map/reduce_scatter | solution.py:842
  682.1 6.5 collective-permute-start.22
  683.4 5.5 collective-permute-start.21
  684.7 8.7 collective-permute-start.23
  712.3 12.4 %collective-permute-start.26 = (bf16[2,4,64,128]{3,2,1,0:T(8,128)(2,1)S(1)}, bf16[2,4,64,128]{3,2,1,0:T(8,128)(2,1)S(1)}, u32[]{:S(2)}, u32[]{:S(2)}) collective-permute-start(bf16[2,4,64,128]{3,2,1,0:T(8,128)(2,1)S(1)} %convert_element_type.309), channel_id=1, source_target_pairs={{4,0},{8,4},{12,8},{5,1},{9,5},{13,9},{6,2},{10,6},{14,10},{7,3},{... | collective-permute-start | bytes 393224 | tf_op jit(solution)/shard_map/ppermute | solution.py:28
  713.6 27.1 %collective-permute-start.25 = (bf16[2,4,64,128]{3,2,1,0:T(8,128)(2,1)S(1)}, bf16[2,4,64,128]{3,2,1,0:T(8,128)(2,1)S(1)}, u32[]{:S(2)}, u32[]{:S(2)}) collective-permute-start(bf16[2,4,64,128]{3,2,1,0:T(8,128)(2,1)S(1)} %convert_element_type.309), channel_id=1, source_target_pairs={{8,0},{12,4},{9,1},{13,5},{10,2},{14,6},{11,3},{15,7},{24,16},{28,... | collective-permute-start | bytes 393224 | tf_op jit(solution)/shard_map/ppermute | solution.py:28
  714.9 25.8 %collective-permute-start.24 = (bf16[2,4,64,128]{3,2,1,0:T(8,128)(2,1)S(1)}, bf16[2,4,64,128]{3,2,1,0:T(8,128)(2,1)S(1)}, u32[]{:S(2)}, u32[]{:S(2)}) collective-permute-start(bf16[2,4,64,128]{3,2,1,0:T(8,128)(2,1)S(1)} %convert_element_type.309), channel_id=1, source_target_pairs={{12,0},{13,1},{14,2},{15,3},{28,16},{29,17},{30,18},{31,19}} | collective-permute-start | bytes 393224 | tf_op jit(solution)/shard_map/ppermute | solution.py:28
  775.5 108.4 %copy-start.26 = (f32[2048]{0:T(1024)S(1)}, f32[2048]{0:T(1024)}, u32[]{:S(2)}) copy-start(f32[2048]{0:T(1024)} %param.37) | copy-start | bytes 24580
  775.5 108.5 %copy-start.28 = (f32[2048]{0:T(1024)S(1)}, f32[2048]{0:T(1024)}, u32[]{:S(2)}) copy-start(f32[2048]{0:T(1024)} %param.38) | copy-start | bytes 24580
  775.5 108.5 %copy-start.30 = (f32[2048]{0:T(1024)S(1)}, f32[2048]{0:T(1024)}, u32[]{:S(2)}) copy-start(f32[2048]{0:T(1024)} %param.39) | copy-start | bytes 24580
  775.5 108.5 %copy-start.32 = (f32[2048]{0:T(1024)S(1)}, f32[2048]{0:T(1024)}, u32[]{:S(2)}) copy-start(f32[2048]{0:T(1024)} %param.40) | copy-start | bytes 24580
  895.8 6.4 collective-permute-start.27
  965.7 4.2 collective-permute-start.28
  970.8 48.8 %copy-start.33 = (f32[8,2048]{1,0:T(8,128)S(1)}, f32[8,2048]{1,0:T(8,128)}, u32[]{:S(2)}) copy-start(f32[8,2048]{1,0:T(8,128)} %get-tuple-element.83) | copy-start | bytes 196612
  970.8 50.2 %copy-start.17 = (f32[8,2048]{1,0:T(8,128)S(1)}, f32[8,2048]{1,0:T(8,128)}, u32[]{:S(2)}) copy-start(f32[8,2048]{1,0:T(8,128)} %get-tuple-element.80) | copy-start | bytes 196612
  970.8 67.3 %copy-start.2 = (bf16[256,2816]{0,1:T(8,128)(2,1)S(1)}, bf16[256,2816]{0,1:T(8,128)(2,1)}, u32[]{:S(2)}) copy-start(bf16[256,2816]{0,1:T(8,128)(2,1)} %reduce-scatter.6.cloned.1.call-done) | copy-start | bytes 4325380
  970.8 47.7 %collective-permute-start.29 = (bf16[512,2048]{1,0:T(8,128)(2,1)S(1)}, bf16[512,2048]{1,0:T(8,128)(2,1)S(1)}, u32[]{:S(2)}, u32[]{:S(2)}) collective-permute-start(bf16[512,2048]{1,0:T(8,128)(2,1)S(1)} %add_convert_fusion.1), channel_id=1, source_target_pairs={{0,2},{1,3},{2,0},{3,1},{4,6},{5,7},{6,4},{7,5},{8,10},{9,11},{10,... | collective-permute-start | bytes 6291464 | tf_op jit(solution)/shard_map/ppermute | solution.py:46
  1019.5 32.5 %collective-permute-start.30 = (bf16[512,2048]{1,0:T(8,128)(2,1)S(1)}, bf16[512,2048]{1,0:T(8,128)(2,1)}, u32[]{:S(2)}, u32[]{:S(2)}) collective-permute-start(bf16[512,2048]{1,0:T(8,128)(2,1)S(1)} %add_convert_fusion), channel_id=1, source_target_pairs={{0,1},{1,0},{2,3},{3,2},{4,5},{5,4},{6,7},{7,6},{8,9},{9,8},{10,11... | collective-permute-start | bytes 6291464 | tf_op jit(solution)/shard_map/ppermute | solution.py:46
  1021.1 2.8 collective-permute-start.31
  1023.9 5.6 collective-permute-start.32
  1029.6 5.0 collective-permute-start.33
  1035.3 5.3 collective-permute-start.34
  1042.2 8.5 collective-permute-start.35
  (25 other events, 129.7 us)
Sparse Core Ops, SparseCore 0:
  13.6 153.6 all-gather.2
  169.4 236.4 all-gather.4
  483.4 132.1 reduce-scatter.3
  681.6 202.2 reduce-scatter.5
  887.4 147.0 reduce-scatter.7

commit v3 on v2

--- a/solution.py
+++ b/solution.py
@@ -10,6 +10,8 @@
 SUBSPACE_SIZE = 64
 PAIR = 128
 GROUP = 16
+HALO = 8
+SPAN = 64
 TILE = 256
 
 
@@ -68,14 +70,51 @@
     )
 
 
-def tp_sum(x):
+def after(value, *earlier):
+    return lax.optimization_barrier((value,) + earlier)
+
+
+def tp_sum(x, work=None):
     mine, other = halves(x, 0, 1)
     part = add_low(mine, partner(other, 1))
+    made = work(part) if work else None
     bit = 2
     while bit < lax.axis_size("tp"):
-        part = add_low(part, partner(part, bit))
+        arrived = partner(part, bit)
+        if work and bit == 2:
+            part = after(part, made)[0]
+        part = add_low(part, arrived)
         bit *= 2
-    return ordered(part, partner(part, 1), 0, 1)
+    whole = ordered(part, partner(part, 1), 0, 1)
+    return (whole, made) if work else whole
+
+
+def axis_bits(axis):
+    bits, bit = [], 1
+    while bit < lax.axis_size(axis):
+        bits.append((axis, bit))
+        bit *= 2
+    return bits
+
+
+def swap(x, axis, bit):
+    return lax.ppermute(x, axis, [(i, i ^ bit) for i in range(lax.axis_size(axis))])
+
+
+def owner_scatter_steps(x):
+    fsdp_bits, ctx_bits = axis_bits("fsdp"), axis_bits("ctx")
+    dims = list(reversed(fsdp_bits)) + list(reversed(ctx_bits))
+    rows = x.shape[0] // 2 ** len(dims)
+    part = x.reshape(*([2] * len(dims)), rows, x.shape[1])
+    for axis, bit in fsdp_bits + ctx_bits:
+        dim = dims.index((axis, bit))
+        dims.pop(dim)
+        mine = (lax.axis_index(axis) // bit) % 2
+        own = lax.dynamic_index_in_dim(part, mine, dim, False)
+        arrived = swap(lax.dynamic_index_in_dim(part, 1 - mine, dim, False), axis, bit)
+        part = add_low(own, arrived)
+        part = yield part
+    yield None
 
 
 def whole_sum(x, axes):
@@ -117,10 +156,6 @@
     for relative, part in parts.items():
         whole = lax.dynamic_update_slice_in_dim(whole, part, (place ^ relative) * width, 1)
     return whole
-
-
-def after(value, *earlier):
-    return lax.optimization_barrier((value,) + earlier)
 
 
 def matmul(left, right):
@@ -376,42 +411,88 @@
     )(*arrays)
 
 
-def norm_rows(x, gain, bias_term):
+def unit_rows(x):
     centered = x - jnp.mean(x, -1, keepdims=True)
-    inverse = lax.rsqrt(jnp.mean(centered * centered, -1, keepdims=True) + EPS)
-    unit = centered * inverse
-    return unit * gain + bias_term, unit, inverse
-
-
-def total_rows(refs, rows):
-    total = refs[0][rows, :].astype(jnp.float32)
+    return centered * lax.rsqrt(jnp.mean(centered * centered, -1, keepdims=True) + EPS)
+
+
+def total_at(refs, rows, lanes):
+    total = refs[0][rows, lanes].astype(jnp.float32)
     for ref in refs[1:]:
-        total = total + ref[rows, :].astype(jnp.float32)
+        total = total + ref[rows, lanes].astype(jnp.float32)
     return total
+
+
+def lane_loop(width, body):
+    def step(at, _):
+        body(pl.ds(pl.multiple_of(at * PAIR, PAIR), PAIR))
+        return 0
+
+    lax.fori_loop(0, width // PAIR, step, 0)
+
+
+def row_blocks(rows):
+    return [slice(top, min(top + SPAN, rows)) for top in range(0, rows, SPAN)]
+
+
+def unit_into(refs, unit_scr, rows, width):
+    inverses = []
+    for block in row_blocks(rows):
+        inside = slice(block.start + HALO, block.stop + HALO)
+        zero = jnp.zeros((block.stop - block.start, PAIR), jnp.float32)
+
+        def load(at, total):
+            lanes = pl.ds(pl.multiple_of(at * PAIR, PAIR), PAIR)
+            value = total_at(refs, block, lanes)
+            unit_scr[inside, lanes] = value
+            return total + value
+
+        total = lax.fori_loop(0, width // PAIR, load, zero, unroll=4)
+        mean = jnp.sum(total, -1, keepdims=True) * (1.0 / width)
+
+        def square(at, total):
+            lanes = pl.ds(pl.multiple_of(at * PAIR, PAIR), PAIR)
+            value = unit_scr[inside, lanes] - mean
+            return total + value * value
+
+        total = lax.fori_loop(0, width // PAIR, square, zero, unroll=4)
+        inverse = lax.rsqrt(jnp.sum(total, -1, keepdims=True) * (1.0 / width) + EPS)
+
+        def scale(at, _):
+            lanes = pl.ds(pl.multiple_of(at * PAIR, PAIR), PAIR)
+            unit_scr[inside, lanes] = (unit_scr[inside, lanes] - mean) * inverse
+            return 0
+
+        lax.fori_loop(0, width // PAIR, scale, 0, unroll=4)
+        inverses.append(inverse)
+    return inverses
 
 
 def blend_kernel(parts, mixes, per_seq, *refs):
     x_refs, refs = refs[:parts], refs[parts:]
     keep_ref, edge_ref, norm_ref, mix_ref = refs[:4]
-    outs, before = refs[4 : 4 + mixes], refs[4 + mixes]
-    rows = x_refs[0].shape[0]
+    outs, unit_scr = refs[4 : 4 + mixes], refs[4 + mixes]
+    rows, width = x_refs[0].shape
 
     @pl.when(pl.program_id(0) % per_seq == 0)
     def _():
-        before[...] = jnp.broadcast_to(edge_ref[0], before.shape)
-
-    def group(g, _):
-        place = pl.ds(pl.multiple_of(g * GROUP, GROUP), GROUP)
-        normed, _, _ = norm_rows(total_rows(x_refs, place), norm_ref[0:1, :], norm_ref[1:2, :])
-        top = lax.broadcasted_iota(jnp.int32, normed.shape, 0) == 0
-        previous = jnp.where(top, before[0:1, :], pltpu.roll(normed, 1, 0)) * keep_ref[place, 0:1]
-        before[0:1, :] = normed[GROUP - 1 :, :]
-        delta = normed - previous
-        for at, out in enumerate(outs):
-            out[place, :] = (previous + mix_ref[at : at + 1, :] * delta).astype(jnp.bfloat16)
-        return 0
-
-    lax.fori_loop(0, rows // GROUP, group, 0)
+        unit_scr[HALO - 1 : HALO, :] = edge_ref[0]
+
+    unit_into(x_refs, unit_scr, rows, width)
+
+    def lane_block(lanes):
+        gain, bias_term = norm_ref[0:1, lanes], norm_ref[1:2, lanes]
+        mixers = [mix_ref[at : at + 1, lanes] for at in range(mixes)]
+        for block in row_blocks(rows):
+            normed = unit_scr[block.start + HALO : block.stop + HALO, lanes] * gain + bias_term
+            before = pltpu.roll(unit_scr[block.start : block.stop + HALO, lanes], 1, 0)[HALO:]
+            previous = (before * gain + bias_term) * keep_ref[block, 0:1]
+            delta = normed - previous
+            for mixer, out in zip(mixers, outs):
+                out[block, lanes] = (previous + mixer * delta).astype(jnp.bfloat16)
+
+    lane_loop(width, lane_block)
+    unit_scr[HALO - 1 : HALO, :] = unit_scr[rows + HALO - 1 : rows + HALO, :]
 
 
 def blend(xs, keep, edge, norm, mixers, piece, name):
@@ -432,7 +513,7 @@
         ],
         out_specs=[wide] * mixes,
         out_shape=[jax.ShapeDtypeStruct((tokens, width), jnp.bfloat16)] * mixes,
-        scratch_shapes=[pltpu.VMEM((8, width), jnp.float32)],
+        scratch_shapes=[pltpu.VMEM((rows + HALO, width), jnp.float32)],
         cost_estimate=pl.CostEstimate(
             flops=20 * tokens * width,
             bytes_accessed=2 * tokens * width * (len(xs) + mixes),
@@ -450,11 +531,10 @@
     keep_ref, edge_ref, back_ref, norm_ref, mix_ref = refs[:5]
     refs = refs[5:]
     own_refs, refs = refs[: 2 * own], refs[2 * own :]
-    out_ref, small_ref, d_scr, unit_scr, inv_scr, sums, after_row = refs
+    out_ref, small_ref, d_scr, unit_scr, prev_scr, row_scr, sums = refs
     rows, width = x_refs[0].shape
     tiles = pl.num_programs(0)
     tile = tiles - 1 - pl.program_id(0)
-    gain, bias_term = norm_ref[0:1, :], norm_ref[1:2, :]
 
     @pl.when(pl.program_id(0) == 0)
     def _():
@@ -462,68 +542,94 @@
 
     @pl.when(tile % per_seq == per_seq - 1)
     def _():
-        after_row[...] = jnp.broadcast_to(back_ref[0], after_row.shape)
+        prev_scr[rows : rows + 1, :] = back_ref[0]
+
+    @pl.when(tile % per_seq < per_seq - 1)
+    def _():
+        prev_scr[rows : rows + 1, :] = prev_scr[0:1, :]
 
     for at in range(mixes):
         d_scr[at] = matmul_nt(grad_refs[at][...], weight_refs[at][...])
 
-    halo, _, _ = norm_rows(total_rows(halo_refs, slice(None)), gain, bias_term)
-    first = jnp.where(tile % per_seq == 0, edge_ref[0], halo[GROUP - 1 :, :])
-
-    def unit_group(g, _):
-        place = pl.ds(pl.multiple_of(g * GROUP, GROUP), GROUP)
-        _, unit, inverse = norm_rows(total_rows(x_refs, place), gain, bias_term)
-        unit_scr[place, :] = unit
-        inv_scr[place, :] = jnp.broadcast_to(inverse, (GROUP, inv_scr.shape[1]))
+    halo = unit_rows(total_at(halo_refs, slice(None), slice(None)))[GROUP - 1 :, :]
+    unit_scr[HALO - 1 : HALO, :] = jnp.where(tile % per_seq == 0, edge_ref[0], halo)
+    inverses = unit_into(x_refs, unit_scr, rows, width)
+    row_scr[...] = jnp.zeros_like(row_scr)
+
+    def gather(at, value):
+        total = value[0:8]
+        for top in range(8, value.shape[0], 8):
+            total = total + value[top : top + 8]
+        return total
+
+    def first_pass(lanes):
+        gain, bias_term = norm_ref[0:1, lanes], norm_ref[1:2, lanes]
+        mixers = [mix_ref[at : at + 1, lanes] for at in range(mixes)]
+        totals = [jnp.zeros((8, PAIR), jnp.float32)] * mixes
+        for block in row_blocks(rows):
+            keep = keep_ref[block, 0:1]
+            normed = unit_scr[block.start + HALO : block.stop + HALO, lanes] * gain + bias_term
+            before = pltpu.roll(unit_scr[block.start : block.stop + HALO, lanes], 1, 0)[HALO:]
+            delta = normed - (before * gain + bias_term) * keep
+            d_norm, d_all = None, None
+            for at in range(mixes):
+                d_in = d_scr[at, block, lanes]
+                totals[at] = totals[at] + gather(at, d_in * delta)
+                share = d_in * mixers[at]
+                d_norm = share if d_norm is None else d_norm + share
+                d_all = d_in if d_all is None else d_all + d_in
+            prev_scr[block, lanes] = (d_all - d_norm) * keep
+            d_scr[0, block, lanes] = d_norm
+        for at in range(mixes):
+            sums[2 + at, :, lanes] += totals[at]
+
+    lane_loop(width, first_pass)
+
+    def second_pass(lanes):
+        gain = norm_ref[0:1, lanes]
+        totals = [jnp.zeros((8, PAIR), jnp.float32)] * 2
+        for block in row_blocks(rows):
+            size = block.stop - block.start
+            later = pltpu.roll(
+                prev_scr[block.start : block.stop + HALO, lanes], size + HALO - 1, 0
+            )[:size]
+            d_norm = d_scr[0, block, lanes] + later
+            unit = unit_scr[block.start + HALO : block.stop + HALO, lanes]
+            product = d_norm * unit
+            totals[0] = totals[0] + gather(0, product)
+            totals[1] = totals[1] + gather(1, d_norm)
+            d_scr[0, block, lanes] = d_norm * gain
+            row_scr[0, block, :] += d_norm * gain
+            row_scr[1, block, :] += product * gain
+        for at in range(2):
+            sums[at, :, lanes] += totals[at]
+
+    lane_loop(width, second_pass)
+    means, tilts = [], []
+    for block in row_blocks(rows):
+        means.append(jnp.sum(row_scr[0, block, :], -1, keepdims=True) * (1.0 / width))
+        tilts.append(jnp.sum(row_scr[1, block, :], -1, keepdims=True) * (1.0 / width))
+    blocks = list(zip(row_blocks(rows), inverses, means, tilts))
+
+    def last_pass(start, lanes):
+        for block, inverse, mean, tilt in blocks:
+            unit = unit_scr[block.start + HALO : block.stop + HALO, lanes]
+            value = inverse * (d_scr[0, block, lanes] - mean - unit * tilt)
+            if own:
+                extra = own_refs[0][block, start].astype(jnp.float32)
+                value = value + extra * own_refs[1][0:1, lanes]
+            out_ref[block, lanes] = value.astype(jnp.bfloat16)
+
+    def last_step(at, _):
+        lanes = pl.ds(pl.multiple_of(at * PAIR, PAIR), PAIR)
+        inner = None
+        if own:
+            count = own_refs[0].shape[1] // PAIR
+            inner = pl.ds(pl.multiple_of((at % count) * PAIR, PAIR), PAIR)
+        last_pass(inner, lanes)
         return 0
 
-    groups = rows // GROUP
-    lax.fori_loop(0, groups, unit_group, 0)
-
-    def group(step, _):
-        g = groups - 1 - step
-        start = pl.multiple_of(g * GROUP, GROUP)
-        place = pl.ds(start, GROUP)
-        unit = unit_scr[place, :]
-        inverse = inv_scr[place, 0:1]
-        keep = keep_ref[place, 0:1]
-        normed = unit * gain + bias_term
-        before_at = pl.multiple_of(jnp.maximum(start - 8, 0), 8)
-        inside = unit_scr[pl.ds(before_at, 8), :][7:8, :] * gain + bias_term
-        before = jnp.where(g == 0, first, inside)
-        place_in = lax.broadcasted_iota(jnp.int32, normed.shape, 0)
-        delta = normed - jnp.where(place_in == 0, before, pltpu.roll(normed, 1, 0)) * keep
-        d_norm = jnp.zeros_like(normed)
-        d_all = jnp.zeros_like(normed)
-        for at in range(mixes):
-            d_in = d_scr[at, place, :]
-            d_norm = d_norm + d_in * mix_ref[at : at + 1, :]
-            d_all = d_all + d_in
-            product = d_in * delta
-            sums[2 + at] += product[:8] + product[8:]
-        d_prev = (d_all - d_norm) * keep
-        d_next = jnp.where(
-            place_in == GROUP - 1, after_row[0:1, :], pltpu.roll(d_prev, GROUP - 1, 0)
-        )
-        after_row[0:1, :] = d_prev[0:1, :]
-        d_norm = d_norm + d_next
-        product = d_norm * unit
-        sums[0] += product[:8] + product[8:]
-        sums[1] += d_norm[:8] + d_norm[8:]
-        scaled = d_norm * gain
-        d_in = inverse * (
-            scaled
-            - jnp.mean(scaled, -1, keepdims=True)
-            - unit * jnp.mean(scaled * unit, -1, keepdims=True)
-        )
-        if own:
-            extra = own_refs[0][place, :].astype(jnp.float32)
-            extra = jnp.concatenate([extra] * (width // extra.shape[1]), axis=1)
-            d_in = d_in + extra * own_refs[1][...]
-        out_ref[place, :] = d_in.astype(jnp.bfloat16)
-        return 0
-
-    lax.fori_loop(0, groups, group, 0)
+    lax.fori_loop(0, width // PAIR, last_step, 0)
 
     @pl.when(pl.program_id(0) == tiles - 1)
     def _():
@@ -533,7 +639,7 @@
 
 def blend_back(xs, grads, weights, keep, edge, back, norm, mixers, piece, own, name):
     tokens, width = xs[0].shape
-    rows = min(piece, 128)
+    rows = min(piece, 256)
     mixes = mixers.shape[0]
     per_seq = piece // rows
     tiles = tokens // rows
@@ -584,10 +690,10 @@
         ],
         scratch_shapes=[
             pltpu.VMEM((mixes, rows, width), jnp.float32),
-            pltpu.VMEM((rows, width), jnp.float32),
-            pltpu.VMEM((rows, PAIR), jnp.float32),
+            pltpu.VMEM((rows + HALO, width), jnp.float32),
+            pltpu.VMEM((rows + HALO, width), jnp.float32),
+            pltpu.VMEM((2, rows, PAIR), jnp.float32),
             pltpu.VMEM((2 + mixes, 8, width), jnp.float32),
-            pltpu.VMEM((8, width), jnp.float32),
         ],
         cost_estimate=pl.CostEstimate(
             flops=2 * tokens * width * sum(grad.shape[1] for grad in grads),
@@ -656,7 +762,7 @@
         tiled=True,
     )
     w_chan = lax.all_gather(
-        jnp.concatenate([ffn_lookup_matrix, ffn_payload_matrix.T, ffn_acceptor_matrix], axis=1),
+        jnp.concatenate([ffn_lookup_matrix, ffn_acceptor_matrix], axis=1),
         owners,
         axis=0,
         tiled=True,
@@ -666,8 +772,8 @@
         w_time[:, at * fourth_extent : (at + 1) * fourth_extent] for at in range(5)
     )
     w_chankey = w_chan[:, :units]
-    w_chanvalue_t = w_chan[:, units : 2 * units]
-    w_chanrecept = w_chan[:, 2 * units :]
+    w_chanrecept = w_chan[:, units:]
+    w_chanvalue_t = lax.all_gather(ffn_payload_matrix.T, owners, axis=0, tiled=True)
     x_low = entering_activations.reshape(token_count, embedding_extent)
     norm_one = jnp.stack([first_standardize_scaling, first_standardize_offset])
     norm_two = jnp.stack([second_standardize_scaling, second_standardize_offset])
@@ -676,9 +782,8 @@
     )
     mix_two = jnp.stack([ffn_lookup_lerp, ffn_acceptor_lerp])
 
-    def edge_from(last_rows, norm):
-        last, _, _ = norm_rows(last_rows, norm[0], norm[1])
-        return shifted(last, "ctx", 1)[:, None]
+    def edge_from(last_rows):
+        return shifted(unit_rows(last_rows), "ctx", 1)[:, None]
 
     def back_from(grads, weights, mixers):
         first = jnp.zeros((seqs_here, embedding_extent), jnp.float32)
@@ -687,7 +792,7 @@
             first = first + matmul_nt(rows, weight) * (1.0 - mixers[at])
         return shifted(first * keep_first, "ctx", -1)[:, None]
 
-    edge_one = edge_from(entering_activations[:, -1].astype(jnp.float32), norm_one)
+    edge_one = edge_from(entering_activations[:, -1].astype(jnp.float32))
     mixed_in = blend((x_low,), keep, edge_one, norm_one, mix_one, piece_len, "blend_one")
     key_low = matmul(mixed_in[1], w_key).astype(jnp.bfloat16)
     value_low = matmul(mixed_in[2], w_value).astype(jnp.bfloat16)
@@ -735,7 +840,7 @@
     last_rows = entering_activations[:, -1].astype(jnp.float32) + mixed_out.reshape(
         seqs_here, piece_len, embedding_extent
     )[:, -1].astype(jnp.float32)
-    edge_two = edge_from(last_rows, norm_two)
+    edge_two = edge_from(last_rows)
     key_in, rec_in = blend(
         (x_low, mixed_out), keep, edge_two, norm_two, mix_two, piece_len, "blend_two"
     )
@@ -761,8 +866,6 @@
     d_rec_pre = (d_result * chan_sum * rec_gate * (1.0 - rec_gate)).astype(jnp.bfloat16)
     d_hidden = matmul(d_chan_full, w_chanvalue_t)
     d_key_pre = (d_hidden * 2.0 * jax.nn.relu(key_pre)).astype(jnp.bfloat16)
-    grad_chankey = matmul_tn(key_in, d_key_pre)
-    grad_chanrecept = matmul_tn(rec_in, d_rec_pre)
     full_shape = (seqs_here, piece_len, embedding_extent)
     own_mask = (jnp.arange(embedding_extent) // fourth_extent == lax.axis_index("tp")).astype(
         jnp.float32
@@ -770,7 +873,7 @@
     d_middle_part, chan_small = blend_back(
         (x_low, mixed_out),
         (d_key_pre, d_rec_pre),
-        ((w_chan, 0), (w_chan, 2 * units // fourth_extent)),
+        ((w_chan, 0), (w_chanrecept, 0)),
         keep,
         edge_two,
         back_from((d_key_pre, d_rec_pre), (w_chankey, w_chanrecept), mix_two),
@@ -780,14 +883,21 @@
         (d_result_low, own_mask),
         "blend_two_back",
     )
-    d_mixed = tp_sum(d_middle_part)
-    grad_output_t = matmul_tn(d_mixed, joined_low)
-    grads_chan = jnp.concatenate(
-        [item.astype(jnp.bfloat16) for item in (grad_output_t, grad_chanrecept, grad_chankey)],
-        axis=1,
-    )
+
+    def chan_grads(token):
+        d_key_late, d_rec_late, _ = after(d_key_pre, d_rec_pre, token)
+        return jnp.concatenate(
+            [
+                matmul_tn(key_in, d_key_late).astype(jnp.bfloat16),
+                matmul_tn(rec_in, d_rec_late).astype(jnp.bfloat16),
+            ],
+            axis=1,
+        )
+
+    d_mixed, grads_chan = tp_sum(d_middle_part, chan_grads)
     d_mixed, grads_chan, g_chanvalue = after(d_mixed, grads_chan, g_chanvalue)
     g_chan = lax.psum_scatter(grads_chan, owners, scatter_dimension=0, tiled=True)
+    grad_output_t = matmul_tn(d_mixed, joined_low).astype(jnp.bfloat16)
     d_joined = matmul(d_mixed, w_output_t)
     d_gate_pre, d_attend, local_grad, group_small = call(
         gate_back_kernel,
@@ -809,6 +919,11 @@
         name="gate_back",
         flops=square // 8,
     )
+    grads_early = jnp.concatenate(
+        [grad_output_t, matmul_tn(mixed_in[3], d_gate_pre).astype(jnp.bfloat16)], axis=1
+    )
+    early = owner_scatter_steps(grads_early)
+    g_early = next(early)
     outgoing_state = carried(carry_mult, local_grad, "ctx", -1)
     d_recept, d_key, d_value, state_small = call(
         mix_back_kernel,
@@ -829,16 +944,21 @@
         name="mix_back",
         flops=6 * square,
     )
+    early_steps = len(axis_bits("fsdp")) + len(axis_bits("ctx"))
+    d_recept, d_key, d_value, g_early = after(d_recept, d_key, d_value, g_early)
+    for _ in range(early_steps - 2):
+        g_early = early.send(g_early)
     d_lows = [d_recept, d_key, d_value, d_gate_pre]
     weights_time = (w_recept, w_key, w_value, w_gate)
     grads_time = jnp.concatenate(
         [
             matmul_tn(mixed, grad_low).astype(jnp.bfloat16)
-            for mixed, grad_low in zip(mixed_in, d_lows)
+            for mixed, grad_low in zip(mixed_in, d_lows[:3])
         ],
         axis=1,
     )
-    *d_lows, grads_time, g_chan = after(d_lows[0], *d_lows[1:], grads_time, g_chan)
+    *d_lows, _, g_early = after(d_lows[0], *d_lows[1:], grads_time, g_early)
+    g_early = early.send(g_early)
     g_time = lax.psum_scatter(grads_time, owners, scatter_dimension=0, tiled=True)
     d_input_part, time_small = blend_back(
         (x_low,),
@@ -853,6 +973,7 @@
         None,
         "blend_one_back",
     )
+    d_input_part, g_early, g_chan = after(d_input_part, g_early, g_chan)
     head_small = jnp.concatenate([state_small[:2], group_small[:2]])
     head_small = lax.dynamic_update_slice_in_dim(
         jnp.zeros((4, embedding_extent), jnp.float32), head_small, sharded_layout, 1
@@ -875,12 +996,14 @@
     g_chanvalue = g_chanvalue.astype(jnp.float32)
     g_chan = g_chan.astype(jnp.float32)
     g_time = g_time.astype(jnp.float32)
-    g_recept, g_key, g_value, g_gate = (
-        g_time[:, at * fourth_extent : (at + 1) * fourth_extent] for at in range(4)
-    )
-    g_output = g_chan[:, :fourth_extent].T
-    g_chanrecept = g_chan[:, fourth_extent : 2 * fourth_extent]
-    g_chankey = g_chan[:, 2 * fourth_extent :]
+    g_early = g_early.astype(jnp.float32)
+    g_recept, g_key, g_value = (
+        g_time[:, at * fourth_extent : (at + 1) * fourth_extent] for at in range(3)
+    )
+    g_output = g_early[:, :fourth_extent].T
+    g_gate = g_early[:, fourth_extent:]
+    g_chankey = g_chan[:, :units]
+    g_chanrecept = g_chan[:, units:]
     return (
         result,
         grad_inputs,

time: 1080 us -> 992 us (0.919)
  waiting for transfers between devices: 528 us -> 433 us
  Pallas kernels: 217 us -> 179 us
  local copies, waits for them, and re-layouts: 51.9 us -> 77 us
  starting transfers between devices: 55.3 us -> 70.9 us
    reduce_scatter x1, waiting for transfers between devices: 108 us -> 0.01 us  [per_device(): lax.psum_scatter(grads_chan, owners, scatter_dimension=0, tiled=True)]
    ppermute x0 -> x3, waiting for transfers between devices: none -> 63.9 us  [swap(): lax.ppermute(x, axis, [(i, i ^ bit) for i in range(lax.axis_size(axis))])]
    all_gather x1 -> x2, waiting for transfers between devices: 78 us -> 37.8 us  [the longest x1 37.8 us: per_device(): lax.all_gather(ffn_payload_matrix.T, owners, axis=0, tiled=True)]
    pallas_call x2, Pallas kernels: 123 us -> 89.1 us  [blend_back(): pl.pallas_call(partial(blend_back_kernel, len(xs), mixes, per_seq, int(ow...]
    ppermute x15, waiting for transfers between devices: 187 us -> 165 us  [partner(): return lax.ppermute(x, 'tp', [(i, i ^ bit) for i in range(count)])]
    ppermute x5, waiting for transfers between devices: 12.8 us -> 30.2 us  [whole_sum(): x = x + lax.ppermute(x, axis, [(i, i ^ bit) for i in range(count)])]
    ppermute x0 -> x3, starting transfers between devices: none -> 14.4 us  [swap(): lax.ppermute(x, axis, [(i, i ^ bit) for i in range(lax.axis_size(axis))])]
    concatenate x2 -> x3, other arithmetic: 23.9 us -> 15.2 us  [the longest x1 11.5 us: chan_grads(): jnp.concatenate([matmul_tn(key_in, d_key_late).astype(jnp.bfloat16), matm...]
  transfers between devices with their start and end apart: 41 -> 45, of which waited for: 25 -> 27; matrix products, arithmetic and copies ran while one was open for 19% -> 26% of each run, Pallas kernels for 20% -> 18%
where the time goes in v3:
time: 992 us; the launch traced here: 984 us
  waiting for transfers between devices  433 us (44%)
  Pallas kernels  179 us (18%)
  matrix products  132 us (13%)
  other arithmetic  77.5 us (8%)
  local copies, waits for them, and re-layouts  77 us (8%)
  starting transfers between devices  70.9 us (7%)
  between operations  15.5 us (2%)
    ppermute x15, waiting for transfers between devices, partner(): return lax.ppermute(x, 'tp', [(i, i ^ bit) for i in range(count)])  165 us
    all_gather x1, waiting for transfers between devices, per_device(): lax.all_gather(jnp.concatenate([acceptor_matrix, lookup_matrix, payload_m...  108 us
    pallas_call x2, Pallas kernels, blend_back(): pl.pallas_call(partial(blend_back_kernel, len(xs), mixes, per_seq, int(ow...  89.1 us
    dot_general x8, matrix products, matmul(): return jnp.dot(left, right, preferred_element_type=jnp.float32)  64.1 us
    ppermute x3, waiting for transfers between devices, swap(): lax.ppermute(x, axis, [(i, i ^ bit) for i in range(lax.axis_size(axis))])  63.9 us
    pallas_call x4, Pallas kernels, pair_call(): pl.pallas_call(kernel, grid=(pairs, seqs), in_specs=[specs[kind] for kind...  49.6 us
    dot_general x8, matrix products, matmul_tn(): lax.dot_general(left, right, (((0,), (0,)), ((), ())), preferred_element_...  40.3 us
    pallas_call x2, Pallas kernels, blend(): pl.pallas_call(partial(blend_kernel, len(xs), mixes, per_seq), grid=(toke...  39.9 us
  transfers between devices with their start and end apart: 45, of which 27 were waited for; matrix products, arithmetic and copies ran while one was open for 26% of the time, Pallas kernels for 18%

profile of v3, /device:TPU:0, one launch (start us, length us, event | category | flops | bytes accessed | tf_op | source)
XLA Modules:
  0.0 984.4 jit_solution(7414440332759732905)
XLA Ops:
  17.3 4.9 collective-permute-start.1
  22.2 4.5 collective-permute-start.2
  38.3 20.8 %blend_one.1 = (bf16[1024,2048]{1,0:T(8,128)(2,1)}, bf16[1024,2048]{1,0:T(8,128)(2,1)}, bf16[1024,2048]{1,0:T(8,128)(2,1)}, bf16[1024,2048]{1,0:T(8,128)(2,1)}) custom-call(bf16[1024,2048]{1,0:T(8,128)(2,1)} %bitcast.177, f32[1024,1]{1,0:T(8,128)} %bitcast.187, f32[2,1,2048]{2,1,0:T(1,128)} %broadcast_in_dim.20.refs_2_.refs_11_, ...), custom_call_target="tpu_custom_call" | custom-call | flops 41943040 | bytes 20971520 | tf_op jit(solution)/shard_map/blend_one/pallas_call | solution.py:504
  59.2 108.1 %all-gather.4.cloned.1.call-done.refs_6_.refs_7_.refs_8_.refs_9_ = bf16[2048,2560]{1,0:T(8,128)(2,1)} async-done(((bf16[256,2560]{1,0:T(8,128)(2,1)}), bf16[2048,2560]{1,0:T(8,128)(2,1)}) %all-gather.4.cloned.1.call-update) | async-done | bytes 10485776 | tf_op jit(solution)/shard_map/all_gather | solution.py:756
  167.2 6.3 fusion.39.k_ref
  173.5 4.9 fusion.42.v_ref
  178.5 6.9 carry.1
  186.3 3.5 collective-permute-start.4
  191.2 2.9 collective-permute-start.6
  194.1 6.3 fusion.36.r_ref
  200.5 5.3 fusion.25.gate_ref
  208.2 11.3 %mix.1 = (bf16[1024,512]{1,0:T(8,128)(2,1)}, f32[1024,512]{1,0:T(8,128)}) custom-call(bf16[1024,512]{1,0:T(8,128)(2,1)} %fusion.36.r_ref, bf16[1024,512]{1,0:T(8,128)(2,1)} %fusion.39.k_ref, bf16[1024,512]{1,0:T(8,128)(2,1)} %fusion.42.v_ref, f32[1024,512]{1,0:T(8,128)} %fusion.25.gate_ref, f32[1,512]{1,0:T(1,128)} %bitcast.209, ...), custom_call_target="tpu_custom_call" | custom-call | flops 1073741824 | bytes 11087872 | tf_op jit(solution)/shard_map/mix/pallas_call | solution.py:403
  219.6 4.3 convolution_convert_fusion.3
  226.2 4.3 collective-permute-done.7
  230.5 3.0 add_convert_fusion.5
  235.1 46.2 %collective-permute-done.8 = bf16[512,2048]{1,0:T(8,128)(2,1)} collective-permute-done((bf16[512,2048]{1,0:T(8,128)(2,1)S(1)}, bf16[512,2048]{1,0:T(8,128)(2,1)}, u32[]{:S(2)}, u32[]{:S(2)}) %collective-permute-start.8) | collective-permute-done | bytes 2097184 | tf_op jit(solution)/shard_map/ppermute | solution.py:48
  281.3 3.7 add_convert_fusion.4
  285.1 4.3 collective-permute-done.9
  289.4 3.7 maximum_select_fusion.refs_1_.refs_3_
  295.7 11.2 %collective-permute-start.10 = (f32[2,2048]{1,0:T(2,128)S(1)}, f32[2,2048]{1,0:T(2,128)S(1)}, u32[]{:S(2)}, u32[]{:S(2)}) collective-permute-start(f32[2,2048]{1,0:T(2,128)S(1)} %fusion.53), channel_id=1, source_target_pairs={{0,4},{4,8},{8,12},{1,5},{5,9},{9,13},{2,6},{6,10},{10,14},{3,7},{... | collective-permute-start | bytes 49160 | tf_op jit(solution)/shard_map/ppermute | solution.py:25
  309.0 19.1 %blend_two.1 = (bf16[1024,2048]{1,0:T(8,128)(2,1)}, bf16[1024,2048]{1,0:T(8,128)(2,1)}) custom-call(bf16[1024,2048]{1,0:T(8,128)(2,1)} %bitcast.178, bf16[1024,2048]{1,0:T(8,128)(2,1)} %copy-done, f32[1024,1]{1,0:T(8,128)} %bitcast.188, f32[2,1,2048]{2,1,0:T(1,128)} %copy.99.refs_3_.refs_9_, f32[2,2048]{1,0:T(2,128)} %get-tuple-element.221.refs_4_.refs_11_, ...), custom_call_target="tpu_custom_call" | custom-call | flops 41943040 | bytes 16777216 | tf_op jit(solution)/shard_map/blend_two/pallas_call | solution.py:504
  330.7 6.9 constant_dynamic-update-slice_fusion.7
  339.2 22.9 %collective-permute-done.11 = bf16[1024,512]{1,0:T(8,128)(2,1)S(1)} collective-permute-done((bf16[1024,512]{1,0:T(8,128)(2,1)}, bf16[1024,512]{1,0:T(8,128)(2,1)S(1)}, u32[]{:S(2)}, u32[]{:S(2)}) %collective-permute-start.11) | collective-permute-done | bytes 1048608 | tf_op jit(solution)/shard_map/ppermute | solution.py:48
  362.1 13.6 %multiply_convert_fusion.1 = (bf16[1024,1792]{1,0:T(8,128)(2,1)S(1)}, f32[1024,1792]{1,0:T(8,128)}) fusion(bf16[1024,2048]{1,0:T(8,128)(2,1)} %get-tuple-element.69, bf16[2048,2304]{1,0:T(8,128)(2,1)} %all-gather.6.cloned.1.call-done.refs_6_), kind=kOutput, calls=%fused_computation.5 | convolution fusion | flops 7521697792 | bytes 22544384 | tf_op jit(solution)/shard_map/dot_general | solution.py:162
  379.3 12.1 %convolution_convert_fusion.1 = bf16[1792,2048]{1,0:T(8,128)(2,1)} fusion(bf16[1024,1792]{1,0:T(8,128)(2,1)S(1)} %get-tuple-element.70, bf16[1024,2048]{1,0:T(8,128)(2,1)} %constant_dynamic-update-slice_fusion.4), kind=kOutput, calls=%fused_computation.3 | convolution fusion | flops 7519862784 | bytes 15204352 | tf_op jit(solution)/shard_map/dot_general | solution.py:166
  391.4 37.8 %all-gather.8.cloned.1.call-done = bf16[2048,1792]{0,1:T(8,128)(2,1)} async-done(((bf16[256,1792]{0,1:T(8,128)(2,1)}), bf16[2048,1792]{0,1:T(8,128)(2,1)}) %all-gather.8.cloned.1.call-update) | async-done | bytes 7340048 | tf_op jit(solution)/shard_map/all_gather | solution.py:776
  429.1 11.3 %convolution_convert_fusion.2 = bf16[1024,2048]{1,0:T(8,128)(2,1)S(1)} fusion(bf16[1024,1792]{1,0:T(8,128)(2,1)} %copy-done.49, bf16[2048,1792]{0,1:T(8,128)(2,1)} %all-gather.8.cloned.1.call-done), kind=kOutput, calls=%fused_computation.23 | convolution fusion | flops 7518289920 | bytes 15204352 | tf_op jit(solution)/shard_map/dot_general | solution.py:172
  450.2 14.2 %multiply_convert_fusion.refs_4_ = bf16[1024,1792]{1,0:T(8,128)(2,1)} fusion(f32[1024,1792]{1,0:T(8,128)} %get-tuple-element.215, bf16[1024,2048]{1,0:T(8,128)(2,1)} %constant_dynamic-update-slice_fusion.4, bf16[2048,1792]{0,1:T(8,128)(2,1)} %all-gather.8.cloned.1.call-done), kind=kOutput, calls=%fused_computation.4 | convolution fusion | flops 7523532800 | bytes 22544384 | tf_op jit(solution)/shard_map/dot_general | solution.py:162
  467.4 6.6 collective-permute-done.16
  474.0 4.7 fusion.19
  482.8 3.2 collective-permute-done.17
  486.6 45.1 %blend_two_back.1 = (bf16[1024,2048]{1,0:T(8,128)(2,1)}, f32[8,2048]{1,0:T(8,128)}) custom-call(bf16[1024,2048]{1,0:T(8,128)(2,1)} %bitcast.180, bf16[1024,2048]{1,0:T(8,128)(2,1)} %copy-done, bf16[1024,2048]{1,0:T(8,128)(2,1)} %bitcast.181, bf16[1024,2048]{1,0:T(8,128)(2,1)} %copy-done, bf16[1024,1792]{1,0:T(8,128)(2,1)} %multiply_convert_fusion.refs_4_, ...), custom_call_target="tpu_custom_call" | custom-call | flops 9663676416 | bytes 16777216 | tf_op jit(solution)/shard_map/blend_two_back/pallas_call | solution.py:664
  533.8 4.1 collective-permute-done.18
  540.5 10.9 %convolution_convert_fusion = bf16[2048,1792]{0,1:T(8,128)(2,1)S(1)} fusion(bf16[1024,2048]{1,0:T(8,128)(2,1)} %get-tuple-element.69, bf16[1024,1792]{1,0:T(8,128)(2,1)S(1)} %copy-done.40), kind=kOutput, calls=%fused_computation.2 | convolution fusion | flops 7519862784 | bytes 15204352 | tf_op jit(solution)/shard_map/dot_general | solution.py:166
  553.9 11.5 %pad_maximum_fusion = bf16[2048,2304]{0,1:T(8,128)(2,1)} fusion(bf16[2048,512]{0,1:T(8,128)(2,1)S(1)} %convolution_convert_fusion.9, bf16[2048,1792]{0,1:T(8,128)(2,1)S(1)} %convolution_convert_fusion), kind=kLoop, calls=%fused_computation | loop fusion | flops 18874368 | bytes 18874368 | tf_op jit(solution)/shard_map/concatenate | solution.py:889
  565.4 21.3 %collective-permute-done.19 = bf16[512,2048]{1,0:T(8,128)(2,1)} collective-permute-done((bf16[512,2048]{1,0:T(8,128)(2,1)S(1)}, bf16[512,2048]{1,0:T(8,128)(2,1)}, u32[]{:S(2)}, u32[]{:S(2)}) %collective-permute-start.19) | collective-permute-done | bytes 2097184 | tf_op jit(solution)/shard_map/ppermute | solution.py:48
  589.2 4.1 collective-permute-done.20
  593.3 3.7 maximum_select_fusion.1
  597.1 6.5 fusion.21.dj_ref
  603.6 11.3 %gate_back.1 = (bf16[1024,512]{1,0:T(8,128)(2,1)}, bf16[1024,512]{1,0:T(8,128)(2,1)}, f32[2,4,64,128]{3,2,1,0:T(8,128)}, f32[8,512]{1,0:T(8,128)}) custom-call(f32[1024,512]{1,0:T(8,128)} %fusion.21.dj_ref, f32[1024,512]{1,0:T(8,128)} %get-tuple-element.76.attend_ref, f32[1024,512]{1,0:T(8,128)} %fusion.25.gate_ref, bf16[1024,512]{1,0:T(8,128)(2,1)} %fusion.36.r_ref, ...), custom_call_target="tpu_custom_call" | custom-call | flops 67108864 | bytes 14749696 | tf_op jit(solution)/shard_map/gate_back/pallas_call | solution.py:403
  615.0 4.7 convolution_convert_fusion.8
  622.2 2.6 pad_maximum_fusion.2
  624.8 7.9 reshape.218
  632.7 6.4 constant_dynamic-slice_fusion.2
  654.3 8.9 collective-permute-done.24
  663.3 9.3 collective-permute-done.25
  673.4 20.1 %mix_back.1 = (bf16[1024,512]{1,0:T(8,128)(2,1)}, bf16[1024,512]{1,0:T(8,128)(2,1)}, bf16[1024,512]{1,0:T(8,128)(2,1)}, f32[8,512]{1,0:T(8,128)}) custom-call(bf16[1024,512]{1,0:T(8,128)(2,1)} %fusion.36.r_ref, bf16[1024,512]{1,0:T(8,128)(2,1)} %fusion.39.k_ref, bf16[1024,512]{1,0:T(8,128)(2,1)} %fusion.42.v_ref, ...), custom_call_target="tpu_custom_call" | custom-call | flops 3221225472 | bytes 9523200 | tf_op jit(solution)/shard_map/mix_back/pallas_call | solution.py:403
  693.5 6.7 collective-permute-done.27
  701.5 2.6 fusion.4
  711.8 11.4 %pad_maximum_fusion.1 = bf16[2048,1536]{0,1:T(8,128)(2,1)} fusion(bf16[2048,512]{0,1:T(8,128)(2,1)S(1)} %convolution_convert_fusion.4, bf16[2048,512]{0,1:T(8,128)(2,1)S(1)} %convolution_convert_fusion.5, bf16[2048,512]{0,1:T(8,128)(2,1)S(1)} %convolution_convert_fusion.6), kind=kLoop, calls=%fused_computation.10 | loop fusion | flops 18874368 | bytes 12582912 | tf_op jit(solution)/shard_map/concatenate | solution.py:953
  723.3 5.9 collective-permute-start.28
  729.2 57.2 %collective-permute-done.28 = bf16[2,256,1024]{1,2,0:T(8,128)(2,1)} collective-permute-done((bf16[2,256,1024]{1,2,0:T(8,128)(2,1)S(1)}, bf16[2,256,1024]{1,2,0:T(8,128)(2,1)}, u32[]{:S(2)}, u32[]{:S(2)}) %collective-permute-start.28) | collective-permute-done | bytes 1048608 | tf_op jit(solution)/shard_map/ppermute | solution.py:101
  801.2 6.9 collective-permute-start.30
  808.6 43.9 %blend_one_back.1 = (bf16[1024,2048]{1,0:T(8,128)(2,1)}, f32[8,2048]{1,0:T(8,128)}) custom-call(bf16[1024,2048]{1,0:T(8,128)(2,1)} %bitcast.182, bf16[1024,2048]{1,0:T(8,128)(2,1)} %bitcast.183, bf16[1024,512]{1,0:T(8,128)(2,1)} %get-tuple-element.87.refs_2_, bf16[1024,512]{1,0:T(8,128)(2,1)} %get-tuple-element.88.refs_3_, ...), custom_call_target="tpu_custom_call" | custom-call | flops 8589934592 | bytes 16777216 | tf_op jit(solution)/shard_map/blend_one_back/pallas_call | solution.py:664
  855.5 4.1 collective-permute-done.31
  863.6 44.7 %collective-permute-done.32 = bf16[512,2048]{1,0:T(8,128)(2,1)S(1)} collective-permute-done((bf16[512,2048]{1,0:T(8,128)(2,1)S(1)}, bf16[512,2048]{1,0:T(8,128)(2,1)S(1)}, u32[]{:S(2)}, u32[]{:S(2)}) %collective-permute-start.32) | collective-permute-done | bytes 2097184 | tf_op jit(solution)/shard_map/ppermute | solution.py:48
  909.9 3.7 collective-permute-done.34
  915.2 4.1 collective-permute-done.35
  919.4 4.9 collective-permute-done.36
  924.4 3.4 collective-permute-start.37
  927.8 11.0 %collective-permute-done.37 = f32[14,2048]{1,0:T(8,128)S(1)} collective-permute-done((f32[14,2048]{1,0:T(8,128)S(1)}, f32[14,2048]{1,0:T(8,128)S(1)}, u32[]{:S(2)}, u32[]{:S(2)}) %collective-permute-start.37) | collective-permute-done | bytes 114720 | tf_op jit(solution)/shard_map/ppermute | solution.py:125
  940.8 6.4 collective-permute-done.38
  962.4 2.8 copy.116
  970.1 7.3 convert_add_fusion
  (298 shorter events, 144.2 us)
Async XLA Ops:
  7.2 23.5 %copy-start.35 = (f32[2048]{0:T(1024)S(1)}, f32[2048]{0:T(1024)}, u32[]{:S(2)}) copy-start(f32[2048]{0:T(1024)} %param.35) | copy-start | bytes 24580
  7.2 23.5 %copy-start.34 = (f32[2048]{0:T(1024)S(1)}, f32[2048]{0:T(1024)}, u32[]{:S(2)}) copy-start(f32[2048]{0:T(1024)} %param.36) | copy-start | bytes 24580
  7.2 24.1 %copy-start.25 = (f32[2048]{0:T(1024)S(1)}, f32[2048]{0:T(1024)}, u32[]{:S(2)}) copy-start(f32[2048]{0:T(1024)} %param.37) | copy-start | bytes 24580
  7.3 24.1 %copy-start.27 = (f32[2048]{0:T(1024)S(1)}, f32[2048]{0:T(1024)}, u32[]{:S(2)}) copy-start(f32[2048]{0:T(1024)} %param.38) | copy-start | bytes 24580
  7.3 24.1 %copy-start.29 = (f32[2048]{0:T(1024)S(1)}, f32[2048]{0:T(1024)}, u32[]{:S(2)}) copy-start(f32[2048]{0:T(1024)} %param.39) | copy-start | bytes 24580
  7.3 24.1 %copy-start.31 = (f32[2048]{0:T(1024)S(1)}, f32[2048]{0:T(1024)}, u32[]{:S(2)}) copy-start(f32[2048]{0:T(1024)} %param.40) | copy-start | bytes 24580
  7.3 159.9 %all-gather.4.cloned.1.call-start = ((), (), s32[]{:S(2)}) async-start(), calls=%async_computation.3 | async-start | bytes 11796480 | tf_op jit(solution)/shard_map/all_gather | solution.py:756
  13.5 314.6 %all-gather.6.cloned.1.call-start = ((), (), s32[]{:S(2)}) async-start(), calls=%async_computation.4 | async-start | bytes 10616832 | tf_op jit(solution)/shard_map/all_gather | solution.py:764
  14.7 414.5 %all-gather.8.cloned.1.call-start = ((), (), s32[]{:S(2)}) async-start(), calls=%async_computation.5 | async-start | bytes 8257536 | tf_op jit(solution)/shard_map/all_gather | solution.py:776
  17.3 156.3 %copy-start.38 = (bf16[2,4,1,128]{3,2,1,0:T(2,128)(2,1)}, bf16[2,4,1,128]{3,2,1,0:T(2,128)(2,1)S(1)}, u32[]{:S(2)}) copy-start(bf16[2,4,1,128]{3,2,1,0:T(2,128)(2,1)S(1)} %get-tuple-element.176) | copy-start | bytes 6148
  17.3 20.4 %collective-permute-start.1 = (bf16[2,4,1,128]{3,2,1,0:T(2,128)(2,1)S(1)}, bf16[2,4,1,128]{3,2,1,0:T(2,128)(2,1)S(1)}, u32[]{:S(2)}, u32[]{:S(2)}) collective-permute-start(bf16[2,4,1,128]{3,2,1,0:T(2,128)(2,1)S(1)} %get-tuple-element.176), channel_id=1, source_target_pairs={{0,4},{4,8},{8,12},{1,5},{5,9},{9,13},{2,6},{6,10},{10,14},{3,7},{... | collective-permute-start | bytes 6152 | tf_op jit(solution)/shard_map/ppermute | solution.py:30
  22.2 15.5 %collective-permute-start.2 = (bf16[2,4,1,128]{3,2,1,0:T(2,128)(2,1)S(1)}, bf16[2,4,1,128]{3,2,1,0:T(2,128)(2,1)S(1)}, u32[]{:S(2)}, u32[]{:S(2)}) collective-permute-start(bf16[2,4,1,128]{3,2,1,0:T(2,128)(2,1)S(1)} %get-tuple-element.176), channel_id=1, source_target_pairs={{0,8},{4,12},{1,9},{5,13},{2,10},{6,14},{3,11},{7,15},{16,24},{20,... | collective-permute-start | bytes 6152 | tf_op jit(solution)/shard_map/ppermute | solution.py:30
  26.7 10.9 %collective-permute-start.3 = (bf16[2,4,1,128]{3,2,1,0:T(2,128)(2,1)S(1)}, bf16[2,4,1,128]{3,2,1,0:T(2,128)(2,1)S(1)}, u32[]{:S(2)}, u32[]{:S(2)}) collective-permute-start(bf16[2,4,1,128]{3,2,1,0:T(2,128)(2,1)S(1)} %get-tuple-element.176), channel_id=1, source_target_pairs={{0,12},{1,13},{2,14},{3,15},{16,28},{17,29},{18,30},{19,31}} | collective-permute-start | bytes 6152 | tf_op jit(solution)/shard_map/ppermute | solution.py:30
  29.3 8.4 collective-permute-start
  186.3 19.4 %collective-permute-start.4 = (bf16[2,4,64,128]{3,2,1,0:T(8,128)(2,1)S(1)}, bf16[2,4,64,128]{3,2,1,0:T(8,128)(2,1)S(1)}, u32[]{:S(2)}, u32[]{:S(2)}) collective-permute-start(bf16[2,4,64,128]{3,2,1,0:T(8,128)(2,1)S(1)} %convert_element_type.304), channel_id=1, source_target_pairs={{0,12},{1,13},{2,14},{3,15},{16,28},{17,29},{18,30},{19,31}} | collective-permute-start | bytes 393224 | tf_op jit(solution)/shard_map/ppermute | solution.py:30
  189.9 15.9 %collective-permute-start.5 = (bf16[2,4,64,128]{3,2,1,0:T(8,128)(2,1)S(1)}, bf16[2,4,64,128]{3,2,1,0:T(8,128)(2,1)S(1)}, u32[]{:S(2)}, u32[]{:S(2)}) collective-permute-start(bf16[2,4,64,128]{3,2,1,0:T(8,128)(2,1)S(1)} %convert_element_type.304), channel_id=1, source_target_pairs={{0,8},{4,12},{1,9},{5,13},{2,10},{6,14},{3,11},{7,15},{16,24},{20,... | collective-permute-start | bytes 393224 | tf_op jit(solution)/shard_map/ppermute | solution.py:30
  191.2 16.3 %collective-permute-start.6 = (bf16[2,4,64,128]{3,2,1,0:T(8,128)(2,1)S(1)}, bf16[2,4,64,128]{3,2,1,0:T(8,128)(2,1)S(1)}, u32[]{:S(2)}, u32[]{:S(2)}) collective-permute-start(bf16[2,4,64,128]{3,2,1,0:T(8,128)(2,1)S(1)} %convert_element_type.304), channel_id=1, source_target_pairs={{0,4},{4,8},{8,12},{1,5},{5,9},{9,13},{2,6},{6,10},{10,14},{3,7},{... | collective-permute-start | bytes 393224 | tf_op jit(solution)/shard_map/ppermute | solution.py:30
  226.1 4.4 collective-permute-start.7
  233.5 47.8 %collective-permute-start.8 = (bf16[512,2048]{1,0:T(8,128)(2,1)S(1)}, bf16[512,2048]{1,0:T(8,128)(2,1)}, u32[]{:S(2)}, u32[]{:S(2)}) collective-permute-start(bf16[512,2048]{1,0:T(8,128)(2,1)S(1)} %add_convert_fusion.5), channel_id=1, source_target_pairs={{0,2},{1,3},{2,0},{3,1},{4,6},{5,7},{6,4},{7,5},{8,10},{9,11},{10,... | collective-permute-start | bytes 6291464 | tf_op jit(solution)/shard_map/ppermute | solution.py:48
  235.1 361.9 %reduce-scatter.4.cloned.1.call-start = ((), (), s32[]{:S(2)}) async-start(), calls=%async_computation.6 | async-start | bytes 8257536 | tf_op jit(solution)/shard_map/reduce_scatter | solution.py:855
  285.0 4.4 collective-permute-start.9
  285.0 21.8 %copy-start.23 = (f32[2048]{0:T(1024)S(1)}, f32[2048]{0:T(1024)}, u32[]{:S(2)}) copy-start(f32[2048]{0:T(1024)} %param.47) | copy-start | bytes 24580
  285.0 21.8 %copy-start.24 = (f32[2048]{0:T(1024)S(1)}, f32[2048]{0:T(1024)}, u32[]{:S(2)}) copy-start(f32[2048]{0:T(1024)} %param.48) | copy-start | bytes 24580
  285.0 21.9 %copy-start.36 = (f32[2048]{0:T(1024)S(1)}, f32[2048]{0:T(1024)}, u32[]{:S(2)}) copy-start(f32[2048]{0:T(1024)} %param.46) | copy-start | bytes 24580
  285.0 21.9 %copy-start.37 = (f32[2048]{0:T(1024)S(1)}, f32[2048]{0:T(1024)}, u32[]{:S(2)}) copy-start(f32[2048]{0:T(1024)} %param.45) | copy-start | bytes 24580
  295.7 12.8 %collective-permute-start.10 = (f32[2,2048]{1,0:T(2,128)S(1)}, f32[2,2048]{1,0:T(2,128)S(1)}, u32[]{:S(2)}, u32[]{:S(2)}) collective-permute-start(f32[2,2048]{1,0:T(2,128)S(1)} %fusion.53), channel_id=1, source_target_pairs={{0,4},{4,8},{8,12},{1,5},{5,9},{9,13},{2,6},{6,10},{10,14},{3,7},{... | collective-permute-start | bytes 49160 | tf_op jit(solution)/shard_map/ppermute | solution.py:25
  337.6 24.5 %collective-permute-start.11 = (bf16[1024,512]{1,0:T(8,128)(2,1)}, bf16[1024,512]{1,0:T(8,128)(2,1)S(1)}, u32[]{:S(2)}, u32[]{:S(2)}) collective-permute-start(bf16[1024,512]{1,0:T(8,128)(2,1)} %get-tuple-element.219), channel_id=1, source_target_pairs={{0,2},{1,3},{2,0},{3,1},{4,6},{5,7},{6,4},{7,5},{8,10},{9,11},{10,... | collective-permute-start | bytes 3145736 | tf_op jit(solution)/shard_map/ppermute | solution.py:48
  339.2 37.7 %collective-permute-start.12 = (bf16[1024,512]{1,0:T(8,128)(2,1)}, bf16[1024,512]{1,0:T(8,128)(2,1)S(1)}, u32[]{:S(2)}, u32[]{:S(2)}) collective-permute-start(bf16[1024,512]{1,0:T(8,128)(2,1)} %get-tuple-element.219), channel_id=1, source_target_pairs={{0,1},{1,0},{2,3},{3,2},{4,5},{5,4},{6,7},{7,6},{8,9},{9,8},{10,11... | collective-permute-start | bytes 3145736 | tf_op jit(solution)/shard_map/ppermute | solution.py:48
  362.1 16.1 %collective-permute-start.13 = (bf16[1024,512]{1,0:T(8,128)(2,1)S(1)}, bf16[1024,512]{1,0:T(8,128)(2,1)S(1)}, u32[]{:S(2)}, u32[]{:S(2)}) collective-permute-start(bf16[1024,512]{1,0:T(8,128)(2,1)S(1)} %collective-permute-done.11), channel_id=1, source_target_pairs={{0,1},{1,0},{2,3},{3,2},{4,5},{5,4},{6,7},{7,6},{8,9},{9,8},{10,11... | collective-permute-start | bytes 3145736 | tf_op jit(solution)/shard_map/ppermute | solution.py:48
  443.7 3.0 collective-permute-start.15
  443.7 409.8 %reduce-scatter.6.cloned.1.call-start = ((), (), s32[]{:S(2)}) async-start(), calls=%async_computation.7 | async-start | bytes 10616832 | tf_op jit(solution)/shard_map/reduce_scatter | solution.py:899
  443.9 23.6 %collective-permute-start.14 = (bf16[1024,512]{1,0:T(8,128)(2,1)S(1)}, bf16[1024,512]{1,0:T(8,128)(2,1)}, u32[]{:S(2)}, u32[]{:S(2)}) collective-permute-start(bf16[1024,512]{1,0:T(8,128)(2,1)S(1)} %get-tuple-element.190), channel_id=1, source_target_pairs={{0,1},{1,0},{2,3},{3,2},{4,5},{5,4},{6,7},{7,6},{8,9},{9,8},{10,11... | collective-permute-start | bytes 3145736 | tf_op jit(solution)/shard_map/ppermute | solution.py:48
  446.7 18.7 %slice-start = ((s8[9437184]{0:T(1024)(128)(4,1)}), s8[4194304]{0:T(1024)(128)(4,1)S(1)}, s32[]{:S(2)}) async-start(s8[9437184]{0:T(1024)(128)(4,1)} %bitcast.185), calls=%async_computation.9 | async-start | bytes 8388608
  448.7 25.4 %collective-permute-start.16 = (bf16[1024,512]{1,0:T(8,128)(2,1)S(1)}, bf16[1024,512]{1,0:T(8,128)(2,1)}, u32[]{:S(2)}, u32[]{:S(2)}) collective-permute-start(bf16[1024,512]{1,0:T(8,128)(2,1)S(1)} %add_convert_fusion.7), channel_id=1, source_target_pairs={{0,2},{1,3},{2,0},{3,1},{4,6},{5,7},{6,4},{7,5},{8,10},{9,11},{10,... | collective-permute-start | bytes 3145736 | tf_op jit(solution)/shard_map/ppermute | solution.py:48
  450.2 15.2 %slice-start.1 = ((s8[9437184]{0:T(1024)(128)(4,1)}), s8[4194304]{0:T(1024)(128)(4,1)S(1)}, s32[]{:S(2)}) async-start(s8[9437184]{0:T(1024)(128)(4,1)} %bitcast.185), calls=%async_computation.10 | async-start | bytes 8388608
  450.2 15.2 %slice-start.2 = ((s8[9437184]{0:T(1024)(128)(4,1)}), s8[1048576]{0:T(1024)(128)(4,1)S(1)}, s32[]{:S(2)}) async-start(s8[9437184]{0:T(1024)(128)(4,1)} %bitcast.185), calls=%async_computation.11 | async-start | bytes 2097152
  479.3 6.7 collective-permute-start.17
  533.7 4.2 collective-permute-start.18
  538.9 12.5 %copy-start.14 = (bf16[1024,512]{1,0:T(8,128)(2,1)S(1)}, bf16[1024,512]{1,0:T(8,128)(2,1)}, u32[]{:S(2)}) copy-start(bf16[1024,512]{1,0:T(8,128)(2,1)} %copy-done.13) | copy-start | bytes 3145732
  538.9 12.5 %copy-start.47 = (bf16[1024,2048]{1,0:T(8,128)(2,1)S(1)}, bf16[1024,2048]{1,0:T(8,128)(2,1)}, u32[]{:S(2)}) copy-start(bf16[1024,2048]{1,0:T(8,128)(2,1)} %get-tuple-element.68) | copy-start | bytes 12582916
  538.9 47.8 %collective-permute-start.19 = (bf16[512,2048]{1,0:T(8,128)(2,1)S(1)}, bf16[512,2048]{1,0:T(8,128)(2,1)}, u32[]{:S(2)}, u32[]{:S(2)}) collective-permute-start(bf16[512,2048]{1,0:T(8,128)(2,1)S(1)} %add_convert_fusion.3), channel_id=1, source_target_pairs={{0,2},{1,3},{2,0},{3,1},{4,6},{5,7},{6,4},{7,5},{8,10},{9,11},{10,... | collective-permute-start | bytes 6291464 | tf_op jit(solution)/shard_map/ppermute | solution.py:48
  589.1 4.2 collective-permute-start.20
  597.0 350.8 %reduce-scatter.8.cloned.1.call-start = ((), (), s32[]{:S(2)}) async-start(), calls=%async_computation.8 | async-start | bytes 7077888 | tf_op jit(solution)/shard_map/reduce_scatter | solution.py:962
  640.7 59.5 %collective-permute-start.27 = (bf16[2,2,256,1024]{2,3,0,1:T(8,128)(2,1)}, bf16[2,2,256,1024]{2,3,0,1:T(8,128)(2,1)S(1)}, u32[]{:S(2)}, u32[]{:S(2)}) collective-permute-start(bf16[2,2,256,1024]{2,3,0,1:T(8,128)(2,1)} %bitcast.175), channel_id=1, source_target_pairs={{0,16},{16,0},{1,17},{17,1},{2,18},{18,2},{3,19},{19,3},{4,20},{20... | collective-permute-start | bytes 6291464 | tf_op jit(solution)/shard_map/ppermute | solution.py:101
  642.4 5.8 collective-permute-start.21
  643.7 6.7 collective-permute-start.22
  645.0 9.4 collective-permute-start.23
  650.4 12.9 %collective-permute-start.24 = (bf16[2,4,64,128]{3,2,1,0:T(8,128)(2,1)S(1)}, bf16[2,4,64,128]{3,2,1,0:T(8,128)(2,1)S(1)}, u32[]{:S(2)}, u32[]{:S(2)}) collective-permute-start(bf16[2,4,64,128]{3,2,1,0:T(8,128)(2,1)S(1)} %convert_element_type.347), channel_id=1, source_target_pairs={{12,0},{13,1},{14,2},{15,3},{28,16},{29,17},{30,18},{31,19}} | collective-permute-start | bytes 393224 | tf_op jit(solution)/shard_map/ppermute | solution.py:30
  651.7 20.9 %collective-permute-start.25 = (bf16[2,4,64,128]{3,2,1,0:T(8,128)(2,1)S(1)}, bf16[2,4,64,128]{3,2,1,0:T(8,128)(2,1)S(1)}, u32[]{:S(2)}, u32[]{:S(2)}) collective-permute-start(bf16[2,4,64,128]{3,2,1,0:T(8,128)(2,1)S(1)} %convert_element_type.347), channel_id=1, source_target_pairs={{8,0},{12,4},{9,1},{13,5},{10,2},{14,6},{11,3},{15,7},{24,16},{28,... | collective-permute-start | bytes 393224 | tf_op jit(solution)/shard_map/ppermute | solution.py:30
  653.0 19.6 %collective-permute-start.26 = (bf16[2,4,64,128]{3,2,1,0:T(8,128)(2,1)S(1)}, bf16[2,4,64,128]{3,2,1,0:T(8,128)(2,1)S(1)}, u32[]{:S(2)}, u32[]{:S(2)}) collective-permute-start(bf16[2,4,64,128]{3,2,1,0:T(8,128)(2,1)S(1)} %convert_element_type.347), channel_id=1, source_target_pairs={{4,0},{8,4},{12,8},{5,1},{9,5},{13,9},{6,2},{10,6},{14,10},{7,3},{... | collective-permute-start | bytes 393224 | tf_op jit(solution)/shard_map/ppermute | solution.py:30
  723.3 63.2 %collective-permute-start.28 = (bf16[2,256,1024]{1,2,0:T(8,128)(2,1)S(1)}, bf16[2,256,1024]{1,2,0:T(8,128)(2,1)}, u32[]{:S(2)}, u32[]{:S(2)}) collective-permute-start(bf16[2,256,1024]{1,2,0:T(8,128)(2,1)S(1)} %dynamic-slice_bitcast_fusion), channel_id=1, source_target_pairs={{0,4},{4,0},{8,12},{12,8},{1,5},{5,1},{9,13},{13,9},{2,6},{6,2},{1... | collective-permute-start | bytes 3145736 | tf_op jit(solution)/shard_map/ppermute | solution.py:101
  799.8 8.2 collective-permute-start.29
  801.2 51.4 %collective-permute-start.30 = (bf16[256,1024]{0,1:T(8,128)(2,1)S(1)}, bf16[256,1024]{0,1:T(8,128)(2,1)S(1)}, u32[]{:S(2)}, u32[]{:S(2)}) collective-permute-start(bf16[256,1024]{0,1:T(8,128)(2,1)S(1)} %dynamic-slice_bitcast_fusion.1), channel_id=1, source_target_pairs={{0,8},{4,12},{8,0},{12,4},{1,9},{5,13},{9,1},{13,5},{2,10},{6,14},... | collective-permute-start | bytes 1572872 | tf_op jit(solution)/shard_map/ppermute | solution.py:101
  855.4 4.2 collective-permute-start.31
  860.6 48.7 %copy-start.21 = (f32[8,2048]{1,0:T(8,128)S(1)}, f32[8,2048]{1,0:T(8,128)}, u32[]{:S(2)}) copy-start(f32[8,2048]{1,0:T(8,128)} %get-tuple-element.98) | copy-start | bytes 196612
  860.6 78.8 %copy-start.18 = (bf16[1792,256]{1,0:T(8,128)(2,1)S(1)}, bf16[1792,256]{1,0:T(8,128)(2,1)}, u32[]{:S(2)}) copy-start(bf16[1792,256]{1,0:T(8,128)(2,1)} %reduce-scatter.4.cloned.1.call-done) | copy-start | bytes 2752516
  860.6 47.7 %collective-permute-start.32 = (bf16[512,2048]{1,0:T(8,128)(2,1)S(1)}, bf16[512,2048]{1,0:T(8,128)(2,1)S(1)}, u32[]{:S(2)}, u32[]{:S(2)}) collective-permute-start(bf16[512,2048]{1,0:T(8,128)(2,1)S(1)} %add_convert_fusion.1), channel_id=1, source_target_pairs={{0,2},{1,3},{2,0},{3,1},{4,6},{5,7},{6,4},{7,5},{8,10},{9,11},{10,... | collective-permute-start | bytes 6291464 | tf_op jit(solution)/shard_map/ppermute | solution.py:48
  909.2 60.9 %collective-permute-start.33 = (bf16[512,2048]{1,0:T(8,128)(2,1)S(1)}, bf16[512,2048]{1,0:T(8,128)(2,1)}, u32[]{:S(2)}, u32[]{:S(2)}) collective-permute-start(bf16[512,2048]{1,0:T(8,128)(2,1)S(1)} %add_convert_fusion), channel_id=1, source_target_pairs={{0,1},{1,0},{2,3},{3,2},{4,5},{5,4},{6,7},{7,6},{8,9},{9,8},{10,11... | collective-permute-start | bytes 6291464 | tf_op jit(solution)/shard_map/ppermute | solution.py:48
  909.4 4.3 collective-permute-start.34
  913.7 5.6 collective-permute-start.35
  919.3 5.0 collective-permute-start.36
  924.4 14.4 %collective-permute-start.37 = (f32[14,2048]{1,0:T(8,128)S(1)}, f32[14,2048]{1,0:T(8,128)S(1)}, u32[]{:S(2)}, u32[]{:S(2)}) collective-permute-start(f32[14,2048]{1,0:T(8,128)S(1)} %add.268), channel_id=1, source_target_pairs={{0,4},{4,0},{8,12},{12,8},{1,5},{5,1},{9,13},{13,9},{2,6},{6,2},{1... | collective-permute-start | bytes 344072 | tf_op jit(solution)/shard_map/ppermute | solution.py:125
  938.8 8.4 collective-permute-start.38
  947.8 12.4 %copy-start.1 = (bf16[256,2304]{0,1:T(8,128)(2,1)S(1)}, bf16[256,2304]{0,1:T(8,128)(2,1)}, u32[]{:S(2)}) copy-start(bf16[256,2304]{0,1:T(8,128)(2,1)} %reduce-scatter.6.cloned.1.call-done) | copy-start | bytes 3538948
  (34 other events, 188.5 us)
Sparse Core Ops, SparseCore 0:
  13.6 153.5 all-gather.3
  169.9 146.5 all-gather.5
  318.5 110.6 all-gather.7
  443.8 131.6 reduce-scatter.3
  597.1 193.7 reduce-scatter.5
  795.0 145.9 reduce-scatter.7

commit v4 on v3

--- a/solution.py
+++ b/solution.py
@@ -851,8 +851,10 @@
     d_chan_full = tp_gather(d_chan)
     key_pre = matmul(key_in, w_chankey)
     hidden = jnp.square(jax.nn.relu(key_pre)).astype(jnp.bfloat16)
-    grad_chanvalue = matmul_tn(hidden, d_chan_full).astype(jnp.bfloat16)
-    g_chanvalue = lax.psum_scatter(grad_chanvalue, owners, scatter_dimension=1, tiled=True)
+    grad_chanvalue = matmul_tn(d_chan_full, hidden).astype(jnp.bfloat16)
+    steps_f, steps_c = len(axis_bits("fsdp")), len(axis_bits("ctx"))
+    value_steps = owner_scatter_steps(grad_chanvalue)
+    g_chanvalue = next(value_steps)
     hidden, grad_chanvalue = after(hidden, grad_chanvalue)
     chan_sum = tp_scatter(matmul_nt(hidden, w_chanvalue_t).astype(jnp.bfloat16)).astype(jnp.float32)
     middle_q = lax.dynamic_slice_in_dim(x_low, sharded_layout, fourth_extent, 1).astype(
@@ -866,6 +868,9 @@
     d_rec_pre = (d_result * chan_sum * rec_gate * (1.0 - rec_gate)).astype(jnp.bfloat16)
     d_hidden = matmul(d_chan_full, w_chanvalue_t)
     d_key_pre = (d_hidden * 2.0 * jax.nn.relu(key_pre)).astype(jnp.bfloat16)
+    d_key_pre, g_chanvalue = after(d_key_pre, g_chanvalue)
+    for _ in range(steps_f + steps_c - 2):
+        g_chanvalue = value_steps.send(g_chanvalue)
     full_shape = (seqs_here, piece_len, embedding_extent)
     own_mask = (jnp.arange(embedding_extent) // fourth_extent == lax.axis_index("tp")).astype(
         jnp.float32
@@ -894,8 +899,10 @@
             axis=1,
         )
 
+    d_middle_part, g_chanvalue = after(d_middle_part, g_chanvalue)
+    g_chanvalue = value_steps.send(g_chanvalue)
     d_mixed, grads_chan = tp_sum(d_middle_part, chan_grads)
-    d_mixed, grads_chan, g_chanvalue = after(d_mixed, grads_chan, g_chanvalue)
+    d_mixed, grads_chan = after(d_mixed, grads_chan)
     g_chan = lax.psum_scatter(grads_chan, owners, scatter_dimension=0, tiled=True)
     grad_output_t = matmul_tn(d_mixed, joined_low).astype(jnp.bfloat16)
     d_joined = matmul(d_mixed, w_output_t)
@@ -944,9 +951,8 @@
         name="mix_back",
         flops=6 * square,
     )
-    early_steps = len(axis_bits("fsdp")) + len(axis_bits("ctx"))
     d_recept, d_key, d_value, g_early = after(d_recept, d_key, d_value, g_early)
-    for _ in range(early_steps - 2):
+    for _ in range(steps_f + steps_c - 2):
         g_early = early.send(g_early)
     d_lows = [d_recept, d_key, d_value, d_gate_pre]
     weights_time = (w_recept, w_key, w_value, w_gate)
@@ -957,8 +963,7 @@
         ],
         axis=1,
     )
-    *d_lows, _, g_early = after(d_lows[0], *d_lows[1:], grads_time, g_early)
-    g_early = early.send(g_early)
+    *d_lows, _ = after(d_lows[0], *d_lows[1:], grads_time)
     g_time = lax.psum_scatter(grads_time, owners, scatter_dimension=0, tiled=True)
     d_input_part, time_small = blend_back(
         (x_low,),
@@ -974,14 +979,17 @@
         "blend_one_back",
     )
     d_input_part, g_early, g_chan = after(d_input_part, g_early, g_chan)
+    g_early = early.send(g_early)
     head_small = jnp.concatenate([state_small[:2], group_small[:2]])
     head_small = lax.dynamic_update_slice_in_dim(
         jnp.zeros((4, embedding_extent), jnp.float32), head_small, sharded_layout, 1
     )
-    small_sum = whole_sum(
-        jnp.concatenate([time_small[:6], head_small, chan_small[:4]], axis=0),
-        ("tp", "fsdp", "ctx"),
-    )
+    small_part = jnp.concatenate([time_small[:6], head_small, chan_small[:4]], axis=0)
+
+    def small_total(token):
+        return whole_sum(after(small_part, token)[0], ("tp", "fsdp", "ctx"))
+
+    d_input_sum, small_sum = tp_sum(d_input_part, small_total)
     owned = embedding_extent // (lax.axis_size("fsdp") * lax.axis_size("ctx"))
     small_owned = lax.dynamic_slice_in_dim(
         small_sum,
@@ -989,11 +997,10 @@
         owned,
         1,
     )
-    d_input_sum = tp_sum(d_input_part)
     grad_inputs = (d_mixed.astype(jnp.float32) + d_input_sum.astype(jnp.float32)).reshape(
         full_shape
     )
-    g_chanvalue = g_chanvalue.astype(jnp.float32)
+    g_chanvalue = g_chanvalue.astype(jnp.float32).T
     g_chan = g_chan.astype(jnp.float32)
     g_time = g_time.astype(jnp.float32)
     g_early = g_early.astype(jnp.float32)

time: 992 us -> 1110 us (1.12)
  waiting for transfers between devices: 433 us -> 541 us
  local copies, waits for them, and re-layouts: 77 us -> 91.6 us
    ppermute x4, waiting for transfers between devices: 4.05 us -> 84.4 us  [shifted(): return lax.ppermute(x, axis, pairs)]
    ppermute x5, waiting for transfers between devices: 30.2 us -> 98 us  [whole_sum(): x = x + lax.ppermute(x, axis, [(i, i ^ bit) for i in range(count)])]
    ppermute x15, waiting for transfers between devices: 165 us -> 118 us  [partner(): return lax.ppermute(x, 'tp', [(i, i ^ bit) for i in range(count)])]
    convert_element_type x10 -> x11, other arithmetic: 18.8 us -> 27.9 us  [add_low(): (left.astype(jnp.float32) + right.astype(jnp.float32)).astype(jnp.bfloat16)]
    unnamed x123 -> x132, local copies, waits for them, and re-layouts: 27.7 us -> 32.1 us
    ppermute x3 -> x6, waiting for transfers between devices: 63.9 us -> 62.4 us  [swap(): lax.ppermute(x, axis, [(i, i ^ bit) for i in range(lax.axis_size(axis))])]
  transfers between devices with their start and end apart: 45 -> 47, of which waited for: 27 -> 26; matrix products, arithmetic and copies ran while one was open for 26% -> 23% of each run, Pallas kernels for 18% -> 16%
where the time goes in v4:
time: 1110 us
  waiting for transfers between devices  541 us (49%)
  Pallas kernels  178 us (16%)
  matrix products  128 us (12%)
  local copies, waits for them, and re-layouts  91.6 us (8%)
  other arithmetic  87.8 us (8%)
  starting transfers between devices  64.6 us (6%)
  between operations  15.2 us (1%)
    ppermute x15, waiting for transfers between devices, partner(): return lax.ppermute(x, 'tp', [(i, i ^ bit) for i in range(count)])  118 us
    all_gather x1, waiting for transfers between devices, per_device(): lax.all_gather(jnp.concatenate([acceptor_matrix, lookup_matrix, payload_m...  107 us
    ppermute x5, waiting for transfers between devices, whole_sum(): x = x + lax.ppermute(x, axis, [(i, i ^ bit) for i in range(count)])  98 us
    pallas_call x2, Pallas kernels, blend_back(): pl.pallas_call(partial(blend_back_kernel, len(xs), mixes, per_seq, int(ow...  88.9 us
    ppermute x4, waiting for transfers between devices, shifted(): return lax.ppermute(x, axis, pairs)  84.4 us
    dot_general x8, matrix products, matmul(): return jnp.dot(left, right, preferred_element_type=jnp.float32)  63.8 us
    ppermute x6, waiting for transfers between devices, swap(): lax.ppermute(x, axis, [(i, i ^ bit) for i in range(lax.axis_size(axis))])  62.4 us
    pallas_call x4, Pallas kernels, pair_call(): pl.pallas_call(kernel, grid=(pairs, seqs), in_specs=[specs[kind] for kind...  49.5 us
  transfers between devices with their start and end apart: 47, of which 26 were waited for; matrix products, arithmetic and copies ran while one was open for 23% of the time, Pallas kernels for 16%

profile of v4, /device:TPU:0, one launch (start us, length us, event | category | flops | bytes accessed | tf_op | source)
XLA Modules:
  0.0 1107.3 jit_solution(12946348970530440987)
XLA Ops:
  17.3 7.0 collective-permute-start.3
  39.0 20.9 %blend_one.1 = (bf16[1024,2048]{1,0:T(8,128)(2,1)}, bf16[1024,2048]{1,0:T(8,128)(2,1)}, bf16[1024,2048]{1,0:T(8,128)(2,1)}, bf16[1024,2048]{1,0:T(8,128)(2,1)}) custom-call(bf16[1024,2048]{1,0:T(8,128)(2,1)} %bitcast.194, f32[1024,1]{1,0:T(8,128)} %bitcast.204, f32[2,1,2048]{2,1,0:T(1,128)} %broadcast_in_dim.20.refs_2_.refs_11_, ...), custom_call_target="tpu_custom_call" | custom-call | flops 41943040 | bytes 20971520 | tf_op jit(solution)/shard_map/blend_one/pallas_call | solution.py:504
  59.9 107.4 %all-gather.4.cloned.1.call-done.refs_6_.refs_7_.refs_8_.refs_9_ = bf16[2048,2560]{1,0:T(8,128)(2,1)} async-done(((bf16[256,2560]{1,0:T(8,128)(2,1)}), bf16[2048,2560]{1,0:T(8,128)(2,1)}) %all-gather.4.cloned.1.call-update) | async-done | bytes 10485776 | tf_op jit(solution)/shard_map/all_gather | solution.py:756
  167.2 6.3 fusion.42.k_ref
  173.5 4.9 fusion.45.v_ref
  178.5 6.9 carry.1
  188.1 4.2 collective-permute-start.5
  193.9 6.4 fusion.39.r_ref
  200.3 5.2 fusion.27.gate_ref
  206.3 11.3 %mix.1 = (bf16[1024,512]{1,0:T(8,128)(2,1)}, f32[1024,512]{1,0:T(8,128)}) custom-call(bf16[1024,512]{1,0:T(8,128)(2,1)} %fusion.39.r_ref, bf16[1024,512]{1,0:T(8,128)(2,1)} %fusion.42.k_ref, bf16[1024,512]{1,0:T(8,128)(2,1)} %fusion.45.v_ref, f32[1024,512]{1,0:T(8,128)} %fusion.27.gate_ref, f32[1,512]{1,0:T(1,128)} %bitcast.227, ...), custom_call_target="tpu_custom_call" | custom-call | flops 1073741824 | bytes 11087872 | tf_op jit(solution)/shard_map/mix/pallas_call | solution.py:403
  217.6 4.3 convolution_convert_fusion.3
  224.3 4.3 collective-permute-done.7
  228.5 3.0 add_convert_fusion.5
  233.2 46.2 %collective-permute-done.8 = bf16[512,2048]{1,0:T(8,128)(2,1)} collective-permute-done((bf16[512,2048]{1,0:T(8,128)(2,1)S(1)}, bf16[512,2048]{1,0:T(8,128)(2,1)}, u32[]{:S(2)}, u32[]{:S(2)}) %collective-permute-start.8) | collective-permute-done | bytes 2097184 | tf_op jit(solution)/shard_map/ppermute | solution.py:48
  279.4 3.7 add_convert_fusion.4
  283.1 4.3 collective-permute-done.9
  287.4 3.8 maximum_select_fusion.refs_1_.refs_3_
  293.8 13.1 %collective-permute-start.10 = (f32[2,2048]{1,0:T(2,128)S(1)}, f32[2,2048]{1,0:T(2,128)S(1)}, u32[]{:S(2)}, u32[]{:S(2)}) collective-permute-start(f32[2,2048]{1,0:T(2,128)S(1)} %fusion.57), channel_id=1, source_target_pairs={{0,4},{4,8},{8,12},{1,5},{5,9},{9,13},{2,6},{6,10},{10,14},{3,7},{... | collective-permute-start | bytes 49160 | tf_op jit(solution)/shard_map/ppermute | solution.py:25
  308.7 19.1 %blend_two.1 = (bf16[1024,2048]{1,0:T(8,128)(2,1)}, bf16[1024,2048]{1,0:T(8,128)(2,1)}) custom-call(bf16[1024,2048]{1,0:T(8,128)(2,1)} %bitcast.195, bf16[1024,2048]{1,0:T(8,128)(2,1)} %copy-done, f32[1024,1]{1,0:T(8,128)} %bitcast.205, f32[2,1,2048]{2,1,0:T(1,128)} %copy.103.refs_3_.refs_9_, f32[2,2048]{1,0:T(2,128)} %get-tuple-element.233.refs_4_.refs_11_, ...), custom_call_target="tpu_custom_call" | custom-call | flops 41943040 | bytes 16777216 | tf_op jit(solution)/shard_map/blend_two/pallas_call | solution.py:504
  330.4 6.8 constant_dynamic-update-slice_fusion.8
  338.8 23.0 %collective-permute-done.11 = bf16[1024,512]{1,0:T(8,128)(2,1)S(1)} collective-permute-done((bf16[1024,512]{1,0:T(8,128)(2,1)}, bf16[1024,512]{1,0:T(8,128)(2,1)S(1)}, u32[]{:S(2)}, u32[]{:S(2)}) %collective-permute-start.11) | collective-permute-done | bytes 1048608 | tf_op jit(solution)/shard_map/ppermute | solution.py:48
  361.9 13.6 %multiply_convert_fusion.1 = (bf16[1024,1792]{1,0:T(8,128)(2,1)S(1)}, f32[1024,1792]{1,0:T(8,128)}) fusion(bf16[1024,2048]{1,0:T(8,128)(2,1)} %get-tuple-element.73, bf16[2048,2304]{1,0:T(8,128)(2,1)} %all-gather.6.cloned.1.call-done.refs_6_), kind=kOutput, calls=%fused_computation.7 | convolution fusion | flops 7521697792 | bytes 22544384 | tf_op jit(solution)/shard_map/dot_general | solution.py:162
  379.1 11.5 %convolution_convert_fusion.1 = bf16[2048,1792]{1,0:T(8,128)(2,1)} fusion(bf16[1024,2048]{1,0:T(8,128)(2,1)} %constant_dynamic-update-slice_fusion.5, bf16[1024,1792]{1,0:T(8,128)(2,1)S(1)} %get-tuple-element.74), kind=kOutput, calls=%fused_computation.3 | convolution fusion | flops 7519862784 | bytes 15204352 | tf_op jit(solution)/shard_map/dot_general | solution.py:166
  390.6 38.6 %all-gather.8.cloned.1.call-done = bf16[2048,1792]{0,1:T(8,128)(2,1)} async-done(((bf16[256,1792]{0,1:T(8,128)(2,1)}), bf16[2048,1792]{0,1:T(8,128)(2,1)}) %all-gather.8.cloned.1.call-update) | async-done | bytes 7340048 | tf_op jit(solution)/shard_map/all_gather | solution.py:776
  429.2 11.4 %convolution_convert_fusion.2 = bf16[1024,2048]{1,0:T(8,128)(2,1)S(1)} fusion(bf16[1024,1792]{1,0:T(8,128)(2,1)} %copy-done.53, bf16[2048,1792]{0,1:T(8,128)(2,1)} %all-gather.8.cloned.1.call-done), kind=kOutput, calls=%fused_computation.25 | convolution fusion | flops 7518289920 | bytes 15204352 | tf_op jit(solution)/shard_map/dot_general | solution.py:172
  443.8 3.5 constant_dynamic-slice_fusion.7
  447.3 6.0 copy.105
  459.4 14.1 %multiply_convert_fusion.refs_4_ = bf16[1024,1792]{1,0:T(8,128)(2,1)} fusion(f32[1024,1792]{1,0:T(8,128)} %get-tuple-element.227, bf16[1024,2048]{1,0:T(8,128)(2,1)} %constant_dynamic-update-slice_fusion.5, bf16[2048,1792]{0,1:T(8,128)(2,1)} %all-gather.8.cloned.1.call-done), kind=kOutput, calls=%fused_computation.6 | convolution fusion | flops 7523532800 | bytes 22544384 | tf_op jit(solution)/shard_map/dot_general | solution.py:162
  473.5 5.9 copy.126
  479.4 4.2 collective-permute-done.16
  483.6 5.1 fusion.21
  488.7 46.6 %collective-permute-done.17 = bf16[2,2,256,1792]{2,3,0,1:T(8,128)(2,1)} collective-permute-done((bf16[2,2,256,1792]{2,3,0,1:T(8,128)(2,1)}, bf16[2,2,256,1792]{2,3,0,1:T(8,128)(2,1)}, u32[]{:S(2)}, u32[]{:S(2)}) %collective-permute-start.17) | collective-permute-done | bytes 3670048 | tf_op jit(solution)/shard_map/ppermute | solution.py:101
  545.2 3.1 slice.184.refs_7_
  548.3 34.4 %collective-permute-done.18 = f32[2,2048]{1,0:T(2,128)S(1)} collective-permute-done((f32[2,2048]{1,0:T(2,128)S(1)}, f32[2,2048]{1,0:T(2,128)S(1)}, u32[]{:S(2)}, u32[]{:S(2)}) %collective-permute-start.18) | collective-permute-done | bytes 16416 | tf_op jit(solution)/shard_map/ppermute | solution.py:25
  583.4 44.8 %blend_two_back.1 = (bf16[1024,2048]{1,0:T(8,128)(2,1)}, f32[8,2048]{1,0:T(8,128)}) custom-call(bf16[1024,2048]{1,0:T(8,128)(2,1)} %bitcast.197, bf16[1024,2048]{1,0:T(8,128)(2,1)} %copy-done, bf16[1024,2048]{1,0:T(8,128)(2,1)} %bitcast.198, bf16[1024,2048]{1,0:T(8,128)(2,1)} %copy-done, bf16[1024,1792]{1,0:T(8,128)(2,1)} %multiply_convert_fusion.refs_4_, ...), custom_call_target="tpu_custom_call" | custom-call | flops 9663676416 | bytes 16777216 | tf_op jit(solution)/shard_map/blend_two_back/pallas_call | solution.py:664
  628.3 3.4 fusion.6
  631.8 4.1 collective-permute-done.20
  638.5 8.3 convolution_convert_fusion
  649.4 11.5 %pad_maximum_fusion = bf16[2048,2304]{0,1:T(8,128)(2,1)} fusion(bf16[2048,512]{0,1:T(8,128)(2,1)S(1)} %convolution_convert_fusion.9, bf16[2048,1792]{0,1:T(8,128)(2,1)S(1)} %convolution_convert_fusion), kind=kLoop, calls=%fused_computation | loop fusion | flops 18874368 | bytes 18874368 | tf_op jit(solution)/shard_map/concatenate | solution.py:894
  660.9 23.9 %collective-permute-done.21 = bf16[512,2048]{1,0:T(8,128)(2,1)} collective-permute-done((bf16[512,2048]{1,0:T(8,128)(2,1)S(1)}, bf16[512,2048]{1,0:T(8,128)(2,1)}, u32[]{:S(2)}, u32[]{:S(2)}) %collective-permute-start.21) | collective-permute-done | bytes 2097184 | tf_op jit(solution)/shard_map/ppermute | solution.py:48
  687.2 4.1 collective-permute-done.22
  691.4 3.7 maximum_select_fusion.1
  695.2 6.5 fusion.23.dj_ref
  701.7 11.3 %gate_back.1 = (bf16[1024,512]{1,0:T(8,128)(2,1)}, bf16[1024,512]{1,0:T(8,128)(2,1)}, f32[2,4,64,128]{3,2,1,0:T(8,128)}, f32[8,512]{1,0:T(8,128)}) custom-call(f32[1024,512]{1,0:T(8,128)} %fusion.23.dj_ref, f32[1024,512]{1,0:T(8,128)} %get-tuple-element.83.attend_ref, f32[1024,512]{1,0:T(8,128)} %fusion.27.gate_ref, bf16[1024,512]{1,0:T(8,128)(2,1)} %fusion.39.r_ref, ...), custom_call_target="tpu_custom_call" | custom-call | flops 67108864 | bytes 14749696 | tf_op jit(solution)/shard_map/gate_back/pallas_call | solution.py:403
  713.0 4.7 convolution_convert_fusion.8
  722.9 7.9 reshape.228
  730.8 5.1 constant_dynamic-slice_fusion.4
  742.9 2.9 collective-permute-done.24
  750.4 10.0 collective-permute-done.28
  760.3 18.5 %collective-permute-done.27 = bf16[2,4,64,128]{3,2,1,0:T(8,128)(2,1)S(1)} collective-permute-done((bf16[2,4,64,128]{3,2,1,0:T(8,128)(2,1)S(1)}, bf16[2,4,64,128]{3,2,1,0:T(8,128)(2,1)S(1)}, u32[]{:S(2)}, u32[]{:S(2)}) %collective-permute-start.27) | collective-permute-done | bytes 131104 | tf_op jit(solution)/shard_map/ppermute | solution.py:30
  779.6 20.0 %mix_back.1 = (bf16[1024,512]{1,0:T(8,128)(2,1)}, bf16[1024,512]{1,0:T(8,128)(2,1)}, bf16[1024,512]{1,0:T(8,128)(2,1)}, f32[8,512]{1,0:T(8,128)}) custom-call(bf16[1024,512]{1,0:T(8,128)(2,1)} %fusion.39.r_ref, bf16[1024,512]{1,0:T(8,128)(2,1)} %fusion.42.k_ref, bf16[1024,512]{1,0:T(8,128)(2,1)} %fusion.45.v_ref, ...), custom_call_target="tpu_custom_call" | custom-call | flops 3221225472 | bytes 9523200 | tf_op jit(solution)/shard_map/mix_back/pallas_call | solution.py:403
  799.6 3.6 fusion.5
  810.9 11.2 %pad_maximum_fusion.1 = bf16[2048,1536]{0,1:T(8,128)(2,1)} fusion(bf16[2048,512]{0,1:T(8,128)(2,1)S(1)} %convolution_convert_fusion.4, bf16[2048,512]{0,1:T(8,128)(2,1)S(1)} %convolution_convert_fusion.5, bf16[2048,512]{0,1:T(8,128)(2,1)S(1)} %convolution_convert_fusion.6), kind=kLoop, calls=%fused_computation.12 | loop fusion | flops 18874368 | bytes 12582912 | tf_op jit(solution)/shard_map/concatenate | solution.py:959
  825.1 4.1 collective-permute-start.31
  839.6 49.4 %collective-permute-done.30 = f32[2,2048]{1,0:T(2,128)S(1)} collective-permute-done((f32[2,2048]{1,0:T(2,128)S(1)}, f32[2,2048]{1,0:T(2,128)S(1)}, u32[]{:S(2)}, u32[]{:S(2)}) %collective-permute-start.30) | collective-permute-done | bytes 16416 | tf_op jit(solution)/shard_map/ppermute | solution.py:25
  889.6 44.1 %blend_one_back.1 = (bf16[1024,2048]{1,0:T(8,128)(2,1)}, f32[8,2048]{1,0:T(8,128)}) custom-call(bf16[1024,2048]{1,0:T(8,128)(2,1)} %bitcast.199, bf16[1024,2048]{1,0:T(8,128)(2,1)} %bitcast.200, bf16[1024,512]{1,0:T(8,128)(2,1)} %get-tuple-element.93.refs_2_, bf16[1024,512]{1,0:T(8,128)(2,1)} %get-tuple-element.94.refs_3_, ...), custom_call_target="tpu_custom_call" | custom-call | flops 8589934592 | bytes 16777216 | tf_op jit(solution)/shard_map/blend_one_back/pallas_call | solution.py:664
  937.5 4.1 collective-permute-done.32
  947.8 45.4 %collective-permute-done.34 = f32[14,2048]{1,0:T(8,128)S(1)} collective-permute-done((f32[14,2048]{1,0:T(8,128)S(1)}, f32[14,2048]{1,0:T(8,128)S(1)}, u32[]{:S(2)}, u32[]{:S(2)}) %collective-permute-start.34) | collective-permute-done | bytes 114720 | tf_op jit(solution)/shard_map/ppermute | solution.py:125
  993.3 5.5 collective-permute-done.35
  1000.3 12.8 %collective-permute-done.36 = f32[14,2048]{1,0:T(8,128)S(1)} collective-permute-done((f32[14,2048]{1,0:T(8,128)S(1)}, f32[14,2048]{1,0:T(8,128)S(1)}, u32[]{:S(2)}, u32[]{:S(2)}) %collective-permute-start.36) | collective-permute-done | bytes 114720 | tf_op jit(solution)/shard_map/ppermute | solution.py:125
  1018.3 33.0 %collective-permute-done.37 = f32[14,2048]{1,0:T(8,128)S(1)} collective-permute-done((f32[14,2048]{1,0:T(8,128)S(1)}, f32[14,2048]{1,0:T(8,128)S(1)}, u32[]{:S(2)}, u32[]{:S(2)}) %collective-permute-start.37) | collective-permute-done | bytes 114720 | tf_op jit(solution)/shard_map/ppermute | solution.py:125
  1051.3 3.0 add_convert_fusion
  1055.3 15.8 %collective-permute-done.41 = bf16[256,1792]{0,1:T(8,128)(2,1)} collective-permute-done((bf16[256,1792]{0,1:T(8,128)(2,1)}, bf16[256,1792]{0,1:T(8,128)(2,1)}, u32[]{:S(2)}, u32[]{:S(2)}) %collective-permute-start.41) | collective-permute-done | bytes 917536 | tf_op jit(solution)/shard_map/ppermute | solution.py:101
  1093.1 7.5 convert_add_fusion
  (314 shorter events, 151.6 us)
Async XLA Ops:
  7.2 24.2 %copy-start.37 = (f32[2048]{0:T(1024)S(1)}, f32[2048]{0:T(1024)}, u32[]{:S(2)}) copy-start(f32[2048]{0:T(1024)} %param.36) | copy-start | bytes 24580
  7.2 24.2 %copy-start.38 = (f32[2048]{0:T(1024)S(1)}, f32[2048]{0:T(1024)}, u32[]{:S(2)}) copy-start(f32[2048]{0:T(1024)} %param.35) | copy-start | bytes 24580
  7.2 24.8 %copy-start.28 = (f32[2048]{0:T(1024)S(1)}, f32[2048]{0:T(1024)}, u32[]{:S(2)}) copy-start(f32[2048]{0:T(1024)} %param.37) | copy-start | bytes 24580
  7.3 24.8 %copy-start.30 = (f32[2048]{0:T(1024)S(1)}, f32[2048]{0:T(1024)}, u32[]{:S(2)}) copy-start(f32[2048]{0:T(1024)} %param.38) | copy-start | bytes 24580
  7.3 24.8 %copy-start.32 = (f32[2048]{0:T(1024)S(1)}, f32[2048]{0:T(1024)}, u32[]{:S(2)}) copy-start(f32[2048]{0:T(1024)} %param.39) | copy-start | bytes 24580
  7.3 24.7 %copy-start.34 = (f32[2048]{0:T(1024)S(1)}, f32[2048]{0:T(1024)}, u32[]{:S(2)}) copy-start(f32[2048]{0:T(1024)} %param.40) | copy-start | bytes 24580
  7.3 159.9 %all-gather.4.cloned.1.call-start = ((), (), s32[]{:S(2)}) async-start(), calls=%async_computation.2 | async-start | bytes 11796480 | tf_op jit(solution)/shard_map/all_gather | solution.py:756
  13.5 314.3 %all-gather.6.cloned.1.call-start = ((), (), s32[]{:S(2)}) async-start(), calls=%async_computation.3 | async-start | bytes 10616832 | tf_op jit(solution)/shard_map/all_gather | solution.py:764
  14.7 414.5 %all-gather.8.cloned.1.call-start = ((), (), s32[]{:S(2)}) async-start(), calls=%async_computation.4 | async-start | bytes 8257536 | tf_op jit(solution)/shard_map/all_gather | solution.py:776
  17.3 156.2 %copy-start.41 = (bf16[2,4,1,128]{3,2,1,0:T(2,128)(2,1)}, bf16[2,4,1,128]{3,2,1,0:T(2,128)(2,1)S(1)}, u32[]{:S(2)}) copy-start(bf16[2,4,1,128]{3,2,1,0:T(2,128)(2,1)S(1)} %get-tuple-element.184) | copy-start | bytes 6148
  17.3 21.0 %collective-permute-start.3 = (bf16[2,4,1,128]{3,2,1,0:T(2,128)(2,1)S(1)}, bf16[2,4,1,128]{3,2,1,0:T(2,128)(2,1)S(1)}, u32[]{:S(2)}, u32[]{:S(2)}) collective-permute-start(bf16[2,4,1,128]{3,2,1,0:T(2,128)(2,1)S(1)} %get-tuple-element.184), channel_id=1, source_target_pairs={{0,12},{1,13},{2,14},{3,15},{16,28},{17,29},{18,30},{19,31}} | collective-permute-start | bytes 6152 | tf_op jit(solution)/shard_map/ppermute | solution.py:30
  24.3 14.1 %collective-permute-start.2 = (bf16[2,4,1,128]{3,2,1,0:T(2,128)(2,1)S(1)}, bf16[2,4,1,128]{3,2,1,0:T(2,128)(2,1)S(1)}, u32[]{:S(2)}, u32[]{:S(2)}) collective-permute-start(bf16[2,4,1,128]{3,2,1,0:T(2,128)(2,1)S(1)} %get-tuple-element.184), channel_id=1, source_target_pairs={{0,8},{4,12},{1,9},{5,13},{2,10},{6,14},{3,11},{7,15},{16,24},{20,... | collective-permute-start | bytes 6152 | tf_op jit(solution)/shard_map/ppermute | solution.py:30
  25.6 12.8 %collective-permute-start.1 = (bf16[2,4,1,128]{3,2,1,0:T(2,128)(2,1)S(1)}, bf16[2,4,1,128]{3,2,1,0:T(2,128)(2,1)S(1)}, u32[]{:S(2)}, u32[]{:S(2)}) collective-permute-start(bf16[2,4,1,128]{3,2,1,0:T(2,128)(2,1)S(1)} %get-tuple-element.184), channel_id=1, source_target_pairs={{0,4},{4,8},{8,12},{1,5},{5,9},{9,13},{2,6},{6,10},{10,14},{3,7},{... | collective-permute-start | bytes 6152 | tf_op jit(solution)/shard_map/ppermute | solution.py:30
  29.3 9.0 collective-permute-start
  186.3 19.2 %collective-permute-start.6 = (bf16[2,4,64,128]{3,2,1,0:T(8,128)(2,1)S(1)}, bf16[2,4,64,128]{3,2,1,0:T(8,128)(2,1)S(1)}, u32[]{:S(2)}, u32[]{:S(2)}) collective-permute-start(bf16[2,4,64,128]{3,2,1,0:T(8,128)(2,1)S(1)} %convert_element_type.338), channel_id=1, source_target_pairs={{0,4},{4,8},{8,12},{1,5},{5,9},{9,13},{2,6},{6,10},{10,14},{3,7},{... | collective-permute-start | bytes 393224 | tf_op jit(solution)/shard_map/ppermute | solution.py:30
  188.1 17.5 %collective-permute-start.5 = (bf16[2,4,64,128]{3,2,1,0:T(8,128)(2,1)S(1)}, bf16[2,4,64,128]{3,2,1,0:T(8,128)(2,1)S(1)}, u32[]{:S(2)}, u32[]{:S(2)}) collective-permute-start(bf16[2,4,64,128]{3,2,1,0:T(8,128)(2,1)S(1)} %convert_element_type.338), channel_id=1, source_target_pairs={{0,8},{4,12},{1,9},{5,13},{2,10},{6,14},{3,11},{7,15},{16,24},{20,... | collective-permute-start | bytes 393224 | tf_op jit(solution)/shard_map/ppermute | solution.py:30
  192.3 13.2 %collective-permute-start.4 = (bf16[2,4,64,128]{3,2,1,0:T(8,128)(2,1)S(1)}, bf16[2,4,64,128]{3,2,1,0:T(8,128)(2,1)S(1)}, u32[]{:S(2)}, u32[]{:S(2)}) collective-permute-start(bf16[2,4,64,128]{3,2,1,0:T(8,128)(2,1)S(1)} %convert_element_type.338), channel_id=1, source_target_pairs={{0,12},{1,13},{2,14},{3,15},{16,28},{17,29},{18,30},{19,31}} | collective-permute-start | bytes 393224 | tf_op jit(solution)/shard_map/ppermute | solution.py:30
  224.2 4.4 collective-permute-start.7
  231.5 47.8 %collective-permute-start.8 = (bf16[512,2048]{1,0:T(8,128)(2,1)S(1)}, bf16[512,2048]{1,0:T(8,128)(2,1)}, u32[]{:S(2)}, u32[]{:S(2)}) collective-permute-start(bf16[512,2048]{1,0:T(8,128)(2,1)S(1)} %add_convert_fusion.5), channel_id=1, source_target_pairs={{0,2},{1,3},{2,0},{3,1},{4,6},{5,7},{6,4},{7,5},{8,10},{9,11},{10,... | collective-permute-start | bytes 6291464 | tf_op jit(solution)/shard_map/ppermute | solution.py:48
  233.1 702.2 %reduce-scatter.3.cloned.1.call-start = ((), (), s32[]{:S(2)}) async-start(), calls=%async_computation.5 | async-start | bytes 10616832 | tf_op jit(solution)/shard_map/reduce_scatter | solution.py:906
  283.1 4.4 collective-permute-start.9
  283.1 23.8 %copy-start.39 = (f32[2048]{0:T(1024)S(1)}, f32[2048]{0:T(1024)}, u32[]{:S(2)}) copy-start(f32[2048]{0:T(1024)} %param.46) | copy-start | bytes 24580
  283.1 23.8 %copy-start.40 = (f32[2048]{0:T(1024)S(1)}, f32[2048]{0:T(1024)}, u32[]{:S(2)}) copy-start(f32[2048]{0:T(1024)} %param.45) | copy-start | bytes 24580
  293.8 14.3 %collective-permute-start.10 = (f32[2,2048]{1,0:T(2,128)S(1)}, f32[2,2048]{1,0:T(2,128)S(1)}, u32[]{:S(2)}, u32[]{:S(2)}) collective-permute-start(f32[2,2048]{1,0:T(2,128)S(1)} %fusion.57), channel_id=1, source_target_pairs={{0,4},{4,8},{8,12},{1,5},{5,9},{9,13},{2,6},{6,10},{10,14},{3,7},{... | collective-permute-start | bytes 49160 | tf_op jit(solution)/shard_map/ppermute | solution.py:25
  337.2 24.6 %collective-permute-start.11 = (bf16[1024,512]{1,0:T(8,128)(2,1)}, bf16[1024,512]{1,0:T(8,128)(2,1)S(1)}, u32[]{:S(2)}, u32[]{:S(2)}) collective-permute-start(bf16[1024,512]{1,0:T(8,128)(2,1)} %get-tuple-element.231), channel_id=1, source_target_pairs={{0,2},{1,3},{2,0},{3,1},{4,6},{5,7},{6,4},{7,5},{8,10},{9,11},{10,... | collective-permute-start | bytes 3145736 | tf_op jit(solution)/shard_map/ppermute | solution.py:48
  338.8 37.9 %collective-permute-start.12 = (bf16[1024,512]{1,0:T(8,128)(2,1)}, bf16[1024,512]{1,0:T(8,128)(2,1)S(1)}, u32[]{:S(2)}, u32[]{:S(2)}) collective-permute-start(bf16[1024,512]{1,0:T(8,128)(2,1)} %get-tuple-element.231), channel_id=1, source_target_pairs={{0,1},{1,0},{2,3},{3,2},{4,5},{5,4},{6,7},{7,6},{8,9},{9,8},{10,11... | collective-permute-start | bytes 3145736 | tf_op jit(solution)/shard_map/ppermute | solution.py:48
  361.9 16.1 %collective-permute-start.13 = (bf16[1024,512]{1,0:T(8,128)(2,1)S(1)}, bf16[1024,512]{1,0:T(8,128)(2,1)S(1)}, u32[]{:S(2)}, u32[]{:S(2)}) collective-permute-start(bf16[1024,512]{1,0:T(8,128)(2,1)S(1)} %collective-permute-done.11), channel_id=1, source_target_pairs={{0,1},{1,0},{2,3},{3,2},{4,5},{5,4},{6,7},{7,6},{8,9},{9,8},{10,11... | collective-permute-start | bytes 3145736 | tf_op jit(solution)/shard_map/ppermute | solution.py:48
  443.8 11.3 %collective-permute-start.15 = (bf16[1024,512]{1,0:T(8,128)(2,1)}, bf16[1024,512]{1,0:T(8,128)(2,1)}, u32[]{:S(2)}, u32[]{:S(2)}) collective-permute-start(bf16[1024,512]{1,0:T(8,128)(2,1)} %get-tuple-element.201), channel_id=1, source_target_pairs={{0,1},{1,0},{2,3},{3,2},{4,5},{5,4},{6,7},{7,6},{8,9},{9,8},{10,11... | collective-permute-start | bytes 3145736 | tf_op jit(solution)/shard_map/ppermute | solution.py:48
  453.3 82.1 %collective-permute-start.17 = (bf16[2,2,256,1792]{2,3,0,1:T(8,128)(2,1)}, bf16[2,2,256,1792]{2,3,0,1:T(8,128)(2,1)}, u32[]{:S(2)}, u32[]{:S(2)}) collective-permute-start(bf16[2,2,256,1792]{2,3,0,1:T(8,128)(2,1)} %bitcast.210), channel_id=1, source_target_pairs={{0,16},{16,0},{1,17},{17,1},{2,18},{18,2},{3,19},{19,3},{4,20},{20... | collective-permute-start | bytes 11010056 | tf_op jit(solution)/shard_map/ppermute | solution.py:101
  454.9 24.6 %collective-permute-start.14 = (bf16[1024,512]{1,0:T(8,128)(2,1)S(1)}, bf16[1024,512]{1,0:T(8,128)(2,1)}, u32[]{:S(2)}, u32[]{:S(2)}) collective-permute-start(bf16[1024,512]{1,0:T(8,128)(2,1)S(1)} %get-tuple-element.200), channel_id=1, source_target_pairs={{0,1},{1,0},{2,3},{3,2},{4,5},{5,4},{6,7},{7,6},{8,9},{9,8},{10,11... | collective-permute-start | bytes 3145736 | tf_op jit(solution)/shard_map/ppermute | solution.py:48
  458.0 25.7 %collective-permute-start.16 = (bf16[1024,512]{1,0:T(8,128)(2,1)}, bf16[1024,512]{1,0:T(8,128)(2,1)}, u32[]{:S(2)}, u32[]{:S(2)}) collective-permute-start(bf16[1024,512]{1,0:T(8,128)(2,1)} %add_convert_fusion.7), channel_id=1, source_target_pairs={{0,2},{1,3},{2,0},{3,1},{4,6},{5,7},{6,4},{7,5},{8,10},{9,11},{10,... | collective-permute-start | bytes 3145736 | tf_op jit(solution)/shard_map/ppermute | solution.py:48
  483.6 51.7 %copy-start.1 = (bf16[1,2,2,256,1792]{3,4,1,2,0:T(8,128)(2,1)S(1)}, bf16[1,2,2,256,1792]{3,4,1,2,0:T(8,128)(2,1)}, u32[]{:S(2)}) copy-start(bf16[1,2,2,256,1792]{3,4,1,2,0:T(8,128)(2,1)} %copy.126) | copy-start | bytes 11010052
  483.6 57.0 %slice-start = ((s8[9437184]{0:T(1024)(128)(4,1)}), s8[4194304]{0:T(1024)(128)(4,1)S(1)}, s32[]{:S(2)}) async-start(s8[9437184]{0:T(1024)(128)(4,1)} %bitcast.202), calls=%async_computation.7 | async-start | bytes 8388608
  483.6 57.0 %slice-start.1 = ((s8[9437184]{0:T(1024)(128)(4,1)}), s8[4194304]{0:T(1024)(128)(4,1)S(1)}, s32[]{:S(2)}) async-start(s8[9437184]{0:T(1024)(128)(4,1)} %bitcast.202), calls=%async_computation.8 | async-start | bytes 8388608
  488.7 49.5 %copy-start.18 = (bf16[1024,512]{1,0:T(8,128)(2,1)}, bf16[1024,512]{1,0:T(8,128)(2,1)S(1)}, u32[]{:S(2)}) copy-start(bf16[1024,512]{1,0:T(8,128)(2,1)S(1)} %get-tuple-element.80.refs_5_) | copy-start | bytes 3145732
  488.7 52.0 %slice-start.2 = ((s8[9437184]{0:T(1024)(128)(4,1)}), s8[1048576]{0:T(1024)(128)(4,1)S(1)}, s32[]{:S(2)}) async-start(s8[9437184]{0:T(1024)(128)(4,1)} %bitcast.202), calls=%async_computation.9 | async-start | bytes 2097152
  540.7 87.6 %collective-permute-start.19 = (bf16[2,256,1792]{1,2,0:T(8,128)(2,1)}, bf16[2,256,1792]{1,2,0:T(8,128)(2,1)S(1)}, u32[]{:S(2)}, u32[]{:S(2)}) collective-permute-start(bf16[2,256,1792]{1,2,0:T(8,128)(2,1)} %dynamic-slice_bitcast_fusion), channel_id=1, source_target_pairs={{0,4},{4,0},{8,12},{12,8},{1,5},{5,1},{9,13},{13,9},{2,6},{6,2},{1... | collective-permute-start | bytes 5505032 | tf_op jit(solution)/shard_map/ppermute | solution.py:101
  543.3 39.4 %collective-permute-start.18 = (f32[2,2048]{1,0:T(2,128)S(1)}, f32[2,2048]{1,0:T(2,128)S(1)}, u32[]{:S(2)}, u32[]{:S(2)}) collective-permute-start(f32[2,2048]{1,0:T(2,128)S(1)} %fusion.12), channel_id=1, source_target_pairs={{4,0},{8,4},{12,8},{5,1},{9,5},{13,9},{6,2},{10,6},{14,10},{7,3},{... | collective-permute-start | bytes 49160 | tf_op jit(solution)/shard_map/ppermute | solution.py:25
  631.8 4.2 collective-permute-start.20
  636.9 47.8 %collective-permute-start.21 = (bf16[512,2048]{1,0:T(8,128)(2,1)S(1)}, bf16[512,2048]{1,0:T(8,128)(2,1)}, u32[]{:S(2)}, u32[]{:S(2)}) collective-permute-start(bf16[512,2048]{1,0:T(8,128)(2,1)S(1)} %add_convert_fusion.3), channel_id=1, source_target_pairs={{0,2},{1,3},{2,0},{3,1},{4,6},{5,7},{6,4},{7,5},{8,10},{9,11},{10,... | collective-permute-start | bytes 6291464 | tf_op jit(solution)/shard_map/ppermute | solution.py:48
  687.1 4.2 collective-permute-start.22
  695.1 378.8 %reduce-scatter.5.cloned.1.call-start = ((), (), s32[]{:S(2)}) async-start(), calls=%async_computation.6 | async-start | bytes 7077888 | tf_op jit(solution)/shard_map/reduce_scatter | solution.py:967
  737.5 62.1 %collective-permute-start.29 = (bf16[2,2,256,1024]{2,3,0,1:T(8,128)(2,1)}, bf16[2,2,256,1024]{2,3,0,1:T(8,128)(2,1)}, u32[]{:S(2)}, u32[]{:S(2)}) collective-permute-start(bf16[2,2,256,1024]{2,3,0,1:T(8,128)(2,1)} %bitcast.192), channel_id=1, source_target_pairs={{0,16},{16,0},{1,17},{17,1},{2,18},{18,2},{3,19},{19,3},{4,20},{20... | collective-permute-start | bytes 6291464 | tf_op jit(solution)/shard_map/ppermute | solution.py:101
  739.0 6.8 collective-permute-start.24
  740.3 5.8 collective-permute-start.23
  741.6 8.8 collective-permute-start.25
  746.1 14.2 %collective-permute-start.28 = (bf16[2,4,64,128]{3,2,1,0:T(8,128)(2,1)S(1)}, bf16[2,4,64,128]{3,2,1,0:T(8,128)(2,1)S(1)}, u32[]{:S(2)}, u32[]{:S(2)}) collective-permute-start(bf16[2,4,64,128]{3,2,1,0:T(8,128)(2,1)S(1)} %convert_element_type.389), channel_id=1, source_target_pairs={{4,0},{8,4},{12,8},{5,1},{9,5},{13,9},{6,2},{10,6},{14,10},{7,3},{... | collective-permute-start | bytes 393224 | tf_op jit(solution)/shard_map/ppermute | solution.py:30
  747.4 31.4 %collective-permute-start.27 = (bf16[2,4,64,128]{3,2,1,0:T(8,128)(2,1)S(1)}, bf16[2,4,64,128]{3,2,1,0:T(8,128)(2,1)S(1)}, u32[]{:S(2)}, u32[]{:S(2)}) collective-permute-start(bf16[2,4,64,128]{3,2,1,0:T(8,128)(2,1)S(1)} %convert_element_type.389), channel_id=1, source_target_pairs={{8,0},{12,4},{9,1},{13,5},{10,2},{14,6},{11,3},{15,7},{24,16},{28,... | collective-permute-start | bytes 393224 | tf_op jit(solution)/shard_map/ppermute | solution.py:30
  748.7 30.1 %collective-permute-start.26 = (bf16[2,4,64,128]{3,2,1,0:T(8,128)(2,1)S(1)}, bf16[2,4,64,128]{3,2,1,0:T(8,128)(2,1)S(1)}, u32[]{:S(2)}, u32[]{:S(2)}) collective-permute-start(bf16[2,4,64,128]{3,2,1,0:T(8,128)(2,1)S(1)} %convert_element_type.389), channel_id=1, source_target_pairs={{12,0},{13,1},{14,2},{15,3},{28,16},{29,17},{30,18},{31,19}} | collective-permute-start | bytes 393224 | tf_op jit(solution)/shard_map/ppermute | solution.py:30
  825.1 108.6 %collective-permute-start.31 = (bf16[2,256,1024]{1,2,0:T(8,128)(2,1)S(1)}, bf16[2,256,1024]{1,2,0:T(8,128)(2,1)}, u32[]{:S(2)}, u32[]{:S(2)}) collective-permute-start(bf16[2,256,1024]{1,2,0:T(8,128)(2,1)S(1)} %dynamic-slice_bitcast_fusion.1), channel_id=1, source_target_pairs={{0,4},{4,0},{8,12},{12,8},{1,5},{5,1},{9,13},{13,9},{2,6},{6,2},{1... | collective-permute-start | bytes 3145736 | tf_op jit(solution)/shard_map/ppermute | solution.py:101
  838.3 50.7 %collective-permute-start.30 = (f32[2,2048]{1,0:T(2,128)S(1)}, f32[2,2048]{1,0:T(2,128)S(1)}, u32[]{:S(2)}, u32[]{:S(2)}) collective-permute-start(f32[2,2048]{1,0:T(2,128)S(1)} %fusion.8), channel_id=1, source_target_pairs={{4,0},{8,4},{12,8},{5,1},{9,5},{13,9},{6,2},{10,6},{14,10},{7,3},{... | collective-permute-start | bytes 49160 | tf_op jit(solution)/shard_map/ppermute | solution.py:25
  935.2 119.2 %copy-start.10 = (bf16[2,256,1024]{1,2,0:T(8,128)(2,1)}, bf16[2,256,1024]{1,2,0:T(8,128)(2,1)S(1)}, u32[]{:S(2)}) copy-start(bf16[2,256,1024]{1,2,0:T(8,128)(2,1)S(1)} %fusion.22) | copy-start | bytes 3145732
  937.5 4.2 collective-permute-start.32
  942.6 108.7 %copy-start.3 = (bf16[512,2048]{1,0:T(8,128)(2,1)}, bf16[512,2048]{1,0:T(8,128)(2,1)S(1)}, u32[]{:S(2)}) copy-start(bf16[512,2048]{1,0:T(8,128)(2,1)S(1)} %add_convert_fusion.1) | copy-start | bytes 6291460
  942.6 108.7 %collective-permute-start.38 = (bf16[512,2048]{1,0:T(8,128)(2,1)S(1)}, bf16[512,2048]{1,0:T(8,128)(2,1)}, u32[]{:S(2)}, u32[]{:S(2)}) collective-permute-start(bf16[512,2048]{1,0:T(8,128)(2,1)S(1)} %add_convert_fusion.1), channel_id=1, source_target_pairs={{0,2},{1,3},{2,0},{3,1},{4,6},{5,7},{6,4},{7,5},{8,10},{9,11},{10,... | collective-permute-start | bytes 6291464 | tf_op jit(solution)/shard_map/ppermute | solution.py:48
  945.7 1.4 collective-permute-start.33
  947.2 46.0 %collective-permute-start.34 = (f32[14,2048]{1,0:T(8,128)S(1)}, f32[14,2048]{1,0:T(8,128)S(1)}, u32[]{:S(2)}, u32[]{:S(2)}) collective-permute-start(f32[14,2048]{1,0:T(8,128)S(1)} %add.281), channel_id=1, source_target_pairs={{0,2},{1,3},{2,0},{3,1},{4,6},{5,7},{6,4},{7,5},{8,10},{9,11},{10,... | collective-permute-start | bytes 344072 | tf_op jit(solution)/shard_map/ppermute | solution.py:125
  993.2 5.6 collective-permute-start.35
  998.7 14.4 %collective-permute-start.36 = (f32[14,2048]{1,0:T(8,128)S(1)}, f32[14,2048]{1,0:T(8,128)S(1)}, u32[]{:S(2)}, u32[]{:S(2)}) collective-permute-start(f32[14,2048]{1,0:T(8,128)S(1)} %add.283), channel_id=1, source_target_pairs={{0,4},{4,0},{8,12},{12,8},{1,5},{5,1},{9,13},{13,9},{2,6},{6,2},{1... | collective-permute-start | bytes 344072 | tf_op jit(solution)/shard_map/ppermute | solution.py:125
  1013.1 38.1 %collective-permute-start.37 = (f32[14,2048]{1,0:T(8,128)S(1)}, f32[14,2048]{1,0:T(8,128)S(1)}, u32[]{:S(2)}, u32[]{:S(2)}) collective-permute-start(f32[14,2048]{1,0:T(8,128)S(1)} %add.284), channel_id=1, source_target_pairs={{0,8},{4,12},{8,0},{12,4},{1,9},{5,13},{9,1},{13,5},{2,10},{6,14},... | collective-permute-start | bytes 344072 | tf_op jit(solution)/shard_map/ppermute | solution.py:125
  1015.4 55.7 %collective-permute-start.41 = (bf16[256,1792]{0,1:T(8,128)(2,1)}, bf16[256,1792]{0,1:T(8,128)(2,1)}, u32[]{:S(2)}, u32[]{:S(2)}) collective-permute-start(bf16[256,1792]{0,1:T(8,128)(2,1)} %dynamic-slice_bitcast_fusion.2), channel_id=1, source_target_pairs={{0,8},{4,12},{8,0},{12,4},{1,9},{5,13},{9,1},{13,5},{2,10},{6,14},... | collective-permute-start | bytes 2752520 | tf_op jit(solution)/shard_map/ppermute | solution.py:101
  1054.3 38.7 %collective-permute-start.39 = (bf16[512,2048]{1,0:T(8,128)(2,1)S(1)}, bf16[512,2048]{1,0:T(8,128)(2,1)}, u32[]{:S(2)}, u32[]{:S(2)}) collective-permute-start(bf16[512,2048]{1,0:T(8,128)(2,1)S(1)} %add_convert_fusion), channel_id=1, source_target_pairs={{0,1},{1,0},{2,3},{3,2},{4,5},{5,4},{6,7},{7,6},{8,9},{9,8},{10,11... | collective-permute-start | bytes 6291464 | tf_op jit(solution)/shard_map/ppermute | solution.py:48
  1055.3 27.0 %copy-start.6 = (bf16[256,2304]{0,1:T(8,128)(2,1)S(1)}, bf16[256,2304]{0,1:T(8,128)(2,1)}, u32[]{:S(2)}) copy-start(bf16[256,2304]{0,1:T(8,128)(2,1)} %reduce-scatter.3.cloned.1.call-done) | copy-start | bytes 3538948
  1055.3 34.1 %collective-permute-start.40 = (bf16[256,1024]{0,1:T(8,128)(2,1)}, bf16[256,1024]{0,1:T(8,128)(2,1)}, u32[]{:S(2)}, u32[]{:S(2)}) collective-permute-start(bf16[256,1024]{0,1:T(8,128)(2,1)} %dynamic-slice_bitcast_fusion.3), channel_id=1, source_target_pairs={{0,8},{4,12},{8,0},{12,4},{1,9},{5,13},{9,1},{13,5},{2,10},{6,14},... | collective-permute-start | bytes 1572872 | tf_op jit(solution)/shard_map/ppermute | solution.py:101
  (40 other events, 233.5 us)
Sparse Core Ops, SparseCore 0:
  13.6 153.5 all-gather.3
  169.9 146.5 all-gather.5
  318.5 110.6 all-gather.7
  695.2 195.7 reduce-scatter.2
  895.1 121.6 reduce-scatter.4

commit v5 on v3

--- a/solution.py
+++ b/solution.py
@@ -101,20 +101,19 @@
     return lax.ppermute(x, axis, [(i, i ^ bit) for i in range(lax.axis_size(axis))])
 
 
-def owner_scatter_steps(x):
-    fsdp_bits, ctx_bits = axis_bits("fsdp"), axis_bits("ctx")
-    dims = list(reversed(fsdp_bits)) + list(reversed(ctx_bits))
-    rows = x.shape[0] // 2 ** len(dims)
-    part = x.reshape(*([2] * len(dims)), rows, x.shape[1])
-    for axis, bit in fsdp_bits + ctx_bits:
-        dim = dims.index((axis, bit))
-        dims.pop(dim)
-        mine = (lax.axis_index(axis) // bit) % 2
-        own = lax.dynamic_index_in_dim(part, mine, dim, False)
-        arrived = swap(lax.dynamic_index_in_dim(part, 1 - mine, dim, False), axis, bit)
-        part = add_low(own, arrived)
-        part = yield part
-    yield None
+def owner_gather(x):
+    whole = x[None]
+    for axis, bit in list(reversed(axis_bits("ctx"))) + axis_bits("fsdp"):
+        whole = jnp.concatenate([whole, swap(whole, axis, bit)])
+    ctx, fsdp = lax.axis_size("ctx"), lax.axis_size("fsdp")
+    ctx_bits = [bit for _, bit in reversed(axis_bits("ctx"))]
+    rows = []
+    for f in range(fsdp):
+        for c in range(ctx):
+            far_f, far_c = lax.axis_index("fsdp") ^ f, lax.axis_index("ctx") ^ c
+            at = far_f * ctx + sum(((far_c // bit) % 2) * (1 << k) for k, bit in enumerate(ctx_bits))
+            rows.append(lax.dynamic_index_in_dim(whole, at, 0, False))
+    return jnp.concatenate(rows)
 
 
 def whole_sum(x, axes):
@@ -755,7 +754,7 @@
     owners = ("fsdp", "ctx")
     w_time = lax.all_gather(
         jnp.concatenate(
-            [acceptor_matrix, lookup_matrix, payload_matrix, valve_matrix, result_matrix.T], axis=1
+            [acceptor_matrix, lookup_matrix, payload_matrix, valve_matrix], axis=1
         ),
         owners,
         axis=0,
@@ -768,9 +767,10 @@
         tiled=True,
     )
     units = ffn_lookup_matrix.shape[1]
-    w_recept, w_key, w_value, w_gate, w_output_t = (
-        w_time[:, at * fourth_extent : (at + 1) * fourth_extent] for at in range(5)
-    )
+    w_recept, w_key, w_value, w_gate = (
+        w_time[:, at * fourth_extent : (at + 1) * fourth_extent] for at in range(4)
+    )
+    w_output_t = owner_gather(result_matrix.T)
     w_chankey = w_chan[:, :units]
     w_chanrecept = w_chan[:, units:]
     w_chanvalue_t = lax.all_gather(ffn_payload_matrix.T, owners, axis=0, tiled=True)
@@ -793,7 +793,8 @@
         return shifted(first * keep_first, "ctx", -1)[:, None]
 
     edge_one = edge_from(entering_activations[:, -1].astype(jnp.float32))
-    mixed_in = blend((x_low,), keep, edge_one, norm_one, mix_one, piece_len, "blend_one")
+    x_first, w_output_t = after(x_low, w_output_t)
+    mixed_in = blend((x_first,), keep, edge_one, norm_one, mix_one, piece_len, "blend_one")
     key_low = matmul(mixed_in[1], w_key).astype(jnp.bfloat16)
     value_low = matmul(mixed_in[2], w_value).astype(jnp.bfloat16)
 
@@ -919,11 +920,6 @@
         name="gate_back",
         flops=square // 8,
     )
-    grads_early = jnp.concatenate(
-        [grad_output_t, matmul_tn(mixed_in[3], d_gate_pre).astype(jnp.bfloat16)], axis=1
-    )
-    early = owner_scatter_steps(grads_early)
-    g_early = next(early)
     outgoing_state = carried(carry_mult, local_grad, "ctx", -1)
     d_recept, d_key, d_value, state_small = call(
         mix_back_kernel,
@@ -944,21 +940,17 @@
         name="mix_back",
         flops=6 * square,
     )
-    early_steps = len(axis_bits("fsdp")) + len(axis_bits("ctx"))
-    d_recept, d_key, d_value, g_early = after(d_recept, d_key, d_value, g_early)
-    for _ in range(early_steps - 2):
-        g_early = early.send(g_early)
     d_lows = [d_recept, d_key, d_value, d_gate_pre]
     weights_time = (w_recept, w_key, w_value, w_gate)
     grads_time = jnp.concatenate(
-        [
+        [grad_output_t]
+        + [
             matmul_tn(mixed, grad_low).astype(jnp.bfloat16)
-            for mixed, grad_low in zip(mixed_in, d_lows[:3])
+            for mixed, grad_low in zip(mixed_in, d_lows)
         ],
         axis=1,
     )
-    *d_lows, _, g_early = after(d_lows[0], *d_lows[1:], grads_time, g_early)
-    g_early = early.send(g_early)
+    *d_lows, _ = after(d_lows[0], *d_lows[1:], grads_time)
     g_time = lax.psum_scatter(grads_time, owners, scatter_dimension=0, tiled=True)
     d_input_part, time_small = blend_back(
         (x_low,),
@@ -973,15 +965,17 @@
         None,
         "blend_one_back",
     )
-    d_input_part, g_early, g_chan = after(d_input_part, g_early, g_chan)
+    d_input_part, g_chan = after(d_input_part, g_chan)
     head_small = jnp.concatenate([state_small[:2], group_small[:2]])
     head_small = lax.dynamic_update_slice_in_dim(
         jnp.zeros((4, embedding_extent), jnp.float32), head_small, sharded_layout, 1
     )
-    small_sum = whole_sum(
-        jnp.concatenate([time_small[:6], head_small, chan_small[:4]], axis=0),
-        ("tp", "fsdp", "ctx"),
-    )
+    small_part = jnp.concatenate([time_small[:6], head_small, chan_small[:4]], axis=0)
+
+    def small_total(token):
+        return whole_sum(after(small_part, token)[0], ("tp", "fsdp", "ctx"))
+
+    d_input_sum, small_sum = tp_sum(d_input_part, small_total)
     owned = embedding_extent // (lax.axis_size("fsdp") * lax.axis_size("ctx"))
     small_owned = lax.dynamic_slice_in_dim(
         small_sum,
@@ -989,19 +983,16 @@
         owned,
         1,
     )
-    d_input_sum = tp_sum(d_input_part)
     grad_inputs = (d_mixed.astype(jnp.float32) + d_input_sum.astype(jnp.float32)).reshape(
         full_shape
     )
     g_chanvalue = g_chanvalue.astype(jnp.float32)
     g_chan = g_chan.astype(jnp.float32)
     g_time = g_time.astype(jnp.float32)
-    g_early = g_early.astype(jnp.float32)
-    g_recept, g_key, g_value = (
-        g_time[:, at * fourth_extent : (at + 1) * fourth_extent] for at in range(3)
-    )
-    g_output = g_early[:, :fourth_extent].T
-    g_gate = g_early[:, fourth_extent:]
+    g_output = g_time[:, :fourth_extent].T
+    g_recept, g_key, g_value, g_gate = (
+        g_time[:, at * fourth_extent : (at + 1) * fourth_extent] for at in range(1, 5)
+    )
     g_chankey = g_chan[:, :units]
     g_chanrecept = g_chan[:, units:]
     return (

time: 992 us -> 1000 us (level)
  waiting for transfers between devices: 433 us -> 483 us
  local copies, waits for them, and re-layouts: 77 us -> 52.3 us
  other arithmetic: 77.5 us -> 63.3 us
  starting transfers between devices: 70.9 us -> 59.2 us
    all_gather x1, waiting for transfers between devices: 108 us -> 25.6 us  [per_device(): lax.all_gather(jnp.concatenate([acceptor_matrix, lookup_matrix, payload_m...]
    reduce_scatter x1, waiting for transfers between devices: 0.02 us -> 76.5 us  [per_device(): lax.psum_scatter(grads_time, owners, scatter_dimension=0, tiled=True)]
    ppermute x5, waiting for transfers between devices: 30.2 us -> 87.1 us  [whole_sum(): x = x + lax.ppermute(x, axis, [(i, i ^ bit) for i in range(count)])]
    ppermute x15, waiting for transfers between devices: 165 us -> 121 us  [partner(): return lax.ppermute(x, 'tp', [(i, i ^ bit) for i in range(count)])]
    ppermute x3, waiting for transfers between devices: 63.9 us -> 83.3 us  [swap(): lax.ppermute(x, axis, [(i, i ^ bit) for i in range(lax.axis_size(axis))])]
    reduce_scatter x1, waiting for transfers between devices: 0.01 us -> 13.2 us  [per_device(): lax.psum_scatter(grads_chan, owners, scatter_dimension=0, tiled=True)]
    ppermute x4, waiting for transfers between devices: 4.05 us -> 17.3 us  [shifted(): return lax.ppermute(x, axis, pairs)]
    ppermute x3, starting transfers between devices: 14.4 us -> 1.67 us  [swap(): lax.ppermute(x, axis, [(i, i ^ bit) for i in range(lax.axis_size(axis))])]
  transfers between devices with their start and end apart: 45 -> 45, of which waited for: 27 -> 31; matrix products, arithmetic and copies ran while one was open for 26% -> 23% of each run, Pallas kernels for 18% -> 18%
where the time goes in v5:
time: 1000 us; the launch traced here: 992 us
  waiting for transfers between devices  483 us (48%)
  Pallas kernels  180 us (18%)
  matrix products  139 us (14%)
  other arithmetic  63.3 us (6%)
  starting transfers between devices  59.2 us (6%)
  local copies, waits for them, and re-layouts  52.3 us (5%)
  between operations  15.6 us (2%)
    ppermute x15, waiting for transfers between devices, partner(): return lax.ppermute(x, 'tp', [(i, i ^ bit) for i in range(count)])  121 us
    pallas_call x2, Pallas kernels, blend_back(): pl.pallas_call(partial(blend_back_kernel, len(xs), mixes, per_seq, int(ow...  89.1 us
    ppermute x5, waiting for transfers between devices, whole_sum(): x = x + lax.ppermute(x, axis, [(i, i ^ bit) for i in range(count)])  87.1 us
    ppermute x3, waiting for transfers between devices, swap(): lax.ppermute(x, axis, [(i, i ^ bit) for i in range(lax.axis_size(axis))])  83.3 us
    reduce_scatter x1, waiting for transfers between devices, per_device(): lax.psum_scatter(grads_time, owners, scatter_dimension=0, tiled=True)  76.5 us
    dot_general x8, matrix products, matmul(): return jnp.dot(left, right, preferred_element_type=jnp.float32)  63.3 us
    pallas_call x4, Pallas kernels, pair_call(): pl.pallas_call(kernel, grid=(pairs, seqs), in_specs=[specs[kind] for kind...  49.7 us
    dot_general x8, matrix products, matmul_tn(): lax.dot_general(left, right, (((0,), (0,)), ((), ())), preferred_element_...  49.2 us
  transfers between devices with their start and end apart: 45, of which 31 were waited for; matrix products, arithmetic and copies ran while one was open for 23% of the time, Pallas kernels for 18%

profile of v5, /device:TPU:0, one launch (start us, length us, event | category | flops | bytes accessed | tf_op | source)
XLA Modules:
  0.0 992.2 jit_solution(4392475241931169492)
XLA Ops:
  14.7 4.9 collective-permute-start.4
  19.6 4.5 collective-permute-start.5
  26.7 28.6 %collective-permute-done = bf16[1,256,512]{1,2,0:T(8,128)(2,1)S(1)} collective-permute-done((bf16[1,256,512]{1,2,0:T(8,128)(2,1)S(1)}, bf16[1,256,512]{1,2,0:T(8,128)(2,1)S(1)}, u32[]{:S(2)}, u32[]{:S(2)}) %collective-permute-start) | collective-permute-done | bytes 262176 | tf_op jit(solution)/shard_map/ppermute | solution.py:101
  55.6 3.9 collective-permute-start.3
  59.5 19.2 %collective-permute-done.1 = bf16[2,256,512]{1,2,0:T(8,128)(2,1)S(1)} collective-permute-done((bf16[2,256,512]{1,2,0:T(8,128)(2,1)S(1)}, bf16[2,256,512]{1,2,0:T(8,128)(2,1)S(1)}, u32[]{:S(2)}, u32[]{:S(2)}) %collective-permute-start.1) | collective-permute-done | bytes 524320 | tf_op jit(solution)/shard_map/ppermute | solution.py:101
  88.0 35.5 %collective-permute-done.2 = bf16[4,256,512]{1,2,0:T(8,128)(2,1)} collective-permute-done((bf16[4,256,512]{1,2,0:T(8,128)(2,1)S(1)}, bf16[4,256,512]{1,2,0:T(8,128)(2,1)}, u32[]{:S(2)}, u32[]{:S(2)}) %collective-permute-start.2) | collective-permute-done | bytes 1048608 | tf_op jit(solution)/shard_map/ppermute | solution.py:101
  125.3 21.6 %blend_one.1 = (bf16[1024,2048]{1,0:T(8,128)(2,1)}, bf16[1024,2048]{1,0:T(8,128)(2,1)}, bf16[1024,2048]{1,0:T(8,128)(2,1)}, bf16[1024,2048]{1,0:T(8,128)(2,1)}) custom-call(bf16[1024,2048]{1,0:T(8,128)(2,1)} %bitcast.176, f32[1024,1]{1,0:T(8,128)} %bitcast.186, f32[2,1,2048]{2,1,0:T(1,128)} %broadcast_in_dim.23.refs_2_.refs_11_, ...), custom_call_target="tpu_custom_call" | custom-call | flops 41943040 | bytes 20971520 | tf_op jit(solution)/shard_map/blend_one/pallas_call | solution.py:503
  146.9 25.6 %all-gather.4.cloned.1.call-done.refs_6_.refs_7_.refs_8_.refs_9_ = bf16[2048,2048]{1,0:T(8,128)(2,1)} async-done(((bf16[256,2048]{1,0:T(8,128)(2,1)}), bf16[2048,2048]{1,0:T(8,128)(2,1)}) %all-gather.4.cloned.1.call-update) | async-done | bytes 8388624 | tf_op jit(solution)/shard_map/all_gather | solution.py:755
  172.5 6.3 fusion.39.k_ref
  178.8 4.9 fusion.42.v_ref
  183.7 7.1 carry.1
  191.8 6.3 collective-permute-start.7
  199.4 3.0 collective-permute-start.9
  202.4 6.7 fusion.25.gate_ref
  209.0 4.9 fusion.36.r_ref
  216.4 11.4 %mix.1 = (bf16[1024,512]{1,0:T(8,128)(2,1)}, f32[1024,512]{1,0:T(8,128)}) custom-call(bf16[1024,512]{1,0:T(8,128)(2,1)} %fusion.36.r_ref, bf16[1024,512]{1,0:T(8,128)(2,1)} %fusion.39.k_ref, bf16[1024,512]{1,0:T(8,128)(2,1)} %fusion.42.v_ref, f32[1024,512]{1,0:T(8,128)} %fusion.25.gate_ref, f32[1,512]{1,0:T(1,128)} %bitcast.211, ...), custom_call_target="tpu_custom_call" | custom-call | flops 1073741824 | bytes 11087872 | tf_op jit(solution)/shard_map/mix/pallas_call | solution.py:402
  227.8 3.6 convolution_convert_fusion.3
  233.7 4.3 collective-permute-done.10
  237.9 3.0 add_convert_fusion.5
  242.3 46.5 %collective-permute-done.11 = bf16[512,2048]{1,0:T(8,128)(2,1)} collective-permute-done((bf16[512,2048]{1,0:T(8,128)(2,1)S(1)}, bf16[512,2048]{1,0:T(8,128)(2,1)}, u32[]{:S(2)}, u32[]{:S(2)}) %collective-permute-start.11) | collective-permute-done | bytes 2097184 | tf_op jit(solution)/shard_map/ppermute | solution.py:48
  288.8 3.7 add_convert_fusion.4
  292.5 4.3 collective-permute-done.12
  296.9 3.9 maximum_select_fusion.refs_1_.refs_3_
  303.2 11.6 %collective-permute-start.13 = (f32[2,2048]{1,0:T(2,128)S(1)}, f32[2,2048]{1,0:T(2,128)S(1)}, u32[]{:S(2)}, u32[]{:S(2)}) collective-permute-start(f32[2,2048]{1,0:T(2,128)S(1)} %fusion.52), channel_id=1, source_target_pairs={{0,4},{4,8},{8,12},{1,5},{5,9},{9,13},{2,6},{6,10},{10,14},{3,7},{... | collective-permute-start | bytes 49160 | tf_op jit(solution)/shard_map/ppermute | solution.py:25
  317.0 19.1 %blend_two.1 = (bf16[1024,2048]{1,0:T(8,128)(2,1)}, bf16[1024,2048]{1,0:T(8,128)(2,1)}) custom-call(bf16[1024,2048]{1,0:T(8,128)(2,1)} %bitcast.177, bf16[1024,2048]{1,0:T(8,128)(2,1)} %copy-done, f32[1024,1]{1,0:T(8,128)} %bitcast.187, f32[2,1,2048]{2,1,0:T(1,128)} %copy.92.refs_3_.refs_9_, f32[2,2048]{1,0:T(2,128)} %get-tuple-element.216.refs_4_.refs_11_, ...), custom_call_target="tpu_custom_call" | custom-call | flops 41943040 | bytes 16777216 | tf_op jit(solution)/shard_map/blend_two/pallas_call | solution.py:503
  338.6 6.8 constant_dynamic-update-slice_fusion.3
  346.4 23.6 %collective-permute-done.14 = bf16[1024,512]{1,0:T(8,128)(2,1)S(1)} collective-permute-done((bf16[1024,512]{1,0:T(8,128)(2,1)}, bf16[1024,512]{1,0:T(8,128)(2,1)S(1)}, u32[]{:S(2)}, u32[]{:S(2)}) %collective-permute-start.14) | collective-permute-done | bytes 1048608 | tf_op jit(solution)/shard_map/ppermute | solution.py:48
  370.0 13.5 %multiply_convert_fusion.1 = (bf16[1024,1792]{1,0:T(8,128)(2,1)S(1)}, f32[1024,1792]{1,0:T(8,128)}) fusion(bf16[1024,2048]{1,0:T(8,128)(2,1)} %get-tuple-element.69, bf16[2048,2304]{1,0:T(8,128)(2,1)} %all-gather.6.cloned.1.call-done.refs_6_), kind=kOutput, calls=%fused_computation.5 | convolution fusion | flops 7521697792 | bytes 22544384 | tf_op jit(solution)/shard_map/dot_general | solution.py:161
  387.4 12.1 %convolution_convert_fusion.1 = bf16[1792,2048]{1,0:T(8,128)(2,1)} fusion(bf16[1024,1792]{1,0:T(8,128)(2,1)S(1)} %get-tuple-element.70, bf16[1024,2048]{1,0:T(8,128)(2,1)} %constant_dynamic-update-slice_fusion), kind=kOutput, calls=%fused_computation.3 | convolution fusion | flops 7519862784 | bytes 15204352 | tf_op jit(solution)/shard_map/dot_general | solution.py:165
  399.5 38.4 %all-gather.8.cloned.1.call-done = bf16[2048,1792]{0,1:T(8,128)(2,1)} async-done(((bf16[256,1792]{0,1:T(8,128)(2,1)}), bf16[2048,1792]{0,1:T(8,128)(2,1)}) %all-gather.8.cloned.1.call-update) | async-done | bytes 7340048 | tf_op jit(solution)/shard_map/all_gather | solution.py:776
  437.9 11.3 %convolution_convert_fusion.2 = bf16[1024,2048]{1,0:T(8,128)(2,1)S(1)} fusion(bf16[1024,1792]{1,0:T(8,128)(2,1)} %copy-done.45, bf16[2048,1792]{0,1:T(8,128)(2,1)} %all-gather.8.cloned.1.call-done), kind=kOutput, calls=%fused_computation.19 | convolution fusion | flops 7518289920 | bytes 15204352 | tf_op jit(solution)/shard_map/dot_general | solution.py:171
  459.0 14.3 %multiply_convert_fusion.refs_4_ = bf16[1024,1792]{1,0:T(8,128)(2,1)} fusion(f32[1024,1792]{1,0:T(8,128)} %get-tuple-element.210, bf16[1024,2048]{1,0:T(8,128)(2,1)} %constant_dynamic-update-slice_fusion, bf16[2048,1792]{0,1:T(8,128)(2,1)} %all-gather.8.cloned.1.call-done), kind=kOutput, calls=%fused_computation.4 | convolution fusion | flops 7523532800 | bytes 22544384 | tf_op jit(solution)/shard_map/dot_general | solution.py:161
  476.2 6.6 collective-permute-done.19
  482.7 4.7 fusion.23
  491.5 3.2 collective-permute-done.20
  495.3 44.9 %blend_two_back.1 = (bf16[1024,2048]{1,0:T(8,128)(2,1)}, f32[8,2048]{1,0:T(8,128)}) custom-call(bf16[1024,2048]{1,0:T(8,128)(2,1)} %bitcast.179, bf16[1024,2048]{1,0:T(8,128)(2,1)} %copy-done, bf16[1024,2048]{1,0:T(8,128)(2,1)} %bitcast.180, bf16[1024,2048]{1,0:T(8,128)(2,1)} %copy-done, bf16[1024,1792]{1,0:T(8,128)(2,1)} %multiply_convert_fusion.refs_4_, ...), custom_call_target="tpu_custom_call" | custom-call | flops 9663676416 | bytes 16777216 | tf_op jit(solution)/shard_map/blend_two_back/pallas_call | solution.py:663
  542.3 4.1 collective-permute-done.21
  548.9 10.9 %convolution_convert_fusion = bf16[2048,1792]{0,1:T(8,128)(2,1)S(1)} fusion(bf16[1024,2048]{1,0:T(8,128)(2,1)} %get-tuple-element.69, bf16[1024,1792]{1,0:T(8,128)(2,1)S(1)} %copy-done.37), kind=kOutput, calls=%fused_computation.2 | convolution fusion | flops 7519862784 | bytes 15204352 | tf_op jit(solution)/shard_map/dot_general | solution.py:165
  562.4 11.5 %pad_maximum_fusion = bf16[2048,2304]{0,1:T(8,128)(2,1)} fusion(bf16[2048,512]{0,1:T(8,128)(2,1)S(1)} %convolution_convert_fusion.9, bf16[2048,1792]{0,1:T(8,128)(2,1)S(1)} %convolution_convert_fusion), kind=kLoop, calls=%fused_computation | loop fusion | flops 18874368 | bytes 18874368 | tf_op jit(solution)/shard_map/concatenate | solution.py:890
  573.8 21.4 %collective-permute-done.22 = bf16[512,2048]{1,0:T(8,128)(2,1)} collective-permute-done((bf16[512,2048]{1,0:T(8,128)(2,1)S(1)}, bf16[512,2048]{1,0:T(8,128)(2,1)}, u32[]{:S(2)}, u32[]{:S(2)}) %collective-permute-start.22) | collective-permute-done | bytes 2097184 | tf_op jit(solution)/shard_map/ppermute | solution.py:48
  597.6 4.1 collective-permute-done.23
  601.8 3.6 maximum_select_fusion.1
  613.9 3.5 collective-permute-done.26
  617.4 5.9 fusion.67.dj_ref
  623.2 11.3 %gate_back.1 = (bf16[1024,512]{1,0:T(8,128)(2,1)}, bf16[1024,512]{1,0:T(8,128)(2,1)}, f32[2,4,64,128]{3,2,1,0:T(8,128)}, f32[8,512]{1,0:T(8,128)}) custom-call(f32[1024,512]{1,0:T(8,128)} %fusion.67.dj_ref, f32[1024,512]{1,0:T(8,128)} %get-tuple-element.76.attend_ref, f32[1024,512]{1,0:T(8,128)} %fusion.25.gate_ref, bf16[1024,512]{1,0:T(8,128)(2,1)} %fusion.36.r_ref, ...), custom_call_target="tpu_custom_call" | custom-call | flops 67108864 | bytes 14749696 | tf_op jit(solution)/shard_map/gate_back/pallas_call | solution.py:402
  639.5 6.0 fusion.8
  645.4 3.0 collective-permute-done.27
  648.4 8.2 collective-permute-done.28
  657.5 19.9 %mix_back.1 = (bf16[1024,512]{1,0:T(8,128)(2,1)}, bf16[1024,512]{1,0:T(8,128)(2,1)}, bf16[1024,512]{1,0:T(8,128)(2,1)}, f32[8,512]{1,0:T(8,128)}) custom-call(bf16[1024,512]{1,0:T(8,128)(2,1)} %fusion.36.r_ref, bf16[1024,512]{1,0:T(8,128)(2,1)} %fusion.39.k_ref, bf16[1024,512]{1,0:T(8,128)(2,1)} %fusion.42.v_ref, ...), custom_call_target="tpu_custom_call" | custom-call | flops 3221225472 | bytes 9523200 | tf_op jit(solution)/shard_map/mix_back/pallas_call | solution.py:402
  677.4 6.4 fusion.7
  683.8 3.8 fusion.6
  687.6 3.8 fusion.5
  691.4 3.8 fusion.4
  707.2 13.2 %collective-permute-done.30 = f32[2,2048]{1,0:T(2,128)S(1)} collective-permute-done((f32[2,2048]{1,0:T(2,128)S(1)}, f32[2,2048]{1,0:T(2,128)S(1)}, u32[]{:S(2)}, u32[]{:S(2)}) %collective-permute-start.30) | collective-permute-done | bytes 16416 | tf_op jit(solution)/shard_map/ppermute | solution.py:25
  721.0 44.2 %blend_one_back.1 = (bf16[1024,2048]{1,0:T(8,128)(2,1)}, f32[8,2048]{1,0:T(8,128)}) custom-call(bf16[1024,2048]{1,0:T(8,128)(2,1)} %bitcast.181, bf16[1024,2048]{1,0:T(8,128)(2,1)} %bitcast.182, bf16[1024,512]{1,0:T(8,128)(2,1)} %get-tuple-element.83.refs_2_, bf16[1024,512]{1,0:T(8,128)(2,1)} %get-tuple-element.84.refs_3_, ...), custom_call_target="tpu_custom_call" | custom-call | flops 8589934592 | bytes 16777216 | tf_op jit(solution)/shard_map/blend_one_back/pallas_call | solution.py:663
  765.2 13.2 %reduce-scatter.6.cloned.1.call-done = bf16[256,2304]{0,1:T(8,128)(2,1)} async-done(((bf16[2048,2304]{0,1:T(8,128)(2,1)}), bf16[256,2304]{0,1:T(8,128)(2,1)}) %reduce-scatter.6.cloned.1.call-update) | async-done | bytes 1179664 | tf_op jit(solution)/shard_map/reduce_scatter | solution.py:900
  780.4 4.1 collective-permute-done.31
  790.5 45.4 %collective-permute-done.33 = f32[14,2048]{1,0:T(8,128)S(1)} collective-permute-done((f32[14,2048]{1,0:T(8,128)S(1)}, f32[14,2048]{1,0:T(8,128)S(1)}, u32[]{:S(2)}, u32[]{:S(2)}) %collective-permute-start.33) | collective-permute-done | bytes 114720 | tf_op jit(solution)/shard_map/ppermute | solution.py:124
  837.5 5.5 collective-permute-done.34
  843.1 16.8 %collective-permute-done.35 = f32[14,2048]{1,0:T(8,128)S(1)} collective-permute-done((f32[14,2048]{1,0:T(8,128)S(1)}, f32[14,2048]{1,0:T(8,128)S(1)}, u32[]{:S(2)}, u32[]{:S(2)}) %collective-permute-start.35) | collective-permute-done | bytes 114720 | tf_op jit(solution)/shard_map/ppermute | solution.py:124
  860.0 18.0 %collective-permute-done.36 = f32[14,2048]{1,0:T(8,128)S(1)} collective-permute-done((f32[14,2048]{1,0:T(8,128)S(1)}, f32[14,2048]{1,0:T(8,128)S(1)}, u32[]{:S(2)}, u32[]{:S(2)}) %collective-permute-start.36) | collective-permute-done | bytes 114720 | tf_op jit(solution)/shard_map/ppermute | solution.py:124
  883.9 2.7 copy.107
  888.6 76.5 %reduce-scatter.8.cloned.1.call-done = bf16[256,2560]{0,1:T(8,128)(2,1)} async-done(((bf16[2048,2560]{0,1:T(8,128)(2,1)}), bf16[256,2560]{0,1:T(8,128)(2,1)}) %reduce-scatter.8.cloned.1.call-update) | async-done | bytes 1310736 | tf_op jit(solution)/shard_map/reduce_scatter | solution.py:954
  978.3 6.6 convert_add_fusion
  (285 shorter events, 125.3 us)
Async XLA Ops:
  7.2 18.2 %copy-start.8 = (bf16[512,256]{1,0:T(8,128)(2,1)S(1)}, bf16[512,256]{1,0:T(8,128)(2,1)}, u32[]{:S(2)}) copy-start(bf16[512,256]{1,0:T(8,128)(2,1)} %param.31) | copy-start | bytes 786436
  7.2 165.3 %all-gather.4.cloned.1.call-start = ((), (), s32[]{:S(2)}) async-start(), calls=%async_computation.3 | async-start | bytes 9437184 | tf_op jit(solution)/shard_map/all_gather | solution.py:755
  9.6 70.9 %copy-start.31 = (f32[2048]{0:T(1024)S(1)}, f32[2048]{0:T(1024)}, u32[]{:S(2)}) copy-start(f32[2048]{0:T(1024)} %param.36) | copy-start | bytes 24580
  9.6 70.9 %copy-start.32 = (f32[2048]{0:T(1024)S(1)}, f32[2048]{0:T(1024)}, u32[]{:S(2)}) copy-start(f32[2048]{0:T(1024)} %param.35) | copy-start | bytes 24580
  9.6 71.5 %copy-start.22 = (f32[2048]{0:T(1024)S(1)}, f32[2048]{0:T(1024)}, u32[]{:S(2)}) copy-start(f32[2048]{0:T(1024)} %param.37) | copy-start | bytes 24580
  9.6 71.5 %copy-start.24 = (f32[2048]{0:T(1024)S(1)}, f32[2048]{0:T(1024)}, u32[]{:S(2)}) copy-start(f32[2048]{0:T(1024)} %param.38) | copy-start | bytes 24580
  9.6 71.5 %copy-start.26 = (f32[2048]{0:T(1024)S(1)}, f32[2048]{0:T(1024)}, u32[]{:S(2)}) copy-start(f32[2048]{0:T(1024)} %param.39) | copy-start | bytes 24580
  9.6 71.5 %copy-start.28 = (f32[2048]{0:T(1024)S(1)}, f32[2048]{0:T(1024)}, u32[]{:S(2)}) copy-start(f32[2048]{0:T(1024)} %param.40) | copy-start | bytes 24580
  9.6 326.4 %all-gather.6.cloned.1.call-start = ((), (), s32[]{:S(2)}) async-start(), calls=%async_computation.4 | async-start | bytes 10616832 | tf_op jit(solution)/shard_map/all_gather | solution.py:763
  12.1 425.8 %all-gather.8.cloned.1.call-start = ((), (), s32[]{:S(2)}) async-start(), calls=%async_computation.5 | async-start | bytes 8257536 | tf_op jit(solution)/shard_map/all_gather | solution.py:776
  14.7 110.3 %copy-start.35 = (bf16[2,4,1,128]{3,2,1,0:T(2,128)(2,1)}, bf16[2,4,1,128]{3,2,1,0:T(2,128)(2,1)S(1)}, u32[]{:S(2)}) copy-start(bf16[2,4,1,128]{3,2,1,0:T(2,128)(2,1)S(1)} %get-tuple-element.172) | copy-start | bytes 6148
  14.7 72.7 %collective-permute-start.4 = (bf16[2,4,1,128]{3,2,1,0:T(2,128)(2,1)S(1)}, bf16[2,4,1,128]{3,2,1,0:T(2,128)(2,1)S(1)}, u32[]{:S(2)}, u32[]{:S(2)}) collective-permute-start(bf16[2,4,1,128]{3,2,1,0:T(2,128)(2,1)S(1)} %get-tuple-element.172), channel_id=1, source_target_pairs={{0,4},{4,8},{8,12},{1,5},{5,9},{9,13},{2,6},{6,10},{10,14},{3,7},{... | collective-permute-start | bytes 6152 | tf_op jit(solution)/shard_map/ppermute | solution.py:30
  19.6 67.8 %collective-permute-start.5 = (bf16[2,4,1,128]{3,2,1,0:T(2,128)(2,1)S(1)}, bf16[2,4,1,128]{3,2,1,0:T(2,128)(2,1)S(1)}, u32[]{:S(2)}, u32[]{:S(2)}) collective-permute-start(bf16[2,4,1,128]{3,2,1,0:T(2,128)(2,1)S(1)} %get-tuple-element.172), channel_id=1, source_target_pairs={{0,8},{4,12},{1,9},{5,13},{2,10},{6,14},{3,11},{7,15},{16,24},{20,... | collective-permute-start | bytes 6152 | tf_op jit(solution)/shard_map/ppermute | solution.py:30
  24.1 63.2 %collective-permute-start.6 = (bf16[2,4,1,128]{3,2,1,0:T(2,128)(2,1)S(1)}, bf16[2,4,1,128]{3,2,1,0:T(2,128)(2,1)S(1)}, u32[]{:S(2)}, u32[]{:S(2)}) collective-permute-start(bf16[2,4,1,128]{3,2,1,0:T(2,128)(2,1)S(1)} %get-tuple-element.172), channel_id=1, source_target_pairs={{0,12},{1,13},{2,14},{3,15},{16,28},{17,29},{18,30},{19,31}} | collective-permute-start | bytes 6152 | tf_op jit(solution)/shard_map/ppermute | solution.py:30
  25.4 29.9 %collective-permute-start = (bf16[1,256,512]{1,2,0:T(8,128)(2,1)S(1)}, bf16[1,256,512]{1,2,0:T(8,128)(2,1)S(1)}, u32[]{:S(2)}, u32[]{:S(2)}) collective-permute-start(bf16[1,256,512]{1,2,0:T(8,128)(2,1)S(1)} %bitcast.191), channel_id=1, source_target_pairs={{0,8},{4,12},{8,0},{12,4},{1,9},{5,13},{9,1},{13,5},{2,10},{6,14},... | collective-permute-start | bytes 786440 | tf_op jit(solution)/shard_map/ppermute | solution.py:101
  55.4 23.3 %collective-permute-start.1 = (bf16[2,256,512]{1,2,0:T(8,128)(2,1)S(1)}, bf16[2,256,512]{1,2,0:T(8,128)(2,1)S(1)}, u32[]{:S(2)}, u32[]{:S(2)}) collective-permute-start(bf16[2,256,512]{1,2,0:T(8,128)(2,1)S(1)} %pad_maximum_fusion.5), channel_id=1, source_target_pairs={{0,4},{4,0},{8,12},{12,8},{1,5},{5,1},{9,13},{13,9},{2,6},{6,2},{1... | collective-permute-start | bytes 1572872 | tf_op jit(solution)/shard_map/ppermute | solution.py:101
  55.6 31.8 %collective-permute-start.3 = (f32[2,2048]{1,0:T(2,128)S(1)}, f32[2,2048]{1,0:T(2,128)S(1)}, u32[]{:S(2)}, u32[]{:S(2)}) collective-permute-start(f32[2,2048]{1,0:T(2,128)S(1)} %fusion.47), channel_id=1, source_target_pairs={{0,4},{4,8},{8,12},{1,5},{5,9},{9,13},{2,6},{6,10},{10,14},{3,7},{... | collective-permute-start | bytes 49160 | tf_op jit(solution)/shard_map/ppermute | solution.py:25
  78.8 44.7 %collective-permute-start.2 = (bf16[4,256,512]{1,2,0:T(8,128)(2,1)S(1)}, bf16[4,256,512]{1,2,0:T(8,128)(2,1)}, u32[]{:S(2)}, u32[]{:S(2)}) collective-permute-start(bf16[4,256,512]{1,2,0:T(8,128)(2,1)S(1)} %pad_maximum_fusion.3), channel_id=1, source_target_pairs={{0,16},{16,0},{1,17},{17,1},{2,18},{18,2},{3,19},{19,3},{4,20},{20... | collective-permute-start | bytes 3145736 | tf_op jit(solution)/shard_map/ppermute | solution.py:101
  125.3 102.5 %copy-start.18 = (bf16[2048,512]{0,1:T(8,128)(2,1)}, bf16[2048,512]{0,1:T(8,128)(2,1)S(1)}, u32[]{:S(2)}) copy-start(bf16[2048,512]{0,1:T(8,128)(2,1)S(1)} %bitcast_dynamic-update-slice_fusion) | copy-start | bytes 6291460
  191.8 22.2 %collective-permute-start.7 = (bf16[2,4,64,128]{3,2,1,0:T(8,128)(2,1)S(1)}, bf16[2,4,64,128]{3,2,1,0:T(8,128)(2,1)S(1)}, u32[]{:S(2)}, u32[]{:S(2)}) collective-permute-start(bf16[2,4,64,128]{3,2,1,0:T(8,128)(2,1)S(1)} %convert_element_type.265), channel_id=1, source_target_pairs={{0,12},{1,13},{2,14},{3,15},{16,28},{17,29},{18,30},{19,31}} | collective-permute-start | bytes 393224 | tf_op jit(solution)/shard_map/ppermute | solution.py:30
  198.1 15.9 %collective-permute-start.8 = (bf16[2,4,64,128]{3,2,1,0:T(8,128)(2,1)S(1)}, bf16[2,4,64,128]{3,2,1,0:T(8,128)(2,1)S(1)}, u32[]{:S(2)}, u32[]{:S(2)}) collective-permute-start(bf16[2,4,64,128]{3,2,1,0:T(8,128)(2,1)S(1)} %convert_element_type.265), channel_id=1, source_target_pairs={{0,8},{4,12},{1,9},{5,13},{2,10},{6,14},{3,11},{7,15},{16,24},{20,... | collective-permute-start | bytes 393224 | tf_op jit(solution)/shard_map/ppermute | solution.py:30
  199.4 16.2 %collective-permute-start.9 = (bf16[2,4,64,128]{3,2,1,0:T(8,128)(2,1)S(1)}, bf16[2,4,64,128]{3,2,1,0:T(8,128)(2,1)S(1)}, u32[]{:S(2)}, u32[]{:S(2)}) collective-permute-start(bf16[2,4,64,128]{3,2,1,0:T(8,128)(2,1)S(1)} %convert_element_type.265), channel_id=1, source_target_pairs={{0,4},{4,8},{8,12},{1,5},{5,9},{9,13},{2,6},{6,10},{10,14},{3,7},{... | collective-permute-start | bytes 393224 | tf_op jit(solution)/shard_map/ppermute | solution.py:30
  233.6 4.4 collective-permute-start.10
  241.0 47.8 %collective-permute-start.11 = (bf16[512,2048]{1,0:T(8,128)(2,1)S(1)}, bf16[512,2048]{1,0:T(8,128)(2,1)}, u32[]{:S(2)}, u32[]{:S(2)}) collective-permute-start(bf16[512,2048]{1,0:T(8,128)(2,1)S(1)} %add_convert_fusion.5), channel_id=1, source_target_pairs={{0,2},{1,3},{2,0},{3,1},{4,6},{5,7},{6,4},{7,5},{8,10},{9,11},{10,... | collective-permute-start | bytes 6291464 | tf_op jit(solution)/shard_map/ppermute | solution.py:48
  242.2 363.2 %reduce-scatter.4.cloned.1.call-start = ((), (), s32[]{:S(2)}) async-start(), calls=%async_computation.6 | async-start | bytes 8257536 | tf_op jit(solution)/shard_map/reduce_scatter | solution.py:856
  292.5 4.4 collective-permute-start.12
  292.5 22.3 %copy-start.20 = (f32[2048]{0:T(1024)S(1)}, f32[2048]{0:T(1024)}, u32[]{:S(2)}) copy-start(f32[2048]{0:T(1024)} %param.47) | copy-start | bytes 24580
  292.5 22.3 %copy-start.21 = (f32[2048]{0:T(1024)S(1)}, f32[2048]{0:T(1024)}, u32[]{:S(2)}) copy-start(f32[2048]{0:T(1024)} %param.48) | copy-start | bytes 24580
  292.5 22.3 %copy-start.33 = (f32[2048]{0:T(1024)S(1)}, f32[2048]{0:T(1024)}, u32[]{:S(2)}) copy-start(f32[2048]{0:T(1024)} %param.46) | copy-start | bytes 24580
  292.5 22.3 %copy-start.34 = (f32[2048]{0:T(1024)S(1)}, f32[2048]{0:T(1024)}, u32[]{:S(2)}) copy-start(f32[2048]{0:T(1024)} %param.45) | copy-start | bytes 24580
  303.2 13.1 %collective-permute-start.13 = (f32[2,2048]{1,0:T(2,128)S(1)}, f32[2,2048]{1,0:T(2,128)S(1)}, u32[]{:S(2)}, u32[]{:S(2)}) collective-permute-start(f32[2,2048]{1,0:T(2,128)S(1)} %fusion.52), channel_id=1, source_target_pairs={{0,4},{4,8},{8,12},{1,5},{5,9},{9,13},{2,6},{6,10},{10,14},{3,7},{... | collective-permute-start | bytes 49160 | tf_op jit(solution)/shard_map/ppermute | solution.py:25
  345.5 24.6 %collective-permute-start.14 = (bf16[1024,512]{1,0:T(8,128)(2,1)}, bf16[1024,512]{1,0:T(8,128)(2,1)S(1)}, u32[]{:S(2)}, u32[]{:S(2)}) collective-permute-start(bf16[1024,512]{1,0:T(8,128)(2,1)} %get-tuple-element.214), channel_id=1, source_target_pairs={{0,2},{1,3},{2,0},{3,1},{4,6},{5,7},{6,4},{7,5},{8,10},{9,11},{10,... | collective-permute-start | bytes 3145736 | tf_op jit(solution)/shard_map/ppermute | solution.py:48
  346.4 38.4 %collective-permute-start.15 = (bf16[1024,512]{1,0:T(8,128)(2,1)}, bf16[1024,512]{1,0:T(8,128)(2,1)S(1)}, u32[]{:S(2)}, u32[]{:S(2)}) collective-permute-start(bf16[1024,512]{1,0:T(8,128)(2,1)} %get-tuple-element.214), channel_id=1, source_target_pairs={{0,1},{1,0},{2,3},{3,2},{4,5},{5,4},{6,7},{7,6},{8,9},{9,8},{10,11... | collective-permute-start | bytes 3145736 | tf_op jit(solution)/shard_map/ppermute | solution.py:48
  370.0 16.2 %collective-permute-start.16 = (bf16[1024,512]{1,0:T(8,128)(2,1)S(1)}, bf16[1024,512]{1,0:T(8,128)(2,1)S(1)}, u32[]{:S(2)}, u32[]{:S(2)}) collective-permute-start(bf16[1024,512]{1,0:T(8,128)(2,1)S(1)} %collective-permute-done.14), channel_id=1, source_target_pairs={{0,1},{1,0},{2,3},{3,2},{4,5},{5,4},{6,7},{7,6},{8,9},{9,8},{10,11... | collective-permute-start | bytes 3145736 | tf_op jit(solution)/shard_map/ppermute | solution.py:48
  452.4 3.0 collective-permute-start.18
  452.4 326.0 %reduce-scatter.6.cloned.1.call-start = ((), (), s32[]{:S(2)}) async-start(), calls=%async_computation.7 | async-start | bytes 10616832 | tf_op jit(solution)/shard_map/reduce_scatter | solution.py:900
  452.6 23.6 %collective-permute-start.17 = (bf16[1024,512]{1,0:T(8,128)(2,1)S(1)}, bf16[1024,512]{1,0:T(8,128)(2,1)}, u32[]{:S(2)}, u32[]{:S(2)}) collective-permute-start(bf16[1024,512]{1,0:T(8,128)(2,1)S(1)} %get-tuple-element.184), channel_id=1, source_target_pairs={{0,1},{1,0},{2,3},{3,2},{4,5},{5,4},{6,7},{7,6},{8,9},{9,8},{10,11... | collective-permute-start | bytes 3145736 | tf_op jit(solution)/shard_map/ppermute | solution.py:48
  455.4 18.8 %slice-start = ((s8[9437184]{0:T(1024)(128)(4,1)}), s8[4194304]{0:T(1024)(128)(4,1)S(1)}, s32[]{:S(2)}) async-start(s8[9437184]{0:T(1024)(128)(4,1)} %bitcast.184), calls=%async_computation.9 | async-start | bytes 8388608
  457.4 25.4 %collective-permute-start.19 = (bf16[1024,512]{1,0:T(8,128)(2,1)S(1)}, bf16[1024,512]{1,0:T(8,128)(2,1)}, u32[]{:S(2)}, u32[]{:S(2)}) collective-permute-start(bf16[1024,512]{1,0:T(8,128)(2,1)S(1)} %add_convert_fusion.7), channel_id=1, source_target_pairs={{0,2},{1,3},{2,0},{3,1},{4,6},{5,7},{6,4},{7,5},{8,10},{9,11},{10,... | collective-permute-start | bytes 3145736 | tf_op jit(solution)/shard_map/ppermute | solution.py:48
  459.0 15.2 %slice-start.1 = ((s8[9437184]{0:T(1024)(128)(4,1)}), s8[4194304]{0:T(1024)(128)(4,1)S(1)}, s32[]{:S(2)}) async-start(s8[9437184]{0:T(1024)(128)(4,1)} %bitcast.184), calls=%async_computation.10 | async-start | bytes 8388608
  459.0 15.2 %slice-start.2 = ((s8[9437184]{0:T(1024)(128)(4,1)}), s8[1048576]{0:T(1024)(128)(4,1)S(1)}, s32[]{:S(2)}) async-start(s8[9437184]{0:T(1024)(128)(4,1)} %bitcast.184), calls=%async_computation.11 | async-start | bytes 2097152
  488.1 6.7 collective-permute-start.20
  542.2 4.2 collective-permute-start.21
  547.3 12.5 %copy-start.13 = (bf16[1024,512]{1,0:T(8,128)(2,1)S(1)}, bf16[1024,512]{1,0:T(8,128)(2,1)}, u32[]{:S(2)}) copy-start(bf16[1024,512]{1,0:T(8,128)(2,1)} %copy-done.12) | copy-start | bytes 3145732
  547.3 12.5 %copy-start.43 = (bf16[1024,2048]{1,0:T(8,128)(2,1)S(1)}, bf16[1024,2048]{1,0:T(8,128)(2,1)}, u32[]{:S(2)}) copy-start(bf16[1024,2048]{1,0:T(8,128)(2,1)} %get-tuple-element.68) | copy-start | bytes 12582916
  547.4 47.8 %collective-permute-start.22 = (bf16[512,2048]{1,0:T(8,128)(2,1)S(1)}, bf16[512,2048]{1,0:T(8,128)(2,1)}, u32[]{:S(2)}, u32[]{:S(2)}) collective-permute-start(bf16[512,2048]{1,0:T(8,128)(2,1)S(1)} %add_convert_fusion.3), channel_id=1, source_target_pairs={{0,2},{1,3},{2,0},{3,1},{4,6},{5,7},{6,4},{7,5},{8,10},{9,11},{10,... | collective-permute-start | bytes 6291464 | tf_op jit(solution)/shard_map/ppermute | solution.py:48
  597.6 4.2 collective-permute-start.23
  605.4 359.7 %reduce-scatter.8.cloned.1.call-start = ((), (), s32[]{:S(2)}) async-start(), calls=%async_computation.8 | async-start | bytes 11796480 | tf_op jit(solution)/shard_map/reduce_scatter | solution.py:954
  606.1 5.5 collective-permute-start.24
  607.4 6.5 collective-permute-start.25
  608.7 8.7 collective-permute-start.26
  623.2 16.2 %copy-start.44 = (bf16[1024,512]{1,0:T(8,128)(2,1)S(1)}, bf16[1024,512]{1,0:T(8,128)(2,1)}, u32[]{:S(2)}) copy-start(bf16[1024,512]{1,0:T(8,128)(2,1)} %get-tuple-element.66) | copy-start | bytes 3145732
  635.6 12.9 %collective-permute-start.27 = (bf16[2,4,64,128]{3,2,1,0:T(8,128)(2,1)S(1)}, bf16[2,4,64,128]{3,2,1,0:T(8,128)(2,1)S(1)}, u32[]{:S(2)}, u32[]{:S(2)}) collective-permute-start(bf16[2,4,64,128]{3,2,1,0:T(8,128)(2,1)S(1)} %convert_element_type.308), channel_id=1, source_target_pairs={{12,0},{13,1},{14,2},{15,3},{28,16},{29,17},{30,18},{31,19}} | collective-permute-start | bytes 393224 | tf_op jit(solution)/shard_map/ppermute | solution.py:30
  636.9 19.8 %collective-permute-start.28 = (bf16[2,4,64,128]{3,2,1,0:T(8,128)(2,1)S(1)}, bf16[2,4,64,128]{3,2,1,0:T(8,128)(2,1)S(1)}, u32[]{:S(2)}, u32[]{:S(2)}) collective-permute-start(bf16[2,4,64,128]{3,2,1,0:T(8,128)(2,1)S(1)} %convert_element_type.308), channel_id=1, source_target_pairs={{8,0},{12,4},{9,1},{13,5},{10,2},{14,6},{11,3},{15,7},{24,16},{28,... | collective-permute-start | bytes 393224 | tf_op jit(solution)/shard_map/ppermute | solution.py:30
  638.2 18.5 %collective-permute-start.29 = (bf16[2,4,64,128]{3,2,1,0:T(8,128)(2,1)S(1)}, bf16[2,4,64,128]{3,2,1,0:T(8,128)(2,1)S(1)}, u32[]{:S(2)}, u32[]{:S(2)}) collective-permute-start(bf16[2,4,64,128]{3,2,1,0:T(8,128)(2,1)S(1)} %convert_element_type.308), channel_id=1, source_target_pairs={{4,0},{8,4},{12,8},{5,1},{9,5},{13,9},{6,2},{10,6},{14,10},{7,3},{... | collective-permute-start | bytes 393224 | tf_op jit(solution)/shard_map/ppermute | solution.py:30
  705.9 14.5 %collective-permute-start.30 = (f32[2,2048]{1,0:T(2,128)S(1)}, f32[2,2048]{1,0:T(2,128)S(1)}, u32[]{:S(2)}, u32[]{:S(2)}) collective-permute-start(f32[2,2048]{1,0:T(2,128)S(1)} %fusion.10), channel_id=1, source_target_pairs={{4,0},{8,4},{12,8},{5,1},{9,5},{13,9},{6,2},{10,6},{14,10},{7,3},{... | collective-permute-start | bytes 49160 | tf_op jit(solution)/shard_map/ppermute | solution.py:25
  780.3 4.2 collective-permute-start.31
  785.4 92.6 %collective-permute-start.37 = (bf16[512,2048]{1,0:T(8,128)(2,1)S(1)}, bf16[512,2048]{1,0:T(8,128)(2,1)S(1)}, u32[]{:S(2)}, u32[]{:S(2)}) collective-permute-start(bf16[512,2048]{1,0:T(8,128)(2,1)S(1)} %add_convert_fusion.1), channel_id=1, source_target_pairs={{0,2},{1,3},{2,0},{3,1},{4,6},{5,7},{6,4},{7,5},{8,10},{9,11},{10,... | collective-permute-start | bytes 6291464 | tf_op jit(solution)/shard_map/ppermute | solution.py:48
  788.5 1.4 collective-permute-start.32
  789.9 46.0 %collective-permute-start.33 = (f32[14,2048]{1,0:T(8,128)S(1)}, f32[14,2048]{1,0:T(8,128)S(1)}, u32[]{:S(2)}, u32[]{:S(2)}) collective-permute-start(f32[14,2048]{1,0:T(8,128)S(1)} %add.340), channel_id=1, source_target_pairs={{0,2},{1,3},{2,0},{3,1},{4,6},{5,7},{6,4},{7,5},{8,10},{9,11},{10,... | collective-permute-start | bytes 344072 | tf_op jit(solution)/shard_map/ppermute | solution.py:124
  836.0 7.0 collective-permute-start.34
  843.0 16.9 %collective-permute-start.35 = (f32[14,2048]{1,0:T(8,128)S(1)}, f32[14,2048]{1,0:T(8,128)S(1)}, u32[]{:S(2)}, u32[]{:S(2)}) collective-permute-start(f32[14,2048]{1,0:T(8,128)S(1)} %add.342), channel_id=1, source_target_pairs={{0,4},{4,0},{8,12},{12,8},{1,5},{5,1},{9,13},{13,9},{2,6},{6,2},{1... | collective-permute-start | bytes 344072 | tf_op jit(solution)/shard_map/ppermute | solution.py:124
  859.9 18.1 %collective-permute-start.36 = (f32[14,2048]{1,0:T(8,128)S(1)}, f32[14,2048]{1,0:T(8,128)S(1)}, u32[]{:S(2)}, u32[]{:S(2)}) collective-permute-start(f32[14,2048]{1,0:T(8,128)S(1)} %add.343), channel_id=1, source_target_pairs={{0,8},{4,12},{8,0},{12,4},{1,9},{5,13},{9,1},{13,5},{2,10},{6,14},... | collective-permute-start | bytes 344072 | tf_op jit(solution)/shard_map/ppermute | solution.py:124
  879.0 98.6 %collective-permute-start.38 = (bf16[512,2048]{1,0:T(8,128)(2,1)S(1)}, bf16[512,2048]{1,0:T(8,128)(2,1)}, u32[]{:S(2)}, u32[]{:S(2)}) collective-permute-start(bf16[512,2048]{1,0:T(8,128)(2,1)S(1)} %add_convert_fusion), channel_id=1, source_target_pairs={{0,1},{1,0},{2,3},{3,2},{4,5},{5,4},{6,7},{7,6},{8,9},{9,8},{10,11... | collective-permute-start | bytes 6291464 | tf_op jit(solution)/shard_map/ppermute | solution.py:48
  (30 other events, 142.1 us)
Sparse Core Ops, SparseCore 0:
  10.7 161.7 all-gather.3
  175.2 149.9 all-gather.5
  327.2 110.6 all-gather.7
  452.5 131.6 reduce-scatter.3
  605.6 172.7 reduce-scatter.5
  781.8 183.2 reduce-scatter.7

commit v6 on v3

--- a/solution.py
+++ b/solution.py
@@ -99,6 +99,27 @@
 
 def swap(x, axis, bit):
     return lax.ppermute(x, axis, [(i, i ^ bit) for i in range(lax.axis_size(axis))])
+
+
+def split_kernel(x_ref, *outs):
+    at = 0
+    for out in outs:
+        out[...] = x_ref[:, at : at + out.shape[1]].astype(jnp.float32)
+        at += out.shape[1]
+
+
+def split_columns(x, widths, name):
+    count = x.shape[0]
+    rows = min(count, 64)
+    return pl.pallas_call(
+        split_kernel,
+        grid=(count // rows,),
+        in_specs=[pl.BlockSpec((rows, x.shape[1]), lambda i: (i, 0))],
+        out_specs=[pl.BlockSpec((rows, width), lambda i: (i, 0)) for width in widths],
+        out_shape=[jax.ShapeDtypeStruct((count, width), jnp.float32) for width in widths],
+        cost_estimate=pl.CostEstimate(flops=x.size, bytes_accessed=6 * x.size, transcendentals=0),
+        name=name,
+    )(x)
 
 
 def owner_scatter_steps(x):
@@ -946,7 +967,7 @@
     )
     early_steps = len(axis_bits("fsdp")) + len(axis_bits("ctx"))
     d_recept, d_key, d_value, g_early = after(d_recept, d_key, d_value, g_early)
-    for _ in range(early_steps - 2):
+    for _ in range(early_steps - 3):
         g_early = early.send(g_early)
     d_lows = [d_recept, d_key, d_value, d_gate_pre]
     weights_time = (w_recept, w_key, w_value, w_gate)
@@ -957,16 +978,17 @@
         ],
         axis=1,
     )
-    *d_lows, _, g_early = after(d_lows[0], *d_lows[1:], grads_time, g_early)
-    g_early = early.send(g_early)
+    *d_lows, _ = after(d_lows[0], *d_lows[1:], grads_time)
     g_time = lax.psum_scatter(grads_time, owners, scatter_dimension=0, tiled=True)
+    back_one = back_from(d_lows, weights_time, mix_one)
+    g_early = early.send(after(g_early, back_one)[0])
     d_input_part, time_small = blend_back(
         (x_low,),
         d_lows,
         [(w_time, at) for at in range(4)],
         keep,
         edge_one,
-        back_from(d_lows, weights_time, mix_one),
+        back_one,
         norm_one,
         mix_one,
         piece_len,
@@ -978,10 +1000,13 @@
     head_small = lax.dynamic_update_slice_in_dim(
         jnp.zeros((4, embedding_extent), jnp.float32), head_small, sharded_layout, 1
     )
-    small_sum = whole_sum(
-        jnp.concatenate([time_small[:6], head_small, chan_small[:4]], axis=0),
-        ("tp", "fsdp", "ctx"),
-    )
+    small_part = jnp.concatenate([time_small[:6], head_small, chan_small[:4]], axis=0)
+
+    def small_total(token):
+        return whole_sum(after(small_part, token)[0], ("fsdp", "ctx", "tp"))
+
+    d_input_sum, small_sum = tp_sum(d_input_part, small_total)
+    g_early = early.send(after(g_early, small_sum)[0])
     owned = embedding_extent // (lax.axis_size("fsdp") * lax.axis_size("ctx"))
     small_owned = lax.dynamic_slice_in_dim(
         small_sum,
@@ -989,21 +1014,18 @@
         owned,
         1,
     )
-    d_input_sum = tp_sum(d_input_part)
     grad_inputs = (d_mixed.astype(jnp.float32) + d_input_sum.astype(jnp.float32)).reshape(
         full_shape
     )
     g_chanvalue = g_chanvalue.astype(jnp.float32)
-    g_chan = g_chan.astype(jnp.float32)
-    g_time = g_time.astype(jnp.float32)
+    g_chankey, g_chanrecept = split_columns(g_chan, (units, fourth_extent), "split_chan")
     g_early = g_early.astype(jnp.float32)
-    g_recept, g_key, g_value = (
-        g_time[:, at * fourth_extent : (at + 1) * fourth_extent] for at in range(3)
-    )
     g_output = g_early[:, :fourth_extent].T
     g_gate = g_early[:, fourth_extent:]
-    g_chankey = g_chan[:, :units]
-    g_chanrecept = g_chan[:, units:]
+    g_time = after(
+        g_time, grad_inputs, result, g_chanvalue, g_chankey, g_chanrecept, g_output, g_gate
+    )[0]
+    g_recept, g_key, g_value = split_columns(g_time, (fourth_extent,) * 3, "split_time")
     return (
         result,
         grad_inputs,

time: 992 us -> 960 us (0.968)
  local copies, waits for them, and re-layouts: 77 us -> 59.7 us
  other arithmetic: 77.5 us -> 62 us
  starting transfers between devices: 70.9 us -> 59 us
    reduce_scatter x1, waiting for transfers between devices: 0.02 us -> 38.5 us  [per_device(): lax.psum_scatter(grads_time, owners, scatter_dimension=0, tiled=True)]
    ppermute x15, waiting for transfers between devices: 165 us -> 128 us  [partner(): return lax.ppermute(x, 'tp', [(i, i ^ bit) for i in range(count)])]
    ppermute x3, waiting for transfers between devices: 63.9 us -> 46.4 us  [swap(): lax.ppermute(x, axis, [(i, i ^ bit) for i in range(lax.axis_size(axis))])]
    ppermute x5, waiting for transfers between devices: 30.2 us -> 44.8 us  [whole_sum(): x = x + lax.ppermute(x, axis, [(i, i ^ bit) for i in range(count)])]
    unnamed x123 -> x112, local copies, waits for them, and re-layouts: 27.7 us -> 16.6 us
  transfers between devices with their start and end apart: 45 -> 45, of which waited for: 27 -> 29; matrix products, arithmetic and copies ran while one was open for 26% -> 24% of each run, Pallas kernels for 18% -> 19%
where the time goes in v6:
time: 960 us; the launch traced here: 953 us
  waiting for transfers between devices  440 us (46%)
  Pallas kernels  185 us (19%)
  matrix products  130 us (14%)
  other arithmetic  62 us (6%)
  local copies, waits for them, and re-layouts  59.7 us (6%)
  starting transfers between devices  59 us (6%)
  between operations  15.8 us (2%)
    ppermute x15, waiting for transfers between devices, partner(): return lax.ppermute(x, 'tp', [(i, i ^ bit) for i in range(count)])  128 us
    all_gather x1, waiting for transfers between devices, per_device(): lax.all_gather(jnp.concatenate([acceptor_matrix, lookup_matrix, payload_m...  108 us
    pallas_call x2, Pallas kernels, blend_back(): pl.pallas_call(partial(blend_back_kernel, len(xs), mixes, per_seq, int(ow...  89 us
    dot_general x8, matrix products, matmul(): return jnp.dot(left, right, preferred_element_type=jnp.float32)  64.2 us
    pallas_call x4, Pallas kernels, pair_call(): pl.pallas_call(kernel, grid=(pairs, seqs), in_specs=[specs[kind] for kind...  49.4 us
    ppermute x3, waiting for transfers between devices, swap(): lax.ppermute(x, axis, [(i, i ^ bit) for i in range(lax.axis_size(axis))])  46.4 us
    ppermute x5, waiting for transfers between devices, whole_sum(): x = x + lax.ppermute(x, axis, [(i, i ^ bit) for i in range(count)])  44.8 us
    pallas_call x2, Pallas kernels, blend(): pl.pallas_call(partial(blend_kernel, len(xs), mixes, per_seq), grid=(toke...  39.9 us
  transfers between devices with their start and end apart: 45, of which 29 were waited for; matrix products, arithmetic and copies ran while one was open for 24% of the time, Pallas kernels for 19%

profile of v6, /device:TPU:0, one launch (start us, length us, event | category | flops | bytes accessed | tf_op | source)
XLA Modules:
  0.0 952.7 jit_solution(16169128637852669458)
XLA Ops:
  17.3 4.9 collective-permute-start.1
  22.2 4.5 collective-permute-start.2
  38.3 20.8 %blend_one.1 = (bf16[1024,2048]{1,0:T(8,128)(2,1)}, bf16[1024,2048]{1,0:T(8,128)(2,1)}, bf16[1024,2048]{1,0:T(8,128)(2,1)}, bf16[1024,2048]{1,0:T(8,128)(2,1)}) custom-call(bf16[1024,2048]{1,0:T(8,128)(2,1)} %bitcast.177, f32[1024,1]{1,0:T(8,128)} %bitcast.187, f32[2,1,2048]{2,1,0:T(1,128)} %broadcast_in_dim.20.refs_2_.refs_11_, ...), custom_call_target="tpu_custom_call" | custom-call | flops 41943040 | bytes 20971520 | tf_op jit(solution)/shard_map/blend_one/pallas_call | solution.py:525
  59.2 108.1 %all-gather.4.cloned.1.call-done.refs_6_.refs_7_.refs_8_.refs_9_ = bf16[2048,2560]{1,0:T(8,128)(2,1)} async-done(((bf16[256,2560]{1,0:T(8,128)(2,1)}), bf16[2048,2560]{1,0:T(8,128)(2,1)}) %all-gather.4.cloned.1.call-update) | async-done | bytes 10485776 | tf_op jit(solution)/shard_map/all_gather | solution.py:777
  167.2 6.3 fusion.39.k_ref
  173.5 5.0 fusion.42.v_ref
  178.5 6.9 carry.1
  186.4 3.5 collective-permute-start.4
  191.2 3.0 collective-permute-start.6
  194.2 6.3 fusion.36.r_ref
  200.5 5.3 fusion.25.gate_ref
  208.2 11.3 %mix.1 = (bf16[1024,512]{1,0:T(8,128)(2,1)}, f32[1024,512]{1,0:T(8,128)}) custom-call(bf16[1024,512]{1,0:T(8,128)(2,1)} %fusion.36.r_ref, bf16[1024,512]{1,0:T(8,128)(2,1)} %fusion.39.k_ref, bf16[1024,512]{1,0:T(8,128)(2,1)} %fusion.42.v_ref, f32[1024,512]{1,0:T(8,128)} %fusion.25.gate_ref, f32[1,512]{1,0:T(1,128)} %bitcast.208, ...), custom_call_target="tpu_custom_call" | custom-call | flops 1073741824 | bytes 11087872 | tf_op jit(solution)/shard_map/mix/pallas_call | solution.py:424
  219.6 4.3 convolution_convert_fusion.3
  226.2 4.3 collective-permute-done.7
  230.5 3.0 add_convert_fusion.5
  235.1 46.2 %collective-permute-done.8 = bf16[512,2048]{1,0:T(8,128)(2,1)} collective-permute-done((bf16[512,2048]{1,0:T(8,128)(2,1)S(1)}, bf16[512,2048]{1,0:T(8,128)(2,1)}, u32[]{:S(2)}, u32[]{:S(2)}) %collective-permute-start.8) | collective-permute-done | bytes 2097184 | tf_op jit(solution)/shard_map/ppermute | solution.py:48
  281.4 3.7 add_convert_fusion.4
  285.1 4.3 collective-permute-done.9
  289.4 3.7 maximum_select_fusion.refs_1_.refs_3_
  295.7 11.2 %collective-permute-start.10 = (f32[2,2048]{1,0:T(2,128)S(1)}, f32[2,2048]{1,0:T(2,128)S(1)}, u32[]{:S(2)}, u32[]{:S(2)}) collective-permute-start(f32[2,2048]{1,0:T(2,128)S(1)} %fusion.54), channel_id=1, source_target_pairs={{0,4},{4,8},{8,12},{1,5},{5,9},{9,13},{2,6},{6,10},{10,14},{3,7},{... | collective-permute-start | bytes 49160 | tf_op jit(solution)/shard_map/ppermute | solution.py:25
  309.1 19.0 %blend_two.1 = (bf16[1024,2048]{1,0:T(8,128)(2,1)}, bf16[1024,2048]{1,0:T(8,128)(2,1)}) custom-call(bf16[1024,2048]{1,0:T(8,128)(2,1)} %bitcast.178, bf16[1024,2048]{1,0:T(8,128)(2,1)} %copy-done, f32[1024,1]{1,0:T(8,128)} %bitcast.188, f32[2,1,2048]{2,1,0:T(1,128)} %copy.99.refs_3_.refs_9_, f32[2,2048]{1,0:T(2,128)} %get-tuple-element.238.refs_4_.refs_11_, ...), custom_call_target="tpu_custom_call" | custom-call | flops 41943040 | bytes 16777216 | tf_op jit(solution)/shard_map/blend_two/pallas_call | solution.py:525
  330.7 6.9 constant_dynamic-update-slice_fusion.7
  339.3 22.8 %collective-permute-done.11 = bf16[1024,512]{1,0:T(8,128)(2,1)S(1)} collective-permute-done((bf16[1024,512]{1,0:T(8,128)(2,1)}, bf16[1024,512]{1,0:T(8,128)(2,1)S(1)}, u32[]{:S(2)}, u32[]{:S(2)}) %collective-permute-start.11) | collective-permute-done | bytes 1048608 | tf_op jit(solution)/shard_map/ppermute | solution.py:48
  362.1 13.6 %multiply_convert_fusion.1 = (bf16[1024,1792]{1,0:T(8,128)(2,1)S(1)}, f32[1024,1792]{1,0:T(8,128)}) fusion(bf16[1024,2048]{1,0:T(8,128)(2,1)} %get-tuple-element.78, bf16[2048,2304]{1,0:T(8,128)(2,1)} %all-gather.6.cloned.1.call-done.refs_6_), kind=kOutput, calls=%fused_computation.5 | convolution fusion | flops 7521697792 | bytes 22544384 | tf_op jit(solution)/shard_map/dot_general | solution.py:183
  379.4 12.1 %convolution_convert_fusion.1 = bf16[1792,2048]{1,0:T(8,128)(2,1)} fusion(bf16[1024,1792]{1,0:T(8,128)(2,1)S(1)} %get-tuple-element.79, bf16[1024,2048]{1,0:T(8,128)(2,1)} %constant_dynamic-update-slice_fusion.4), kind=kOutput, calls=%fused_computation.3 | convolution fusion | flops 7519862784 | bytes 15204352 | tf_op jit(solution)/shard_map/dot_general | solution.py:187
  391.5 37.8 %all-gather.8.cloned.1.call-done = bf16[2048,1792]{0,1:T(8,128)(2,1)} async-done(((bf16[256,1792]{0,1:T(8,128)(2,1)}), bf16[2048,1792]{0,1:T(8,128)(2,1)}) %all-gather.8.cloned.1.call-update) | async-done | bytes 7340048 | tf_op jit(solution)/shard_map/all_gather | solution.py:797
  429.3 11.3 %convolution_convert_fusion.2 = bf16[1024,2048]{1,0:T(8,128)(2,1)S(1)} fusion(bf16[1024,1792]{1,0:T(8,128)(2,1)} %copy-done.46, bf16[2048,1792]{0,1:T(8,128)(2,1)} %all-gather.8.cloned.1.call-done), kind=kOutput, calls=%fused_computation.23 | convolution fusion | flops 7518289920 | bytes 15204352 | tf_op jit(solution)/shard_map/dot_general | solution.py:193
  450.4 14.2 %multiply_convert_fusion.refs_4_ = bf16[1024,1792]{1,0:T(8,128)(2,1)} fusion(f32[1024,1792]{1,0:T(8,128)} %get-tuple-element.232, bf16[1024,2048]{1,0:T(8,128)(2,1)} %constant_dynamic-update-slice_fusion.4, bf16[2048,1792]{0,1:T(8,128)(2,1)} %all-gather.8.cloned.1.call-done), kind=kOutput, calls=%fused_computation.4 | convolution fusion | flops 7523532800 | bytes 22544384 | tf_op jit(solution)/shard_map/dot_general | solution.py:183
  467.6 6.6 collective-permute-done.16
  474.2 4.7 fusion.19
  483.0 3.2 collective-permute-done.17
  486.8 44.9 %blend_two_back.1 = (bf16[1024,2048]{1,0:T(8,128)(2,1)}, f32[8,2048]{1,0:T(8,128)}) custom-call(bf16[1024,2048]{1,0:T(8,128)(2,1)} %bitcast.180, bf16[1024,2048]{1,0:T(8,128)(2,1)} %copy-done, bf16[1024,2048]{1,0:T(8,128)(2,1)} %bitcast.181, bf16[1024,2048]{1,0:T(8,128)(2,1)} %copy-done, bf16[1024,1792]{1,0:T(8,128)(2,1)} %multiply_convert_fusion.refs_4_, ...), custom_call_target="tpu_custom_call" | custom-call | flops 9663676416 | bytes 16777216 | tf_op jit(solution)/shard_map/blend_two_back/pallas_call | solution.py:685
  533.7 4.1 collective-permute-done.18
  540.4 10.0 %convolution_convert_fusion = bf16[2048,1792]{1,0:T(8,128)(2,1)S(1)} fusion(bf16[1024,2048]{1,0:T(8,128)(2,1)} %get-tuple-element.78, bf16[1024,1792]{1,0:T(8,128)(2,1)S(1)} %copy-done.37), kind=kOutput, calls=%fused_computation.2 | convolution fusion | flops 7519862784 | bytes 15204352 | tf_op jit(solution)/shard_map/dot_general | solution.py:187
  552.9 4.6 pad_maximum_fusion
  557.5 29.1 %collective-permute-done.19 = bf16[512,2048]{1,0:T(8,128)(2,1)} collective-permute-done((bf16[512,2048]{1,0:T(8,128)(2,1)S(1)}, bf16[512,2048]{1,0:T(8,128)(2,1)}, u32[]{:S(2)}, u32[]{:S(2)}) %collective-permute-start.19) | collective-permute-done | bytes 2097184 | tf_op jit(solution)/shard_map/ppermute | solution.py:48
  589.1 4.1 collective-permute-done.20
  593.2 3.8 maximum_select_fusion.1
  597.1 6.5 fusion.21.dj_ref
  603.6 11.3 %gate_back.1 = (bf16[1024,512]{1,0:T(8,128)(2,1)}, bf16[1024,512]{1,0:T(8,128)(2,1)}, f32[2,4,64,128]{3,2,1,0:T(8,128)}, f32[8,512]{1,0:T(8,128)}) custom-call(f32[1024,512]{1,0:T(8,128)} %fusion.21.dj_ref, f32[1024,512]{1,0:T(8,128)} %get-tuple-element.85.attend_ref, f32[1024,512]{1,0:T(8,128)} %fusion.25.gate_ref, bf16[1024,512]{1,0:T(8,128)(2,1)} %fusion.36.r_ref, ...), custom_call_target="tpu_custom_call" | custom-call | flops 67108864 | bytes 14749696 | tf_op jit(solution)/shard_map/gate_back/pallas_call | solution.py:424
  615.0 4.7 convolution_convert_fusion.8
  622.3 2.6 pad_maximum_fusion.2
  624.9 7.9 reshape.218
  632.8 6.4 constant_dynamic-slice_fusion.4
  654.4 8.9 collective-permute-done.24
  663.4 9.3 collective-permute-done.25
  673.5 19.9 %mix_back.1 = (bf16[1024,512]{1,0:T(8,128)(2,1)}, bf16[1024,512]{1,0:T(8,128)(2,1)}, bf16[1024,512]{1,0:T(8,128)(2,1)}, f32[8,512]{1,0:T(8,128)}) custom-call(bf16[1024,512]{1,0:T(8,128)(2,1)} %fusion.36.r_ref, bf16[1024,512]{1,0:T(8,128)(2,1)} %fusion.39.k_ref, bf16[1024,512]{1,0:T(8,128)(2,1)} %fusion.42.v_ref, ...), custom_call_target="tpu_custom_call" | custom-call | flops 3221225472 | bytes 9523200 | tf_op jit(solution)/shard_map/mix_back/pallas_call | solution.py:424
  693.4 6.4 collective-permute-done.27
  701.2 2.6 fusion.4
  711.3 3.1 pad_maximum_fusion.1
  727.6 8.5 collective-permute-done.28
  738.8 44.1 %blend_one_back.1 = (bf16[1024,2048]{1,0:T(8,128)(2,1)}, f32[8,2048]{1,0:T(8,128)}) custom-call(bf16[1024,2048]{1,0:T(8,128)(2,1)} %bitcast.182, bf16[1024,2048]{1,0:T(8,128)(2,1)} %bitcast.183, bf16[1024,512]{1,0:T(8,128)(2,1)} %get-tuple-element.95.refs_2_, bf16[1024,512]{1,0:T(8,128)(2,1)} %get-tuple-element.96.refs_3_, ...), custom_call_target="tpu_custom_call" | custom-call | flops 8589934592 | bytes 16777216 | tf_op jit(solution)/shard_map/blend_one_back/pallas_call | solution.py:685
  783.0 14.6 %collective-permute-done.29 = bf16[2,256,1024]{1,2,0:T(8,128)(2,1)} collective-permute-done((bf16[2,256,1024]{1,2,0:T(8,128)(2,1)S(1)}, bf16[2,256,1024]{1,2,0:T(8,128)(2,1)}, u32[]{:S(2)}, u32[]{:S(2)}) %collective-permute-start.29) | collective-permute-done | bytes 1048608 | tf_op jit(solution)/shard_map/ppermute | solution.py:101
  801.1 4.1 collective-permute-done.30
  810.6 7.4 collective-permute-done.31
  818.7 13.4 %collective-permute-done.32 = f32[14,2048]{1,0:T(8,128)S(1)} collective-permute-done((f32[14,2048]{1,0:T(8,128)S(1)}, f32[14,2048]{1,0:T(8,128)S(1)}, u32[]{:S(2)}, u32[]{:S(2)}) %collective-permute-start.32) | collective-permute-done | bytes 114720 | tf_op jit(solution)/shard_map/ppermute | solution.py:146
  832.5 17.2 %collective-permute-done.33 = f32[14,2048]{1,0:T(8,128)S(1)} collective-permute-done((f32[14,2048]{1,0:T(8,128)S(1)}, f32[14,2048]{1,0:T(8,128)S(1)}, u32[]{:S(2)}, u32[]{:S(2)}) %collective-permute-start.33) | collective-permute-done | bytes 114720 | tf_op jit(solution)/shard_map/ppermute | solution.py:146
  851.2 5.5 collective-permute-done.35
  860.8 2.6 convert_element_type.365
  863.4 3.6 split_chan.1
  867.7 25.4 %collective-permute-done.38 = bf16[256,1024]{0,1:T(8,128)(2,1)} collective-permute-done((bf16[256,1024]{0,1:T(8,128)(2,1)}, bf16[256,1024]{0,1:T(8,128)(2,1)}, u32[]{:S(2)}, u32[]{:S(2)}) %collective-permute-start.38) | collective-permute-done | bytes 524320 | tf_op jit(solution)/shard_map/ppermute | solution.py:101
  896.1 7.4 convert_add_fusion
  903.5 38.5 %reduce-scatter.8.cloned.1.call-done.x_ref = bf16[256,1536]{1,0:T(8,128)(2,1)} async-done(((bf16[2048,1536]{1,0:T(8,128)(2,1)}), bf16[256,1536]{1,0:T(8,128)(2,1)}) %reduce-scatter.8.cloned.1.call-update) | async-done | bytes 786448 | tf_op jit(solution)/shard_map/reduce_scatter | solution.py:982
  942.0 3.4 split_time.1
  (284 shorter events, 131.5 us)
Async XLA Ops:
  7.2 23.5 %copy-start.32 = (f32[2048]{0:T(1024)S(1)}, f32[2048]{0:T(1024)}, u32[]{:S(2)}) copy-start(f32[2048]{0:T(1024)} %param.35) | copy-start | bytes 24580
  7.2 23.5 %copy-start.31 = (f32[2048]{0:T(1024)S(1)}, f32[2048]{0:T(1024)}, u32[]{:S(2)}) copy-start(f32[2048]{0:T(1024)} %param.36) | copy-start | bytes 24580
  7.2 24.1 %copy-start.22 = (f32[2048]{0:T(1024)S(1)}, f32[2048]{0:T(1024)}, u32[]{:S(2)}) copy-start(f32[2048]{0:T(1024)} %param.37) | copy-start | bytes 24580
  7.3 24.1 %copy-start.24 = (f32[2048]{0:T(1024)S(1)}, f32[2048]{0:T(1024)}, u32[]{:S(2)}) copy-start(f32[2048]{0:T(1024)} %param.38) | copy-start | bytes 24580
  7.3 24.1 %copy-start.26 = (f32[2048]{0:T(1024)S(1)}, f32[2048]{0:T(1024)}, u32[]{:S(2)}) copy-start(f32[2048]{0:T(1024)} %param.39) | copy-start | bytes 24580
  7.3 24.1 %copy-start.28 = (f32[2048]{0:T(1024)S(1)}, f32[2048]{0:T(1024)}, u32[]{:S(2)}) copy-start(f32[2048]{0:T(1024)} %param.40) | copy-start | bytes 24580
  7.3 159.9 %all-gather.4.cloned.1.call-start = ((), (), s32[]{:S(2)}) async-start(), calls=%async_computation.3 | async-start | bytes 11796480 | tf_op jit(solution)/shard_map/all_gather | solution.py:777
  13.5 314.6 %all-gather.6.cloned.1.call-start = ((), (), s32[]{:S(2)}) async-start(), calls=%async_computation.4 | async-start | bytes 10616832 | tf_op jit(solution)/shard_map/all_gather | solution.py:785
  14.7 414.6 %all-gather.8.cloned.1.call-start = ((), (), s32[]{:S(2)}) async-start(), calls=%async_computation.5 | async-start | bytes 8257536 | tf_op jit(solution)/shard_map/all_gather | solution.py:797
  17.3 156.3 %copy-start.35 = (bf16[2,4,1,128]{3,2,1,0:T(2,128)(2,1)}, bf16[2,4,1,128]{3,2,1,0:T(2,128)(2,1)S(1)}, u32[]{:S(2)}) copy-start(bf16[2,4,1,128]{3,2,1,0:T(2,128)(2,1)S(1)} %get-tuple-element.194) | copy-start | bytes 6148
  17.3 20.4 %collective-permute-start.1 = (bf16[2,4,1,128]{3,2,1,0:T(2,128)(2,1)S(1)}, bf16[2,4,1,128]{3,2,1,0:T(2,128)(2,1)S(1)}, u32[]{:S(2)}, u32[]{:S(2)}) collective-permute-start(bf16[2,4,1,128]{3,2,1,0:T(2,128)(2,1)S(1)} %get-tuple-element.194), channel_id=1, source_target_pairs={{0,4},{4,8},{8,12},{1,5},{5,9},{9,13},{2,6},{6,10},{10,14},{3,7},{... | collective-permute-start | bytes 6152 | tf_op jit(solution)/shard_map/ppermute | solution.py:30
  22.2 15.5 %collective-permute-start.2 = (bf16[2,4,1,128]{3,2,1,0:T(2,128)(2,1)S(1)}, bf16[2,4,1,128]{3,2,1,0:T(2,128)(2,1)S(1)}, u32[]{:S(2)}, u32[]{:S(2)}) collective-permute-start(bf16[2,4,1,128]{3,2,1,0:T(2,128)(2,1)S(1)} %get-tuple-element.194), channel_id=1, source_target_pairs={{0,8},{4,12},{1,9},{5,13},{2,10},{6,14},{3,11},{7,15},{16,24},{20,... | collective-permute-start | bytes 6152 | tf_op jit(solution)/shard_map/ppermute | solution.py:30
  26.7 10.9 %collective-permute-start.3 = (bf16[2,4,1,128]{3,2,1,0:T(2,128)(2,1)S(1)}, bf16[2,4,1,128]{3,2,1,0:T(2,128)(2,1)S(1)}, u32[]{:S(2)}, u32[]{:S(2)}) collective-permute-start(bf16[2,4,1,128]{3,2,1,0:T(2,128)(2,1)S(1)} %get-tuple-element.194), channel_id=1, source_target_pairs={{0,12},{1,13},{2,14},{3,15},{16,28},{17,29},{18,30},{19,31}} | collective-permute-start | bytes 6152 | tf_op jit(solution)/shard_map/ppermute | solution.py:30
  29.3 8.4 collective-permute-start
  186.4 19.5 %collective-permute-start.4 = (bf16[2,4,64,128]{3,2,1,0:T(8,128)(2,1)S(1)}, bf16[2,4,64,128]{3,2,1,0:T(8,128)(2,1)S(1)}, u32[]{:S(2)}, u32[]{:S(2)}) collective-permute-start(bf16[2,4,64,128]{3,2,1,0:T(8,128)(2,1)S(1)} %convert_element_type.298), channel_id=1, source_target_pairs={{0,12},{1,13},{2,14},{3,15},{16,28},{17,29},{18,30},{19,31}} | collective-permute-start | bytes 393224 | tf_op jit(solution)/shard_map/ppermute | solution.py:30
  189.9 16.0 %collective-permute-start.5 = (bf16[2,4,64,128]{3,2,1,0:T(8,128)(2,1)S(1)}, bf16[2,4,64,128]{3,2,1,0:T(8,128)(2,1)S(1)}, u32[]{:S(2)}, u32[]{:S(2)}) collective-permute-start(bf16[2,4,64,128]{3,2,1,0:T(8,128)(2,1)S(1)} %convert_element_type.298), channel_id=1, source_target_pairs={{0,8},{4,12},{1,9},{5,13},{2,10},{6,14},{3,11},{7,15},{16,24},{20,... | collective-permute-start | bytes 393224 | tf_op jit(solution)/shard_map/ppermute | solution.py:30
  191.2 16.3 %collective-permute-start.6 = (bf16[2,4,64,128]{3,2,1,0:T(8,128)(2,1)S(1)}, bf16[2,4,64,128]{3,2,1,0:T(8,128)(2,1)S(1)}, u32[]{:S(2)}, u32[]{:S(2)}) collective-permute-start(bf16[2,4,64,128]{3,2,1,0:T(8,128)(2,1)S(1)} %convert_element_type.298), channel_id=1, source_target_pairs={{0,4},{4,8},{8,12},{1,5},{5,9},{9,13},{2,6},{6,10},{10,14},{3,7},{... | collective-permute-start | bytes 393224 | tf_op jit(solution)/shard_map/ppermute | solution.py:30
  226.1 4.4 collective-permute-start.7
  233.5 47.8 %collective-permute-start.8 = (bf16[512,2048]{1,0:T(8,128)(2,1)S(1)}, bf16[512,2048]{1,0:T(8,128)(2,1)}, u32[]{:S(2)}, u32[]{:S(2)}) collective-permute-start(bf16[512,2048]{1,0:T(8,128)(2,1)S(1)} %add_convert_fusion.5), channel_id=1, source_target_pairs={{0,2},{1,3},{2,0},{3,1},{4,6},{5,7},{6,4},{7,5},{8,10},{9,11},{10,... | collective-permute-start | bytes 6291464 | tf_op jit(solution)/shard_map/ppermute | solution.py:48
  235.1 362.0 %reduce-scatter.4.cloned.1.call-start = ((), (), s32[]{:S(2)}) async-start(), calls=%async_computation.6 | async-start | bytes 8257536 | tf_op jit(solution)/shard_map/reduce_scatter | solution.py:876
  285.0 4.4 collective-permute-start.9
  285.0 21.9 %copy-start.20 = (f32[2048]{0:T(1024)S(1)}, f32[2048]{0:T(1024)}, u32[]{:S(2)}) copy-start(f32[2048]{0:T(1024)} %param.47) | copy-start | bytes 24580
  285.1 21.9 %copy-start.21 = (f32[2048]{0:T(1024)S(1)}, f32[2048]{0:T(1024)}, u32[]{:S(2)}) copy-start(f32[2048]{0:T(1024)} %param.48) | copy-start | bytes 24580
  285.1 21.9 %copy-start.33 = (f32[2048]{0:T(1024)S(1)}, f32[2048]{0:T(1024)}, u32[]{:S(2)}) copy-start(f32[2048]{0:T(1024)} %param.46) | copy-start | bytes 24580
  285.1 21.9 %copy-start.34 = (f32[2048]{0:T(1024)S(1)}, f32[2048]{0:T(1024)}, u32[]{:S(2)}) copy-start(f32[2048]{0:T(1024)} %param.45) | copy-start | bytes 24580
  295.7 12.8 %collective-permute-start.10 = (f32[2,2048]{1,0:T(2,128)S(1)}, f32[2,2048]{1,0:T(2,128)S(1)}, u32[]{:S(2)}, u32[]{:S(2)}) collective-permute-start(f32[2,2048]{1,0:T(2,128)S(1)} %fusion.54), channel_id=1, source_target_pairs={{0,4},{4,8},{8,12},{1,5},{5,9},{9,13},{2,6},{6,10},{10,14},{3,7},{... | collective-permute-start | bytes 49160 | tf_op jit(solution)/shard_map/ppermute | solution.py:25
  337.6 24.5 %collective-permute-start.11 = (bf16[1024,512]{1,0:T(8,128)(2,1)}, bf16[1024,512]{1,0:T(8,128)(2,1)S(1)}, u32[]{:S(2)}, u32[]{:S(2)}) collective-permute-start(bf16[1024,512]{1,0:T(8,128)(2,1)} %get-tuple-element.236), channel_id=1, source_target_pairs={{0,2},{1,3},{2,0},{3,1},{4,6},{5,7},{6,4},{7,5},{8,10},{9,11},{10,... | collective-permute-start | bytes 3145736 | tf_op jit(solution)/shard_map/ppermute | solution.py:48
  339.3 37.7 %collective-permute-start.12 = (bf16[1024,512]{1,0:T(8,128)(2,1)}, bf16[1024,512]{1,0:T(8,128)(2,1)S(1)}, u32[]{:S(2)}, u32[]{:S(2)}) collective-permute-start(bf16[1024,512]{1,0:T(8,128)(2,1)} %get-tuple-element.236), channel_id=1, source_target_pairs={{0,1},{1,0},{2,3},{3,2},{4,5},{5,4},{6,7},{7,6},{8,9},{9,8},{10,11... | collective-permute-start | bytes 3145736 | tf_op jit(solution)/shard_map/ppermute | solution.py:48
  362.1 16.1 %collective-permute-start.13 = (bf16[1024,512]{1,0:T(8,128)(2,1)S(1)}, bf16[1024,512]{1,0:T(8,128)(2,1)S(1)}, u32[]{:S(2)}, u32[]{:S(2)}) collective-permute-start(bf16[1024,512]{1,0:T(8,128)(2,1)S(1)} %collective-permute-done.11), channel_id=1, source_target_pairs={{0,1},{1,0},{2,3},{3,2},{4,5},{5,4},{6,7},{7,6},{8,9},{9,8},{10,11... | collective-permute-start | bytes 3145736 | tf_op jit(solution)/shard_map/ppermute | solution.py:48
  443.8 3.0 collective-permute-start.15
  443.8 355.2 %reduce-scatter.6.cloned.1.call-start = ((), (), s32[]{:S(2)}) async-start(), calls=%async_computation.7 | async-start | bytes 10616832 | tf_op jit(solution)/shard_map/reduce_scatter | solution.py:920
  444.0 23.6 %collective-permute-start.14 = (bf16[1024,512]{1,0:T(8,128)(2,1)S(1)}, bf16[1024,512]{1,0:T(8,128)(2,1)}, u32[]{:S(2)}, u32[]{:S(2)}) collective-permute-start(bf16[1024,512]{1,0:T(8,128)(2,1)S(1)} %get-tuple-element.208), channel_id=1, source_target_pairs={{0,1},{1,0},{2,3},{3,2},{4,5},{5,4},{6,7},{7,6},{8,9},{9,8},{10,11... | collective-permute-start | bytes 3145736 | tf_op jit(solution)/shard_map/ppermute | solution.py:48
  446.8 18.8 %slice-start = ((s8[9437184]{0:T(1024)(128)(4,1)}), s8[4194304]{0:T(1024)(128)(4,1)S(1)}, s32[]{:S(2)}) async-start(s8[9437184]{0:T(1024)(128)(4,1)} %bitcast.185), calls=%async_computation.9 | async-start | bytes 8388608
  448.8 25.4 %collective-permute-start.16 = (bf16[1024,512]{1,0:T(8,128)(2,1)S(1)}, bf16[1024,512]{1,0:T(8,128)(2,1)}, u32[]{:S(2)}, u32[]{:S(2)}) collective-permute-start(bf16[1024,512]{1,0:T(8,128)(2,1)S(1)} %add_convert_fusion.7), channel_id=1, source_target_pairs={{0,2},{1,3},{2,0},{3,1},{4,6},{5,7},{6,4},{7,5},{8,10},{9,11},{10,... | collective-permute-start | bytes 3145736 | tf_op jit(solution)/shard_map/ppermute | solution.py:48
  450.4 15.2 %slice-start.1 = ((s8[9437184]{0:T(1024)(128)(4,1)}), s8[4194304]{0:T(1024)(128)(4,1)S(1)}, s32[]{:S(2)}) async-start(s8[9437184]{0:T(1024)(128)(4,1)} %bitcast.185), calls=%async_computation.10 | async-start | bytes 8388608
  450.4 15.2 %slice-start.2 = ((s8[9437184]{0:T(1024)(128)(4,1)}), s8[1048576]{0:T(1024)(128)(4,1)S(1)}, s32[]{:S(2)}) async-start(s8[9437184]{0:T(1024)(128)(4,1)} %bitcast.185), calls=%async_computation.11 | async-start | bytes 2097152
  479.5 6.7 collective-permute-start.17
  533.6 4.2 collective-permute-start.18
  538.8 11.6 %copy-start.12 = (bf16[1024,512]{1,0:T(8,128)(2,1)S(1)}, bf16[1024,512]{1,0:T(8,128)(2,1)}, u32[]{:S(2)}) copy-start(bf16[1024,512]{1,0:T(8,128)(2,1)} %copy-done.11) | copy-start | bytes 3145732
  538.8 11.6 %copy-start.44 = (bf16[1024,2048]{1,0:T(8,128)(2,1)S(1)}, bf16[1024,2048]{1,0:T(8,128)(2,1)}, u32[]{:S(2)}) copy-start(bf16[1024,2048]{1,0:T(8,128)(2,1)} %get-tuple-element.77) | copy-start | bytes 12582916
  538.8 47.8 %collective-permute-start.19 = (bf16[512,2048]{1,0:T(8,128)(2,1)S(1)}, bf16[512,2048]{1,0:T(8,128)(2,1)}, u32[]{:S(2)}, u32[]{:S(2)}) collective-permute-start(bf16[512,2048]{1,0:T(8,128)(2,1)S(1)} %add_convert_fusion.3), channel_id=1, source_target_pairs={{0,2},{1,3},{2,0},{3,1},{4,6},{5,7},{6,4},{7,5},{8,10},{9,11},{10,... | collective-permute-start | bytes 6291464 | tf_op jit(solution)/shard_map/ppermute | solution.py:48
  589.0 4.2 collective-permute-start.20
  597.1 344.9 %reduce-scatter.8.cloned.1.call-start = ((), (), s32[]{:S(2)}) async-start(), calls=%async_computation.8 | async-start | bytes 7077888 | tf_op jit(solution)/shard_map/reduce_scatter | solution.py:982
  603.6 11.3 %copy-start.45 = (bf16[1024,512]{1,0:T(8,128)(2,1)S(1)}, bf16[1024,512]{1,0:T(8,128)(2,1)}, u32[]{:S(2)}) copy-start(bf16[1024,512]{1,0:T(8,128)(2,1)} %get-tuple-element.76) | copy-start | bytes 3145732
  639.2 11.3 %copy-start.17 = (f32[2,4,64,128]{3,2,1,0:T(8,128)S(1)}, f32[2,4,64,128]{3,2,1,0:T(8,128)}, u32[]{:S(2)}) copy-start(f32[2,4,64,128]{3,2,1,0:T(8,128)} %get-tuple-element.87) | copy-start | bytes 786436
  640.7 59.1 %collective-permute-start.27 = (bf16[2,2,256,1024]{2,3,0,1:T(8,128)(2,1)}, bf16[2,2,256,1024]{2,3,0,1:T(8,128)(2,1)S(1)}, u32[]{:S(2)}, u32[]{:S(2)}) collective-permute-start(bf16[2,2,256,1024]{2,3,0,1:T(8,128)(2,1)} %bitcast.175), channel_id=1, source_target_pairs={{0,16},{16,0},{1,17},{17,1},{2,18},{18,2},{3,19},{19,3},{4,20},{20... | collective-permute-start | bytes 6291464 | tf_op jit(solution)/shard_map/ppermute | solution.py:101
  642.5 5.8 collective-permute-start.21
  643.8 6.7 collective-permute-start.22
  645.1 9.4 collective-permute-start.23
  650.5 12.9 %collective-permute-start.24 = (bf16[2,4,64,128]{3,2,1,0:T(8,128)(2,1)S(1)}, bf16[2,4,64,128]{3,2,1,0:T(8,128)(2,1)S(1)}, u32[]{:S(2)}, u32[]{:S(2)}) collective-permute-start(bf16[2,4,64,128]{3,2,1,0:T(8,128)(2,1)S(1)} %convert_element_type.341), channel_id=1, source_target_pairs={{12,0},{13,1},{14,2},{15,3},{28,16},{29,17},{30,18},{31,19}} | collective-permute-start | bytes 393224 | tf_op jit(solution)/shard_map/ppermute | solution.py:30
  651.8 20.9 %collective-permute-start.25 = (bf16[2,4,64,128]{3,2,1,0:T(8,128)(2,1)S(1)}, bf16[2,4,64,128]{3,2,1,0:T(8,128)(2,1)S(1)}, u32[]{:S(2)}, u32[]{:S(2)}) collective-permute-start(bf16[2,4,64,128]{3,2,1,0:T(8,128)(2,1)S(1)} %convert_element_type.341), channel_id=1, source_target_pairs={{8,0},{12,4},{9,1},{13,5},{10,2},{14,6},{11,3},{15,7},{24,16},{28,... | collective-permute-start | bytes 393224 | tf_op jit(solution)/shard_map/ppermute | solution.py:30
  653.1 19.6 %collective-permute-start.26 = (bf16[2,4,64,128]{3,2,1,0:T(8,128)(2,1)S(1)}, bf16[2,4,64,128]{3,2,1,0:T(8,128)(2,1)S(1)}, u32[]{:S(2)}, u32[]{:S(2)}) collective-permute-start(bf16[2,4,64,128]{3,2,1,0:T(8,128)(2,1)S(1)} %convert_element_type.341), channel_id=1, source_target_pairs={{4,0},{8,4},{12,8},{5,1},{9,5},{13,9},{6,2},{10,6},{14,10},{7,3},{... | collective-permute-start | bytes 393224 | tf_op jit(solution)/shard_map/ppermute | solution.py:30
  693.4 10.4 %copy-start.8 = (bf16[1024,512]{1,0:T(8,128)(2,1)S(1)}, bf16[1024,512]{1,0:T(8,128)(2,1)}, u32[]{:S(2)}) copy-start(bf16[1024,512]{1,0:T(8,128)(2,1)} %get-tuple-element.95.refs_2_) | copy-start | bytes 3145732
  726.3 9.8 %collective-permute-start.28 = (f32[2,2048]{1,0:T(2,128)S(1)}, f32[2,2048]{1,0:T(2,128)S(1)}, u32[]{:S(2)}, u32[]{:S(2)}) collective-permute-start(f32[2,2048]{1,0:T(2,128)S(1)} %fusion.6), channel_id=1, source_target_pairs={{4,0},{8,4},{12,8},{5,1},{9,5},{13,9},{6,2},{10,6},{14,10},{7,3},{... | collective-permute-start | bytes 49160 | tf_op jit(solution)/shard_map/ppermute | solution.py:25
  736.8 60.8 %collective-permute-start.29 = (bf16[2,256,1024]{1,2,0:T(8,128)(2,1)S(1)}, bf16[2,256,1024]{1,2,0:T(8,128)(2,1)}, u32[]{:S(2)}, u32[]{:S(2)}) collective-permute-start(bf16[2,256,1024]{1,2,0:T(8,128)(2,1)S(1)} %dynamic-slice_bitcast_fusion), channel_id=1, source_target_pairs={{0,4},{4,0},{8,12},{12,8},{1,5},{5,1},{9,13},{13,9},{2,6},{6,2},{1... | collective-permute-start | bytes 3145736 | tf_op jit(solution)/shard_map/ppermute | solution.py:101
  801.0 4.2 collective-permute-start.30
  806.1 50.7 %collective-permute-start.36 = (bf16[512,2048]{1,0:T(8,128)(2,1)S(1)}, bf16[512,2048]{1,0:T(8,128)(2,1)S(1)}, u32[]{:S(2)}, u32[]{:S(2)}) collective-permute-start(bf16[512,2048]{1,0:T(8,128)(2,1)S(1)} %add_convert_fusion.1), channel_id=1, source_target_pairs={{0,2},{1,3},{2,0},{3,1},{4,6},{5,7},{6,4},{7,5},{8,10},{9,11},{10,... | collective-permute-start | bytes 6291464 | tf_op jit(solution)/shard_map/ppermute | solution.py:48
  809.2 8.8 collective-permute-start.31
  818.0 14.1 %collective-permute-start.32 = (f32[14,2048]{1,0:T(8,128)S(1)}, f32[14,2048]{1,0:T(8,128)S(1)}, u32[]{:S(2)}, u32[]{:S(2)}) collective-permute-start(f32[14,2048]{1,0:T(8,128)S(1)} %add.260), channel_id=1, source_target_pairs={{0,4},{4,0},{8,12},{12,8},{1,5},{5,1},{9,13},{13,9},{2,6},{6,2},{1... | collective-permute-start | bytes 344072 | tf_op jit(solution)/shard_map/ppermute | solution.py:146
  832.2 17.5 %collective-permute-start.33 = (f32[14,2048]{1,0:T(8,128)S(1)}, f32[14,2048]{1,0:T(8,128)S(1)}, u32[]{:S(2)}, u32[]{:S(2)}) collective-permute-start(f32[14,2048]{1,0:T(8,128)S(1)} %add.261), channel_id=1, source_target_pairs={{0,8},{4,12},{8,0},{12,4},{1,9},{5,13},{9,1},{13,5},{2,10},{6,14},... | collective-permute-start | bytes 344072 | tf_op jit(solution)/shard_map/ppermute | solution.py:146
  849.7 1.4 collective-permute-start.34
  851.2 5.6 collective-permute-start.35
  857.7 38.4 %collective-permute-start.37 = (bf16[512,2048]{1,0:T(8,128)(2,1)S(1)}, bf16[512,2048]{1,0:T(8,128)(2,1)}, u32[]{:S(2)}, u32[]{:S(2)}) collective-permute-start(bf16[512,2048]{1,0:T(8,128)(2,1)S(1)} %add_convert_fusion), channel_id=1, source_target_pairs={{0,1},{1,0},{2,3},{3,2},{4,5},{5,4},{6,7},{7,6},{8,9},{9,8},{10,11... | collective-permute-start | bytes 6291464 | tf_op jit(solution)/shard_map/ppermute | solution.py:48
  858.7 34.4 %collective-permute-start.38 = (bf16[256,1024]{0,1:T(8,128)(2,1)}, bf16[256,1024]{0,1:T(8,128)(2,1)}, u32[]{:S(2)}, u32[]{:S(2)}) collective-permute-start(bf16[256,1024]{0,1:T(8,128)(2,1)} %dynamic-slice_bitcast_fusion.1), channel_id=1, source_target_pairs={{0,8},{4,12},{8,0},{12,4},{1,9},{5,13},{9,1},{13,5},{2,10},{6,14},... | collective-permute-start | bytes 1572872 | tf_op jit(solution)/shard_map/ppermute | solution.py:101
  (31 other events, 134.9 us)
Sparse Core Ops, SparseCore 0:
  13.6 153.5 all-gather.3
  169.9 146.5 all-gather.5
  318.5 110.7 all-gather.7
  443.9 131.5 reduce-scatter.3
  597.2 199.5 reduce-scatter.5
  800.3 141.6 reduce-scatter.7

commit v7 on v6

--- a/solution.py
+++ b/solution.py
@@ -138,13 +138,9 @@
     yield None
 
 
-def whole_sum(x, axes):
-    for axis in axes:
-        count = lax.axis_size(axis)
-        bit = 1
-        while bit < count:
-            x = x + lax.ppermute(x, axis, [(i, i ^ bit) for i in range(count)])
-            bit *= 2
+def whole_sum(x, steps):
+    for axis, bit in steps:
+        x = x + swap(x, axis, bit)
     return x
 
 
@@ -974,10 +970,14 @@
     grads_time = jnp.concatenate(
         [
             matmul_tn(mixed, grad_low).astype(jnp.bfloat16)
-            for mixed, grad_low in zip(mixed_in, d_lows[:3])
+            for mixed, grad_low in zip(mixed_in, d_lows[:2])
         ],
         axis=1,
     )
+    value_steps = owner_scatter_steps(matmul_tn(mixed_in[2], d_value).astype(jnp.bfloat16))
+    g_value = next(value_steps)
+    for _ in range(early_steps - 3):
+        g_value = value_steps.send(g_value)
     *d_lows, _ = after(d_lows[0], *d_lows[1:], grads_time)
     g_time = lax.psum_scatter(grads_time, owners, scatter_dimension=0, tiled=True)
     back_one = back_from(d_lows, weights_time, mix_one)
@@ -995,7 +995,9 @@
         None,
         "blend_one_back",
     )
-    d_input_part, g_early, g_chan = after(d_input_part, g_early, g_chan)
+    d_input_part, g_early, g_chan, g_value = after(d_input_part, g_early, g_chan, g_value)
+    g_early = early.send(g_early)
+    g_value = value_steps.send(g_value)
     head_small = jnp.concatenate([state_small[:2], group_small[:2]])
     head_small = lax.dynamic_update_slice_in_dim(
         jnp.zeros((4, embedding_extent), jnp.float32), head_small, sharded_layout, 1
@@ -1003,10 +1005,15 @@
     small_part = jnp.concatenate([time_small[:6], head_small, chan_small[:4]], axis=0)
 
     def small_total(token):
-        return whole_sum(after(small_part, token)[0], ("fsdp", "ctx", "tp"))
-
-    d_input_sum, small_sum = tp_sum(d_input_part, small_total)
-    g_early = early.send(after(g_early, small_sum)[0])
+        tp_bits = axis_bits("tp")
+        total = whole_sum(
+            after(small_part, token)[0],
+            axis_bits("fsdp") + tp_bits[:1] + axis_bits("ctx") + tp_bits[1:],
+        )
+        return total, g_early, g_value
+
+    d_input_sum, (small_sum, g_early, g_value) = tp_sum(d_input_part, small_total)
+    g_value = value_steps.send(after(g_value, small_sum)[0])
     owned = embedding_extent // (lax.axis_size("fsdp") * lax.axis_size("ctx"))
     small_owned = lax.dynamic_slice_in_dim(
         small_sum,
@@ -1020,12 +1027,13 @@
     g_chanvalue = g_chanvalue.astype(jnp.float32)
     g_chankey, g_chanrecept = split_columns(g_chan, (units, fourth_extent), "split_chan")
     g_early = g_early.astype(jnp.float32)
+    g_value = g_value.astype(jnp.float32)
     g_output = g_early[:, :fourth_extent].T
     g_gate = g_early[:, fourth_extent:]
     g_time = after(
-        g_time, grad_inputs, result, g_chanvalue, g_chankey, g_chanrecept, g_output, g_gate
+        g_time, grad_inputs, result, g_chanvalue, g_chankey, g_chanrecept, g_output, g_gate, g_value
     )[0]
-    g_recept, g_key, g_value = split_columns(g_time, (fourth_extent,) * 3, "split_time")
+    g_recept, g_key = split_columns(g_time, (fourth_extent,) * 2, "split_time")
     return (
         result,
         grad_inputs,

time: 960 us -> 955 us (level)
  waiting for transfers between devices: 440 us -> 410 us
  other arithmetic: 62 us -> 73 us
    ppermute x3 -> x11, waiting for transfers between devices: 46.4 us -> 98.7 us  [swap(): lax.ppermute(x, axis, [(i, i ^ bit) for i in range(lax.axis_size(axis))])]
    ppermute x5 -> x0, waiting for transfers between devices: 44.8 us -> none  [whole_sum(): x = x + lax.ppermute(x, axis, [(i, i ^ bit) for i in range(count)])]
    reduce_scatter x1, waiting for transfers between devices: 38.5 us -> 0.01 us  [per_device(): lax.psum_scatter(grads_time, owners, scatter_dimension=0, tiled=True)]
    convert_element_type x9 -> x11, other arithmetic: 17.9 us -> 26.1 us  [add_low(): (left.astype(jnp.float32) + right.astype(jnp.float32)).astype(jnp.bfloat16)]
  transfers between devices with their start and end apart: 45 -> 48, of which waited for: 29 -> 29; matrix products, arithmetic and copies ran while one was open for 24% -> 26% of each run, Pallas kernels for 19% -> 19%
where the time goes in v7:
time: 955 us; the launch traced here: 947 us
  waiting for transfers between devices  410 us (43%)
  Pallas kernels  185 us (19%)
  matrix products  130 us (14%)
  other arithmetic  73 us (8%)
  local copies, waits for them, and re-layouts  68.7 us (7%)
  starting transfers between devices  64.8 us (7%)
  between operations  15.8 us (2%)
    ppermute x15, waiting for transfers between devices, partner(): return lax.ppermute(x, 'tp', [(i, i ^ bit) for i in range(count)])  128 us
    all_gather x1, waiting for transfers between devices, per_device(): lax.all_gather(jnp.concatenate([acceptor_matrix, lookup_matrix, payload_m...  108 us
    ppermute x11, waiting for transfers between devices, swap(): lax.ppermute(x, axis, [(i, i ^ bit) for i in range(lax.axis_size(axis))])  98.7 us
    pallas_call x2, Pallas kernels, blend_back(): pl.pallas_call(partial(blend_back_kernel, len(xs), mixes, per_seq, int(ow...  89 us
    dot_general x8, matrix products, matmul(): return jnp.dot(left, right, preferred_element_type=jnp.float32)  64.2 us
    pallas_call x4, Pallas kernels, pair_call(): pl.pallas_call(kernel, grid=(pairs, seqs), in_specs=[specs[kind] for kind...  49.4 us
    pallas_call x2, Pallas kernels, blend(): pl.pallas_call(partial(blend_kernel, len(xs), mixes, per_seq), grid=(toke...  39.9 us
    dot_general x8, matrix products, matmul_tn(): lax.dot_general(left, right, (((0,), (0,)), ((), ())), preferred_element_...  39.1 us
  transfers between devices with their start and end apart: 48, of which 29 were waited for; matrix products, arithmetic and copies ran while one was open for 26% of the time, Pallas kernels for 19%

profile of v7, /device:TPU:0, one launch (start us, length us, event | category | flops | bytes accessed | tf_op | source)
XLA Modules:
  0.0 947.4 jit_solution(141578247507801481)
XLA Ops:
  17.3 4.9 collective-permute-start.1
  22.3 4.5 collective-permute-start.2
  38.3 20.8 %blend_one.1 = (bf16[1024,2048]{1,0:T(8,128)(2,1)}, bf16[1024,2048]{1,0:T(8,128)(2,1)}, bf16[1024,2048]{1,0:T(8,128)(2,1)}, bf16[1024,2048]{1,0:T(8,128)(2,1)}) custom-call(bf16[1024,2048]{1,0:T(8,128)(2,1)} %bitcast.197, f32[1024,1]{1,0:T(8,128)} %bitcast.207, f32[2,1,2048]{2,1,0:T(1,128)} %broadcast_in_dim.20.refs_2_.refs_11_, ...), custom_call_target="tpu_custom_call" | custom-call | flops 41943040 | bytes 20971520 | tf_op jit(solution)/shard_map/blend_one/pallas_call | solution.py:521
  59.2 108.1 %all-gather.4.cloned.1.call-done.refs_6_.refs_7_.refs_8_.refs_9_ = bf16[2048,2560]{1,0:T(8,128)(2,1)} async-done(((bf16[256,2560]{1,0:T(8,128)(2,1)}), bf16[2048,2560]{1,0:T(8,128)(2,1)}) %all-gather.4.cloned.1.call-update) | async-done | bytes 10485776 | tf_op jit(solution)/shard_map/all_gather | solution.py:773
  167.2 6.3 fusion.40.k_ref
  173.6 4.9 fusion.43.v_ref
  178.5 6.9 carry.1
  186.4 3.5 collective-permute-start.4
  191.2 3.0 collective-permute-start.6
  194.2 6.3 fusion.37.r_ref
  200.5 5.3 fusion.26.gate_ref
  208.2 11.3 %mix.1 = (bf16[1024,512]{1,0:T(8,128)(2,1)}, f32[1024,512]{1,0:T(8,128)}) custom-call(bf16[1024,512]{1,0:T(8,128)(2,1)} %fusion.37.r_ref, bf16[1024,512]{1,0:T(8,128)(2,1)} %fusion.40.k_ref, bf16[1024,512]{1,0:T(8,128)(2,1)} %fusion.43.v_ref, f32[1024,512]{1,0:T(8,128)} %fusion.26.gate_ref, f32[1,512]{1,0:T(1,128)} %bitcast.229, ...), custom_call_target="tpu_custom_call" | custom-call | flops 1073741824 | bytes 11087872 | tf_op jit(solution)/shard_map/mix/pallas_call | solution.py:420
  219.6 4.3 convolution_convert_fusion.3
  226.2 4.3 collective-permute-done.7
  230.5 3.0 add_convert_fusion.5
  235.1 46.2 %collective-permute-done.8 = bf16[512,2048]{1,0:T(8,128)(2,1)} collective-permute-done((bf16[512,2048]{1,0:T(8,128)(2,1)S(1)}, bf16[512,2048]{1,0:T(8,128)(2,1)}, u32[]{:S(2)}, u32[]{:S(2)}) %collective-permute-start.8) | collective-permute-done | bytes 2097184 | tf_op jit(solution)/shard_map/ppermute | solution.py:48
  281.3 3.7 add_convert_fusion.4
  285.0 4.3 collective-permute-done.9
  289.4 3.7 maximum_select_fusion.refs_1_.refs_3_
  295.7 11.2 %collective-permute-start.10 = (f32[2,2048]{1,0:T(2,128)S(1)}, f32[2,2048]{1,0:T(2,128)S(1)}, u32[]{:S(2)}, u32[]{:S(2)}) collective-permute-start(f32[2,2048]{1,0:T(2,128)S(1)} %fusion.57), channel_id=1, source_target_pairs={{0,4},{4,8},{8,12},{1,5},{5,9},{9,13},{2,6},{6,10},{10,14},{3,7},{... | collective-permute-start | bytes 49160 | tf_op jit(solution)/shard_map/ppermute | solution.py:25
  309.1 19.0 %blend_two.1 = (bf16[1024,2048]{1,0:T(8,128)(2,1)}, bf16[1024,2048]{1,0:T(8,128)(2,1)}) custom-call(bf16[1024,2048]{1,0:T(8,128)(2,1)} %bitcast.198, bf16[1024,2048]{1,0:T(8,128)(2,1)} %copy-done, f32[1024,1]{1,0:T(8,128)} %bitcast.208, f32[2,1,2048]{2,1,0:T(1,128)} %copy.101.refs_3_.refs_9_, f32[2,2048]{1,0:T(2,128)} %get-tuple-element.240.refs_4_.refs_11_, ...), custom_call_target="tpu_custom_call" | custom-call | flops 41943040 | bytes 16777216 | tf_op jit(solution)/shard_map/blend_two/pallas_call | solution.py:521
  330.7 6.9 constant_dynamic-update-slice_fusion.8
  339.3 22.9 %collective-permute-done.11 = bf16[1024,512]{1,0:T(8,128)(2,1)S(1)} collective-permute-done((bf16[1024,512]{1,0:T(8,128)(2,1)}, bf16[1024,512]{1,0:T(8,128)(2,1)S(1)}, u32[]{:S(2)}, u32[]{:S(2)}) %collective-permute-start.11) | collective-permute-done | bytes 1048608 | tf_op jit(solution)/shard_map/ppermute | solution.py:48
  362.2 13.6 %multiply_convert_fusion.1 = (bf16[1024,1792]{1,0:T(8,128)(2,1)S(1)}, f32[1024,1792]{1,0:T(8,128)}) fusion(bf16[1024,2048]{1,0:T(8,128)(2,1)} %get-tuple-element.78, bf16[2048,2304]{1,0:T(8,128)(2,1)} %all-gather.6.cloned.1.call-done.refs_6_), kind=kOutput, calls=%fused_computation.5 | convolution fusion | flops 7521697792 | bytes 22544384 | tf_op jit(solution)/shard_map/dot_general | solution.py:179
  379.4 12.1 %convolution_convert_fusion.1 = bf16[1792,2048]{1,0:T(8,128)(2,1)} fusion(bf16[1024,1792]{1,0:T(8,128)(2,1)S(1)} %get-tuple-element.79, bf16[1024,2048]{1,0:T(8,128)(2,1)} %constant_dynamic-update-slice_fusion.5), kind=kOutput, calls=%fused_computation.3 | convolution fusion | flops 7519862784 | bytes 15204352 | tf_op jit(solution)/shard_map/dot_general | solution.py:183
  391.5 37.7 %all-gather.8.cloned.1.call-done = bf16[2048,1792]{0,1:T(8,128)(2,1)} async-done(((bf16[256,1792]{0,1:T(8,128)(2,1)}), bf16[2048,1792]{0,1:T(8,128)(2,1)}) %all-gather.8.cloned.1.call-update) | async-done | bytes 7340048 | tf_op jit(solution)/shard_map/all_gather | solution.py:793
  429.2 11.3 %convolution_convert_fusion.2 = bf16[1024,2048]{1,0:T(8,128)(2,1)S(1)} fusion(bf16[1024,1792]{1,0:T(8,128)(2,1)} %copy-done.48, bf16[2048,1792]{0,1:T(8,128)(2,1)} %all-gather.8.cloned.1.call-done), kind=kOutput, calls=%fused_computation.23 | convolution fusion | flops 7518289920 | bytes 15204352 | tf_op jit(solution)/shard_map/dot_general | solution.py:189
  450.3 14.2 %multiply_convert_fusion.refs_4_ = bf16[1024,1792]{1,0:T(8,128)(2,1)} fusion(f32[1024,1792]{1,0:T(8,128)} %get-tuple-element.234, bf16[1024,2048]{1,0:T(8,128)(2,1)} %constant_dynamic-update-slice_fusion.5, bf16[2048,1792]{0,1:T(8,128)(2,1)} %all-gather.8.cloned.1.call-done), kind=kOutput, calls=%fused_computation.4 | convolution fusion | flops 7523532800 | bytes 22544384 | tf_op jit(solution)/shard_map/dot_general | solution.py:179
  467.5 6.6 collective-permute-done.16
  474.1 4.7 fusion.19
  482.8 3.2 collective-permute-done.17
  486.7 44.9 %blend_two_back.1 = (bf16[1024,2048]{1,0:T(8,128)(2,1)}, f32[8,2048]{1,0:T(8,128)}) custom-call(bf16[1024,2048]{1,0:T(8,128)(2,1)} %bitcast.200, bf16[1024,2048]{1,0:T(8,128)(2,1)} %copy-done, bf16[1024,2048]{1,0:T(8,128)(2,1)} %bitcast.201, bf16[1024,2048]{1,0:T(8,128)(2,1)} %copy-done, bf16[1024,1792]{1,0:T(8,128)(2,1)} %multiply_convert_fusion.refs_4_, ...), custom_call_target="tpu_custom_call" | custom-call | flops 9663676416 | bytes 16777216 | tf_op jit(solution)/shard_map/blend_two_back/pallas_call | solution.py:681
  533.6 4.1 collective-permute-done.18
  540.3 10.0 %convolution_convert_fusion = bf16[2048,1792]{1,0:T(8,128)(2,1)S(1)} fusion(bf16[1024,2048]{1,0:T(8,128)(2,1)} %get-tuple-element.78, bf16[1024,1792]{1,0:T(8,128)(2,1)S(1)} %copy-done.39), kind=kOutput, calls=%fused_computation.2 | convolution fusion | flops 7519862784 | bytes 15204352 | tf_op jit(solution)/shard_map/dot_general | solution.py:183
  552.8 4.6 pad_maximum_fusion
  557.3 29.2 %collective-permute-done.19 = bf16[512,2048]{1,0:T(8,128)(2,1)} collective-permute-done((bf16[512,2048]{1,0:T(8,128)(2,1)S(1)}, bf16[512,2048]{1,0:T(8,128)(2,1)}, u32[]{:S(2)}, u32[]{:S(2)}) %collective-permute-start.19) | collective-permute-done | bytes 2097184 | tf_op jit(solution)/shard_map/ppermute | solution.py:48
  589.0 4.1 collective-permute-done.20
  593.1 3.8 maximum_select_fusion.1
  597.0 6.5 fusion.22.dj_ref
  603.6 11.3 %gate_back.1 = (bf16[1024,512]{1,0:T(8,128)(2,1)}, bf16[1024,512]{1,0:T(8,128)(2,1)}, f32[2,4,64,128]{3,2,1,0:T(8,128)}, f32[8,512]{1,0:T(8,128)}) custom-call(f32[1024,512]{1,0:T(8,128)} %fusion.22.dj_ref, f32[1024,512]{1,0:T(8,128)} %get-tuple-element.85.attend_ref, f32[1024,512]{1,0:T(8,128)} %fusion.26.gate_ref, bf16[1024,512]{1,0:T(8,128)(2,1)} %fusion.37.r_ref, ...), custom_call_target="tpu_custom_call" | custom-call | flops 67108864 | bytes 14749696 | tf_op jit(solution)/shard_map/gate_back/pallas_call | solution.py:420
  614.9 4.7 convolution_convert_fusion.8
  624.8 7.9 reshape.227
  632.6 6.4 constant_dynamic-slice_fusion.6
  654.4 8.9 collective-permute-done.24
  663.3 9.3 collective-permute-done.25
  673.4 19.9 %mix_back.1 = (bf16[1024,512]{1,0:T(8,128)(2,1)}, bf16[1024,512]{1,0:T(8,128)(2,1)}, bf16[1024,512]{1,0:T(8,128)(2,1)}, f32[8,512]{1,0:T(8,128)}) custom-call(bf16[1024,512]{1,0:T(8,128)(2,1)} %fusion.37.r_ref, bf16[1024,512]{1,0:T(8,128)(2,1)} %fusion.40.k_ref, bf16[1024,512]{1,0:T(8,128)(2,1)} %fusion.43.v_ref, ...), custom_call_target="tpu_custom_call" | custom-call | flops 3221225472 | bytes 9523200 | tf_op jit(solution)/shard_map/mix_back/pallas_call | solution.py:420
  693.3 6.9 collective-permute-done.27
  701.5 2.6 fusion.4
  714.4 2.7 pad_maximum_fusion.2
  730.3 7.7 collective-permute-done.28
  741.8 44.1 %blend_one_back.1 = (bf16[1024,2048]{1,0:T(8,128)(2,1)}, f32[8,2048]{1,0:T(8,128)}) custom-call(bf16[1024,2048]{1,0:T(8,128)(2,1)} %bitcast.202, bf16[1024,2048]{1,0:T(8,128)(2,1)} %bitcast.203, bf16[1024,512]{1,0:T(8,128)(2,1)} %get-tuple-element.95.refs_2_, bf16[1024,512]{1,0:T(8,128)(2,1)} %get-tuple-element.96.refs_3_, ...), custom_call_target="tpu_custom_call" | custom-call | flops 8589934592 | bytes 16777216 | tf_op jit(solution)/shard_map/blend_one_back/pallas_call | solution.py:681
  788.4 11.2 %collective-permute-done.29 = bf16[2,256,1024]{1,2,0:T(8,128)(2,1)} collective-permute-done((bf16[2,256,1024]{1,2,0:T(8,128)(2,1)}, bf16[2,256,1024]{1,2,0:T(8,128)(2,1)}, u32[]{:S(2)}, u32[]{:S(2)}) %collective-permute-start.29) | collective-permute-done | bytes 1048608 | tf_op jit(solution)/shard_map/ppermute | solution.py:101
  805.3 4.1 collective-permute-done.31
  815.3 3.5 collective-permute-start.37
  820.5 4.1 collective-permute-done.32
  827.6 36.6 %collective-permute-done.34 = f32[14,2048]{1,0:T(8,128)S(1)} collective-permute-done((f32[14,2048]{1,0:T(8,128)S(1)}, f32[14,2048]{1,0:T(8,128)S(1)}, u32[]{:S(2)}, u32[]{:S(2)}) %collective-permute-start.34) | collective-permute-done | bytes 114720 | tf_op jit(solution)/shard_map/ppermute | solution.py:101
  864.2 2.9 collective-permute-start.35
  869.7 11.6 %collective-permute-done.35 = f32[14,2048]{1,0:T(8,128)S(1)} collective-permute-done((f32[14,2048]{1,0:T(8,128)S(1)}, f32[14,2048]{1,0:T(8,128)S(1)}, u32[]{:S(2)}, u32[]{:S(2)}) %collective-permute-start.35) | collective-permute-done | bytes 114720 | tf_op jit(solution)/shard_map/ppermute | solution.py:101
  886.7 3.7 add_convert_fusion
  890.5 2.7 convert_element_type.416
  893.1 3.6 split_chan.1
  903.1 24.6 %collective-permute-done.41 = bf16[256,512]{1,0:T(8,128)(2,1)S(1)} collective-permute-done((bf16[256,512]{1,0:T(8,128)(2,1)S(1)}, bf16[256,512]{1,0:T(8,128)(2,1)S(1)}, u32[]{:S(2)}, u32[]{:S(2)}) %collective-permute-start.41) | collective-permute-done | bytes 262176 | tf_op jit(solution)/shard_map/ppermute | solution.py:101
  929.5 7.3 convert_add_fusion
  936.9 3.2 split_time.1
  (302 shorter events, 153.6 us)
Async XLA Ops:
  7.2 23.5 %copy-start.34 = (f32[2048]{0:T(1024)S(1)}, f32[2048]{0:T(1024)}, u32[]{:S(2)}) copy-start(f32[2048]{0:T(1024)} %param.35) | copy-start | bytes 24580
  7.2 23.5 %copy-start.33 = (f32[2048]{0:T(1024)S(1)}, f32[2048]{0:T(1024)}, u32[]{:S(2)}) copy-start(f32[2048]{0:T(1024)} %param.36) | copy-start | bytes 24580
  7.2 24.1 %copy-start.24 = (f32[2048]{0:T(1024)S(1)}, f32[2048]{0:T(1024)}, u32[]{:S(2)}) copy-start(f32[2048]{0:T(1024)} %param.37) | copy-start | bytes 24580
  7.3 24.1 %copy-start.26 = (f32[2048]{0:T(1024)S(1)}, f32[2048]{0:T(1024)}, u32[]{:S(2)}) copy-start(f32[2048]{0:T(1024)} %param.38) | copy-start | bytes 24580
  7.3 24.1 %copy-start.28 = (f32[2048]{0:T(1024)S(1)}, f32[2048]{0:T(1024)}, u32[]{:S(2)}) copy-start(f32[2048]{0:T(1024)} %param.39) | copy-start | bytes 24580
  7.3 24.1 %copy-start.30 = (f32[2048]{0:T(1024)S(1)}, f32[2048]{0:T(1024)}, u32[]{:S(2)}) copy-start(f32[2048]{0:T(1024)} %param.40) | copy-start | bytes 24580
  7.3 159.9 %all-gather.4.cloned.1.call-start = ((), (), s32[]{:S(2)}) async-start(), calls=%async_computation.3 | async-start | bytes 11796480 | tf_op jit(solution)/shard_map/all_gather | solution.py:773
  13.5 314.6 %all-gather.6.cloned.1.call-start = ((), (), s32[]{:S(2)}) async-start(), calls=%async_computation.4 | async-start | bytes 10616832 | tf_op jit(solution)/shard_map/all_gather | solution.py:781
  14.7 414.5 %all-gather.8.cloned.1.call-start = ((), (), s32[]{:S(2)}) async-start(), calls=%async_computation.5 | async-start | bytes 8257536 | tf_op jit(solution)/shard_map/all_gather | solution.py:793
  17.3 156.3 %copy-start.37 = (bf16[2,4,1,128]{3,2,1,0:T(2,128)(2,1)}, bf16[2,4,1,128]{3,2,1,0:T(2,128)(2,1)S(1)}, u32[]{:S(2)}) copy-start(bf16[2,4,1,128]{3,2,1,0:T(2,128)(2,1)S(1)} %get-tuple-element.196) | copy-start | bytes 6148
  17.3 20.4 %collective-permute-start.1 = (bf16[2,4,1,128]{3,2,1,0:T(2,128)(2,1)S(1)}, bf16[2,4,1,128]{3,2,1,0:T(2,128)(2,1)S(1)}, u32[]{:S(2)}, u32[]{:S(2)}) collective-permute-start(bf16[2,4,1,128]{3,2,1,0:T(2,128)(2,1)S(1)} %get-tuple-element.196), channel_id=1, source_target_pairs={{0,4},{4,8},{8,12},{1,5},{5,9},{9,13},{2,6},{6,10},{10,14},{3,7},{... | collective-permute-start | bytes 6152 | tf_op jit(solution)/shard_map/ppermute | solution.py:30
  22.3 15.4 %collective-permute-start.2 = (bf16[2,4,1,128]{3,2,1,0:T(2,128)(2,1)S(1)}, bf16[2,4,1,128]{3,2,1,0:T(2,128)(2,1)S(1)}, u32[]{:S(2)}, u32[]{:S(2)}) collective-permute-start(bf16[2,4,1,128]{3,2,1,0:T(2,128)(2,1)S(1)} %get-tuple-element.196), channel_id=1, source_target_pairs={{0,8},{4,12},{1,9},{5,13},{2,10},{6,14},{3,11},{7,15},{16,24},{20,... | collective-permute-start | bytes 6152 | tf_op jit(solution)/shard_map/ppermute | solution.py:30
  26.8 10.9 %collective-permute-start.3 = (bf16[2,4,1,128]{3,2,1,0:T(2,128)(2,1)S(1)}, bf16[2,4,1,128]{3,2,1,0:T(2,128)(2,1)S(1)}, u32[]{:S(2)}, u32[]{:S(2)}) collective-permute-start(bf16[2,4,1,128]{3,2,1,0:T(2,128)(2,1)S(1)} %get-tuple-element.196), channel_id=1, source_target_pairs={{0,12},{1,13},{2,14},{3,15},{16,28},{17,29},{18,30},{19,31}} | collective-permute-start | bytes 6152 | tf_op jit(solution)/shard_map/ppermute | solution.py:30
  29.3 8.4 collective-permute-start
  186.4 19.5 %collective-permute-start.4 = (bf16[2,4,64,128]{3,2,1,0:T(8,128)(2,1)S(1)}, bf16[2,4,64,128]{3,2,1,0:T(8,128)(2,1)S(1)}, u32[]{:S(2)}, u32[]{:S(2)}) collective-permute-start(bf16[2,4,64,128]{3,2,1,0:T(8,128)(2,1)S(1)} %convert_element_type.337), channel_id=1, source_target_pairs={{0,12},{1,13},{2,14},{3,15},{16,28},{17,29},{18,30},{19,31}} | collective-permute-start | bytes 393224 | tf_op jit(solution)/shard_map/ppermute | solution.py:30
  189.9 16.0 %collective-permute-start.5 = (bf16[2,4,64,128]{3,2,1,0:T(8,128)(2,1)S(1)}, bf16[2,4,64,128]{3,2,1,0:T(8,128)(2,1)S(1)}, u32[]{:S(2)}, u32[]{:S(2)}) collective-permute-start(bf16[2,4,64,128]{3,2,1,0:T(8,128)(2,1)S(1)} %convert_element_type.337), channel_id=1, source_target_pairs={{0,8},{4,12},{1,9},{5,13},{2,10},{6,14},{3,11},{7,15},{16,24},{20,... | collective-permute-start | bytes 393224 | tf_op jit(solution)/shard_map/ppermute | solution.py:30
  191.2 16.3 %collective-permute-start.6 = (bf16[2,4,64,128]{3,2,1,0:T(8,128)(2,1)S(1)}, bf16[2,4,64,128]{3,2,1,0:T(8,128)(2,1)S(1)}, u32[]{:S(2)}, u32[]{:S(2)}) collective-permute-start(bf16[2,4,64,128]{3,2,1,0:T(8,128)(2,1)S(1)} %convert_element_type.337), channel_id=1, source_target_pairs={{0,4},{4,8},{8,12},{1,5},{5,9},{9,13},{2,6},{6,10},{10,14},{3,7},{... | collective-permute-start | bytes 393224 | tf_op jit(solution)/shard_map/ppermute | solution.py:30
  226.1 4.4 collective-permute-start.7
  233.5 47.8 %collective-permute-start.8 = (bf16[512,2048]{1,0:T(8,128)(2,1)S(1)}, bf16[512,2048]{1,0:T(8,128)(2,1)}, u32[]{:S(2)}, u32[]{:S(2)}) collective-permute-start(bf16[512,2048]{1,0:T(8,128)(2,1)S(1)} %add_convert_fusion.5), channel_id=1, source_target_pairs={{0,2},{1,3},{2,0},{3,1},{4,6},{5,7},{6,4},{7,5},{8,10},{9,11},{10,... | collective-permute-start | bytes 6291464 | tf_op jit(solution)/shard_map/ppermute | solution.py:48
  235.1 361.9 %reduce-scatter.4.cloned.1.call-start = ((), (), s32[]{:S(2)}) async-start(), calls=%async_computation.6 | async-start | bytes 8257536 | tf_op jit(solution)/shard_map/reduce_scatter | solution.py:872
  285.0 4.4 collective-permute-start.9
  285.0 21.9 %copy-start.22 = (f32[2048]{0:T(1024)S(1)}, f32[2048]{0:T(1024)}, u32[]{:S(2)}) copy-start(f32[2048]{0:T(1024)} %param.47) | copy-start | bytes 24580
  285.0 21.9 %copy-start.23 = (f32[2048]{0:T(1024)S(1)}, f32[2048]{0:T(1024)}, u32[]{:S(2)}) copy-start(f32[2048]{0:T(1024)} %param.48) | copy-start | bytes 24580
  285.0 21.9 %copy-start.35 = (f32[2048]{0:T(1024)S(1)}, f32[2048]{0:T(1024)}, u32[]{:S(2)}) copy-start(f32[2048]{0:T(1024)} %param.46) | copy-start | bytes 24580
  285.0 21.9 %copy-start.36 = (f32[2048]{0:T(1024)S(1)}, f32[2048]{0:T(1024)}, u32[]{:S(2)}) copy-start(f32[2048]{0:T(1024)} %param.45) | copy-start | bytes 24580
  295.7 12.8 %collective-permute-start.10 = (f32[2,2048]{1,0:T(2,128)S(1)}, f32[2,2048]{1,0:T(2,128)S(1)}, u32[]{:S(2)}, u32[]{:S(2)}) collective-permute-start(f32[2,2048]{1,0:T(2,128)S(1)} %fusion.57), channel_id=1, source_target_pairs={{0,4},{4,8},{8,12},{1,5},{5,9},{9,13},{2,6},{6,10},{10,14},{3,7},{... | collective-permute-start | bytes 49160 | tf_op jit(solution)/shard_map/ppermute | solution.py:25
  337.6 24.6 %collective-permute-start.11 = (bf16[1024,512]{1,0:T(8,128)(2,1)}, bf16[1024,512]{1,0:T(8,128)(2,1)S(1)}, u32[]{:S(2)}, u32[]{:S(2)}) collective-permute-start(bf16[1024,512]{1,0:T(8,128)(2,1)} %get-tuple-element.238), channel_id=1, source_target_pairs={{0,2},{1,3},{2,0},{3,1},{4,6},{5,7},{6,4},{7,5},{8,10},{9,11},{10,... | collective-permute-start | bytes 3145736 | tf_op jit(solution)/shard_map/ppermute | solution.py:48
  339.3 37.8 %collective-permute-start.12 = (bf16[1024,512]{1,0:T(8,128)(2,1)}, bf16[1024,512]{1,0:T(8,128)(2,1)S(1)}, u32[]{:S(2)}, u32[]{:S(2)}) collective-permute-start(bf16[1024,512]{1,0:T(8,128)(2,1)} %get-tuple-element.238), channel_id=1, source_target_pairs={{0,1},{1,0},{2,3},{3,2},{4,5},{5,4},{6,7},{7,6},{8,9},{9,8},{10,11... | collective-permute-start | bytes 3145736 | tf_op jit(solution)/shard_map/ppermute | solution.py:48
  362.2 16.2 %collective-permute-start.13 = (bf16[1024,512]{1,0:T(8,128)(2,1)S(1)}, bf16[1024,512]{1,0:T(8,128)(2,1)S(1)}, u32[]{:S(2)}, u32[]{:S(2)}) collective-permute-start(bf16[1024,512]{1,0:T(8,128)(2,1)S(1)} %collective-permute-done.11), channel_id=1, source_target_pairs={{0,1},{1,0},{2,3},{3,2},{4,5},{5,4},{6,7},{7,6},{8,9},{9,8},{10,11... | collective-permute-start | bytes 3145736 | tf_op jit(solution)/shard_map/ppermute | solution.py:48
  443.7 3.0 collective-permute-start.15
  443.7 359.5 %reduce-scatter.6.cloned.1.call-start = ((), (), s32[]{:S(2)}) async-start(), calls=%async_computation.7 | async-start | bytes 10616832 | tf_op jit(solution)/shard_map/reduce_scatter | solution.py:916
  443.9 23.6 %collective-permute-start.14 = (bf16[1024,512]{1,0:T(8,128)(2,1)S(1)}, bf16[1024,512]{1,0:T(8,128)(2,1)}, u32[]{:S(2)}, u32[]{:S(2)}) collective-permute-start(bf16[1024,512]{1,0:T(8,128)(2,1)S(1)} %get-tuple-element.210), channel_id=1, source_target_pairs={{0,1},{1,0},{2,3},{3,2},{4,5},{5,4},{6,7},{7,6},{8,9},{9,8},{10,11... | collective-permute-start | bytes 3145736 | tf_op jit(solution)/shard_map/ppermute | solution.py:48
  446.7 18.7 %slice-start = ((s8[9437184]{0:T(1024)(128)(4,1)}), s8[4194304]{0:T(1024)(128)(4,1)S(1)}, s32[]{:S(2)}) async-start(s8[9437184]{0:T(1024)(128)(4,1)} %bitcast.205), calls=%async_computation.9 | async-start | bytes 8388608
  448.7 25.4 %collective-permute-start.16 = (bf16[1024,512]{1,0:T(8,128)(2,1)S(1)}, bf16[1024,512]{1,0:T(8,128)(2,1)}, u32[]{:S(2)}, u32[]{:S(2)}) collective-permute-start(bf16[1024,512]{1,0:T(8,128)(2,1)S(1)} %add_convert_fusion.7), channel_id=1, source_target_pairs={{0,2},{1,3},{2,0},{3,1},{4,6},{5,7},{6,4},{7,5},{8,10},{9,11},{10,... | collective-permute-start | bytes 3145736 | tf_op jit(solution)/shard_map/ppermute | solution.py:48
  450.3 15.2 %slice-start.1 = ((s8[9437184]{0:T(1024)(128)(4,1)}), s8[4194304]{0:T(1024)(128)(4,1)S(1)}, s32[]{:S(2)}) async-start(s8[9437184]{0:T(1024)(128)(4,1)} %bitcast.205), calls=%async_computation.10 | async-start | bytes 8388608
  450.3 15.2 %slice-start.2 = ((s8[9437184]{0:T(1024)(128)(4,1)}), s8[1048576]{0:T(1024)(128)(4,1)S(1)}, s32[]{:S(2)}) async-start(s8[9437184]{0:T(1024)(128)(4,1)} %bitcast.205), calls=%async_computation.11 | async-start | bytes 2097152
  479.4 6.7 collective-permute-start.17
  533.5 4.2 collective-permute-start.18
  538.7 47.8 %collective-permute-start.19 = (bf16[512,2048]{1,0:T(8,128)(2,1)S(1)}, bf16[512,2048]{1,0:T(8,128)(2,1)}, u32[]{:S(2)}, u32[]{:S(2)}) collective-permute-start(bf16[512,2048]{1,0:T(8,128)(2,1)S(1)} %add_convert_fusion.3), channel_id=1, source_target_pairs={{0,2},{1,3},{2,0},{3,1},{4,6},{5,7},{6,4},{7,5},{8,10},{9,11},{10,... | collective-permute-start | bytes 6291464 | tf_op jit(solution)/shard_map/ppermute | solution.py:48
  588.9 4.2 collective-permute-start.20
  597.0 339.9 %reduce-scatter.8.cloned.1.call-start = ((), (), s32[]{:S(2)}) async-start(), calls=%async_computation.8 | async-start | bytes 4718592 | tf_op jit(solution)/shard_map/reduce_scatter | solution.py:982
  640.7 59.5 %collective-permute-start.27 = (bf16[2,2,256,1024]{2,3,0,1:T(8,128)(2,1)}, bf16[2,2,256,1024]{2,3,0,1:T(8,128)(2,1)S(1)}, u32[]{:S(2)}, u32[]{:S(2)}) collective-permute-start(bf16[2,2,256,1024]{2,3,0,1:T(8,128)(2,1)} %bitcast.194), channel_id=1, source_target_pairs={{0,16},{16,0},{1,17},{17,1},{2,18},{18,2},{3,19},{19,3},{4,20},{20... | collective-permute-start | bytes 6291464 | tf_op jit(solution)/shard_map/ppermute | solution.py:101
  642.4 5.8 collective-permute-start.21
  643.7 6.7 collective-permute-start.22
  645.0 9.4 collective-permute-start.23
  650.4 12.9 %collective-permute-start.24 = (bf16[2,4,64,128]{3,2,1,0:T(8,128)(2,1)S(1)}, bf16[2,4,64,128]{3,2,1,0:T(8,128)(2,1)S(1)}, u32[]{:S(2)}, u32[]{:S(2)}) collective-permute-start(bf16[2,4,64,128]{3,2,1,0:T(8,128)(2,1)S(1)} %convert_element_type.380), channel_id=1, source_target_pairs={{12,0},{13,1},{14,2},{15,3},{28,16},{29,17},{30,18},{31,19}} | collective-permute-start | bytes 393224 | tf_op jit(solution)/shard_map/ppermute | solution.py:30
  651.7 20.9 %collective-permute-start.25 = (bf16[2,4,64,128]{3,2,1,0:T(8,128)(2,1)S(1)}, bf16[2,4,64,128]{3,2,1,0:T(8,128)(2,1)S(1)}, u32[]{:S(2)}, u32[]{:S(2)}) collective-permute-start(bf16[2,4,64,128]{3,2,1,0:T(8,128)(2,1)S(1)} %convert_element_type.380), channel_id=1, source_target_pairs={{8,0},{12,4},{9,1},{13,5},{10,2},{14,6},{11,3},{15,7},{24,16},{28,... | collective-permute-start | bytes 393224 | tf_op jit(solution)/shard_map/ppermute | solution.py:30
  653.0 19.6 %collective-permute-start.26 = (bf16[2,4,64,128]{3,2,1,0:T(8,128)(2,1)S(1)}, bf16[2,4,64,128]{3,2,1,0:T(8,128)(2,1)S(1)}, u32[]{:S(2)}, u32[]{:S(2)}) collective-permute-start(bf16[2,4,64,128]{3,2,1,0:T(8,128)(2,1)S(1)} %convert_element_type.380), channel_id=1, source_target_pairs={{4,0},{8,4},{12,8},{5,1},{9,5},{13,9},{6,2},{10,6},{14,10},{7,3},{... | collective-permute-start | bytes 393224 | tf_op jit(solution)/shard_map/ppermute | solution.py:30
  707.8 78.1 %collective-permute-start.30 = (bf16[2,2,256,512]{3,2,0,1:T(8,128)(2,1)}, bf16[2,2,256,512]{3,2,0,1:T(8,128)(2,1)}, u32[]{:S(2)}, u32[]{:S(2)}) collective-permute-start(bf16[2,2,256,512]{3,2,0,1:T(8,128)(2,1)} %bitcast.195), channel_id=1, source_target_pairs={{0,16},{16,0},{1,17},{17,1},{2,18},{18,2},{3,19},{19,3},{4,20},{20... | collective-permute-start | bytes 3145736 | tf_op jit(solution)/shard_map/ppermute | solution.py:101
  729.0 9.0 collective-permute-start.28
  739.7 59.9 %collective-permute-start.29 = (bf16[2,256,1024]{1,2,0:T(8,128)(2,1)}, bf16[2,256,1024]{1,2,0:T(8,128)(2,1)}, u32[]{:S(2)}, u32[]{:S(2)}) collective-permute-start(bf16[2,256,1024]{1,2,0:T(8,128)(2,1)} %dynamic-slice_bitcast_fusion), channel_id=1, source_target_pairs={{0,4},{4,0},{8,12},{12,8},{1,5},{5,1},{9,13},{13,9},{2,6},{6,2},{1... | collective-permute-start | bytes 3145736 | tf_op jit(solution)/shard_map/ppermute | solution.py:101
  805.1 13.7 %copy-start.21 = (f32[8,2048]{1,0:T(8,128)S(1)}, f32[8,2048]{1,0:T(8,128)}, u32[]{:S(2)}) copy-start(f32[8,2048]{1,0:T(8,128)} %get-tuple-element.104) | copy-start | bytes 196612
  805.2 14.4 %copy-start.4 = (bf16[2,2,256,512]{3,2,0,1:T(8,128)(2,1)S(1)}, bf16[2,2,256,512]{3,2,0,1:T(8,128)(2,1)}, u32[]{:S(2)}) copy-start(bf16[2,2,256,512]{3,2,0,1:T(8,128)(2,1)} %fusion.20) | copy-start | bytes 3145732
  805.2 4.2 collective-permute-start.31
  810.3 76.4 %collective-permute-start.39 = (bf16[512,2048]{1,0:T(8,128)(2,1)S(1)}, bf16[512,2048]{1,0:T(8,128)(2,1)}, u32[]{:S(2)}, u32[]{:S(2)}) collective-permute-start(bf16[512,2048]{1,0:T(8,128)(2,1)S(1)} %add_convert_fusion.1), channel_id=1, source_target_pairs={{0,2},{1,3},{2,0},{3,1},{4,6},{5,7},{6,4},{7,5},{8,10},{9,11},{10,... | collective-permute-start | bytes 6291464 | tf_op jit(solution)/shard_map/ppermute | solution.py:48
  815.3 51.9 %collective-permute-start.37 = (bf16[256,1024]{0,1:T(8,128)(2,1)}, bf16[256,1024]{0,1:T(8,128)(2,1)}, u32[]{:S(2)}, u32[]{:S(2)}) collective-permute-start(bf16[256,1024]{0,1:T(8,128)(2,1)} %dynamic-slice_bitcast_fusion.2), channel_id=1, source_target_pairs={{0,8},{4,12},{8,0},{12,4},{1,9},{5,13},{9,1},{13,5},{2,10},{6,14},... | collective-permute-start | bytes 1572872 | tf_op jit(solution)/shard_map/ppermute | solution.py:101
  818.9 5.8 collective-permute-start.32
  820.4 61.9 %collective-permute-start.38 = (bf16[2,256,512]{2,1,0:T(8,128)(2,1)}, bf16[2,256,512]{2,1,0:T(8,128)(2,1)}, u32[]{:S(2)}, u32[]{:S(2)}) collective-permute-start(bf16[2,256,512]{2,1,0:T(8,128)(2,1)} %dynamic-slice_bitcast_fusion.1), channel_id=1, source_target_pairs={{0,4},{4,0},{8,12},{12,8},{1,5},{5,1},{9,13},{13,9},{2,6},{6,2},{1... | collective-permute-start | bytes 1572872 | tf_op jit(solution)/shard_map/ppermute | solution.py:101
  824.6 1.4 collective-permute-start.33
  826.1 38.1 %collective-permute-start.34 = (f32[14,2048]{1,0:T(8,128)S(1)}, f32[14,2048]{1,0:T(8,128)S(1)}, u32[]{:S(2)}, u32[]{:S(2)}) collective-permute-start(f32[14,2048]{1,0:T(8,128)S(1)} %add.283), channel_id=1, source_target_pairs={{0,4},{4,0},{8,12},{12,8},{1,5},{5,1},{9,13},{13,9},{2,6},{6,2},{1... | collective-permute-start | bytes 344072 | tf_op jit(solution)/shard_map/ppermute | solution.py:101
  864.2 17.0 %collective-permute-start.35 = (f32[14,2048]{1,0:T(8,128)S(1)}, f32[14,2048]{1,0:T(8,128)S(1)}, u32[]{:S(2)}, u32[]{:S(2)}) collective-permute-start(f32[14,2048]{1,0:T(8,128)S(1)} %add.284), channel_id=1, source_target_pairs={{0,8},{4,12},{8,0},{12,4},{1,9},{5,13},{9,1},{13,5},{2,10},{6,14},... | collective-permute-start | bytes 344072 | tf_op jit(solution)/shard_map/ppermute | solution.py:101
  881.3 5.5 collective-permute-start.36
  890.5 39.1 %collective-permute-start.40 = (bf16[512,2048]{1,0:T(8,128)(2,1)}, bf16[512,2048]{1,0:T(8,128)(2,1)S(1)}, u32[]{:S(2)}, u32[]{:S(2)}) collective-permute-start(bf16[512,2048]{1,0:T(8,128)(2,1)} %add_convert_fusion), channel_id=1, source_target_pairs={{0,1},{1,0},{2,3},{3,2},{4,5},{5,4},{6,7},{7,6},{8,9},{9,8},{10,11... | collective-permute-start | bytes 6291464 | tf_op jit(solution)/shard_map/ppermute | solution.py:48
  901.5 26.2 %collective-permute-start.41 = (bf16[256,512]{1,0:T(8,128)(2,1)S(1)}, bf16[256,512]{1,0:T(8,128)(2,1)S(1)}, u32[]{:S(2)}, u32[]{:S(2)}) collective-permute-start(bf16[256,512]{1,0:T(8,128)(2,1)S(1)} %dynamic-slice_bitcast_fusion.3), channel_id=1, source_target_pairs={{0,8},{4,12},{8,0},{12,4},{1,9},{5,13},{9,1},{13,5},{2,10},{6,14},... | collective-permute-start | bytes 786440 | tf_op jit(solution)/shard_map/ppermute | solution.py:101
  (36 other events, 224.6 us)
Sparse Core Ops, SparseCore 0:
  13.6 153.5 all-gather.3
  169.9 146.5 all-gather.5
  318.5 110.6 all-gather.7
  443.9 131.6 reduce-scatter.3
  597.1 206.1 reduce-scatter.5
  806.7 126.6 reduce-scatter.7

commit v8 on v7

--- a/solution.py
+++ b/solution.py
@@ -127,14 +127,19 @@
     dims = list(reversed(fsdp_bits)) + list(reversed(ctx_bits))
     rows = x.shape[0] // 2 ** len(dims)
     part = x.reshape(*([2] * len(dims)), rows, x.shape[1])
+    hold = None
     for axis, bit in fsdp_bits + ctx_bits:
         dim = dims.index((axis, bit))
         dims.pop(dim)
         mine = (lax.axis_index(axis) // bit) % 2
         own = lax.dynamic_index_in_dim(part, mine, dim, False)
         arrived = swap(lax.dynamic_index_in_dim(part, 1 - mine, dim, False), axis, bit)
-        part = add_low(own, arrived)
-        part = yield part
+        if hold is not None:
+            own = after(own, hold)[0]
+        part = yield add_low(own, arrived)
+        hold = None
+        if isinstance(part, tuple):
+            part, hold = part
     yield None
 
 
@@ -1013,7 +1018,6 @@
         return total, g_early, g_value
 
     d_input_sum, (small_sum, g_early, g_value) = tp_sum(d_input_part, small_total)
-    g_value = value_steps.send(after(g_value, small_sum)[0])
     owned = embedding_extent // (lax.axis_size("fsdp") * lax.axis_size("ctx"))
     small_owned = lax.dynamic_slice_in_dim(
         small_sum,
@@ -1027,6 +1031,7 @@
     g_chanvalue = g_chanvalue.astype(jnp.float32)
     g_chankey, g_chanrecept = split_columns(g_chan, (units, fourth_extent), "split_chan")
     g_early = g_early.astype(jnp.float32)
+    g_value = value_steps.send((g_value, (grad_inputs, g_chankey, g_chanrecept)))
     g_value = g_value.astype(jnp.float32)
     g_output = g_early[:, :fourth_extent].T
     g_gate = g_early[:, fourth_extent:]

time: 955 us -> 950 us (level)
    ppermute x11, waiting for transfers between devices: 98.7 us -> 87.4 us  [swap(): lax.ppermute(x, axis, [(i, i ^ bit) for i in range(lax.axis_size(axis))])]
  transfers between devices with their start and end apart: 48 -> 48, of which waited for: 29 -> 30; matrix products, arithmetic and copies ran while one was open for 26% -> 26% of each run, Pallas kernels for 19% -> 19%
where the time goes in v8:
time: 950 us; the launch traced here: 943 us
  waiting for transfers between devices  405 us (43%)
  Pallas kernels  185 us (19%)
  matrix products  131 us (14%)
  other arithmetic  74.7 us (8%)
  local copies, waits for them, and re-layouts  67.2 us (7%)
  starting transfers between devices  64.1 us (7%)
  between operations  15.8 us (2%)
    ppermute x15, waiting for transfers between devices, partner(): return lax.ppermute(x, 'tp', [(i, i ^ bit) for i in range(count)])  128 us
    all_gather x1, waiting for transfers between devices, per_device(): lax.all_gather(jnp.concatenate([acceptor_matrix, lookup_matrix, payload_m...  108 us
    pallas_call x2, Pallas kernels, blend_back(): pl.pallas_call(partial(blend_back_kernel, len(xs), mixes, per_seq, int(ow...  89.1 us
    ppermute x11, waiting for transfers between devices, swap(): lax.ppermute(x, axis, [(i, i ^ bit) for i in range(lax.axis_size(axis))])  87.4 us
    dot_general x8, matrix products, matmul(): return jnp.dot(left, right, preferred_element_type=jnp.float32)  64.2 us
    pallas_call x4, Pallas kernels, pair_call(): pl.pallas_call(kernel, grid=(pairs, seqs), in_specs=[specs[kind] for kind...  49.4 us
    pallas_call x2, Pallas kernels, blend(): pl.pallas_call(partial(blend_kernel, len(xs), mixes, per_seq), grid=(toke...  39.9 us
    dot_general x8, matrix products, matmul_tn(): lax.dot_general(left, right, (((0,), (0,)), ((), ())), preferred_element_...  39.1 us
  transfers between devices with their start and end apart: 48, of which 30 were waited for; matrix products, arithmetic and copies ran while one was open for 26% of the time, Pallas kernels for 19%

profile of v8, /device:TPU:0, one launch (start us, length us, event | category | flops | bytes accessed | tf_op | source)
XLA Modules:
  0.0 942.7 jit_solution(17863080975975771837)
XLA Ops:
  17.3 4.9 collective-permute-start.1
  22.2 4.5 collective-permute-start.2
  38.3 20.8 %blend_one.1 = (bf16[1024,2048]{1,0:T(8,128)(2,1)}, bf16[1024,2048]{1,0:T(8,128)(2,1)}, bf16[1024,2048]{1,0:T(8,128)(2,1)}, bf16[1024,2048]{1,0:T(8,128)(2,1)}) custom-call(bf16[1024,2048]{1,0:T(8,128)(2,1)} %bitcast.193, f32[1024,1]{1,0:T(8,128)} %bitcast.203, f32[2,1,2048]{2,1,0:T(1,128)} %broadcast_in_dim.20.refs_2_.refs_11_, ...), custom_call_target="tpu_custom_call" | custom-call | flops 41943040 | bytes 20971520 | tf_op jit(solution)/shard_map/blend_one/pallas_call | solution.py:526
  59.2 108.1 %all-gather.4.cloned.1.call-done.refs_6_.refs_7_.refs_8_.refs_9_ = bf16[2048,2560]{1,0:T(8,128)(2,1)} async-done(((bf16[256,2560]{1,0:T(8,128)(2,1)}), bf16[2048,2560]{1,0:T(8,128)(2,1)}) %all-gather.4.cloned.1.call-update) | async-done | bytes 10485776 | tf_op jit(solution)/shard_map/all_gather | solution.py:778
  167.2 6.3 fusion.40.k_ref
  173.5 4.9 fusion.43.v_ref
  178.5 6.9 carry.1
  186.3 3.6 collective-permute-start.4
  191.2 3.0 collective-permute-start.6
  194.2 6.4 fusion.37.r_ref
  200.6 5.3 fusion.26.gate_ref
  208.3 11.3 %mix.1 = (bf16[1024,512]{1,0:T(8,128)(2,1)}, f32[1024,512]{1,0:T(8,128)}) custom-call(bf16[1024,512]{1,0:T(8,128)(2,1)} %fusion.37.r_ref, bf16[1024,512]{1,0:T(8,128)(2,1)} %fusion.40.k_ref, bf16[1024,512]{1,0:T(8,128)(2,1)} %fusion.43.v_ref, f32[1024,512]{1,0:T(8,128)} %fusion.26.gate_ref, f32[1,512]{1,0:T(1,128)} %bitcast.226, ...), custom_call_target="tpu_custom_call" | custom-call | flops 1073741824 | bytes 11087872 | tf_op jit(solution)/shard_map/mix/pallas_call | solution.py:425
  219.6 4.3 convolution_convert_fusion.3
  226.2 4.3 collective-permute-done.7
  230.5 3.0 add_convert_fusion.5
  235.1 46.3 %collective-permute-done.8 = bf16[512,2048]{1,0:T(8,128)(2,1)} collective-permute-done((bf16[512,2048]{1,0:T(8,128)(2,1)S(1)}, bf16[512,2048]{1,0:T(8,128)(2,1)}, u32[]{:S(2)}, u32[]{:S(2)}) %collective-permute-start.8) | collective-permute-done | bytes 2097184 | tf_op jit(solution)/shard_map/ppermute | solution.py:48
  281.3 3.7 add_convert_fusion.4
  285.0 4.3 collective-permute-done.9
  289.4 3.7 maximum_select_fusion.refs_1_.refs_3_
  295.7 11.2 %collective-permute-start.10 = (f32[2,2048]{1,0:T(2,128)S(1)}, f32[2,2048]{1,0:T(2,128)S(1)}, u32[]{:S(2)}, u32[]{:S(2)}) collective-permute-start(f32[2,2048]{1,0:T(2,128)S(1)} %fusion.56), channel_id=1, source_target_pairs={{0,4},{4,8},{8,12},{1,5},{5,9},{9,13},{2,6},{6,10},{10,14},{3,7},{... | collective-permute-start | bytes 49160 | tf_op jit(solution)/shard_map/ppermute | solution.py:25
  309.0 19.1 %blend_two.1 = (bf16[1024,2048]{1,0:T(8,128)(2,1)}, bf16[1024,2048]{1,0:T(8,128)(2,1)}) custom-call(bf16[1024,2048]{1,0:T(8,128)(2,1)} %bitcast.194, bf16[1024,2048]{1,0:T(8,128)(2,1)} %copy-done, f32[1024,1]{1,0:T(8,128)} %bitcast.204, f32[2,1,2048]{2,1,0:T(1,128)} %copy.97.refs_3_.refs_9_, f32[2,2048]{1,0:T(2,128)} %get-tuple-element.240.refs_4_.refs_11_, ...), custom_call_target="tpu_custom_call" | custom-call | flops 41943040 | bytes 16777216 | tf_op jit(solution)/shard_map/blend_two/pallas_call | solution.py:526
  330.7 6.9 constant_dynamic-update-slice_fusion.8
  339.3 22.9 %collective-permute-done.11 = bf16[1024,512]{1,0:T(8,128)(2,1)S(1)} collective-permute-done((bf16[1024,512]{1,0:T(8,128)(2,1)}, bf16[1024,512]{1,0:T(8,128)(2,1)S(1)}, u32[]{:S(2)}, u32[]{:S(2)}) %collective-permute-start.11) | collective-permute-done | bytes 1048608 | tf_op jit(solution)/shard_map/ppermute | solution.py:48
  362.1 13.7 %multiply_convert_fusion.1 = (bf16[1024,1792]{1,0:T(8,128)(2,1)S(1)}, f32[1024,1792]{1,0:T(8,128)}) fusion(bf16[1024,2048]{1,0:T(8,128)(2,1)} %get-tuple-element.78, bf16[2048,2304]{1,0:T(8,128)(2,1)} %all-gather.6.cloned.1.call-done.refs_6_), kind=kOutput, calls=%fused_computation.5 | convolution fusion | flops 7521697792 | bytes 22544384 | tf_op jit(solution)/shard_map/dot_general | solution.py:184
  379.4 12.1 %convolution_convert_fusion.1 = bf16[1792,2048]{1,0:T(8,128)(2,1)} fusion(bf16[1024,1792]{1,0:T(8,128)(2,1)S(1)} %get-tuple-element.79, bf16[1024,2048]{1,0:T(8,128)(2,1)} %constant_dynamic-update-slice_fusion.5), kind=kOutput, calls=%fused_computation.3 | convolution fusion | flops 7519862784 | bytes 15204352 | tf_op jit(solution)/shard_map/dot_general | solution.py:188
  391.5 37.7 %all-gather.8.cloned.1.call-done = bf16[2048,1792]{0,1:T(8,128)(2,1)} async-done(((bf16[256,1792]{0,1:T(8,128)(2,1)}), bf16[2048,1792]{0,1:T(8,128)(2,1)}) %all-gather.8.cloned.1.call-update) | async-done | bytes 7340048 | tf_op jit(solution)/shard_map/all_gather | solution.py:798
  429.1 11.3 %convolution_convert_fusion.2 = bf16[1024,2048]{1,0:T(8,128)(2,1)S(1)} fusion(bf16[1024,1792]{1,0:T(8,128)(2,1)} %copy-done.47, bf16[2048,1792]{0,1:T(8,128)(2,1)} %all-gather.8.cloned.1.call-done), kind=kOutput, calls=%fused_computation.23 | convolution fusion | flops 7518289920 | bytes 15204352 | tf_op jit(solution)/shard_map/dot_general | solution.py:194
  450.2 14.2 %multiply_convert_fusion.refs_4_ = bf16[1024,1792]{1,0:T(8,128)(2,1)} fusion(f32[1024,1792]{1,0:T(8,128)} %get-tuple-element.234, bf16[1024,2048]{1,0:T(8,128)(2,1)} %constant_dynamic-update-slice_fusion.5, bf16[2048,1792]{0,1:T(8,128)(2,1)} %all-gather.8.cloned.1.call-done), kind=kOutput, calls=%fused_computation.4 | convolution fusion | flops 7523532800 | bytes 22544384 | tf_op jit(solution)/shard_map/dot_general | solution.py:184
  467.4 6.6 collective-permute-done.16
  474.0 4.7 fusion.19
  482.8 3.2 collective-permute-done.17
  486.6 44.9 %blend_two_back.1 = (bf16[1024,2048]{1,0:T(8,128)(2,1)}, f32[8,2048]{1,0:T(8,128)}) custom-call(bf16[1024,2048]{1,0:T(8,128)(2,1)} %bitcast.196, bf16[1024,2048]{1,0:T(8,128)(2,1)} %copy-done, bf16[1024,2048]{1,0:T(8,128)(2,1)} %bitcast.197, bf16[1024,2048]{1,0:T(8,128)(2,1)} %copy-done, bf16[1024,1792]{1,0:T(8,128)(2,1)} %multiply_convert_fusion.refs_4_, ...), custom_call_target="tpu_custom_call" | custom-call | flops 9663676416 | bytes 16777216 | tf_op jit(solution)/shard_map/blend_two_back/pallas_call | solution.py:686
  533.6 4.1 collective-permute-done.18
  540.2 10.0 %convolution_convert_fusion = bf16[2048,1792]{1,0:T(8,128)(2,1)S(1)} fusion(bf16[1024,2048]{1,0:T(8,128)(2,1)} %get-tuple-element.78, bf16[1024,1792]{1,0:T(8,128)(2,1)S(1)} %copy-done.38), kind=kOutput, calls=%fused_computation.2 | convolution fusion | flops 7519862784 | bytes 15204352 | tf_op jit(solution)/shard_map/dot_general | solution.py:188
  552.7 4.6 pad_maximum_fusion
  557.3 29.2 %collective-permute-done.19 = bf16[512,2048]{1,0:T(8,128)(2,1)} collective-permute-done((bf16[512,2048]{1,0:T(8,128)(2,1)S(1)}, bf16[512,2048]{1,0:T(8,128)(2,1)}, u32[]{:S(2)}, u32[]{:S(2)}) %collective-permute-start.19) | collective-permute-done | bytes 2097184 | tf_op jit(solution)/shard_map/ppermute | solution.py:48
  588.9 4.1 collective-permute-done.20
  593.1 3.8 maximum_select_fusion.1
  597.0 6.5 fusion.22.dj_ref
  603.5 11.3 %gate_back.1 = (bf16[1024,512]{1,0:T(8,128)(2,1)}, bf16[1024,512]{1,0:T(8,128)(2,1)}, f32[2,4,64,128]{3,2,1,0:T(8,128)}, f32[8,512]{1,0:T(8,128)}) custom-call(f32[1024,512]{1,0:T(8,128)} %fusion.22.dj_ref, f32[1024,512]{1,0:T(8,128)} %get-tuple-element.85.attend_ref, f32[1024,512]{1,0:T(8,128)} %fusion.26.gate_ref, bf16[1024,512]{1,0:T(8,128)(2,1)} %fusion.37.r_ref, ...), custom_call_target="tpu_custom_call" | custom-call | flops 67108864 | bytes 14749696 | tf_op jit(solution)/shard_map/gate_back/pallas_call | solution.py:425
  614.8 4.7 convolution_convert_fusion.8
  624.7 7.9 reshape.225
  632.5 6.4 constant_dynamic-slice_fusion.4
  654.3 8.9 collective-permute-done.24
  663.2 9.3 collective-permute-done.25
  673.3 19.9 %mix_back.1 = (bf16[1024,512]{1,0:T(8,128)(2,1)}, bf16[1024,512]{1,0:T(8,128)(2,1)}, bf16[1024,512]{1,0:T(8,128)(2,1)}, f32[8,512]{1,0:T(8,128)}) custom-call(bf16[1024,512]{1,0:T(8,128)(2,1)} %fusion.37.r_ref, bf16[1024,512]{1,0:T(8,128)(2,1)} %fusion.40.k_ref, bf16[1024,512]{1,0:T(8,128)(2,1)} %fusion.43.v_ref, ...), custom_call_target="tpu_custom_call" | custom-call | flops 3221225472 | bytes 9523200 | tf_op jit(solution)/shard_map/mix_back/pallas_call | solution.py:425
  693.2 6.9 collective-permute-done.27
  713.2 2.7 pad_maximum_fusion.2
  728.4 7.7 collective-permute-done.28
  739.8 44.2 %blend_one_back.1 = (bf16[1024,2048]{1,0:T(8,128)(2,1)}, f32[8,2048]{1,0:T(8,128)}) custom-call(bf16[1024,2048]{1,0:T(8,128)(2,1)} %bitcast.198, bf16[1024,2048]{1,0:T(8,128)(2,1)} %bitcast.199, bf16[1024,512]{1,0:T(8,128)(2,1)} %get-tuple-element.95.refs_2_, bf16[1024,512]{1,0:T(8,128)(2,1)} %get-tuple-element.96.refs_3_, ...), custom_call_target="tpu_custom_call" | custom-call | flops 8589934592 | bytes 16777216 | tf_op jit(solution)/shard_map/blend_one_back/pallas_call | solution.py:686
  785.8 8.1 collective-permute-done.29
  796.4 4.5 reduce-scatter.6.cloned.1.call-done.x_ref
  802.8 4.2 collective-permute-done.31
  807.0 3.0 add_convert_fusion.1
  814.8 3.9 collective-permute-start.37
  826.2 39.3 %collective-permute-done.34 = f32[14,2048]{1,0:T(8,128)S(1)} collective-permute-done((f32[14,2048]{1,0:T(8,128)S(1)}, f32[14,2048]{1,0:T(8,128)S(1)}, u32[]{:S(2)}, u32[]{:S(2)}) %collective-permute-start.34) | collective-permute-done | bytes 114720 | tf_op jit(solution)/shard_map/ppermute | solution.py:101
  869.7 10.7 %collective-permute-done.35 = f32[14,2048]{1,0:T(8,128)S(1)} collective-permute-done((f32[14,2048]{1,0:T(8,128)S(1)}, f32[14,2048]{1,0:T(8,128)S(1)}, u32[]{:S(2)}, u32[]{:S(2)}) %collective-permute-start.35) | collective-permute-done | bytes 114720 | tf_op jit(solution)/shard_map/ppermute | solution.py:101
  885.7 3.7 add_convert_fusion
  889.5 2.7 convert_element_type.413
  892.1 3.6 split_chan.1
  902.8 7.6 convert_add_fusion
  910.5 16.5 %collective-permute-done.41 = bf16[256,512]{1,0:T(8,128)(2,1)} collective-permute-done((bf16[256,512]{1,0:T(8,128)(2,1)}, bf16[256,512]{1,0:T(8,128)(2,1)}, u32[]{:S(2)}, u32[]{:S(2)}) %collective-permute-start.41) | collective-permute-done | bytes 262176 | tf_op jit(solution)/shard_map/ppermute | solution.py:101
  928.8 3.5 reduce-scatter.8.cloned.1.call-done.x_ref
  932.2 3.2 split_time.1
  (299 shorter events, 156.1 us)
Async XLA Ops:
  7.2 23.5 %copy-start.33 = (f32[2048]{0:T(1024)S(1)}, f32[2048]{0:T(1024)}, u32[]{:S(2)}) copy-start(f32[2048]{0:T(1024)} %param.35) | copy-start | bytes 24580
  7.2 23.5 %copy-start.32 = (f32[2048]{0:T(1024)S(1)}, f32[2048]{0:T(1024)}, u32[]{:S(2)}) copy-start(f32[2048]{0:T(1024)} %param.36) | copy-start | bytes 24580
  7.2 24.1 %copy-start.23 = (f32[2048]{0:T(1024)S(1)}, f32[2048]{0:T(1024)}, u32[]{:S(2)}) copy-start(f32[2048]{0:T(1024)} %param.37) | copy-start | bytes 24580
  7.3 24.1 %copy-start.25 = (f32[2048]{0:T(1024)S(1)}, f32[2048]{0:T(1024)}, u32[]{:S(2)}) copy-start(f32[2048]{0:T(1024)} %param.38) | copy-start | bytes 24580
  7.3 24.1 %copy-start.27 = (f32[2048]{0:T(1024)S(1)}, f32[2048]{0:T(1024)}, u32[]{:S(2)}) copy-start(f32[2048]{0:T(1024)} %param.39) | copy-start | bytes 24580
  7.3 24.1 %copy-start.29 = (f32[2048]{0:T(1024)S(1)}, f32[2048]{0:T(1024)}, u32[]{:S(2)}) copy-start(f32[2048]{0:T(1024)} %param.40) | copy-start | bytes 24580
  7.3 159.9 %all-gather.4.cloned.1.call-start = ((), (), s32[]{:S(2)}) async-start(), calls=%async_computation.3 | async-start | bytes 11796480 | tf_op jit(solution)/shard_map/all_gather | solution.py:778
  13.5 314.6 %all-gather.6.cloned.1.call-start = ((), (), s32[]{:S(2)}) async-start(), calls=%async_computation.4 | async-start | bytes 10616832 | tf_op jit(solution)/shard_map/all_gather | solution.py:786
  14.7 414.5 %all-gather.8.cloned.1.call-start = ((), (), s32[]{:S(2)}) async-start(), calls=%async_computation.5 | async-start | bytes 8257536 | tf_op jit(solution)/shard_map/all_gather | solution.py:798
  17.3 156.3 %copy-start.36 = (bf16[2,4,1,128]{3,2,1,0:T(2,128)(2,1)}, bf16[2,4,1,128]{3,2,1,0:T(2,128)(2,1)S(1)}, u32[]{:S(2)}) copy-start(bf16[2,4,1,128]{3,2,1,0:T(2,128)(2,1)S(1)} %get-tuple-element.196) | copy-start | bytes 6148
  17.3 20.4 %collective-permute-start.1 = (bf16[2,4,1,128]{3,2,1,0:T(2,128)(2,1)S(1)}, bf16[2,4,1,128]{3,2,1,0:T(2,128)(2,1)S(1)}, u32[]{:S(2)}, u32[]{:S(2)}) collective-permute-start(bf16[2,4,1,128]{3,2,1,0:T(2,128)(2,1)S(1)} %get-tuple-element.196), channel_id=1, source_target_pairs={{0,4},{4,8},{8,12},{1,5},{5,9},{9,13},{2,6},{6,10},{10,14},{3,7},{... | collective-permute-start | bytes 6152 | tf_op jit(solution)/shard_map/ppermute | solution.py:30
  22.2 15.4 %collective-permute-start.2 = (bf16[2,4,1,128]{3,2,1,0:T(2,128)(2,1)S(1)}, bf16[2,4,1,128]{3,2,1,0:T(2,128)(2,1)S(1)}, u32[]{:S(2)}, u32[]{:S(2)}) collective-permute-start(bf16[2,4,1,128]{3,2,1,0:T(2,128)(2,1)S(1)} %get-tuple-element.196), channel_id=1, source_target_pairs={{0,8},{4,12},{1,9},{5,13},{2,10},{6,14},{3,11},{7,15},{16,24},{20,... | collective-permute-start | bytes 6152 | tf_op jit(solution)/shard_map/ppermute | solution.py:30
  26.8 10.9 %collective-permute-start.3 = (bf16[2,4,1,128]{3,2,1,0:T(2,128)(2,1)S(1)}, bf16[2,4,1,128]{3,2,1,0:T(2,128)(2,1)S(1)}, u32[]{:S(2)}, u32[]{:S(2)}) collective-permute-start(bf16[2,4,1,128]{3,2,1,0:T(2,128)(2,1)S(1)} %get-tuple-element.196), channel_id=1, source_target_pairs={{0,12},{1,13},{2,14},{3,15},{16,28},{17,29},{18,30},{19,31}} | collective-permute-start | bytes 6152 | tf_op jit(solution)/shard_map/ppermute | solution.py:30
  29.3 8.4 collective-permute-start
  186.3 19.6 %collective-permute-start.4 = (bf16[2,4,64,128]{3,2,1,0:T(8,128)(2,1)S(1)}, bf16[2,4,64,128]{3,2,1,0:T(8,128)(2,1)S(1)}, u32[]{:S(2)}, u32[]{:S(2)}) collective-permute-start(bf16[2,4,64,128]{3,2,1,0:T(8,128)(2,1)S(1)} %convert_element_type.334), channel_id=1, source_target_pairs={{0,12},{1,13},{2,14},{3,15},{16,28},{17,29},{18,30},{19,31}} | collective-permute-start | bytes 393224 | tf_op jit(solution)/shard_map/ppermute | solution.py:30
  189.9 16.0 %collective-permute-start.5 = (bf16[2,4,64,128]{3,2,1,0:T(8,128)(2,1)S(1)}, bf16[2,4,64,128]{3,2,1,0:T(8,128)(2,1)S(1)}, u32[]{:S(2)}, u32[]{:S(2)}) collective-permute-start(bf16[2,4,64,128]{3,2,1,0:T(8,128)(2,1)S(1)} %convert_element_type.334), channel_id=1, source_target_pairs={{0,8},{4,12},{1,9},{5,13},{2,10},{6,14},{3,11},{7,15},{16,24},{20,... | collective-permute-start | bytes 393224 | tf_op jit(solution)/shard_map/ppermute | solution.py:30
  191.2 16.3 %collective-permute-start.6 = (bf16[2,4,64,128]{3,2,1,0:T(8,128)(2,1)S(1)}, bf16[2,4,64,128]{3,2,1,0:T(8,128)(2,1)S(1)}, u32[]{:S(2)}, u32[]{:S(2)}) collective-permute-start(bf16[2,4,64,128]{3,2,1,0:T(8,128)(2,1)S(1)} %convert_element_type.334), channel_id=1, source_target_pairs={{0,4},{4,8},{8,12},{1,5},{5,9},{9,13},{2,6},{6,10},{10,14},{3,7},{... | collective-permute-start | bytes 393224 | tf_op jit(solution)/shard_map/ppermute | solution.py:30
  226.1 4.4 collective-permute-start.7
  233.5 47.8 %collective-permute-start.8 = (bf16[512,2048]{1,0:T(8,128)(2,1)S(1)}, bf16[512,2048]{1,0:T(8,128)(2,1)}, u32[]{:S(2)}, u32[]{:S(2)}) collective-permute-start(bf16[512,2048]{1,0:T(8,128)(2,1)S(1)} %add_convert_fusion.5), channel_id=1, source_target_pairs={{0,2},{1,3},{2,0},{3,1},{4,6},{5,7},{6,4},{7,5},{8,10},{9,11},{10,... | collective-permute-start | bytes 6291464 | tf_op jit(solution)/shard_map/ppermute | solution.py:48
  235.0 361.8 %reduce-scatter.4.cloned.1.call-start = ((), (), s32[]{:S(2)}) async-start(), calls=%async_computation.6 | async-start | bytes 8257536 | tf_op jit(solution)/shard_map/reduce_scatter | solution.py:877
  285.0 4.4 collective-permute-start.9
  285.0 21.9 %copy-start.21 = (f32[2048]{0:T(1024)S(1)}, f32[2048]{0:T(1024)}, u32[]{:S(2)}) copy-start(f32[2048]{0:T(1024)} %param.47) | copy-start | bytes 24580
  285.0 21.9 %copy-start.22 = (f32[2048]{0:T(1024)S(1)}, f32[2048]{0:T(1024)}, u32[]{:S(2)}) copy-start(f32[2048]{0:T(1024)} %param.48) | copy-start | bytes 24580
  285.0 21.9 %copy-start.34 = (f32[2048]{0:T(1024)S(1)}, f32[2048]{0:T(1024)}, u32[]{:S(2)}) copy-start(f32[2048]{0:T(1024)} %param.46) | copy-start | bytes 24580
  285.0 21.9 %copy-start.35 = (f32[2048]{0:T(1024)S(1)}, f32[2048]{0:T(1024)}, u32[]{:S(2)}) copy-start(f32[2048]{0:T(1024)} %param.45) | copy-start | bytes 24580
  295.7 12.7 %collective-permute-start.10 = (f32[2,2048]{1,0:T(2,128)S(1)}, f32[2,2048]{1,0:T(2,128)S(1)}, u32[]{:S(2)}, u32[]{:S(2)}) collective-permute-start(f32[2,2048]{1,0:T(2,128)S(1)} %fusion.56), channel_id=1, source_target_pairs={{0,4},{4,8},{8,12},{1,5},{5,9},{9,13},{2,6},{6,10},{10,14},{3,7},{... | collective-permute-start | bytes 49160 | tf_op jit(solution)/shard_map/ppermute | solution.py:25
  337.6 24.5 %collective-permute-start.11 = (bf16[1024,512]{1,0:T(8,128)(2,1)}, bf16[1024,512]{1,0:T(8,128)(2,1)S(1)}, u32[]{:S(2)}, u32[]{:S(2)}) collective-permute-start(bf16[1024,512]{1,0:T(8,128)(2,1)} %get-tuple-element.238), channel_id=1, source_target_pairs={{0,2},{1,3},{2,0},{3,1},{4,6},{5,7},{6,4},{7,5},{8,10},{9,11},{10,... | collective-permute-start | bytes 3145736 | tf_op jit(solution)/shard_map/ppermute | solution.py:48
  339.3 37.7 %collective-permute-start.12 = (bf16[1024,512]{1,0:T(8,128)(2,1)}, bf16[1024,512]{1,0:T(8,128)(2,1)S(1)}, u32[]{:S(2)}, u32[]{:S(2)}) collective-permute-start(bf16[1024,512]{1,0:T(8,128)(2,1)} %get-tuple-element.238), channel_id=1, source_target_pairs={{0,1},{1,0},{2,3},{3,2},{4,5},{5,4},{6,7},{7,6},{8,9},{9,8},{10,11... | collective-permute-start | bytes 3145736 | tf_op jit(solution)/shard_map/ppermute | solution.py:48
  362.1 16.1 %collective-permute-start.13 = (bf16[1024,512]{1,0:T(8,128)(2,1)S(1)}, bf16[1024,512]{1,0:T(8,128)(2,1)S(1)}, u32[]{:S(2)}, u32[]{:S(2)}) collective-permute-start(bf16[1024,512]{1,0:T(8,128)(2,1)S(1)} %collective-permute-done.11), channel_id=1, source_target_pairs={{0,1},{1,0},{2,3},{3,2},{4,5},{5,4},{6,7},{7,6},{8,9},{9,8},{10,11... | collective-permute-start | bytes 3145736 | tf_op jit(solution)/shard_map/ppermute | solution.py:48
  443.7 3.0 collective-permute-start.15
  443.7 357.2 %reduce-scatter.6.cloned.1.call-start = ((), (), s32[]{:S(2)}) async-start(), calls=%async_computation.7 | async-start | bytes 10616832 | tf_op jit(solution)/shard_map/reduce_scatter | solution.py:921
  443.9 23.6 %collective-permute-start.14 = (bf16[1024,512]{1,0:T(8,128)(2,1)S(1)}, bf16[1024,512]{1,0:T(8,128)(2,1)}, u32[]{:S(2)}, u32[]{:S(2)}) collective-permute-start(bf16[1024,512]{1,0:T(8,128)(2,1)S(1)} %get-tuple-element.210), channel_id=1, source_target_pairs={{0,1},{1,0},{2,3},{3,2},{4,5},{5,4},{6,7},{7,6},{8,9},{9,8},{10,11... | collective-permute-start | bytes 3145736 | tf_op jit(solution)/shard_map/ppermute | solution.py:48
  446.7 18.7 %slice-start = ((s8[9437184]{0:T(1024)(128)(4,1)}), s8[4194304]{0:T(1024)(128)(4,1)S(1)}, s32[]{:S(2)}) async-start(s8[9437184]{0:T(1024)(128)(4,1)} %bitcast.201), calls=%async_computation.9 | async-start | bytes 8388608
  448.7 25.4 %collective-permute-start.16 = (bf16[1024,512]{1,0:T(8,128)(2,1)S(1)}, bf16[1024,512]{1,0:T(8,128)(2,1)}, u32[]{:S(2)}, u32[]{:S(2)}) collective-permute-start(bf16[1024,512]{1,0:T(8,128)(2,1)S(1)} %add_convert_fusion.7), channel_id=1, source_target_pairs={{0,2},{1,3},{2,0},{3,1},{4,6},{5,7},{6,4},{7,5},{8,10},{9,11},{10,... | collective-permute-start | bytes 3145736 | tf_op jit(solution)/shard_map/ppermute | solution.py:48
  450.2 15.2 %slice-start.1 = ((s8[9437184]{0:T(1024)(128)(4,1)}), s8[4194304]{0:T(1024)(128)(4,1)S(1)}, s32[]{:S(2)}) async-start(s8[9437184]{0:T(1024)(128)(4,1)} %bitcast.201), calls=%async_computation.10 | async-start | bytes 8388608
  450.2 15.2 %slice-start.2 = ((s8[9437184]{0:T(1024)(128)(4,1)}), s8[1048576]{0:T(1024)(128)(4,1)S(1)}, s32[]{:S(2)}) async-start(s8[9437184]{0:T(1024)(128)(4,1)} %bitcast.201), calls=%async_computation.11 | async-start | bytes 2097152
  479.3 6.7 collective-permute-start.17
  533.5 4.2 collective-permute-start.18
  538.6 47.8 %collective-permute-start.19 = (bf16[512,2048]{1,0:T(8,128)(2,1)S(1)}, bf16[512,2048]{1,0:T(8,128)(2,1)}, u32[]{:S(2)}, u32[]{:S(2)}) collective-permute-start(bf16[512,2048]{1,0:T(8,128)(2,1)S(1)} %add_convert_fusion.3), channel_id=1, source_target_pairs={{0,2},{1,3},{2,0},{3,1},{4,6},{5,7},{6,4},{7,5},{8,10},{9,11},{10,... | collective-permute-start | bytes 6291464 | tf_op jit(solution)/shard_map/ppermute | solution.py:48
  588.8 4.2 collective-permute-start.20
  596.9 335.3 %reduce-scatter.8.cloned.1.call-start = ((), (), s32[]{:S(2)}) async-start(), calls=%async_computation.8 | async-start | bytes 4718592 | tf_op jit(solution)/shard_map/reduce_scatter | solution.py:987
  640.6 59.5 %collective-permute-start.27 = (bf16[2,2,256,1024]{2,3,0,1:T(8,128)(2,1)}, bf16[2,2,256,1024]{2,3,0,1:T(8,128)(2,1)S(1)}, u32[]{:S(2)}, u32[]{:S(2)}) collective-permute-start(bf16[2,2,256,1024]{2,3,0,1:T(8,128)(2,1)} %bitcast.191), channel_id=1, source_target_pairs={{0,16},{16,0},{1,17},{17,1},{2,18},{18,2},{3,19},{19,3},{4,20},{20... | collective-permute-start | bytes 6291464 | tf_op jit(solution)/shard_map/ppermute | solution.py:101
  642.3 5.8 collective-permute-start.21
  643.6 6.7 collective-permute-start.22
  644.9 9.3 collective-permute-start.23
  650.4 12.9 %collective-permute-start.24 = (bf16[2,4,64,128]{3,2,1,0:T(8,128)(2,1)S(1)}, bf16[2,4,64,128]{3,2,1,0:T(8,128)(2,1)S(1)}, u32[]{:S(2)}, u32[]{:S(2)}) collective-permute-start(bf16[2,4,64,128]{3,2,1,0:T(8,128)(2,1)S(1)} %convert_element_type.377), channel_id=1, source_target_pairs={{12,0},{13,1},{14,2},{15,3},{28,16},{29,17},{30,18},{31,19}} | collective-permute-start | bytes 393224 | tf_op jit(solution)/shard_map/ppermute | solution.py:30
  651.7 20.9 %collective-permute-start.25 = (bf16[2,4,64,128]{3,2,1,0:T(8,128)(2,1)S(1)}, bf16[2,4,64,128]{3,2,1,0:T(8,128)(2,1)S(1)}, u32[]{:S(2)}, u32[]{:S(2)}) collective-permute-start(bf16[2,4,64,128]{3,2,1,0:T(8,128)(2,1)S(1)} %convert_element_type.377), channel_id=1, source_target_pairs={{8,0},{12,4},{9,1},{13,5},{10,2},{14,6},{11,3},{15,7},{24,16},{28,... | collective-permute-start | bytes 393224 | tf_op jit(solution)/shard_map/ppermute | solution.py:30
  653.0 19.6 %collective-permute-start.26 = (bf16[2,4,64,128]{3,2,1,0:T(8,128)(2,1)S(1)}, bf16[2,4,64,128]{3,2,1,0:T(8,128)(2,1)S(1)}, u32[]{:S(2)}, u32[]{:S(2)}) collective-permute-start(bf16[2,4,64,128]{3,2,1,0:T(8,128)(2,1)S(1)} %convert_element_type.377), channel_id=1, source_target_pairs={{4,0},{8,4},{12,8},{5,1},{9,5},{13,9},{6,2},{10,6},{14,10},{7,3},{... | collective-permute-start | bytes 393224 | tf_op jit(solution)/shard_map/ppermute | solution.py:30
  707.7 76.3 %collective-permute-start.30 = (bf16[2,2,256,512]{3,2,1,0:T(8,128)(2,1)}, bf16[2,2,256,512]{3,2,1,0:T(8,128)(2,1)}, u32[]{:S(2)}, u32[]{:S(2)}) collective-permute-start(bf16[2,2,256,512]{3,2,1,0:T(8,128)(2,1)} %dynamic-slice_bitcast_fusion), channel_id=1, source_target_pairs={{0,16},{16,0},{1,17},{17,1},{2,18},{18,2},{3,19},{19,3},{4,20},{20... | collective-permute-start | bytes 3145736 | tf_op jit(solution)/shard_map/ppermute | solution.py:101
  727.0 9.1 collective-permute-start.28
  737.8 56.1 %collective-permute-start.29 = (bf16[2,256,1024]{1,2,0:T(8,128)(2,1)}, bf16[2,256,1024]{1,2,0:T(8,128)(2,1)}, u32[]{:S(2)}, u32[]{:S(2)}) collective-permute-start(bf16[2,256,1024]{1,2,0:T(8,128)(2,1)} %dynamic-slice_bitcast_fusion.1), channel_id=1, source_target_pairs={{0,4},{4,0},{8,12},{12,8},{1,5},{5,1},{9,13},{13,9},{2,6},{6,2},{1... | collective-permute-start | bytes 3145736 | tf_op jit(solution)/shard_map/ppermute | solution.py:101
  802.7 4.4 collective-permute-start.31
  802.8 15.9 %copy-start.20 = (f32[8,2048]{1,0:T(8,128)S(1)}, f32[8,2048]{1,0:T(8,128)}, u32[]{:S(2)}) copy-start(f32[8,2048]{1,0:T(8,128)} %get-tuple-element.104) | copy-start | bytes 196612
  810.0 75.7 %collective-permute-start.39 = (bf16[512,2048]{1,0:T(8,128)(2,1)S(1)}, bf16[512,2048]{1,0:T(8,128)(2,1)}, u32[]{:S(2)}, u32[]{:S(2)}) collective-permute-start(bf16[512,2048]{1,0:T(8,128)(2,1)S(1)} %add_convert_fusion.1), channel_id=1, source_target_pairs={{0,2},{1,3},{2,0},{3,1},{4,6},{5,7},{6,4},{7,5},{8,10},{9,11},{10,... | collective-permute-start | bytes 6291464 | tf_op jit(solution)/shard_map/ppermute | solution.py:48
  814.8 52.4 %collective-permute-start.37 = (bf16[256,1024]{0,1:T(8,128)(2,1)}, bf16[256,1024]{0,1:T(8,128)(2,1)}, u32[]{:S(2)}, u32[]{:S(2)}) collective-permute-start(bf16[256,1024]{0,1:T(8,128)(2,1)} %dynamic-slice_bitcast_fusion.3), channel_id=1, source_target_pairs={{0,8},{4,12},{8,0},{12,4},{1,9},{5,13},{9,1},{13,5},{2,10},{6,14},... | collective-permute-start | bytes 1572872 | tf_op jit(solution)/shard_map/ppermute | solution.py:101
  818.8 5.1 collective-permute-start.32
  821.0 60.7 %collective-permute-start.38 = (bf16[2,256,512]{2,1,0:T(8,128)(2,1)}, bf16[2,256,512]{2,1,0:T(8,128)(2,1)}, u32[]{:S(2)}, u32[]{:S(2)}) collective-permute-start(bf16[2,256,512]{2,1,0:T(8,128)(2,1)} %dynamic-slice_bitcast_fusion.2), channel_id=1, source_target_pairs={{0,4},{4,0},{8,12},{12,8},{1,5},{5,1},{9,13},{13,9},{2,6},{6,2},{1... | collective-permute-start | bytes 1572872 | tf_op jit(solution)/shard_map/ppermute | solution.py:101
  823.8 1.4 collective-permute-start.33
  825.3 40.3 %collective-permute-start.34 = (f32[14,2048]{1,0:T(8,128)S(1)}, f32[14,2048]{1,0:T(8,128)S(1)}, u32[]{:S(2)}, u32[]{:S(2)}) collective-permute-start(f32[14,2048]{1,0:T(8,128)S(1)} %add.283), channel_id=1, source_target_pairs={{0,4},{4,0},{8,12},{12,8},{1,5},{5,1},{9,13},{13,9},{2,6},{6,2},{1... | collective-permute-start | bytes 344072 | tf_op jit(solution)/shard_map/ppermute | solution.py:101
  865.6 14.8 %collective-permute-start.35 = (f32[14,2048]{1,0:T(8,128)S(1)}, f32[14,2048]{1,0:T(8,128)S(1)}, u32[]{:S(2)}, u32[]{:S(2)}) collective-permute-start(f32[14,2048]{1,0:T(8,128)S(1)} %add.284), channel_id=1, source_target_pairs={{0,8},{4,12},{8,0},{12,4},{1,9},{5,13},{9,1},{13,5},{2,10},{6,14},... | collective-permute-start | bytes 344072 | tf_op jit(solution)/shard_map/ppermute | solution.py:101
  880.4 5.3 collective-permute-start.36
  889.5 11.9 %copy-start.4 = (f32[256,1024]{0,1:T(8,128)S(1)}, f32[256,1024]{0,1:T(8,128)}, u32[]{:S(2)}) copy-start(f32[256,1024]{0,1:T(8,128)} %get-tuple-element.194) | copy-start | bytes 3145732
  889.5 13.4 %collective-permute-start.40 = (bf16[512,2048]{1,0:T(8,128)(2,1)}, bf16[512,2048]{1,0:T(8,128)(2,1)S(1)}, u32[]{:S(2)}, u32[]{:S(2)}) collective-permute-start(bf16[512,2048]{1,0:T(8,128)(2,1)} %add_convert_fusion), channel_id=1, source_target_pairs={{0,1},{1,0},{2,3},{3,2},{4,5},{5,4},{6,7},{7,6},{8,9},{9,8},{10,11... | collective-permute-start | bytes 6291464 | tf_op jit(solution)/shard_map/ppermute | solution.py:48
  899.3 27.7 %collective-permute-start.41 = (bf16[256,512]{1,0:T(8,128)(2,1)}, bf16[256,512]{1,0:T(8,128)(2,1)}, u32[]{:S(2)}, u32[]{:S(2)}) collective-permute-start(bf16[256,512]{1,0:T(8,128)(2,1)} %get-tuple-element.213), channel_id=1, source_target_pairs={{0,8},{4,12},{8,0},{12,4},{1,9},{5,13},{9,1},{13,5},{2,10},{6,14},... | collective-permute-start | bytes 786440 | tf_op jit(solution)/shard_map/ppermute | solution.py:101
  (35 other events, 214.8 us)
Sparse Core Ops, SparseCore 0:
  13.6 153.5 all-gather.3
  169.9 146.5 all-gather.5
  318.5 110.6 all-gather.7
  443.8 131.6 reduce-scatter.3
  597.0 203.8 reduce-scatter.5
  804.4 127.7 reduce-scatter.7

commit v9 on v8

--- a/solution.py
+++ b/solution.py
@@ -86,7 +86,7 @@
         part = add_low(part, arrived)
         bit *= 2
     whole = ordered(part, partner(part, 1), 0, 1)
-    return (whole, made) if work else whole
+    return (whole, made, part) if work else whole
 
 
 def axis_bits(axis):
@@ -916,8 +916,8 @@
             axis=1,
         )
 
-    d_mixed, grads_chan = tp_sum(d_middle_part, chan_grads)
-    d_mixed, grads_chan, g_chanvalue = after(d_mixed, grads_chan, g_chanvalue)
+    d_mixed, grads_chan, exchanged = tp_sum(d_middle_part, chan_grads)
+    grads_chan, g_chanvalue, _ = after(grads_chan, g_chanvalue, exchanged)
     g_chan = lax.psum_scatter(grads_chan, owners, scatter_dimension=0, tiled=True)
     grad_output_t = matmul_tn(d_mixed, joined_low).astype(jnp.bfloat16)
     d_joined = matmul(d_mixed, w_output_t)
@@ -1017,7 +1017,7 @@
         )
         return total, g_early, g_value
 
-    d_input_sum, (small_sum, g_early, g_value) = tp_sum(d_input_part, small_total)
+    d_input_sum, (small_sum, g_early, g_value), _ = tp_sum(d_input_part, small_total)
     owned = embedding_extent // (lax.axis_size("fsdp") * lax.axis_size("ctx"))
     small_owned = lax.dynamic_slice_in_dim(
         small_sum,

time: 950 us -> 944 us (level)
  waiting for transfers between devices: 405 us -> 390 us
  transfers between devices with their start and end apart: 48 -> 48, of which waited for: 30 -> 29; matrix products, arithmetic and copies ran while one was open for 26% -> 28% of each run, Pallas kernels for 19% -> 19%
where the time goes in v9:
time: 944 us; the launch traced here: 937 us
  waiting for transfers between devices  390 us (41%)
  Pallas kernels  184 us (19%)
  matrix products  135 us (14%)
  other arithmetic  76.6 us (8%)
  starting transfers between devices  69 us (7%)
  local copies, waits for them, and re-layouts  67 us (7%)
  between operations  15.5 us (2%)
    ppermute x15, waiting for transfers between devices, partner(): return lax.ppermute(x, 'tp', [(i, i ^ bit) for i in range(count)])  127 us
    all_gather x1, waiting for transfers between devices, per_device(): lax.all_gather(jnp.concatenate([acceptor_matrix, lookup_matrix, payload_m...  108 us
    pallas_call x2, Pallas kernels, blend_back(): pl.pallas_call(partial(blend_back_kernel, len(xs), mixes, per_seq, int(ow...  88.5 us
    ppermute x11, waiting for transfers between devices, swap(): lax.ppermute(x, axis, [(i, i ^ bit) for i in range(lax.axis_size(axis))])  82.1 us
    dot_general x8, matrix products, matmul(): return jnp.dot(left, right, preferred_element_type=jnp.float32)  65.5 us
    pallas_call x4, Pallas kernels, pair_call(): pl.pallas_call(kernel, grid=(pairs, seqs), in_specs=[specs[kind] for kind...  49.1 us
    dot_general x8, matrix products, matmul_tn(): lax.dot_general(left, right, (((0,), (0,)), ((), ())), preferred_element_...  42.4 us
    pallas_call x2, Pallas kernels, blend(): pl.pallas_call(partial(blend_kernel, len(xs), mixes, per_seq), grid=(toke...  39.9 us
  transfers between devices with their start and end apart: 48, of which 29 were waited for; matrix products, arithmetic and copies ran while one was open for 28% of the time, Pallas kernels for 19%

profile of v9, /device:TPU:0, one launch (start us, length us, event | category | flops | bytes accessed | tf_op | source)
XLA Modules:
  0.0 937.0 jit_solution(3491612577548019152)
XLA Ops:
  17.3 4.9 collective-permute-start.1
  22.2 4.5 collective-permute-start.2
  38.3 20.8 %blend_one.1 = (bf16[1024,2048]{1,0:T(8,128)(2,1)}, bf16[1024,2048]{1,0:T(8,128)(2,1)}, bf16[1024,2048]{1,0:T(8,128)(2,1)}, bf16[1024,2048]{1,0:T(8,128)(2,1)}) custom-call(bf16[1024,2048]{1,0:T(8,128)(2,1)} %bitcast.191, f32[1024,1]{1,0:T(8,128)} %bitcast.201, f32[2,1,2048]{2,1,0:T(1,128)} %broadcast_in_dim.20.refs_2_.refs_11_, ...), custom_call_target="tpu_custom_call" | custom-call | flops 41943040 | bytes 20971520 | tf_op jit(solution)/shard_map/blend_one/pallas_call | solution.py:526
  59.1 108.1 %all-gather.4.cloned.1.call-done.refs_6_.refs_7_.refs_8_.refs_9_ = bf16[2048,2560]{1,0:T(8,128)(2,1)} async-done(((bf16[256,2560]{1,0:T(8,128)(2,1)}), bf16[2048,2560]{1,0:T(8,128)(2,1)}) %all-gather.4.cloned.1.call-update) | async-done | bytes 10485776 | tf_op jit(solution)/shard_map/all_gather | solution.py:778
  167.2 6.4 fusion.40.k_ref
  173.6 4.9 fusion.43.v_ref
  178.5 6.9 carry.1
  186.4 3.5 collective-permute-start.4
  193.9 6.3 fusion.37.r_ref
  200.2 5.2 fusion.26.gate_ref
  208.3 11.3 %mix.1 = (bf16[1024,512]{1,0:T(8,128)(2,1)}, f32[1024,512]{1,0:T(8,128)}) custom-call(bf16[1024,512]{1,0:T(8,128)(2,1)} %fusion.37.r_ref, bf16[1024,512]{1,0:T(8,128)(2,1)} %fusion.40.k_ref, bf16[1024,512]{1,0:T(8,128)(2,1)} %fusion.43.v_ref, f32[1024,512]{1,0:T(8,128)} %fusion.26.gate_ref, f32[1,512]{1,0:T(1,128)} %bitcast.224, ...), custom_call_target="tpu_custom_call" | custom-call | flops 1073741824 | bytes 11087872 | tf_op jit(solution)/shard_map/mix/pallas_call | solution.py:425
  219.6 4.3 convolution_convert_fusion.3
  226.2 4.3 collective-permute-done.7
  230.5 3.0 add_convert_fusion.5
  235.1 46.2 %collective-permute-done.8 = bf16[512,2048]{1,0:T(8,128)(2,1)} collective-permute-done((bf16[512,2048]{1,0:T(8,128)(2,1)S(1)}, bf16[512,2048]{1,0:T(8,128)(2,1)}, u32[]{:S(2)}, u32[]{:S(2)}) %collective-permute-start.8) | collective-permute-done | bytes 2097184 | tf_op jit(solution)/shard_map/ppermute | solution.py:48
  281.4 3.7 add_convert_fusion.4
  285.1 4.3 collective-permute-done.9
  289.4 3.7 maximum_select_fusion.refs_1_.refs_3_
  295.7 11.3 %collective-permute-start.10 = (f32[2,2048]{1,0:T(2,128)S(1)}, f32[2,2048]{1,0:T(2,128)S(1)}, u32[]{:S(2)}, u32[]{:S(2)}) collective-permute-start(f32[2,2048]{1,0:T(2,128)S(1)} %fusion.56), channel_id=1, source_target_pairs={{0,4},{4,8},{8,12},{1,5},{5,9},{9,13},{2,6},{6,10},{10,14},{3,7},{... | collective-permute-start | bytes 49160 | tf_op jit(solution)/shard_map/ppermute | solution.py:25
  309.1 19.1 %blend_two.1 = (bf16[1024,2048]{1,0:T(8,128)(2,1)}, bf16[1024,2048]{1,0:T(8,128)(2,1)}) custom-call(bf16[1024,2048]{1,0:T(8,128)(2,1)} %bitcast.192, bf16[1024,2048]{1,0:T(8,128)(2,1)} %copy-done, f32[1024,1]{1,0:T(8,128)} %bitcast.202, f32[2,1,2048]{2,1,0:T(1,128)} %copy.97.refs_3_.refs_9_, f32[2,2048]{1,0:T(2,128)} %get-tuple-element.238.refs_4_.refs_11_, ...), custom_call_target="tpu_custom_call" | custom-call | flops 41943040 | bytes 16777216 | tf_op jit(solution)/shard_map/blend_two/pallas_call | solution.py:526
  330.7 7.3 constant_dynamic-update-slice_fusion.8
  339.7 22.6 %collective-permute-done.11 = bf16[1024,512]{1,0:T(8,128)(2,1)S(1)} collective-permute-done((bf16[1024,512]{1,0:T(8,128)(2,1)S(1)}, bf16[1024,512]{1,0:T(8,128)(2,1)S(1)}, u32[]{:S(2)}, u32[]{:S(2)}) %collective-permute-start.11) | collective-permute-done | bytes 1048608 | tf_op jit(solution)/shard_map/ppermute | solution.py:48
  362.3 13.7 %multiply_convert_fusion.1 = (bf16[1024,1792]{1,0:T(8,128)(2,1)S(1)}, f32[1024,1792]{1,0:T(8,128)}) fusion(bf16[1024,2048]{1,0:T(8,128)(2,1)} %get-tuple-element.77, bf16[2048,2304]{1,0:T(8,128)(2,1)} %all-gather.6.cloned.1.call-done.refs_6_), kind=kOutput, calls=%fused_computation.5 | convolution fusion | flops 7521697792 | bytes 22544384 | tf_op jit(solution)/shard_map/dot_general | solution.py:184
  379.7 12.1 %convolution_convert_fusion.1 = bf16[1792,2048]{1,0:T(8,128)(2,1)} fusion(bf16[1024,1792]{1,0:T(8,128)(2,1)S(1)} %get-tuple-element.78, bf16[1024,2048]{1,0:T(8,128)(2,1)} %constant_dynamic-update-slice_fusion.5), kind=kOutput, calls=%fused_computation.3 | convolution fusion | flops 7519862784 | bytes 15204352 | tf_op jit(solution)/shard_map/dot_general | solution.py:188
  392.3 37.0 %all-gather.8.cloned.1.call-done = bf16[2048,1792]{0,1:T(8,128)(2,1)} async-done(((bf16[256,1792]{0,1:T(8,128)(2,1)}), bf16[2048,1792]{0,1:T(8,128)(2,1)}) %all-gather.8.cloned.1.call-update) | async-done | bytes 7340048 | tf_op jit(solution)/shard_map/all_gather | solution.py:798
  429.3 11.1 %convolution_convert_fusion.2 = bf16[1024,2048]{1,0:T(8,128)(2,1)S(1)} fusion(bf16[1024,1792]{1,0:T(8,128)(2,1)} %copy-done.45, bf16[2048,1792]{0,1:T(8,128)(2,1)} %all-gather.8.cloned.1.call-done), kind=kOutput, calls=%fused_computation.23 | convolution fusion | flops 7518289920 | bytes 15204352 | tf_op jit(solution)/shard_map/dot_general | solution.py:194
  447.2 14.3 %multiply_convert_fusion.refs_4_ = bf16[1024,1792]{1,0:T(8,128)(2,1)} fusion(f32[1024,1792]{1,0:T(8,128)} %get-tuple-element.232, bf16[1024,2048]{1,0:T(8,128)(2,1)} %constant_dynamic-update-slice_fusion.5, bf16[2048,1792]{0,1:T(8,128)(2,1)} %all-gather.8.cloned.1.call-done), kind=kOutput, calls=%fused_computation.4 | convolution fusion | flops 7523532800 | bytes 22544384 | tf_op jit(solution)/shard_map/dot_general | solution.py:184
  464.5 6.7 collective-permute-done.16
  471.2 4.6 fusion.19
  483.2 44.6 %blend_two_back.1 = (bf16[1024,2048]{1,0:T(8,128)(2,1)}, f32[8,2048]{1,0:T(8,128)}) custom-call(bf16[1024,2048]{1,0:T(8,128)(2,1)} %bitcast.194, bf16[1024,2048]{1,0:T(8,128)(2,1)} %copy-done, bf16[1024,2048]{1,0:T(8,128)(2,1)} %bitcast.195, bf16[1024,2048]{1,0:T(8,128)(2,1)} %copy-done, bf16[1024,1792]{1,0:T(8,128)(2,1)} %multiply_convert_fusion.refs_4_, ...), custom_call_target="tpu_custom_call" | custom-call | flops 9663676416 | bytes 16777216 | tf_op jit(solution)/shard_map/blend_two_back/pallas_call | solution.py:686
  529.8 4.1 collective-permute-done.18
  536.5 10.7 %convolution_convert_fusion = bf16[2048,1792]{1,0:T(8,128)(2,1)S(1)} fusion(bf16[1024,2048]{1,0:T(8,128)(2,1)} %get-tuple-element.77, bf16[1024,1792]{1,0:T(8,128)(2,1)S(1)} %copy-done.37), kind=kOutput, calls=%fused_computation.2 | convolution fusion | flops 7519862784 | bytes 15204352 | tf_op jit(solution)/shard_map/dot_general | solution.py:188
  549.7 4.6 pad_maximum_fusion
  554.3 28.4 %collective-permute-done.19 = bf16[512,2048]{1,0:T(8,128)(2,1)} collective-permute-done((bf16[512,2048]{1,0:T(8,128)(2,1)S(1)}, bf16[512,2048]{1,0:T(8,128)(2,1)}, u32[]{:S(2)}, u32[]{:S(2)}) %collective-permute-start.19) | collective-permute-done | bytes 2097184 | tf_op jit(solution)/shard_map/ppermute | solution.py:48
  582.8 3.0 add_convert_fusion.2
  586.2 4.3 collective-permute-done.20
  590.5 7.3 fusion.22.dj_ref
  597.8 11.2 %gate_back.1 = (bf16[1024,512]{1,0:T(8,128)(2,1)}, bf16[1024,512]{1,0:T(8,128)(2,1)}, f32[2,4,64,128]{3,2,1,0:T(8,128)}, f32[8,512]{1,0:T(8,128)}) custom-call(f32[1024,512]{1,0:T(8,128)} %fusion.22.dj_ref, f32[1024,512]{1,0:T(8,128)} %get-tuple-element.83.attend_ref, f32[1024,512]{1,0:T(8,128)} %fusion.26.gate_ref, bf16[1024,512]{1,0:T(8,128)(2,1)} %fusion.37.r_ref, ...), custom_call_target="tpu_custom_call" | custom-call | flops 67108864 | bytes 14749696 | tf_op jit(solution)/shard_map/gate_back/pallas_call | solution.py:425
  609.0 5.0 convolution_convert_fusion.7
  614.0 4.8 convolution_convert_fusion.8
  621.4 7.8 reshape.234
  629.3 6.5 constant_dynamic-slice_fusion.4
  651.7 8.9 collective-permute-done.24
  660.6 9.0 collective-permute-done.25
  670.5 19.6 %mix_back.1 = (bf16[1024,512]{1,0:T(8,128)(2,1)}, bf16[1024,512]{1,0:T(8,128)(2,1)}, bf16[1024,512]{1,0:T(8,128)(2,1)}, f32[8,512]{1,0:T(8,128)}) custom-call(bf16[1024,512]{1,0:T(8,128)(2,1)} %fusion.37.r_ref, bf16[1024,512]{1,0:T(8,128)(2,1)} %fusion.40.k_ref, bf16[1024,512]{1,0:T(8,128)(2,1)} %fusion.43.v_ref, ...), custom_call_target="tpu_custom_call" | custom-call | flops 3221225472 | bytes 9523200 | tf_op jit(solution)/shard_map/mix_back/pallas_call | solution.py:425
  690.1 7.4 collective-permute-done.27
  697.5 4.0 fusion.4
  712.6 2.7 pad_maximum_fusion.2
  727.9 4.1 collective-permute-done.28
  736.9 43.9 %blend_one_back.1 = (bf16[1024,2048]{1,0:T(8,128)(2,1)}, f32[8,2048]{1,0:T(8,128)}) custom-call(bf16[1024,2048]{1,0:T(8,128)(2,1)} %bitcast.196, bf16[1024,2048]{1,0:T(8,128)(2,1)} %bitcast.197, bf16[1024,512]{1,0:T(8,128)(2,1)} %get-tuple-element.93.refs_2_, bf16[1024,512]{1,0:T(8,128)(2,1)} %get-tuple-element.94.refs_3_, ...), custom_call_target="tpu_custom_call" | custom-call | flops 8589934592 | bytes 16777216 | tf_op jit(solution)/shard_map/blend_one_back/pallas_call | solution.py:686
  782.7 12.4 %collective-permute-done.29 = bf16[2,256,1024]{1,2,0:T(8,128)(2,1)} collective-permute-done((bf16[2,256,1024]{1,2,0:T(8,128)(2,1)}, bf16[2,256,1024]{1,2,0:T(8,128)(2,1)}, u32[]{:S(2)}, u32[]{:S(2)}) %collective-permute-start.29) | collective-permute-done | bytes 1048608 | tf_op jit(solution)/shard_map/ppermute | solution.py:101
  795.1 2.8 fusion.21
  797.9 3.1 constant_dynamic-slice_fusion.2
  801.1 4.5 collective-permute-done.31
  805.5 4.4 add_convert_fusion.1
  824.3 38.0 %collective-permute-done.34 = f32[14,2048]{1,0:T(8,128)S(1)} collective-permute-done((f32[14,2048]{1,0:T(8,128)S(1)}, f32[14,2048]{1,0:T(8,128)S(1)}, u32[]{:S(2)}, u32[]{:S(2)}) %collective-permute-start.34) | collective-permute-done | bytes 114720 | tf_op jit(solution)/shard_map/ppermute | solution.py:101
  862.4 3.3 collective-permute-start.35
  868.1 7.4 collective-permute-done.35
  881.1 4.5 add_convert_fusion
  888.2 3.6 split_chan.1
  899.0 9.5 %convert_add_fusion = f32[1024,2048]{1,0:T(8,128)} fusion(bf16[512,2048]{1,0:T(8,128)(2,1)} %collective-permute-done.40, bf16[512,2048]{1,0:T(8,128)(2,1)} %add_convert_fusion, pred[]{:T(512)S(6)} %eq.54, bf16[512,2048]{1,0:T(8,128)(2,1)S(1)} %add_convert_fusion.2, bf16[512,2048]{1,0:T(8,128)(2,1)} %collective-permute-done.20), kind=kLoop, calls=%fused_computation.1 | loop fusion | flops 44040192 | bytes 16777216 | tf_op jit(solution)/shard_map/add | solution.py:1028
  908.4 13.0 %collective-permute-done.41 = bf16[256,512]{1,0:T(8,128)(2,1)} collective-permute-done((bf16[256,512]{1,0:T(8,128)(2,1)}, bf16[256,512]{1,0:T(8,128)(2,1)}, u32[]{:S(2)}, u32[]{:S(2)}) %collective-permute-start.41) | collective-permute-done | bytes 262176 | tf_op jit(solution)/shard_map/ppermute | solution.py:101
  923.3 3.4 reduce-scatter.8.cloned.1.call-done.x_ref
  926.7 3.2 split_time.1
  (294 shorter events, 154.0 us)
Async XLA Ops:
  7.2 23.5 %copy-start.32 = (f32[2048]{0:T(1024)S(1)}, f32[2048]{0:T(1024)}, u32[]{:S(2)}) copy-start(f32[2048]{0:T(1024)} %param.35) | copy-start | bytes 24580
  7.2 23.5 %copy-start.31 = (f32[2048]{0:T(1024)S(1)}, f32[2048]{0:T(1024)}, u32[]{:S(2)}) copy-start(f32[2048]{0:T(1024)} %param.36) | copy-start | bytes 24580
  7.2 24.1 %copy-start.22 = (f32[2048]{0:T(1024)S(1)}, f32[2048]{0:T(1024)}, u32[]{:S(2)}) copy-start(f32[2048]{0:T(1024)} %param.37) | copy-start | bytes 24580
  7.3 24.1 %copy-start.24 = (f32[2048]{0:T(1024)S(1)}, f32[2048]{0:T(1024)}, u32[]{:S(2)}) copy-start(f32[2048]{0:T(1024)} %param.38) | copy-start | bytes 24580
  7.3 24.1 %copy-start.26 = (f32[2048]{0:T(1024)S(1)}, f32[2048]{0:T(1024)}, u32[]{:S(2)}) copy-start(f32[2048]{0:T(1024)} %param.39) | copy-start | bytes 24580
  7.3 24.1 %copy-start.28 = (f32[2048]{0:T(1024)S(1)}, f32[2048]{0:T(1024)}, u32[]{:S(2)}) copy-start(f32[2048]{0:T(1024)} %param.40) | copy-start | bytes 24580
  7.3 159.9 %all-gather.4.cloned.1.call-start = ((), (), s32[]{:S(2)}) async-start(), calls=%async_computation.3 | async-start | bytes 11796480 | tf_op jit(solution)/shard_map/all_gather | solution.py:778
  13.5 314.7 %all-gather.6.cloned.1.call-start = ((), (), s32[]{:S(2)}) async-start(), calls=%async_computation.4 | async-start | bytes 10616832 | tf_op jit(solution)/shard_map/all_gather | solution.py:786
  14.7 414.6 %all-gather.8.cloned.1.call-start = ((), (), s32[]{:S(2)}) async-start(), calls=%async_computation.5 | async-start | bytes 8257536 | tf_op jit(solution)/shard_map/all_gather | solution.py:798
  17.3 156.3 %copy-start.35 = (bf16[2,4,1,128]{3,2,1,0:T(2,128)(2,1)}, bf16[2,4,1,128]{3,2,1,0:T(2,128)(2,1)S(1)}, u32[]{:S(2)}) copy-start(bf16[2,4,1,128]{3,2,1,0:T(2,128)(2,1)S(1)} %get-tuple-element.194) | copy-start | bytes 6148
  17.3 20.4 %collective-permute-start.1 = (bf16[2,4,1,128]{3,2,1,0:T(2,128)(2,1)S(1)}, bf16[2,4,1,128]{3,2,1,0:T(2,128)(2,1)S(1)}, u32[]{:S(2)}, u32[]{:S(2)}) collective-permute-start(bf16[2,4,1,128]{3,2,1,0:T(2,128)(2,1)S(1)} %get-tuple-element.194), channel_id=1, source_target_pairs={{0,4},{4,8},{8,12},{1,5},{5,9},{9,13},{2,6},{6,10},{10,14},{3,7},{... | collective-permute-start | bytes 6152 | tf_op jit(solution)/shard_map/ppermute | solution.py:30
  22.2 15.4 %collective-permute-start.2 = (bf16[2,4,1,128]{3,2,1,0:T(2,128)(2,1)S(1)}, bf16[2,4,1,128]{3,2,1,0:T(2,128)(2,1)S(1)}, u32[]{:S(2)}, u32[]{:S(2)}) collective-permute-start(bf16[2,4,1,128]{3,2,1,0:T(2,128)(2,1)S(1)} %get-tuple-element.194), channel_id=1, source_target_pairs={{0,8},{4,12},{1,9},{5,13},{2,10},{6,14},{3,11},{7,15},{16,24},{20,... | collective-permute-start | bytes 6152 | tf_op jit(solution)/shard_map/ppermute | solution.py:30
  26.7 10.9 %collective-permute-start.3 = (bf16[2,4,1,128]{3,2,1,0:T(2,128)(2,1)S(1)}, bf16[2,4,1,128]{3,2,1,0:T(2,128)(2,1)S(1)}, u32[]{:S(2)}, u32[]{:S(2)}) collective-permute-start(bf16[2,4,1,128]{3,2,1,0:T(2,128)(2,1)S(1)} %get-tuple-element.194), channel_id=1, source_target_pairs={{0,12},{1,13},{2,14},{3,15},{16,28},{17,29},{18,30},{19,31}} | collective-permute-start | bytes 6152 | tf_op jit(solution)/shard_map/ppermute | solution.py:30
  29.3 8.4 collective-permute-start
  186.4 19.0 %collective-permute-start.4 = (bf16[2,4,64,128]{3,2,1,0:T(8,128)(2,1)S(1)}, bf16[2,4,64,128]{3,2,1,0:T(8,128)(2,1)S(1)}, u32[]{:S(2)}, u32[]{:S(2)}) collective-permute-start(bf16[2,4,64,128]{3,2,1,0:T(8,128)(2,1)S(1)} %convert_element_type.338), channel_id=1, source_target_pairs={{0,12},{1,13},{2,14},{3,15},{16,28},{17,29},{18,30},{19,31}} | collective-permute-start | bytes 393224 | tf_op jit(solution)/shard_map/ppermute | solution.py:30
  189.9 15.5 %collective-permute-start.5 = (bf16[2,4,64,128]{3,2,1,0:T(8,128)(2,1)S(1)}, bf16[2,4,64,128]{3,2,1,0:T(8,128)(2,1)S(1)}, u32[]{:S(2)}, u32[]{:S(2)}) collective-permute-start(bf16[2,4,64,128]{3,2,1,0:T(8,128)(2,1)S(1)} %convert_element_type.338), channel_id=1, source_target_pairs={{0,8},{4,12},{1,9},{5,13},{2,10},{6,14},{3,11},{7,15},{16,24},{20,... | collective-permute-start | bytes 393224 | tf_op jit(solution)/shard_map/ppermute | solution.py:30
  191.2 16.3 %collective-permute-start.6 = (bf16[2,4,64,128]{3,2,1,0:T(8,128)(2,1)S(1)}, bf16[2,4,64,128]{3,2,1,0:T(8,128)(2,1)S(1)}, u32[]{:S(2)}, u32[]{:S(2)}) collective-permute-start(bf16[2,4,64,128]{3,2,1,0:T(8,128)(2,1)S(1)} %convert_element_type.338), channel_id=1, source_target_pairs={{0,4},{4,8},{8,12},{1,5},{5,9},{9,13},{2,6},{6,10},{10,14},{3,7},{... | collective-permute-start | bytes 393224 | tf_op jit(solution)/shard_map/ppermute | solution.py:30
  226.2 4.4 collective-permute-start.7
  233.5 47.8 %collective-permute-start.8 = (bf16[512,2048]{1,0:T(8,128)(2,1)S(1)}, bf16[512,2048]{1,0:T(8,128)(2,1)}, u32[]{:S(2)}, u32[]{:S(2)}) collective-permute-start(bf16[512,2048]{1,0:T(8,128)(2,1)S(1)} %add_convert_fusion.5), channel_id=1, source_target_pairs={{0,2},{1,3},{2,0},{3,1},{4,6},{5,7},{6,4},{7,5},{8,10},{9,11},{10,... | collective-permute-start | bytes 6291464 | tf_op jit(solution)/shard_map/ppermute | solution.py:48
  235.1 350.7 %reduce-scatter.4.cloned.1.call-start = ((), (), s32[]{:S(2)}) async-start(), calls=%async_computation.6 | async-start | bytes 8257536 | tf_op jit(solution)/shard_map/reduce_scatter | solution.py:877
  285.0 4.4 collective-permute-start.9
  285.1 21.9 %copy-start.20 = (f32[2048]{0:T(1024)S(1)}, f32[2048]{0:T(1024)}, u32[]{:S(2)}) copy-start(f32[2048]{0:T(1024)} %param.47) | copy-start | bytes 24580
  285.1 21.9 %copy-start.21 = (f32[2048]{0:T(1024)S(1)}, f32[2048]{0:T(1024)}, u32[]{:S(2)}) copy-start(f32[2048]{0:T(1024)} %param.48) | copy-start | bytes 24580
  285.1 21.9 %copy-start.33 = (f32[2048]{0:T(1024)S(1)}, f32[2048]{0:T(1024)}, u32[]{:S(2)}) copy-start(f32[2048]{0:T(1024)} %param.46) | copy-start | bytes 24580
  285.1 21.9 %copy-start.34 = (f32[2048]{0:T(1024)S(1)}, f32[2048]{0:T(1024)}, u32[]{:S(2)}) copy-start(f32[2048]{0:T(1024)} %param.45) | copy-start | bytes 24580
  295.7 12.8 %collective-permute-start.10 = (f32[2,2048]{1,0:T(2,128)S(1)}, f32[2,2048]{1,0:T(2,128)S(1)}, u32[]{:S(2)}, u32[]{:S(2)}) collective-permute-start(f32[2,2048]{1,0:T(2,128)S(1)} %fusion.56), channel_id=1, source_target_pairs={{0,4},{4,8},{8,12},{1,5},{5,9},{9,13},{2,6},{6,10},{10,14},{3,7},{... | collective-permute-start | bytes 49160 | tf_op jit(solution)/shard_map/ppermute | solution.py:25
  338.0 24.3 %collective-permute-start.11 = (bf16[1024,512]{1,0:T(8,128)(2,1)S(1)}, bf16[1024,512]{1,0:T(8,128)(2,1)S(1)}, u32[]{:S(2)}, u32[]{:S(2)}) collective-permute-start(bf16[1024,512]{1,0:T(8,128)(2,1)S(1)} %get-tuple-element.236), channel_id=1, source_target_pairs={{0,2},{1,3},{2,0},{3,1},{4,6},{5,7},{6,4},{7,5},{8,10},{9,11},{10,... | collective-permute-start | bytes 3145736 | tf_op jit(solution)/shard_map/ppermute | solution.py:48
  339.7 37.5 %collective-permute-start.12 = (bf16[1024,512]{1,0:T(8,128)(2,1)S(1)}, bf16[1024,512]{1,0:T(8,128)(2,1)S(1)}, u32[]{:S(2)}, u32[]{:S(2)}) collective-permute-start(bf16[1024,512]{1,0:T(8,128)(2,1)S(1)} %get-tuple-element.236), channel_id=1, source_target_pairs={{0,1},{1,0},{2,3},{3,2},{4,5},{5,4},{6,7},{7,6},{8,9},{9,8},{10,11... | collective-permute-start | bytes 3145736 | tf_op jit(solution)/shard_map/ppermute | solution.py:48
  362.3 16.2 %collective-permute-start.13 = (bf16[1024,512]{1,0:T(8,128)(2,1)S(1)}, bf16[1024,512]{1,0:T(8,128)(2,1)S(1)}, u32[]{:S(2)}, u32[]{:S(2)}) collective-permute-start(bf16[1024,512]{1,0:T(8,128)(2,1)S(1)} %collective-permute-done.11), channel_id=1, source_target_pairs={{0,1},{1,0},{2,3},{3,2},{4,5},{5,4},{6,7},{7,6},{8,9},{9,8},{10,11... | collective-permute-start | bytes 3145736 | tf_op jit(solution)/shard_map/ppermute | solution.py:48
  391.8 406.0 %reduce-scatter.6.cloned.1.call-start = ((), (), s32[]{:S(2)}) async-start(), calls=%async_computation.7 | async-start | bytes 10616832 | tf_op jit(solution)/shard_map/reduce_scatter | solution.py:921
  441.6 2.7 collective-permute-start.15
  441.7 22.8 %collective-permute-start.14 = (bf16[1024,512]{1,0:T(8,128)(2,1)}, bf16[1024,512]{1,0:T(8,128)(2,1)}, u32[]{:S(2)}, u32[]{:S(2)}) collective-permute-start(bf16[1024,512]{1,0:T(8,128)(2,1)} %get-tuple-element.208), channel_id=1, source_target_pairs={{0,1},{1,0},{2,3},{3,2},{4,5},{5,4},{6,7},{7,6},{8,9},{9,8},{10,11... | collective-permute-start | bytes 3145736 | tf_op jit(solution)/shard_map/ppermute | solution.py:48
  444.3 18.2 %slice-start = ((s8[9437184]{0:T(1024)(128)(4,1)}), s8[4194304]{0:T(1024)(128)(4,1)S(1)}, s32[]{:S(2)}) async-start(s8[9437184]{0:T(1024)(128)(4,1)} %bitcast.199), calls=%async_computation.9 | async-start | bytes 8388608
  445.6 25.5 %collective-permute-start.16 = (bf16[1024,512]{1,0:T(8,128)(2,1)}, bf16[1024,512]{1,0:T(8,128)(2,1)}, u32[]{:S(2)}, u32[]{:S(2)}) collective-permute-start(bf16[1024,512]{1,0:T(8,128)(2,1)} %add_convert_fusion.7), channel_id=1, source_target_pairs={{0,2},{1,3},{2,0},{3,1},{4,6},{5,7},{6,4},{7,5},{8,10},{9,11},{10,... | collective-permute-start | bytes 3145736 | tf_op jit(solution)/shard_map/ppermute | solution.py:48
  447.2 15.4 %slice-start.1 = ((s8[9437184]{0:T(1024)(128)(4,1)}), s8[4194304]{0:T(1024)(128)(4,1)S(1)}, s32[]{:S(2)}) async-start(s8[9437184]{0:T(1024)(128)(4,1)} %bitcast.199), calls=%async_computation.10 | async-start | bytes 8388608
  447.2 15.4 %slice-start.2 = ((s8[9437184]{0:T(1024)(128)(4,1)}), s8[1048576]{0:T(1024)(128)(4,1)S(1)}, s32[]{:S(2)}) async-start(s8[9437184]{0:T(1024)(128)(4,1)} %bitcast.199), calls=%async_computation.11 | async-start | bytes 2097152
  476.5 6.2 collective-permute-start.17
  529.8 4.2 collective-permute-start.18
  534.9 12.4 %copy-start.1 = (bf16[512,2048]{1,0:T(8,128)(2,1)}, bf16[512,2048]{1,0:T(8,128)(2,1)S(1)}, u32[]{:S(2)}) copy-start(bf16[512,2048]{1,0:T(8,128)(2,1)S(1)} %add_convert_fusion.3) | copy-start | bytes 6291460
  534.9 47.8 %collective-permute-start.19 = (bf16[512,2048]{1,0:T(8,128)(2,1)S(1)}, bf16[512,2048]{1,0:T(8,128)(2,1)}, u32[]{:S(2)}, u32[]{:S(2)}) collective-permute-start(bf16[512,2048]{1,0:T(8,128)(2,1)S(1)} %add_convert_fusion.3), channel_id=1, source_target_pairs={{0,2},{1,3},{2,0},{3,1},{4,6},{5,7},{6,4},{7,5},{8,10},{9,11},{10,... | collective-permute-start | bytes 6291464 | tf_op jit(solution)/shard_map/ppermute | solution.py:48
  585.8 340.9 %reduce-scatter.8.cloned.1.call-start = ((), (), s32[]{:S(2)}) async-start(), calls=%async_computation.8 | async-start | bytes 4718592 | tf_op jit(solution)/shard_map/reduce_scatter | solution.py:987
  586.1 4.4 collective-permute-start.20
  637.5 60.0 %collective-permute-start.27 = (bf16[2,2,256,1024]{2,3,0,1:T(8,128)(2,1)}, bf16[2,2,256,1024]{2,3,0,1:T(8,128)(2,1)}, u32[]{:S(2)}, u32[]{:S(2)}) collective-permute-start(bf16[2,2,256,1024]{2,3,0,1:T(8,128)(2,1)} %bitcast.189), channel_id=1, source_target_pairs={{0,16},{16,0},{1,17},{17,1},{2,18},{18,2},{3,19},{19,3},{4,20},{20... | collective-permute-start | bytes 6291464 | tf_op jit(solution)/shard_map/ppermute | solution.py:101
  639.2 6.9 collective-permute-start.21
  640.5 7.2 collective-permute-start.22
  642.2 9.4 %collective-permute-start.23 = (bf16[2,4,1,128]{3,2,1,0:T(2,128)(2,1)S(1)}, bf16[2,4,1,128]{3,2,1,0:T(2,128)(2,1)S(1)}, u32[]{:S(2)}, u32[]{:S(2)}) collective-permute-start(bf16[2,4,1,128]{3,2,1,0:T(2,128)(2,1)S(1)} %copy-done.36), channel_id=1, source_target_pairs={{12,0},{13,1},{14,2},{15,3},{28,16},{29,17},{30,18},{31,19}} | collective-permute-start | bytes 6152 | tf_op jit(solution)/shard_map/ppermute | solution.py:30
  647.8 12.9 %collective-permute-start.24 = (bf16[2,4,64,128]{3,2,1,0:T(8,128)(2,1)S(1)}, bf16[2,4,64,128]{3,2,1,0:T(8,128)(2,1)S(1)}, u32[]{:S(2)}, u32[]{:S(2)}) collective-permute-start(bf16[2,4,64,128]{3,2,1,0:T(8,128)(2,1)S(1)} %convert_element_type.381), channel_id=1, source_target_pairs={{12,0},{13,1},{14,2},{15,3},{28,16},{29,17},{30,18},{31,19}} | collective-permute-start | bytes 393224 | tf_op jit(solution)/shard_map/ppermute | solution.py:30
  649.1 20.6 %collective-permute-start.25 = (bf16[2,4,64,128]{3,2,1,0:T(8,128)(2,1)S(1)}, bf16[2,4,64,128]{3,2,1,0:T(8,128)(2,1)S(1)}, u32[]{:S(2)}, u32[]{:S(2)}) collective-permute-start(bf16[2,4,64,128]{3,2,1,0:T(8,128)(2,1)S(1)} %convert_element_type.381), channel_id=1, source_target_pairs={{8,0},{12,4},{9,1},{13,5},{10,2},{14,6},{11,3},{15,7},{24,16},{28,... | collective-permute-start | bytes 393224 | tf_op jit(solution)/shard_map/ppermute | solution.py:30
  650.4 19.3 %collective-permute-start.26 = (bf16[2,4,64,128]{3,2,1,0:T(8,128)(2,1)S(1)}, bf16[2,4,64,128]{3,2,1,0:T(8,128)(2,1)S(1)}, u32[]{:S(2)}, u32[]{:S(2)}) collective-permute-start(bf16[2,4,64,128]{3,2,1,0:T(8,128)(2,1)S(1)} %convert_element_type.381), channel_id=1, source_target_pairs={{4,0},{8,4},{12,8},{5,1},{9,5},{13,9},{6,2},{10,6},{14,10},{7,3},{... | collective-permute-start | bytes 393224 | tf_op jit(solution)/shard_map/ppermute | solution.py:30
  705.1 75.7 %collective-permute-start.30 = (bf16[2,2,256,512]{3,2,1,0:T(8,128)(2,1)}, bf16[2,2,256,512]{3,2,1,0:T(8,128)(2,1)}, u32[]{:S(2)}, u32[]{:S(2)}) collective-permute-start(bf16[2,2,256,512]{3,2,1,0:T(8,128)(2,1)} %dynamic-slice_bitcast_fusion), channel_id=1, source_target_pairs={{0,16},{16,0},{1,17},{17,1},{2,18},{18,2},{3,19},{19,3},{4,20},{20... | collective-permute-start | bytes 3145736 | tf_op jit(solution)/shard_map/ppermute | solution.py:101
  726.4 5.6 collective-permute-start.28
  735.1 60.0 %collective-permute-start.29 = (bf16[2,256,1024]{1,2,0:T(8,128)(2,1)}, bf16[2,256,1024]{1,2,0:T(8,128)(2,1)}, u32[]{:S(2)}, u32[]{:S(2)}) collective-permute-start(bf16[2,256,1024]{1,2,0:T(8,128)(2,1)} %dynamic-slice_bitcast_fusion.1), channel_id=1, source_target_pairs={{0,4},{4,0},{8,12},{12,8},{1,5},{5,1},{9,13},{13,9},{2,6},{6,2},{1... | collective-permute-start | bytes 3145736 | tf_op jit(solution)/shard_map/ppermute | solution.py:101
  801.0 4.5 collective-permute-start.31
  801.1 14.7 %copy-start.19 = (f32[8,2048]{1,0:T(8,128)S(1)}, f32[8,2048]{1,0:T(8,128)}, u32[]{:S(2)}) copy-start(f32[8,2048]{1,0:T(8,128)} %get-tuple-element.102) | copy-start | bytes 196612
  809.9 71.1 %collective-permute-start.39 = (bf16[512,2048]{1,0:T(8,128)(2,1)}, bf16[512,2048]{1,0:T(8,128)(2,1)}, u32[]{:S(2)}, u32[]{:S(2)}) collective-permute-start(bf16[512,2048]{1,0:T(8,128)(2,1)} %add_convert_fusion.1), channel_id=1, source_target_pairs={{0,2},{1,3},{2,0},{3,1},{4,6},{5,7},{6,4},{7,5},{8,10},{9,11},{10,... | collective-permute-start | bytes 6291464 | tf_op jit(solution)/shard_map/ppermute | solution.py:48
  814.8 50.9 %collective-permute-start.37 = (bf16[256,1024]{0,1:T(8,128)(2,1)}, bf16[256,1024]{0,1:T(8,128)(2,1)}, u32[]{:S(2)}, u32[]{:S(2)}) collective-permute-start(bf16[256,1024]{0,1:T(8,128)(2,1)} %dynamic-slice_bitcast_fusion.3), channel_id=1, source_target_pairs={{0,8},{4,12},{8,0},{12,4},{1,9},{5,13},{9,1},{13,5},{2,10},{6,14},... | collective-permute-start | bytes 1572872 | tf_op jit(solution)/shard_map/ppermute | solution.py:101
  815.8 5.0 collective-permute-start.32
  818.1 59.2 %collective-permute-start.38 = (bf16[2,256,512]{2,1,0:T(8,128)(2,1)}, bf16[2,256,512]{2,1,0:T(8,128)(2,1)}, u32[]{:S(2)}, u32[]{:S(2)}) collective-permute-start(bf16[2,256,512]{2,1,0:T(8,128)(2,1)} %dynamic-slice_bitcast_fusion.2), channel_id=1, source_target_pairs={{0,4},{4,0},{8,12},{12,8},{1,5},{5,1},{9,13},{13,9},{2,6},{6,2},{1... | collective-permute-start | bytes 1572872 | tf_op jit(solution)/shard_map/ppermute | solution.py:101
  820.8 1.4 collective-permute-start.33
  822.3 40.1 %collective-permute-start.34 = (f32[14,2048]{1,0:T(8,128)S(1)}, f32[14,2048]{1,0:T(8,128)S(1)}, u32[]{:S(2)}, u32[]{:S(2)}) collective-permute-start(f32[14,2048]{1,0:T(8,128)S(1)} %add.287), channel_id=1, source_target_pairs={{0,4},{4,0},{8,12},{12,8},{1,5},{5,1},{9,13},{13,9},{2,6},{6,2},{1... | collective-permute-start | bytes 344072 | tf_op jit(solution)/shard_map/ppermute | solution.py:101
  862.4 13.1 %collective-permute-start.35 = (f32[14,2048]{1,0:T(8,128)S(1)}, f32[14,2048]{1,0:T(8,128)S(1)}, u32[]{:S(2)}, u32[]{:S(2)}) collective-permute-start(f32[14,2048]{1,0:T(8,128)S(1)} %add.288), channel_id=1, source_target_pairs={{0,8},{4,12},{8,0},{12,4},{1,9},{5,13},{9,1},{13,5},{2,10},{6,14},... | collective-permute-start | bytes 344072 | tf_op jit(solution)/shard_map/ppermute | solution.py:101
  875.5 5.5 collective-permute-start.36
  885.6 13.4 %collective-permute-start.40 = (bf16[512,2048]{1,0:T(8,128)(2,1)}, bf16[512,2048]{1,0:T(8,128)(2,1)}, u32[]{:S(2)}, u32[]{:S(2)}) collective-permute-start(bf16[512,2048]{1,0:T(8,128)(2,1)} %add_convert_fusion), channel_id=1, source_target_pairs={{0,1},{1,0},{2,3},{3,2},{4,5},{5,4},{6,7},{7,6},{8,9},{9,8},{10,11... | collective-permute-start | bytes 6291464 | tf_op jit(solution)/shard_map/ppermute | solution.py:48
  895.4 26.1 %collective-permute-start.41 = (bf16[256,512]{1,0:T(8,128)(2,1)}, bf16[256,512]{1,0:T(8,128)(2,1)}, u32[]{:S(2)}, u32[]{:S(2)}) collective-permute-start(bf16[256,512]{1,0:T(8,128)(2,1)} %get-tuple-element.211), channel_id=1, source_target_pairs={{0,8},{4,12},{8,0},{12,4},{1,9},{5,13},{9,1},{13,5},{2,10},{6,14},... | collective-permute-start | bytes 786440 | tf_op jit(solution)/shard_map/ppermute | solution.py:101
  (33 other events, 230.8 us)
Sparse Core Ops, SparseCore 0:
  13.6 153.5 all-gather.3
  169.9 146.5 all-gather.5
  318.5 110.7 all-gather.7
  432.7 131.4 reduce-scatter.3
  586.0 208.3 reduce-scatter.5
  801.2 125.5 reduce-scatter.7
